TPU v7x, 256 devices: a whole 4x4x8 slice. The times are simulated.
256 devices in a mesh: wide: 32 (over x, z_lo, core), narrow: 8 (over z_hi, y).
Axes of the slice: x: 4, y: 4, z: 8 (z_hi: 2, z_lo: 4; z = z_hi * 4 + z_lo), core: 2. Of those that a mesh axis runs over, the one named last changes fastest.
Arguments:
- tensor: bfloat16 [16, 8192, 8192], P(None, 'wide', 'narrow'), may hold values from -100 to 100
- first_factor: bfloat16 [16, 256], replicated, may hold values from -8 to 8
- third_factor: bfloat16 [8192, 256], P('narrow'), may hold values from -10 to 10
Outputs:
- second_factor: bfloat16 [8192, 256], P('wide')
- third_new: bfloat16 [8192, 256], P('narrow')
- first_mode: float32 [16, 256], replicated
All inputs are finite; a program needn't handle non-finite values.
Results may differ from a plain program's by a relative error of at most 0.008.
Values may be sent and summed in bfloat16 or wider, within the bound.
No kernel may reach another device: no remote copies, remote signals or barrier semaphores. Data moves between devices by JAX's collectives and lax.ppermute only.
A program may use at most 128 MiB of HBM per device.

v0:
```python
import math

import jax
import jax.numpy as jnp
from jax import lax
from jax.sharding import PartitionSpec as P

ridge = 0.5


def solve_rows(rows, system):
    lower = jnp.linalg.cholesky(system)
    return jax.scipy.linalg.cho_solve((lower, True), rows.T).T


def on_device(tensor, first_factor, third_factor):
    window, second_local, third_local = tensor.shape
    rank = first_factor.shape[1]
    second_total = second_local * lax.axis_size("wide")
    third_total = third_local * lax.axis_size("narrow")
    first_wide = first_factor.astype(jnp.float32)
    identity = jnp.eye(rank, dtype=jnp.float32)
    gram_first = jnp.dot(first_factor.T, first_factor, preferred_element_type=jnp.float32) / window
    gram_part = jnp.dot(third_factor.T, third_factor, preferred_element_type=jnp.float32)
    gram_third = lax.psum(gram_part, "narrow") / third_total
    system_second = gram_first * gram_third + ridge * identity
    contracted = jnp.dot(
        tensor.reshape(window * second_local, third_local),
        third_factor,
        preferred_element_type=jnp.float32,
    )
    contracted = contracted.reshape(window, second_local, rank)
    partial_second = jnp.einsum(
        "ijr,ir->jr", contracted, first_wide, precision=lax.Precision.HIGHEST
    ) / math.sqrt(window * third_total)
    mttkrp_second = lax.psum(partial_second, "narrow")
    second_factor = solve_rows(mttkrp_second, system_second).astype(jnp.bfloat16)
    gram_local = jnp.dot(second_factor.T, second_factor, preferred_element_type=jnp.float32)
    gram_second = lax.psum(gram_local, "wide") / second_total
    system_third = gram_first * gram_second + ridge * identity
    middle = jnp.einsum("ijk,jr->ikr", tensor, second_factor, preferred_element_type=jnp.float32)
    partial_third = jnp.einsum(
        "ikr,ir->kr", middle, first_wide, precision=lax.Precision.HIGHEST
    ) / math.sqrt(window * second_total)
    mttkrp_third = lax.psum(partial_third, "wide")
    third_solution = solve_rows(mttkrp_third, system_third)
    third_new = third_solution.astype(jnp.bfloat16)
    partial_first = jnp.einsum(
        "ikr,kr->ir", middle, third_solution, precision=lax.Precision.HIGHEST
    ) / math.sqrt(second_total * third_total)
    first_mode = lax.psum(partial_first, ("wide", "narrow"))
    return (second_factor, third_new, first_mode)


def solution(mesh):
    in_specs = (P(None, "wide", "narrow"), P(), P("narrow", None))
    out_specs = (P("wide", None), P("narrow", None), P())
    return jax.shard_map(
        on_device, mesh=mesh, in_specs=in_specs, out_specs=out_specs, check_vma=False
    )
```

profile of v0, /device:TPU:1, one launch (start us, length us, event | category | flops | bytes accessed | tf_op | source)
XLA Modules:
  0.0 683.6 jit_solution(7579650863137644660)
XLA Ops:
  7.2 0.7 bitcast_convert_fusion.1
  8.2 1.0 fusion.37
  9.3 5.7 multiply_reduce_fusion
  15.2 0.7 broadcast_multiply_fusion
  15.9 0.5 all-reduce.6.cloned.1.call-start
  16.6 107.2 %all-reduce.8.cloned.1.call-done = (f32[256,256]{1,0:T(8,128)}, f32[256,256]{0,1:T(8,128)}) async-done(((f32[256,256]{1,0:T(8,128)}, f32[256,256]{0,1:T(8,128)}), (f32[256,256]{1,0:T(8,128)}, f32[256,256]{0,1:T(8,128)})) %all-reduce.8.cloned.1.call-update) | async-done | bytes 524304 | tf_op jit(solution)/shard_map/psum | solution.py:36
  123.8 1.2 select_add_fusion.1
  125.2 11.7 %cholesky.130 = f32[128,128]{1,0:T(8,128)S(1)} custom-call(f32[128,128]{1,0:T(8,128)S(1)} %cholesky.194), custom_call_target="Cholesky" | custom-call | tf_op jit(solution)/shard_map/jit(cholesky)/cholesky | solution.py:12
  136.9 9.8 %custom-call.25 = f32[1,128,128]{1,2,0:T(8,128)S(1)} custom-call(f32[1,128,128]{2,1,0:T(8,128)S(1)} %get-tuple-element.58), custom_call_target="InvertDiagBlocksLowerTriangular" | custom-call | tf_op jit(solution)/shard_map/jit(cholesky)/cholesky | solution.py:12
  147.2 11.7 %cholesky.147 = f32[128,128]{1,0:T(8,128)S(1)} custom-call(f32[128,128]{1,0:T(8,128)S(1)} %convolution_subtract_fusion.5), custom_call_target="Cholesky" | custom-call | tf_op jit(solution)/shard_map/jit(cholesky)/cholesky | solution.py:12
  159.3 0.7 compare_reduce_fusion.2
  161.4 4.4 while.2
  161.6 0.6 fusion.61
  162.2 1.4 dynamic-slice.13
  163.7 0.6 fusion.61
  164.3 1.4 dynamic-slice.13
  165.8 19.7 %custom-call.22 = f32[2,128,128]{1,2,0:T(8,128)S(1)} custom-call(f32[2,128,128]{2,1,0:T(8,128)S(1)} %get-tuple-element.11), custom_call_target="InvertDiagBlocksLowerTriangular" | custom-call | tf_op jit(solution)/shard_map/jit(_cho_solve)/triangular_solve | solution.py:13
  185.5 1.2 fusion.11
  186.7 1.2 convolution_subtract_fusion.3
  187.9 0.3 fusion.21
  189.0 5.7 convolution_bitcast_fusion
  194.8 1.1 fusion.29
  195.9 4.6 copy-done.1
  200.6 13.3 %fusion.2 = f32[256,1,1024]{2,1,0:T(1,128)S(1)} fusion(bf16[16,256,1]{0,2,1:T(2,128)(2,1)S(1)} %copy.32, f32[16,1024,256]{1,2,0:T(8,128)S(1)} %convolution_bitcast_fusion), kind=kOutput, calls=%fused_computation.6 | convolution fusion | flops 50331648 | bytes 17833984 | tf_op jit(solution)/shard_map/ikr,ir->kr/dot_general | solution.py:42
  213.9 1.3 bitcast_multiply_fusion
  215.2 0.8 copy.19
  216.0 281.6 %all-reduce.6.cloned.1.call-done = (f32[256,1024]{1,0:T(8,128)}, f32[256,256]{0,1:T(8,128)}) async-done(((f32[256,1024]{1,0:T(8,128)}, f32[256,256]{0,1:T(8,128)}), (f32[256,1024]{1,0:T(8,128)}, f32[256,256]{0,1:T(8,128)})) %all-reduce.6.cloned.1.call-update) | async-done | bytes 1310736 | tf_op jit(solution)/shard_map/psum | solution.py:45
  497.6 1.0 select_add_fusion
  498.7 11.7 %cholesky.164 = f32[128,128]{1,0:T(8,128)S(1)} custom-call(f32[128,128]{1,0:T(8,128)S(1)} %cholesky.197), custom_call_target="Cholesky" | custom-call | tf_op jit(solution)/shard_map/jit(cholesky)/cholesky | solution.py:12
  510.5 9.8 %custom-call.26 = f32[1,128,128]{1,2,0:T(8,128)S(1)} custom-call(f32[1,128,128]{2,1,0:T(8,128)S(1)} %get-tuple-element.56), custom_call_target="InvertDiagBlocksLowerTriangular" | custom-call | tf_op jit(solution)/shard_map/jit(cholesky)/cholesky | solution.py:12
  520.8 11.7 %cholesky.181 = f32[128,128]{1,0:T(8,128)S(1)} custom-call(f32[128,128]{1,0:T(8,128)S(1)} %convolution_subtract_fusion.4), custom_call_target="Cholesky" | custom-call | tf_op jit(solution)/shard_map/jit(cholesky)/cholesky | solution.py:12
  532.8 0.6 compare_reduce_fusion
  533.5 0.6 compare_reduce_fusion.1
  535.4 4.1 while.3
  535.5 0.6 fusion.62
  536.1 1.3 dynamic-slice.15
  537.5 0.6 fusion.62
  538.1 1.3 dynamic-slice.15
  539.5 19.8 %custom-call.23 = f32[2,128,128]{1,2,0:T(8,128)S(1)} custom-call(f32[2,128,128]{2,1,0:T(8,128)S(1)} %get-tuple-element.19), custom_call_target="InvertDiagBlocksLowerTriangular" | custom-call | tf_op jit(solution)/shard_map/jit(_cho_solve)/triangular_solve | solution.py:13
  559.4 1.7 fusion.6
  561.0 1.7 convolution_subtract_fusion.1
  562.7 0.6 fusion.24
  563.4 0.6 fusion.23
  564.0 0.6 convolution_subtract_fusion
  564.5 0.6 fusion.22
  565.3 32.0 %fusion = f32[256,1,16]{2,1,0:T(1,128)S(1)} fusion(f32[16,1024,256]{1,2,0:T(8,128)} %copy-done.1, f32[1024,256,1]{0,1,2:T(8,128)S(1)} %fusion.5), kind=kOutput, calls=%fused_computation.4 | convolution fusion | flops 50331648 | bytes 17842176 | tf_op jit(solution)/shard_map/ikr,kr->ir/dot_general | solution.py:48
  597.4 78.2 %psum.39 = f32[16,256]{1,0:T(8,128)} all-reduce(f32[16,256]{1,0:T(8,128)S(1)} %fusion.31), channel_id=1, replica_groups=mesh['wide'=32,'narrow'=8] {'wide','narrow'}, use_global_device_ids=true, to_apply=%region_8.10 | all-reduce | flops 4096 | bytes 32768 | tf_op jit(solution)/shard_map/psum | solution.py:51
  675.6 1.0 copy.20
  (62 shorter events, 4.3 us)
Async XLA Ops:
  7.2 1.1 copy-start
  7.2 9.3 %copy-start.2 = (bf16[16,256]{1,0:T(8,128)(2,1)S(1)}, bf16[16,256]{1,0:T(8,128)(2,1)}, u32[]{:S(2)}) copy-start(bf16[16,256]{1,0:T(8,128)(2,1)} %param.5) | copy-start | bytes 24580
  7.2 116.6 %all-reduce.8.cloned.1.call-start = ((), (), s32[]{:S(2)}) async-start(), calls=%async_computation.1 | async-start | bytes 1048576 | tf_op jit(solution)/shard_map/psum | solution.py:36
  15.9 481.6 %all-reduce.6.cloned.1.call-start = ((), (), s32[]{:S(2)}) async-start(), calls=%async_computation | async-start | bytes 2621440 | tf_op jit(solution)/shard_map/psum | solution.py:45
  194.8 5.8 copy-start.1
Sparse Core Ops, SparseCore 0:
  16.0 107.7 all-reduce.7
  215.3 282.2 all-reduce.5
where the time goes:
time: 687 us; the launch traced here: 684 us
  waiting for transfers between devices  389 us (57%)
  other arithmetic  112 us (16%)
  blocking collectives  78.2 us (11%)
  matrix products  70.3 us (10%)
  between operations  17.1 us (2%)
  local copies, waits for them, and re-layouts  16 us (2%)
    psum x1, waiting for transfers between devices, on_device(): mttkrp_third = lax.psum(partial_third, 'wide')  282 us
    psum x1, waiting for transfers between devices, on_device(): mttkrp_second = lax.psum(partial_second, 'narrow')  107 us
    psum x1, blocking collectives, on_device(): first_mode = lax.psum(partial_first, ('wide', 'narrow'))  78.2 us
    another operation x13, other arithmetic, solve_rows(): lower = jnp.linalg.cholesky(system)  68.6 us
    another operation x5, other arithmetic, solve_rows(): return jax.scipy.linalg.cho_solve((lower, True), rows.T).T  39.6 us
    dot_general x1, matrix products, on_device(): jnp.einsum('ikr,kr->ir', middle, third_solution, precision=lax.Precision....  32 us
  transfers between devices with their start and end apart: 2, of which 2 were waited for; matrix products, arithmetic and copies ran while one was open for 0% of the time, Pallas kernels for 0%

commit v1 on v0

v1 whole, which is shorter than its diff:
```python
import math

import jax
import jax.numpy as jnp
from jax import lax
from jax.experimental import pallas as pl
from jax.experimental.pallas import tpu as pltpu
from jax.sharding import Mesh, PartitionSpec as P

ridge = 0.5
B = 16
WIDE = ("x", "zl", "core")
CHIP = ("x", "zl")
NARROW = ("zh", "y")
HIGHEST = lax.Precision.HIGHEST


def pieces(x):
    high = x.astype(jnp.bfloat16)
    rest = x - high.astype(jnp.float32)
    middle = rest.astype(jnp.bfloat16)
    low = (rest - middle.astype(jnp.float32)).astype(jnp.bfloat16)
    return high, middle, low


def inverse_kernel(s_ref, x_ref, m_ref, w_ref):
    n = s_ref.shape[0]
    m_ref[...] = s_ref[...]
    row = lax.broadcasted_iota(jnp.int32, (B, n), 0)
    lane = lax.broadcasted_iota(jnp.int32, (B, n), 1)
    half_row = lax.broadcasted_iota(jnp.int32, (B, 128), 0)
    whole_row = lax.broadcasted_iota(jnp.int32, (n, n), 0)
    whole_lane = lax.broadcasted_iota(jnp.int32, (n, n), 1)

    def step(k, carry):
        o = pl.multiple_of(k * B, B)
        panel = m_ref[pl.ds(o, B), :]
        front = pltpu.roll(panel, n - o, 1)
        cols = [jnp.broadcast_to(front[:, j:j + 1], (B, 128)) for j in range(B)]
        inside = (lane >= o) & (lane < o + B)
        unit = jnp.where(lane - o == row, 1.0, 0.0)
        work = jnp.where(inside, unit, panel)
        parts = [work[:, t * 128:(t + 1) * 128] for t in range(n // 128)]
        for j in range(B):
            col = cols[j]
            scale = 1.0 / col[j:j + 1, :]
            other = half_row != j
            for t in range(len(parts)):
                pivot = parts[t][j:j + 1, :] * scale
                parts[t] = jnp.where(other, parts[t] - col * pivot, pivot)
            for m in range(j + 1, B):
                pivot = cols[m][j:j + 1, :] * scale
                cols[m] = jnp.where(other, cols[m] - col * pivot, pivot)
        solved = jnp.concatenate(parts, axis=1)
        below = jnp.where(lane >= o + B, panel, 0.0)
        uh, um, ul = pieces(below)
        wh, wm, wl = pieces(solved)
        left = jnp.concatenate([uh, uh, um, uh, ul, um], axis=0)
        right = jnp.concatenate([wh, wm, wh, wl, wh, wm], axis=0)
        update = lax.dot_general(
            left, right, (((0,), (0,)), ((), ())), preferred_element_type=jnp.float32
        )
        cleared = (whole_row >= o + B) & (whole_lane >= o) & (whole_lane < o + B)
        m_ref[...] = jnp.where(cleared, 0.0, m_ref[...]) - update
        m_ref[pl.ds(o, B), :] = jnp.where(lane < o, panel, jnp.where(inside, unit, 0.0))
        w_ref[pl.ds(o, B), :] = jnp.where(lane < o + B, solved, 0.0)
        return carry

    lax.fori_loop(0, n // B, step, 0)
    x_ref[...] = lax.dot_general(
        m_ref[...], w_ref[...], (((0,), (0,)), ((), ())),
        precision=lax.Precision.HIGHEST, preferred_element_type=jnp.float32,
    )


def inverse(s):
    n = s.shape[0]
    return pl.pallas_call(
        inverse_kernel,
        out_shape=jax.ShapeDtypeStruct((n, n), jnp.float32),
        in_specs=[pl.BlockSpec(memory_space=pltpu.VMEM)],
        out_specs=pl.BlockSpec(memory_space=pltpu.VMEM),
        scratch_shapes=[pltpu.VMEM((n, n), jnp.float32), pltpu.VMEM((n, n), jnp.float32)],
        name="inverse",
    )(s)


def middle_kernel(t_ref, s_ref, f_ref, o_ref):
    i = pl.program_id(0)
    product = jnp.dot(s_ref[...], t_ref[0], preferred_element_type=jnp.float32)
    term = f_ref[0] * product

    @pl.when(i == 0)
    def _():
        o_ref[...] = term

    @pl.when(i > 0)
    def _():
        o_ref[...] += term


def third_products(tensor, second_t, first_columns):
    window, second_local, third_local = tensor.shape
    rank = second_t.shape[0]
    flops = 2 * window * second_local * third_local * rank
    return pl.pallas_call(
        middle_kernel,
        grid=(window,),
        out_shape=jax.ShapeDtypeStruct((rank, third_local), jnp.float32),
        in_specs=[
            pl.BlockSpec((1, second_local, third_local), lambda i: (i, 0, 0)),
            pl.BlockSpec((rank, second_local), lambda i: (0, 0)),
            pl.BlockSpec((1, rank, 1), lambda i: (i, 0, 0)),
        ],
        out_specs=pl.BlockSpec((rank, third_local), lambda i: (0, 0)),
        cost_estimate=pl.CostEstimate(flops=flops, bytes_accessed=tensor.size * 2, transcendentals=0),
        name="third_products",
    )(tensor, second_t, first_columns)


def first_kernel(t_ref, v_ref, s_ref, o_ref):
    product = jnp.dot(t_ref[0], v_ref[...], preferred_element_type=jnp.float32)
    o_ref[0] = jnp.sum(product * s_ref[...], axis=0, keepdims=True)


def first_products(tensor, third_new, second_wide):
    window, second_local, third_local = tensor.shape
    rank = third_new.shape[1]
    flops = 2 * window * second_local * third_local * rank
    out = pl.pallas_call(
        first_kernel,
        grid=(window,),
        out_shape=jax.ShapeDtypeStruct((window, 1, rank), jnp.float32),
        in_specs=[
            pl.BlockSpec((1, second_local, third_local), lambda i: (i, 0, 0)),
            pl.BlockSpec((third_local, rank), lambda i: (0, 0)),
            pl.BlockSpec((second_local, rank), lambda i: (0, 0)),
        ],
        out_specs=pl.BlockSpec((1, 1, rank), lambda i: (i, 0, 0)),
        cost_estimate=pl.CostEstimate(flops=flops, bytes_accessed=tensor.size * 2, transcendentals=0),
        name="first_products",
    )(tensor, third_new, second_wide)
    return out.reshape(window, rank)


def exchange(x, axes):
    return lax.all_to_all(x, axes, 0, 0, tiled=True)


def scatter_sum(x, axes):
    n = lax.axis_size(axes)
    return jnp.sum(exchange(x.reshape(n, x.shape[0] // n, x.shape[1]), axes), axis=0)


def gather(x, axes):
    n = lax.axis_size(axes)
    return exchange(jnp.broadcast_to(x[None], (n,) + x.shape), axes).reshape(n * x.shape[0], x.shape[1])


def gather_sum(x, axes):
    n = lax.axis_size(axes)
    return jnp.sum(exchange(jnp.broadcast_to(x[None], (n,) + x.shape), axes), axis=0)


def swap(x):
    return lax.ppermute(x, "core", [(0, 1), (1, 0)])


def on_device(tensor, first_factor, third_factor):
    window, second_local, third_local = tensor.shape
    rank = first_factor.shape[1]
    second_total = second_local * lax.axis_size(WIDE)
    third_total = third_local * lax.axis_size(NARROW)
    core = lax.axis_index("core")
    first_wide = first_factor.astype(jnp.float32)
    identity = jnp.eye(rank, dtype=jnp.float32)
    gram_first = jnp.dot(first_factor.T, first_factor, preferred_element_type=jnp.float32) / window

    gram_part = jnp.dot(third_factor.T, third_factor, preferred_element_type=jnp.float32)
    gram_third = gather(scatter_sum(gram_part, NARROW), NARROW) / third_total
    inverse_second = inverse(gram_first * gram_third + ridge * identity)

    contracted = jnp.dot(
        tensor.reshape(window * second_local, third_local),
        third_factor,
        preferred_element_type=jnp.float32,
    ).reshape(window, second_local, rank)
    partial_second = jnp.einsum(
        "ijr,ir->jr", contracted, first_wide, precision=HIGHEST
    ) / math.sqrt(window * third_total)
    mttkrp_second = gather(scatter_sum(partial_second, NARROW), NARROW)
    second_factor = jnp.dot(mttkrp_second, inverse_second, precision=HIGHEST).astype(jnp.bfloat16)

    gram_local = jnp.dot(second_factor.T, second_factor, preferred_element_type=jnp.float32)
    gram_second = gather(scatter_sum(gram_local, WIDE), WIDE) / second_total
    inverse_third = inverse(gram_first * gram_second + ridge * identity)

    partial_third = third_products(tensor, second_factor.T, first_wide[:, :, None])
    partial_third = partial_third / math.sqrt(window * second_total)
    halves = partial_third.reshape(2, rank // 2, third_local)
    mine = jnp.where(core == 0, halves[0], halves[1])
    other = jnp.where(core == 0, halves[1], halves[0])
    mine = mine + swap(other)
    mine = gather(scatter_sum(mine, CHIP), CHIP)
    theirs = swap(mine)
    mttkrp_third = jnp.where(
        core == 0, jnp.concatenate([mine, theirs], 0), jnp.concatenate([theirs, mine], 0)
    )
    third_solution = jnp.dot(inverse_third, mttkrp_third, precision=HIGHEST)
    third_new = third_solution.astype(jnp.bfloat16).T

    partial_first = first_products(tensor, third_new, second_factor.astype(jnp.float32))
    partial_first = partial_first / math.sqrt(second_total * third_total)
    partial_first = partial_first + swap(partial_first)
    first_mode = gather_sum(gather_sum(partial_first, CHIP), NARROW)
    return (second_factor, third_new, first_mode)


def solution(mesh):
    fine = Mesh(mesh.devices.reshape(4, 4, 2, 2, 4), WIDE + NARROW)
    in_specs = (P(None, WIDE, NARROW), P(), P(NARROW, None))
    out_specs = (P(WIDE, None), P(NARROW, None), P())
    return jax.shard_map(
        on_device, mesh=fine, in_specs=in_specs, out_specs=out_specs, check_vma=False
    )
```

time: 687 us -> 235 us (0.34)
  waiting for transfers between devices: 389 us -> 76.9 us
  other arithmetic: 112 us -> 5.99 us
  matrix products: 70.3 us -> 14.2 us
  starting transfers between devices: 0.54 us -> 49.8 us
  Pallas kernels: 0 us -> 47.1 us
  blocking collectives: 78.2 us -> 31.3 us
  between operations: 17.1 us -> 0.81 us
  local copies, waits for them, and re-layouts: 16 us -> 6.83 us
    psum x2 -> x0, waiting for transfers between devices: 389 us -> none  [the longest x1 282 us: on_device(): mttkrp_third = lax.psum(partial_third, 'wide')]
    another operation x18 -> x0, other arithmetic: 108 us -> none  [the longest x13 68.6 us: solve_rows(): lower = jnp.linalg.cholesky(system)]
    psum x1 -> x0, blocking collectives: 78.2 us -> none  [on_device(): first_mode = lax.psum(partial_first, ('wide', 'narrow'))]
    all_to_all x0 -> x8, waiting for transfers between devices: none -> 74.2 us  [exchange(): return lax.all_to_all(x, axes, 0, 0, tiled=True)]
    pallas_call x0 -> x4, Pallas kernels: none -> 47.1 us  [the longest x2 21 us: inverse(): pl.pallas_call(inverse_kernel, out_shape=jax.ShapeDtypeStruct((n, n), jnp...]
    dot_general x3 -> x2, matrix products: 51 us -> 5.6 us  [the longest x1 3.56 us: on_device(): third_solution = jnp.dot(inverse_third, mttkrp_third, precision=HIGHEST)]
    all_to_all x0 -> x8, starting transfers between devices: none -> 45.4 us  [exchange(): return lax.all_to_all(x, axes, 0, 0, tiled=True)]
    all_to_all x0 -> x2, blocking collectives: none -> 31.3 us  [exchange(): return lax.all_to_all(x, axes, 0, 0, tiled=True)]
  transfers between devices with their start and end apart: 2 -> 11, of which waited for: 2 -> 9; matrix products, arithmetic and copies ran while one was open for 0% -> 5% of each run, Pallas kernels for 0% -> 9%
where the time goes in v1:
time: 235 us; the launch traced here: 233 us
  waiting for transfers between devices  76.9 us (33%)
  starting transfers between devices  49.8 us (21%)
  Pallas kernels  47.1 us (20%)
  blocking collectives  31.3 us (13%)
  matrix products  14.2 us (6%)
  local copies, waits for them, and re-layouts  6.83 us (3%)
  other arithmetic  5.99 us (3%)
    all_to_all x8, waiting for transfers between devices, exchange(): return lax.all_to_all(x, axes, 0, 0, tiled=True)  74.2 us
    all_to_all x8, starting transfers between devices, exchange(): return lax.all_to_all(x, axes, 0, 0, tiled=True)  45.4 us
    all_to_all x2, blocking collectives, exchange(): return lax.all_to_all(x, axes, 0, 0, tiled=True)  31.3 us
    pallas_call x2, Pallas kernels, inverse(): pl.pallas_call(inverse_kernel, out_shape=jax.ShapeDtypeStruct((n, n), jnp...  21 us
    pallas_call x1, Pallas kernels, third_products(): pl.pallas_call(middle_kernel, grid=(window,), out_shape=jax.ShapeDtypeStr...  13.6 us
    pallas_call x1, Pallas kernels, first_products(): pl.pallas_call(first_kernel, grid=(window,), out_shape=jax.ShapeDtypeStru...  12.6 us
    dot_general x1, matrix products, on_device(): jnp.dot(tensor.reshape(window * second_local, third_local), third_factor,...  5.75 us
  transfers between devices with their start and end apart: 11, of which 9 were waited for; matrix products, arithmetic and copies ran while one was open for 5% of the time, Pallas kernels for 9%

profile of v1, /device:TPU:1, one launch (start us, length us, event | category | flops | bytes accessed | tf_op | source)
XLA Modules:
  0.0 233.0 jit_solution(1284422571518920355)
XLA Ops:
  0.6 0.0 copy-start
  0.6 1.0 copy-done
  1.7 1.0 fusion.10
  2.7 11.6 %all-to-all-start.2 = ((f32[8,32,256]{2,1,0:T(8,128)}), f32[8,32,256]{2,1,0:T(8,128)S(1)}, u32[]{:S(2)}, u32[]{:S(2)}) async-start(f32[8,32,256]{2,1,0:T(8,128)} %bitcast.6), calls=%async_computation.2 | async-start | bytes 524288 | tf_op jit(solution)/shard_map/all_to_all | solution.py:147
  14.3 0.7 bitcast_convert_fusion
  15.0 5.7 %multiply_reduce_fusion = f32[256,256]{0,1:T(8,128)S(1)} fusion(bf16[16,256,1024]{2,1,0:T(8,128)(2,1)} %t_ref.3, f32[256,16]{0,1:T(8,128)S(1)} %get-tuple-element.4, bf16[1024,256]{1,0:T(8,128)(2,1)S(1)} %copy-done), kind=kOutput, calls=%fused_computation | convolution fusion | flops 2149515264 | bytes 9191424 | tf_op jit(solution)/shard_map/dot_general | solution.py:183
  20.8 0.7 broadcast_multiply_fusion.2
  21.5 2.9 %all-to-all-done.2 = f32[8,32,256]{2,1,0:T(8,128)S(1)} async-done(((f32[8,32,256]{2,1,0:T(8,128)}), f32[8,32,256]{2,1,0:T(8,128)S(1)}, u32[]{:S(2)}, u32[]{:S(2)}) %all-to-all-start.2) | async-done | bytes 262176 | tf_op jit(solution)/shard_map/all_to_all | solution.py:147
  24.4 6.2 %all-to-all-start = ((f32[8,32,256]{2,1,0:T(8,128)}), f32[8,32,256]{2,1,0:T(8,128)S(1)}, u32[]{:S(2)}, u32[]{:S(2)}) async-start(f32[8,32,256]{2,1,0:T(8,128)} %bitcast.4), calls=%async_computation | async-start | bytes 524288 | tf_op jit(solution)/shard_map/all_to_all | solution.py:147
  30.6 10.1 %all-to-all-done = f32[8,32,256]{2,1,0:T(8,128)S(1)} async-done(((f32[8,32,256]{2,1,0:T(8,128)}), f32[8,32,256]{2,1,0:T(8,128)S(1)}, u32[]{:S(2)}, u32[]{:S(2)}) %all-to-all-start) | async-done | bytes 262176 | tf_op jit(solution)/shard_map/all_to_all | solution.py:147
  40.7 0.7 broadcast_in_dim.17
  41.4 3.4 %all-to-all-start.3 = ((f32[8,32,256]{2,1,0:T(8,128)}), f32[8,32,256]{2,1,0:T(8,128)S(1)}, u32[]{:S(2)}, u32[]{:S(2)}) async-start(f32[8,32,256]{2,1,0:T(8,128)} %broadcast_in_dim.17), calls=%async_computation.3 | async-start | bytes 524288 | tf_op jit(solution)/shard_map/all_to_all | solution.py:147
  44.8 2.0 copy.10.f_ref
  46.8 7.9 %all-to-all-done.3 = f32[8,32,256]{2,1,0:T(8,128)S(1)} async-done(((f32[8,32,256]{2,1,0:T(8,128)}), f32[8,32,256]{2,1,0:T(8,128)S(1)}, u32[]{:S(2)}, u32[]{:S(2)}) %all-to-all-start.3) | async-done | bytes 262176 | tf_op jit(solution)/shard_map/all_to_all | solution.py:147
  54.7 0.7 broadcast_in_dim.16
  55.5 3.4 %all-to-all-start.1 = ((f32[8,32,256]{2,1,0:T(8,128)}), f32[8,32,256]{2,1,0:T(8,128)S(1)}, u32[]{:S(2)}, u32[]{:S(2)}) async-start(f32[8,32,256]{2,1,0:T(8,128)} %broadcast_in_dim.16), calls=%async_computation.1 | async-start | bytes 524288 | tf_op jit(solution)/shard_map/all_to_all | solution.py:147
  58.9 0.9 select_add_fusion.1
  59.8 10.5 %inverse.2 = f32[256,256]{1,0:T(8,128)} custom-call(f32[256,256]{1,0:T(8,128)} %get-tuple-element.5.s_ref), custom_call_target="tpu_custom_call" | custom-call | tf_op jit(solution)/shard_map/inverse/pallas_call | solution.py:78
  70.4 2.0 fusion.9
  72.4 0.8 copy.9.s_ref
  73.2 13.6 %third_products.1 = f32[256,1024]{1,0:T(8,128)} custom-call(bf16[16,256,1024]{2,1,0:T(8,128)(2,1)} %t_ref.3, bf16[256,256]{1,0:T(8,128)(2,1)} %copy.9.s_ref, f32[16,256,1]{2,1,0:T(8,128)} %copy.10.f_ref), custom_call_target="tpu_custom_call" | custom-call | flops 2147483648 | bytes 8388608 | tf_op jit(solution)/shard_map/third_products/pallas_call | solution.py:106
  86.7 1.4 broadcast_multiply_fusion
  88.1 0.1 slice_select_fusion
  88.2 3.9 %collective-permute-start = (f32[128,1024]{1,0:T(8,128)S(1)}, f32[128,1024]{1,0:T(8,128)S(1)}, u32[]{:S(2)}, u32[]{:S(2)}) collective-permute-start(f32[128,1024]{1,0:T(8,128)S(1)} %slice_select_fusion), channel_id=1, source_target_pairs={{0,8},{8,0},{1,9},{9,1},{2,10},{10,2},{3,11},{11,3},{4,12},{12,4},... | collective-permute-start | bytes 1572872 | tf_op jit(solution)/shard_map/ppermute | solution.py:166
  92.1 1.5 collective-permute-done
  93.6 0.9 add_bitcast_fusion
  94.5 7.3 %all-to-all-start.4 = ((f32[16,8,1024]{2,1,0:T(8,128)}), f32[16,8,1024]{2,1,0:T(8,128)S(1)}, u32[]{:S(2)}, u32[]{:S(2)}) async-start(f32[16,8,1024]{2,1,0:T(8,128)} %add_bitcast_fusion), calls=%async_computation.4 | async-start | bytes 1048576 | tf_op jit(solution)/shard_map/all_to_all | solution.py:147
  101.8 0.9 convolution_bitcast_fusion
  102.8 14.8 %all-to-all-done.4 = f32[16,8,1024]{2,1,0:T(8,128)S(1)} async-done(((f32[16,8,1024]{2,1,0:T(8,128)}), f32[16,8,1024]{2,1,0:T(8,128)S(1)}, u32[]{:S(2)}, u32[]{:S(2)}) %all-to-all-start.4) | async-done | bytes 524320 | tf_op jit(solution)/shard_map/all_to_all | solution.py:147
  117.6 5.2 %all-to-all-start.6 = ((f32[32,8,256]{2,1,0:T(8,128)}), f32[32,8,256]{2,1,0:T(8,128)S(1)}, u32[]{:S(2)}, u32[]{:S(2)}) async-start(f32[32,8,256]{2,1,0:T(8,128)} %convolution_bitcast_fusion), calls=%async_computation.6 | async-start | bytes 524288 | tf_op jit(solution)/shard_map/all_to_all | solution.py:147
  122.9 11.3 %all-to-all-done.6 = f32[32,8,256]{2,1,0:T(8,128)S(1)} async-done(((f32[32,8,256]{2,1,0:T(8,128)}), f32[32,8,256]{2,1,0:T(8,128)S(1)}, u32[]{:S(2)}, u32[]{:S(2)}) %all-to-all-start.6) | async-done | bytes 262176 | tf_op jit(solution)/shard_map/all_to_all | solution.py:147
  134.2 0.8 broadcast_in_dim.20
  135.0 3.6 %all-to-all-start.5 = ((f32[16,8,1024]{2,1,0:T(8,128)}), f32[16,8,1024]{2,1,0:T(8,128)S(1)}, u32[]{:S(2)}, u32[]{:S(2)}) async-start(f32[16,8,1024]{2,1,0:T(8,128)} %broadcast_in_dim.20), calls=%async_computation.5 | async-start | bytes 1048576 | tf_op jit(solution)/shard_map/all_to_all | solution.py:147
  138.6 16.3 %all-to-all-done.5 = f32[16,8,1024]{2,1,0:T(8,128)S(1)} async-done(((f32[16,8,1024]{2,1,0:T(8,128)}), f32[16,8,1024]{2,1,0:T(8,128)S(1)}, u32[]{:S(2)}, u32[]{:S(2)}) %all-to-all-start.5) | async-done | bytes 524320 | tf_op jit(solution)/shard_map/all_to_all | solution.py:147
  154.9 0.7 broadcast_in_dim.21
  155.6 4.6 %all-to-all-start.7 = ((f32[32,8,256]{2,1,0:T(8,128)}), f32[32,8,256]{2,1,0:T(8,128)S(1)}, u32[]{:S(2)}, u32[]{:S(2)}) async-start(f32[32,8,256]{2,1,0:T(8,128)} %broadcast_in_dim.21), calls=%async_computation.7 | async-start | bytes 524288 | tf_op jit(solution)/shard_map/all_to_all | solution.py:147
  160.3 0.4 collective-permute-start.1
  160.7 10.9 %all-to-all-done.7 = f32[32,8,256]{2,1,0:T(8,128)S(1)} async-done(((f32[32,8,256]{2,1,0:T(8,128)}), f32[32,8,256]{2,1,0:T(8,128)S(1)}, u32[]{:S(2)}, u32[]{:S(2)}) %all-to-all-start.7) | async-done | bytes 262176 | tf_op jit(solution)/shard_map/all_to_all | solution.py:147
  171.6 0.7 select_add_fusion.s_ref
  172.4 10.5 %inverse.3 = f32[256,256]{1,0:T(8,128)} custom-call(f32[256,256]{1,0:T(8,128)} %select_add_fusion.s_ref), custom_call_target="tpu_custom_call" | custom-call | tf_op jit(solution)/shard_map/inverse/pallas_call | solution.py:78
  182.9 3.6 %convolution_convert_fusion.v_ref = bf16[1024,256]{1,0:T(8,128)(2,1)} fusion(f32[256,256]{1,0:T(8,128)} %inverse.3, f32[128,1024]{1,0:T(8,128)S(1)} %collective-permute-done.1, f32[128,1024]{1,0:T(8,128)S(1)} %bitcast.47, pred[]{:T(512)S(6)} %eq.11), kind=kOutput, calls=%fused_computation.1 | convolution fusion | flops 806354944 | bytes 1835009 | tf_op jit(solution)/shard_map/dot_general | solution.py:209
  186.4 12.6 %first_products.1 = f32[16,1,256]{2,1,0:T(1,128)} custom-call(bf16[16,256,1024]{2,1,0:T(8,128)(2,1)} %t_ref.3, bf16[1024,256]{1,0:T(8,128)(2,1)} %convolution_convert_fusion.v_ref, f32[256,256]{1,0:T(8,128)} %get-tuple-element.7.s_ref), custom_call_target="tpu_custom_call" | custom-call | flops 2147483648 | bytes 8388608 | tf_op jit(solution)/shard_map/first_products/pallas_call | solution.py:130
  199.0 0.7 broadcast_multiply_fusion.3
  199.8 0.1 collective-permute-start.2
  199.9 1.2 collective-permute-done.2
  201.1 12.9 %all_to_all.50 = f32[16,16,256]{2,1,0:T(8,128)S(1)} all-to-all(f32[16,16,256]{2,1,0:T(8,128)S(1)} %broadcast_in_dim.22), channel_id=1, replica_groups=mesh['x'=4,'zl'=4,'core'=2,'zh'=2,'y'=4] {'x','zl'}, dimensions={0} | all-to-all | bytes 524288 | tf_op jit(solution)/shard_map/all_to_all | solution.py:147
  214.0 18.4 %all_to_all.51 = f32[8,16,256]{2,1,0:T(8,128)S(1)} all-to-all(f32[8,16,256]{2,1,0:T(8,128)S(1)} %broadcast_in_dim.23), channel_id=1, replica_groups=mesh['x'=4,'zl'=4,'core'=2,'zh'=2,'y'=4] {'zh','y'}, dimensions={0} | all-to-all | bytes 262144 | tf_op jit(solution)/shard_map/all_to_all | solution.py:147
  232.4 0.6 reduce_sum.59
  (16 shorter events, 0.2 us)
Async XLA Ops:
  0.6 1.0 copy-start
  2.7 21.7 %all-to-all-start.2 = ((f32[8,32,256]{2,1,0:T(8,128)}), f32[8,32,256]{2,1,0:T(8,128)S(1)}, u32[]{:S(2)}, u32[]{:S(2)}) async-start(f32[8,32,256]{2,1,0:T(8,128)} %bitcast.6), calls=%async_computation.2 | async-start | bytes 524288 | tf_op jit(solution)/shard_map/all_to_all | solution.py:147
  15.0 43.9 %copy-start.2 = (bf16[16,256]{1,0:T(8,128)(2,1)S(1)}, bf16[16,256]{1,0:T(8,128)(2,1)}, u32[]{:S(2)}) copy-start(bf16[16,256]{1,0:T(8,128)(2,1)} %param.4) | copy-start | bytes 24580
  24.4 16.2 %all-to-all-start = ((f32[8,32,256]{2,1,0:T(8,128)}), f32[8,32,256]{2,1,0:T(8,128)S(1)}, u32[]{:S(2)}, u32[]{:S(2)}) async-start(f32[8,32,256]{2,1,0:T(8,128)} %bitcast.4), calls=%async_computation | async-start | bytes 524288 | tf_op jit(solution)/shard_map/all_to_all | solution.py:147
  41.4 13.3 %all-to-all-start.3 = ((f32[8,32,256]{2,1,0:T(8,128)}), f32[8,32,256]{2,1,0:T(8,128)S(1)}, u32[]{:S(2)}, u32[]{:S(2)}) async-start(f32[8,32,256]{2,1,0:T(8,128)} %broadcast_in_dim.17), calls=%async_computation.3 | async-start | bytes 524288 | tf_op jit(solution)/shard_map/all_to_all | solution.py:147
  55.5 14.9 %all-to-all-start.1 = ((f32[8,32,256]{2,1,0:T(8,128)}), f32[8,32,256]{2,1,0:T(8,128)S(1)}, u32[]{:S(2)}, u32[]{:S(2)}) async-start(f32[8,32,256]{2,1,0:T(8,128)} %broadcast_in_dim.16), calls=%async_computation.1 | async-start | bytes 524288 | tf_op jit(solution)/shard_map/all_to_all | solution.py:147
  72.4 29.4 %copy-start.1 = (bf16[256,256]{1,0:T(8,128)(2,1)}, bf16[256,256]{1,0:T(8,128)(2,1)S(1)}, u32[]{:S(2)}) copy-start(bf16[256,256]{1,0:T(8,128)(2,1)S(1)} %get-tuple-element.8) | copy-start | bytes 393220
  88.2 5.4 %collective-permute-start = (f32[128,1024]{1,0:T(8,128)S(1)}, f32[128,1024]{1,0:T(8,128)S(1)}, u32[]{:S(2)}, u32[]{:S(2)}) collective-permute-start(f32[128,1024]{1,0:T(8,128)S(1)} %slice_select_fusion), channel_id=1, source_target_pairs={{0,8},{8,0},{1,9},{9,1},{2,10},{10,2},{3,11},{11,3},{4,12},{12,4},... | collective-permute-start | bytes 1572872 | tf_op jit(solution)/shard_map/ppermute | solution.py:166
  94.5 23.1 %all-to-all-start.4 = ((f32[16,8,1024]{2,1,0:T(8,128)}), f32[16,8,1024]{2,1,0:T(8,128)S(1)}, u32[]{:S(2)}, u32[]{:S(2)}) async-start(f32[16,8,1024]{2,1,0:T(8,128)} %add_bitcast_fusion), calls=%async_computation.4 | async-start | bytes 1048576 | tf_op jit(solution)/shard_map/all_to_all | solution.py:147
  117.6 16.6 %all-to-all-start.6 = ((f32[32,8,256]{2,1,0:T(8,128)}), f32[32,8,256]{2,1,0:T(8,128)S(1)}, u32[]{:S(2)}, u32[]{:S(2)}) async-start(f32[32,8,256]{2,1,0:T(8,128)} %convolution_bitcast_fusion), calls=%async_computation.6 | async-start | bytes 524288 | tf_op jit(solution)/shard_map/all_to_all | solution.py:147
  135.0 19.9 %all-to-all-start.5 = ((f32[16,8,1024]{2,1,0:T(8,128)}), f32[16,8,1024]{2,1,0:T(8,128)S(1)}, u32[]{:S(2)}, u32[]{:S(2)}) async-start(f32[16,8,1024]{2,1,0:T(8,128)} %broadcast_in_dim.20), calls=%async_computation.5 | async-start | bytes 1048576 | tf_op jit(solution)/shard_map/all_to_all | solution.py:147
  155.6 16.0 %all-to-all-start.7 = ((f32[32,8,256]{2,1,0:T(8,128)}), f32[32,8,256]{2,1,0:T(8,128)S(1)}, u32[]{:S(2)}, u32[]{:S(2)}) async-start(f32[32,8,256]{2,1,0:T(8,128)} %broadcast_in_dim.21), calls=%async_computation.7 | async-start | bytes 524288 | tf_op jit(solution)/shard_map/all_to_all | solution.py:147
  160.3 22.6 %collective-permute-start.1 = (f32[128,1024]{1,0:T(8,128)S(1)}, f32[128,1024]{1,0:T(8,128)S(1)}, u32[]{:S(2)}, u32[]{:S(2)}) collective-permute-start(f32[128,1024]{1,0:T(8,128)S(1)} %bitcast.46), channel_id=1, source_target_pairs={{0,8},{8,0},{1,9},{9,1},{2,10},{10,2},{3,11},{11,3},{4,12},{12,4},... | collective-permute-start | bytes 1572872 | tf_op jit(solution)/shard_map/ppermute | solution.py:166
  199.8 1.3 collective-permute-start.2

commit v2 on v1

v2 whole, which is shorter than its diff:
```python
import functools
import math

import jax
import jax.numpy as jnp
from jax import lax
from jax.experimental import pallas as pl
from jax.experimental.pallas import tpu as pltpu
from jax.sharding import Mesh, PartitionSpec as P

ridge = 0.5
B = 16
WIDE = ("x", "zl", "core")
CHIP = ("x", "zl")
NARROW = ("zh", "y")
HIGHEST = lax.Precision.HIGHEST


def pieces(x):
    high = x.astype(jnp.bfloat16)
    rest = x - high.astype(jnp.float32)
    middle = rest.astype(jnp.bfloat16)
    low = (rest - middle.astype(jnp.float32)).astype(jnp.bfloat16)
    return high, middle, low


def inverse_kernel(places, total, *refs):
    part_refs, (f_ref, x_ref, m_ref, w_ref) = refs[:-4], refs[-4:]
    n = f_ref.shape[0]
    depth = part_refs[0].shape[0]
    for place, part_ref in zip(places(), part_refs):
        base = pl.multiple_of(place * depth, depth)
        here = (depth, n)
        diagonal = lax.broadcasted_iota(jnp.int32, here, 0) + base == lax.broadcasted_iota(jnp.int32, here, 1)
        m_ref[pl.ds(base, depth), :] = f_ref[pl.ds(base, depth), :] * (
            part_ref[...] * (1.0 / total)
        ) + jnp.where(diagonal, ridge, 0.0)
    row = lax.broadcasted_iota(jnp.int32, (B, n), 0)
    lane = lax.broadcasted_iota(jnp.int32, (B, n), 1)
    half_row = lax.broadcasted_iota(jnp.int32, (B, 128), 0)
    whole_row = lax.broadcasted_iota(jnp.int32, (n, n), 0)
    whole_lane = lax.broadcasted_iota(jnp.int32, (n, n), 1)

    def step(k, carry):
        o = pl.multiple_of(k * B, B)
        panel = m_ref[pl.ds(o, B), :]
        front = pltpu.roll(panel, n - o, 1)
        cols = [jnp.broadcast_to(front[:, j:j + 1], (B, 128)) for j in range(B)]
        inside = (lane >= o) & (lane < o + B)
        unit = jnp.where(lane - o == row, 1.0, 0.0)
        work = jnp.where(inside, unit, panel)
        parts = [work[:, t * 128:(t + 1) * 128] for t in range(n // 128)]
        for j in range(B):
            col = cols[j]
            scale = 1.0 / col[j:j + 1, :]
            other = half_row != j
            for t in range(len(parts)):
                pivot = parts[t][j:j + 1, :] * scale
                parts[t] = jnp.where(other, parts[t] - col * pivot, pivot)
            for m in range(j + 1, B):
                pivot = cols[m][j:j + 1, :] * scale
                cols[m] = jnp.where(other, cols[m] - col * pivot, pivot)
        solved = jnp.concatenate(parts, axis=1)
        below = jnp.where(lane >= o + B, panel, 0.0)
        uh, um, ul = pieces(below)
        wh, wm, wl = pieces(solved)
        left = jnp.concatenate([uh, uh, um, uh, ul, um], axis=0)
        right = jnp.concatenate([wh, wm, wh, wl, wh, wm], axis=0)
        update = lax.dot_general(
            left, right, (((0,), (0,)), ((), ())), preferred_element_type=jnp.float32
        )
        cleared = (whole_row >= o + B) & (whole_lane >= o) & (whole_lane < o + B)
        m_ref[...] = jnp.where(cleared, 0.0, m_ref[...]) - update
        m_ref[pl.ds(o, B), :] = jnp.where(lane < o, panel, jnp.where(inside, unit, 0.0))
        w_ref[pl.ds(o, B), :] = jnp.where(lane < o + B, solved, 0.0)
        return carry

    lax.fori_loop(0, n // B, step, 0)
    x_ref[...] = lax.dot_general(
        m_ref[...], w_ref[...], (((0,), (0,)), ((), ())),
        precision=lax.Precision.HIGHEST, preferred_element_type=jnp.float32,
    )


def inverse(parts, places, gram_first, total):
    n = gram_first.shape[0]
    return pl.pallas_call(
        functools.partial(inverse_kernel, places, total),
        out_shape=jax.ShapeDtypeStruct((n, n), jnp.float32),
        in_specs=[pl.BlockSpec(memory_space=pltpu.VMEM)] * (len(parts) + 1),
        out_specs=pl.BlockSpec(memory_space=pltpu.VMEM),
        scratch_shapes=[pltpu.VMEM((n, n), jnp.float32), pltpu.VMEM((n, n), jnp.float32)],
        cost_estimate=pl.CostEstimate(flops=6 * 2 * n**3, bytes_accessed=8 * n * n, transcendentals=0),
        compiler_params=pltpu.CompilerParams(vmem_limit_bytes=8 << 20),
        name="inverse",
    )(*parts, gram_first)


def exchange(x, axes):
    return lax.all_to_all(x, axes, 0, 0, tiled=True)


def scatter_sum(x, axes):
    n = lax.axis_size(axes)
    return jnp.sum(exchange(x.reshape(n, x.shape[0] // n, x.shape[1]), axes), axis=0)


def gather(x, axes):
    n = lax.axis_size(axes)
    return exchange(jnp.broadcast_to(x[None], (n,) + x.shape), axes).reshape(n * x.shape[0], x.shape[1])


def shift(x, axis, d):
    n = lax.axis_size(axis)
    return lax.ppermute(x, axis, [(s, (s + d) % n) for s in range(n)])


def ring_scatter(x, axis):
    n = lax.axis_size(axis)
    me = lax.axis_index(axis)
    blocks = x.reshape(n, x.shape[0] // n, x.shape[1])
    take = lambda d: lax.dynamic_index_in_dim(blocks, lax.rem(me + d, n), 0, keepdims=False)
    arrived = [shift(take(d), axis, d) for d in range(1, n)]
    return sum(arrived, take(0))


def ring_sum(x, axis):
    return sum([shift(x, axis, d) for d in range(1, lax.axis_size(axis))], x)


def ring_gather(x, axis):
    return [x] + [shift(x, axis, d) for d in range(1, lax.axis_size(axis))]


def keep(x, bit):
    half = x.shape[0] // 2
    low, high = x[:half], x[half:]
    return jnp.where(bit == 0, low, high), jnp.where(bit == 0, high, low)


def join(mine, theirs, bit):
    return jnp.where(
        bit == 0, jnp.concatenate([mine, theirs], 0), jnp.concatenate([theirs, mine], 0)
    )


def narrow_places():
    me = lax.axis_index("y")
    return [lax.rem(me + 4 - d, 4) for d in range(4)]


def wide_places():
    me = lax.axis_index("x")
    core = lax.axis_index("core")
    ring = [lax.rem(me + 4 - d, 4) for d in range(4)]
    return [core * 4 + r for r in ring] + [(1 - core) * 4 + r for r in ring]


def on_device(tensor, first_factor, third_factor):
    window, second_local, third_local = tensor.shape
    second_total = second_local * lax.axis_size(WIDE)
    third_total = third_local * lax.axis_size(NARROW)
    core = lax.axis_index("core")
    first_wide = first_factor.astype(jnp.float32)
    first_second = first_wide / math.sqrt(window * third_total)
    first_third = first_wide / math.sqrt(window * second_total)
    gram_first = jnp.dot(first_factor.T, first_factor, preferred_element_type=jnp.float32) / window

    gram_part = jnp.dot(third_factor.T, third_factor, preferred_element_type=jnp.float32)
    gram_part = ring_scatter(gram_part, "y")
    gram_part = ring_sum(gram_part, "zh")
    parts = ring_gather(gram_part, "y")
    inverse_second = inverse(parts, narrow_places, gram_first, third_total)

    contracted = jnp.einsum("ijk,kr->ijr", tensor, third_factor, preferred_element_type=jnp.float32)
    partial_second = jnp.einsum(
        "ijr,ir->jr", contracted, first_second, precision=HIGHEST
    )
    row = scatter_sum(partial_second, NARROW)
    mttkrp_second = gather(row, NARROW)
    second_factor = jnp.dot(mttkrp_second, inverse_second, precision=HIGHEST).astype(jnp.bfloat16)

    gram_local = jnp.dot(second_factor.T, second_factor, preferred_element_type=jnp.float32)
    mine, other = keep(gram_local, core)
    mine = mine + shift(other, "core", 1)
    mine = ring_scatter(mine, "x")
    mine = ring_sum(mine, "zl")
    parts = ring_gather(mine, "x")
    parts = parts + [shift(part, "core", 1) for part in parts]
    inverse_third = inverse(parts, wide_places, gram_first, second_total)

    middle = jnp.einsum("ijk,jr->ikr", tensor, second_factor, preferred_element_type=jnp.float32)
    partial_third = jnp.einsum(
        "ikr,ir->kr", middle, first_third, precision=HIGHEST
    )
    mine, other = keep(partial_third, core)
    mine = mine + shift(other, "core", 1)
    mttkrp_third = scatter_sum(mine, CHIP)
    third_solution = jnp.dot(mttkrp_third, inverse_third, precision=HIGHEST)
    mine = gather(third_solution.astype(jnp.bfloat16), CHIP)
    third_new = join(mine, shift(mine, "core", 1), core)

    back = jnp.einsum("ijk,kr->ijr", tensor, third_new, preferred_element_type=jnp.float32)
    partial_first = jnp.einsum(
        "ijr,jr->ir", back, second_factor.astype(jnp.float32), precision=HIGHEST
    )
    partial_first = partial_first + shift(partial_first, "core", 1)
    partial_first = ring_sum(partial_first, "x").astype(jnp.bfloat16)
    axes = ("zl",) + NARROW
    n = lax.axis_size(axes)
    copies = jnp.broadcast_to(partial_first[None], (n,) + partial_first.shape)
    first_mode = jnp.sum(exchange(copies, axes), axis=0, dtype=jnp.float32)
    first_mode = first_mode / math.sqrt(second_total * third_total)
    return (second_factor, third_new, first_mode)


def solution(mesh):
    fine = Mesh(mesh.devices.reshape(4, 4, 2, 2, 4), WIDE + NARROW)
    in_specs = (P(None, WIDE, NARROW), P(), P(NARROW, None))
    out_specs = (P(WIDE, None), P(NARROW, None), P())
    return jax.shard_map(
        on_device, mesh=fine, in_specs=in_specs, out_specs=out_specs, check_vma=False
    )
```

time: 235 us -> 170 us (0.72)
  waiting for transfers between devices: 76.9 us -> 29.5 us
  Pallas kernels: 47.1 us -> 17.8 us
  starting transfers between devices: 49.8 us -> 65.8 us
  matrix products: 14.2 us -> 21 us
  local copies, waits for them, and re-layouts: 6.83 us -> 1.57 us
  other arithmetic: 5.99 us -> 2.78 us
  blocking collectives: 31.3 us -> 28.1 us
    all_to_all x8 -> x3, waiting for transfers between devices: 74.2 us -> 5.31 us  [exchange(): return lax.all_to_all(x, axes, 0, 0, tiled=True)]
    ppermute x3 -> x27, starting transfers between devices: 4.43 us -> 44.3 us  [shift(): return lax.ppermute(x, axis, [(s, (s + d) % n) for s in range(n)])]
    pallas_call x4 -> x2, Pallas kernels: 47.1 us -> 17.8 us  [inverse(): pl.pallas_call(functools.partial(inverse_kernel, places, total), out_shap...]
    all_to_all x8 -> x3, starting transfers between devices: 45.4 us -> 21.5 us  [exchange(): return lax.all_to_all(x, axes, 0, 0, tiled=True)]
    ppermute x3 -> x27, waiting for transfers between devices: 2.71 us -> 24.2 us  [shift(): return lax.ppermute(x, axis, [(s, (s + d) % n) for s in range(n)])]
    dot_general x2 -> x4, matrix products: 9.31 us -> 19.9 us  [the longest x1 6.63 us: on_device(): jnp.einsum('ijk,kr->ijr', tensor, third_new, preferred_element_type=jnp.f...]
    all_to_all x2, blocking collectives: 31.3 us -> 28.1 us  [exchange(): return lax.all_to_all(x, axes, 0, 0, tiled=True)]
  transfers between devices with their start and end apart: 11 -> 30, of which waited for: 9 -> 17; matrix products, arithmetic and copies ran while one was open for 5% -> 2% of each run, Pallas kernels for 9% -> 11%
where the time goes in v2:
time: 170 us; the launch traced here: 168 us
  starting transfers between devices  65.8 us (39%)
  waiting for transfers between devices  29.5 us (17%)
  blocking collectives  28.1 us (17%)
  matrix products  21 us (12%)
  Pallas kernels  17.8 us (10%)
  other arithmetic  2.78 us (2%)
    ppermute x27, starting transfers between devices, shift(): return lax.ppermute(x, axis, [(s, (s + d) % n) for s in range(n)])  44.3 us
    all_to_all x2, blocking collectives, exchange(): return lax.all_to_all(x, axes, 0, 0, tiled=True)  28.1 us
    ppermute x27, waiting for transfers between devices, shift(): return lax.ppermute(x, axis, [(s, (s + d) % n) for s in range(n)])  24.2 us
    all_to_all x3, starting transfers between devices, exchange(): return lax.all_to_all(x, axes, 0, 0, tiled=True)  21.5 us
    pallas_call x2, Pallas kernels, inverse(): pl.pallas_call(functools.partial(inverse_kernel, places, total), out_shap...  17.8 us
    dot_general x1, matrix products, on_device(): jnp.einsum('ijk,kr->ijr', tensor, third_new, preferred_element_type=jnp.f...  6.63 us
    dot_general x1, matrix products, on_device(): jnp.einsum('ijk,jr->ikr', tensor, second_factor, preferred_element_type=j...  6.56 us
    dot_general x1, matrix products, on_device(): jnp.einsum('ijk,kr->ijr', tensor, third_factor, preferred_element_type=jn...  6.45 us
  transfers between devices with their start and end apart: 30, of which 17 were waited for; matrix products, arithmetic and copies ran while one was open for 2% of the time, Pallas kernels for 11%

profile of v2, /device:TPU:1, one launch (start us, length us, event | category | flops | bytes accessed | tf_op | source)
XLA Modules:
  0.0 167.5 jit_solution(16320056094613752297)
XLA Ops:
  0.6 0.8 multiply_bitcast_fusion
  1.7 6.5 %multiply_reduce_fusion.1 = f32[256,256]{0,1:T(8,128)} fusion(bf16[16,256,1024]{2,1,0:T(8,128)(2,1)} %param.3, f32[256,16]{0,1:T(8,128)S(1)} %multiply_bitcast_fusion, bf16[1024,256]{1,0:T(8,128)(2,1)S(1)} %copy-done), kind=kOutput, calls=%fused_computation.3 | convolution fusion | flops 2149515264 | bytes 9191424 | tf_op jit(solution)/shard_map/ijk,kr->ijr/dot_general | solution.py:175
  8.1 11.6 %all-to-all-start = ((f32[8,32,256]{2,1,0:T(8,128)}), f32[8,32,256]{2,1,0:T(8,128)S(1)}, u32[]{:S(2)}, u32[]{:S(2)}) async-start(f32[8,32,256]{2,1,0:T(8,128)} %bitcast.8), calls=%async_computation | async-start | bytes 524288 | tf_op jit(solution)/shard_map/all_to_all | solution.py:100
  20.2 1.5 collective-permute-start
  21.7 1.3 collective-permute-start.2
  23.0 1.7 collective-permute-start.1
  24.7 5.3 %all-to-all-done = f32[8,32,256]{2,1,0:T(8,128)S(1)} async-done(((f32[8,32,256]{2,1,0:T(8,128)}), f32[8,32,256]{2,1,0:T(8,128)S(1)}, u32[]{:S(2)}, u32[]{:S(2)}) %all-to-all-start) | async-done | bytes 262176 | tf_op jit(solution)/shard_map/all_to_all | solution.py:100
  30.0 0.7 broadcast_in_dim.6
  30.7 3.4 %all-to-all-start.1 = ((f32[8,32,256]{2,1,0:T(8,128)}), f32[8,32,256]{2,1,0:T(8,128)S(1)}, u32[]{:S(2)}, u32[]{:S(2)}) async-start(f32[8,32,256]{2,1,0:T(8,128)} %broadcast_in_dim.6), calls=%async_computation.1 | async-start | bytes 524288 | tf_op jit(solution)/shard_map/all_to_all | solution.py:100
  34.2 5.4 %collective-permute-start.3 = (f32[64,256]{1,0:T(8,128)S(1)}, f32[64,256]{1,0:T(8,128)S(1)}, u32[]{:S(2)}, u32[]{:S(2)}) collective-permute-start(f32[64,256]{1,0:T(8,128)S(1)} %fusion.5), channel_id=1, source_target_pairs={{0,4},{4,0},{1,5},{5,1},{2,6},{6,2},{3,7},{7,3},{8,12},{12,8},{9,1... | collective-permute-start | bytes 196616 | tf_op jit(solution)/shard_map/ppermute | solution.py:115
  39.6 4.5 %collective-permute-done.3 = f32[64,256]{1,0:T(8,128)S(1)} collective-permute-done((f32[64,256]{1,0:T(8,128)S(1)}, f32[64,256]{1,0:T(8,128)S(1)}, u32[]{:S(2)}, u32[]{:S(2)}) %collective-permute-start.3) | collective-permute-done | bytes 65568 | tf_op jit(solution)/shard_map/ppermute | solution.py:115
  44.0 3.1 %collective-permute-start.6 = (f32[64,256]{1,0:T(8,128)S(1)}, f32[64,256]{1,0:T(8,128)S(1)}, u32[]{:S(2)}, u32[]{:S(2)}) collective-permute-start(f32[64,256]{1,0:T(8,128)S(1)} %add.102.refs_0_), channel_id=1, source_target_pairs={{0,3},{1,0},{2,1},{3,2},{4,7},{5,4},{6,5},{7,6},{8,11},{9,8},{10,9... | collective-permute-start | bytes 196616 | tf_op jit(solution)/shard_map/ppermute | solution.py:115
  47.7 0.6 collective-permute-start.4
  48.5 3.3 %collective-permute-done.5.refs_2_ = f32[64,256]{1,0:T(8,128)S(1)} collective-permute-done((f32[64,256]{1,0:T(8,128)S(1)}, f32[64,256]{1,0:T(8,128)S(1)}, u32[]{:S(2)}, u32[]{:S(2)}) %collective-permute-start.5) | collective-permute-done | bytes 65568 | tf_op jit(solution)/shard_map/ppermute | solution.py:115
  51.8 0.7 collective-permute-done.4.refs_1_
  52.4 8.9 %inverse.2 = f32[256,256]{1,0:T(8,128)S(1)} custom-call(f32[64,256]{1,0:T(8,128)S(1)} %add.102.refs_0_, f32[64,256]{1,0:T(8,128)S(1)} %collective-permute-done.4.refs_1_, f32[64,256]{1,0:T(8,128)S(1)} %collective-permute-done.5.refs_2_, f32[64,256]{1,0:T(8,128)S(1)} %collective-permute-done.6.refs_3_, f32[256,256]{1,0:T(8,128)S(1)} %convolution_multiply_fusion.refs_4_.refs_8_), custom_call_target="tpu_custom_call" | custom-call | flops 201326592 | bytes 524288 | tf_op jit(solution)/shard_map/inverse/pallas_call | solution.py:87
  61.8 6.6 %multiply_reduce_fusion = f32[256,1024]{1,0:T(8,128)S(1)} fusion(bf16[16,256,1024]{2,1,0:T(8,128)(2,1)} %param.3, f32[256,16]{0,1:T(8,128)S(1)} %multiply_bitcast_fusion, bf16[256,256]{1,0:T(8,128)(2,1)S(1)} %get-tuple-element.10), kind=kOutput, calls=%fused_computation | convolution fusion | flops 2155610112 | bytes 9584640 | tf_op jit(solution)/shard_map/ijk,jr->ikr/dot_general | solution.py:192
  68.7 6.0 %collective-permute-start.7 = (f32[512,256]{1,0:T(8,128)S(1)}, f32[512,256]{1,0:T(8,128)S(1)}, u32[]{:S(2)}, u32[]{:S(2)}) collective-permute-start(f32[512,256]{1,0:T(8,128)S(1)} %slice_select_fusion), channel_id=1, source_target_pairs={{0,8},{8,0},{1,9},{9,1},{2,10},{10,2},{3,11},{11,3},{4,12},{12,4},... | collective-permute-start | bytes 1572872 | tf_op jit(solution)/shard_map/ppermute | solution.py:115
  75.3 1.0 collective-permute-done.7
  76.3 0.9 select_add_fusion
  77.2 6.5 %all-to-all-start.2 = ((f32[16,32,256]{2,1,0:T(8,128)}), f32[16,32,256]{2,1,0:T(8,128)S(1)}, u32[]{:S(2)}, u32[]{:S(2)}) async-start(f32[16,32,256]{2,1,0:T(8,128)} %bitcast.19), calls=%async_computation.2 | async-start | bytes 1048576 | tf_op jit(solution)/shard_map/all_to_all | solution.py:100
  83.8 1.4 collective-permute-start.9
  85.2 1.3 collective-permute-start.11
  86.6 1.6 collective-permute-start.10
  88.2 1.8 %collective-permute-done.11 = f32[32,256]{1,0:T(8,128)S(1)} collective-permute-done((f32[32,256]{1,0:T(8,128)S(1)}, f32[32,256]{1,0:T(8,128)S(1)}, u32[]{:S(2)}, u32[]{:S(2)}) %collective-permute-start.11) | collective-permute-done | bytes 32800 | tf_op jit(solution)/shard_map/ppermute | solution.py:115
  90.0 2.2 %collective-permute-done.10 = f32[32,256]{1,0:T(8,128)S(1)} collective-permute-done((f32[32,256]{1,0:T(8,128)S(1)}, f32[32,256]{1,0:T(8,128)S(1)}, u32[]{:S(2)}, u32[]{:S(2)}) %collective-permute-start.10) | collective-permute-done | bytes 32800 | tf_op jit(solution)/shard_map/ppermute | solution.py:115
  92.2 4.7 %collective-permute-start.14 = (f32[32,256]{1,0:T(8,128)S(1)}, f32[32,256]{1,0:T(8,128)S(1)}, u32[]{:S(2)}, u32[]{:S(2)}) collective-permute-start(f32[32,256]{1,0:T(8,128)S(1)} %fusion.7), channel_id=1, source_target_pairs={{0,48},{16,0},{32,16},{48,32},{1,49},{17,1},{33,17},{49,33},{2,50}... | collective-permute-start | bytes 98312 | tf_op jit(solution)/shard_map/ppermute | solution.py:115
  97.3 0.6 collective-permute-done.14
  98.0 2.6 %collective-permute-done.13 = f32[32,256]{1,0:T(8,128)S(1)} collective-permute-done((f32[32,256]{1,0:T(8,128)S(1)}, f32[32,256]{1,0:T(8,128)S(1)}, u32[]{:S(2)}, u32[]{:S(2)}) %collective-permute-start.13) | collective-permute-done | bytes 32800 | tf_op jit(solution)/shard_map/ppermute | solution.py:115
  100.6 0.9 collective-permute-done.12
  101.5 0.8 collective-permute-start.17
  102.3 0.7 collective-permute-start.16
  103.0 0.8 collective-permute-start.15
  103.8 3.7 %collective-permute-start.18 = (f32[32,256]{1,0:T(8,128)S(1)}, f32[32,256]{1,0:T(8,128)S(1)}, u32[]{:S(2)}, u32[]{:S(2)}) collective-permute-start(f32[32,256]{1,0:T(8,128)S(1)} %add_add_fusion.refs_0_), channel_id=1, source_target_pairs={{0,8},{8,0},{1,9},{9,1},{2,10},{10,2},{3,11},{11,3},{4,12},{12,4},... | collective-permute-start | bytes 98312 | tf_op jit(solution)/shard_map/ppermute | solution.py:115
  107.5 0.6 collective-permute-start.21
  108.1 3.9 %collective-permute-start.20 = (f32[32,256]{1,0:T(8,128)S(1)}, f32[32,256]{1,0:T(8,128)S(1)}, u32[]{:S(2)}, u32[]{:S(2)}) collective-permute-start(f32[32,256]{1,0:T(8,128)S(1)} %collective-permute-done.16.refs_2_), channel_id=1, source_target_pairs={{0,8},{8,0},{1,9},{9,1},{2,10},{10,2},{3,11},{11,3},{4,12},{12,4},... | collective-permute-start | bytes 98312 | tf_op jit(solution)/shard_map/ppermute | solution.py:115
  112.0 0.8 collective-permute-done.20.refs_6_
  113.2 8.9 %inverse.3 = f32[256,256]{1,0:T(8,128)S(1)} custom-call(f32[32,256]{1,0:T(8,128)S(1)} %add_add_fusion.refs_0_, f32[32,256]{1,0:T(8,128)S(1)} %collective-permute-done.15.refs_1_, f32[32,256]{1,0:T(8,128)S(1)} %collective-permute-done.16.refs_2_, f32[32,256]{1,0:T(8,128)S(1)} %collective-permute-done.17.refs_3_, ...), custom_call_target="tpu_custom_call" | custom-call | flops 201326592 | bytes 524288 | tf_op jit(solution)/shard_map/inverse/pallas_call | solution.py:87
  122.5 13.0 %all_to_all.25 = bf16[16,32,256]{2,1,0:T(8,128)(2,1)S(1)} all-to-all(bf16[16,32,256]{2,1,0:T(8,128)(2,1)S(1)} %broadcast_in_dim.7), channel_id=1, replica_groups=mesh['x'=4,'zl'=4,'core'=2,'zh'=2,'y'=4] {'x','zl'}, dimensions={0} | all-to-all | bytes 524288 | tf_op jit(solution)/shard_map/all_to_all | solution.py:100
  135.5 1.9 %collective-permute-start.22 = (bf16[512,256]{1,0:T(8,128)(2,1)S(1)}, bf16[512,256]{1,0:T(8,128)(2,1)S(1)}, u32[]{:S(2)}, u32[]{:S(2)}) collective-permute-start(bf16[512,256]{1,0:T(8,128)(2,1)S(1)} %bitcast.78), channel_id=1, source_target_pairs={{0,8},{8,0},{1,9},{9,1},{2,10},{10,2},{3,11},{11,3},{4,12},{12,4},... | collective-permute-start | bytes 786440 | tf_op jit(solution)/shard_map/ppermute | solution.py:115
  137.6 1.0 collective-permute-done.22
  138.8 6.6 %fusion = f32[256,16]{0,1:T(8,128)S(1)} fusion(bf16[16,256,1024]{2,1,0:T(8,128)(2,1)} %param.3, f32[256,256]{1,0:T(8,128)S(1)} %copy.34, bf16[1024,256]{1,0:T(8,128)(2,1)S(1)} %maximum_select_fusion), kind=kOutput, calls=%fused_computation.2 | convolution fusion | flops 2149576704 | bytes 9191424 | tf_op jit(solution)/shard_map/ijk,kr->ijr/dot_general | solution.py:203
  145.9 0.8 collective-permute-done.23
  147.6 0.6 collective-permute-start.24
  148.2 1.1 collective-permute-done.26
  149.3 2.1 %collective-permute-done.25 = f32[16,256]{1,0:T(8,128)S(1)} collective-permute-done((f32[16,256]{1,0:T(8,128)S(1)}, f32[16,256]{1,0:T(8,128)S(1)}, u32[]{:S(2)}, u32[]{:S(2)}) %collective-permute-start.25) | collective-permute-done | bytes 16416 | tf_op jit(solution)/shard_map/ppermute | solution.py:115
  151.8 15.1 %all_to_all.26 = bf16[32,16,256]{2,1,0:T(8,128)(2,1)S(1)} all-to-all(bf16[32,16,256]{2,1,0:T(8,128)(2,1)S(1)} %broadcast_in_dim.8), channel_id=1, replica_groups=mesh['x'=4,'zl'=4,'core'=2,'zh'=2,'y'=4] {'zl','zh','y'}, dimensions={0} | all-to-all | bytes 524288 | tf_op jit(solution)/shard_map/all_to_all | solution.py:100
  166.9 0.6 broadcast_multiply_fusion
  (55 shorter events, 6.0 us)
Async XLA Ops:
  0.6 1.1 copy-start
  1.7 46.6 %copy-start.3 = (bf16[16,256]{1,0:T(8,128)(2,1)S(1)}, bf16[16,256]{1,0:T(8,128)(2,1)}, u32[]{:S(2)}) copy-start(bf16[16,256]{1,0:T(8,128)(2,1)} %param.4) | copy-start | bytes 24580
  8.1 21.8 %all-to-all-start = ((f32[8,32,256]{2,1,0:T(8,128)}), f32[8,32,256]{2,1,0:T(8,128)S(1)}, u32[]{:S(2)}, u32[]{:S(2)}) async-start(f32[8,32,256]{2,1,0:T(8,128)} %bitcast.8), calls=%async_computation | async-start | bytes 524288 | tf_op jit(solution)/shard_map/all_to_all | solution.py:100
  20.2 14.0 %collective-permute-start = (f32[64,256]{1,0:T(8,128)S(1)}, f32[64,256]{1,0:T(8,128)S(1)}, u32[]{:S(2)}, u32[]{:S(2)}) collective-permute-start(f32[64,256]{1,0:T(8,128)S(1)} %get-tuple-element.3), channel_id=1, source_target_pairs={{0,1},{1,2},{2,3},{3,0},{4,5},{5,6},{6,7},{7,4},{8,9},{9,10},{10,1... | collective-permute-start | bytes 196616 | tf_op jit(solution)/shard_map/ppermute | solution.py:115
  21.7 12.5 %collective-permute-start.2 = (f32[64,256]{1,0:T(8,128)S(1)}, f32[64,256]{1,0:T(8,128)S(1)}, u32[]{:S(2)}, u32[]{:S(2)}) collective-permute-start(f32[64,256]{1,0:T(8,128)S(1)} %get-tuple-element.4), channel_id=1, source_target_pairs={{0,3},{1,0},{2,1},{3,2},{4,7},{5,4},{6,5},{7,6},{8,11},{9,8},{10,9... | collective-permute-start | bytes 196616 | tf_op jit(solution)/shard_map/ppermute | solution.py:115
  23.0 11.2 %collective-permute-start.1 = (f32[64,256]{1,0:T(8,128)S(1)}, f32[64,256]{1,0:T(8,128)S(1)}, u32[]{:S(2)}, u32[]{:S(2)}) collective-permute-start(f32[64,256]{1,0:T(8,128)S(1)} %get-tuple-element.5), channel_id=1, source_target_pairs={{0,2},{1,3},{2,0},{3,1},{4,6},{5,7},{6,4},{7,5},{8,10},{9,11},{10,... | collective-permute-start | bytes 196616 | tf_op jit(solution)/shard_map/ppermute | solution.py:115
  30.7 30.6 %all-to-all-start.1 = ((f32[8,32,256]{2,1,0:T(8,128)}), f32[8,32,256]{2,1,0:T(8,128)S(1)}, u32[]{:S(2)}, u32[]{:S(2)}) async-start(f32[8,32,256]{2,1,0:T(8,128)} %broadcast_in_dim.6), calls=%async_computation.1 | async-start | bytes 524288 | tf_op jit(solution)/shard_map/all_to_all | solution.py:100
  34.2 9.8 %collective-permute-start.3 = (f32[64,256]{1,0:T(8,128)S(1)}, f32[64,256]{1,0:T(8,128)S(1)}, u32[]{:S(2)}, u32[]{:S(2)}) collective-permute-start(f32[64,256]{1,0:T(8,128)S(1)} %fusion.5), channel_id=1, source_target_pairs={{0,4},{4,0},{1,5},{5,1},{2,6},{6,2},{3,7},{7,3},{8,12},{12,8},{9,1... | collective-permute-start | bytes 196616 | tf_op jit(solution)/shard_map/ppermute | solution.py:115
  44.0 4.5 %collective-permute-start.6 = (f32[64,256]{1,0:T(8,128)S(1)}, f32[64,256]{1,0:T(8,128)S(1)}, u32[]{:S(2)}, u32[]{:S(2)}) collective-permute-start(f32[64,256]{1,0:T(8,128)S(1)} %add.102.refs_0_), channel_id=1, source_target_pairs={{0,3},{1,0},{2,1},{3,2},{4,7},{5,4},{6,5},{7,6},{8,11},{9,8},{10,9... | collective-permute-start | bytes 196616 | tf_op jit(solution)/shard_map/ppermute | solution.py:115
  47.1 4.7 %collective-permute-start.5 = (f32[64,256]{1,0:T(8,128)S(1)}, f32[64,256]{1,0:T(8,128)S(1)}, u32[]{:S(2)}, u32[]{:S(2)}) collective-permute-start(f32[64,256]{1,0:T(8,128)S(1)} %add.102.refs_0_), channel_id=1, source_target_pairs={{0,2},{1,3},{2,0},{3,1},{4,6},{5,7},{6,4},{7,5},{8,10},{9,11},{10,... | collective-permute-start | bytes 196616 | tf_op jit(solution)/shard_map/ppermute | solution.py:115
  47.7 4.8 %collective-permute-start.4 = (f32[64,256]{1,0:T(8,128)S(1)}, f32[64,256]{1,0:T(8,128)S(1)}, u32[]{:S(2)}, u32[]{:S(2)}) collective-permute-start(f32[64,256]{1,0:T(8,128)S(1)} %add.102.refs_0_), channel_id=1, source_target_pairs={{0,1},{1,2},{2,3},{3,0},{4,5},{5,6},{6,7},{7,4},{8,9},{9,10},{10,1... | collective-permute-start | bytes 196616 | tf_op jit(solution)/shard_map/ppermute | solution.py:115
  61.7 13.0 %copy-start.1 = (bf16[256,256]{1,0:T(8,128)(2,1)}, bf16[256,256]{1,0:T(8,128)(2,1)S(1)}, u32[]{:S(2)}) copy-start(bf16[256,256]{1,0:T(8,128)(2,1)S(1)} %get-tuple-element.10) | copy-start | bytes 393220
  68.7 7.6 %collective-permute-start.7 = (f32[512,256]{1,0:T(8,128)S(1)}, f32[512,256]{1,0:T(8,128)S(1)}, u32[]{:S(2)}, u32[]{:S(2)}) collective-permute-start(f32[512,256]{1,0:T(8,128)S(1)} %slice_select_fusion), channel_id=1, source_target_pairs={{0,8},{8,0},{1,9},{9,1},{2,10},{10,2},{3,11},{11,3},{4,12},{12,4},... | collective-permute-start | bytes 1572872 | tf_op jit(solution)/shard_map/ppermute | solution.py:115
  75.0 8.7 %collective-permute-start.8 = (f32[128,256]{1,0:T(8,128)S(1)}, f32[128,256]{1,0:T(8,128)S(1)}, u32[]{:S(2)}, u32[]{:S(2)}) collective-permute-start(f32[128,256]{1,0:T(8,128)S(1)} %slice_select_fusion.1), channel_id=1, source_target_pairs={{0,8},{8,0},{1,9},{9,1},{2,10},{10,2},{3,11},{11,3},{4,12},{12,4},... | collective-permute-start | bytes 393224 | tf_op jit(solution)/shard_map/ppermute | solution.py:115
  77.2 45.0 %all-to-all-start.2 = ((f32[16,32,256]{2,1,0:T(8,128)}), f32[16,32,256]{2,1,0:T(8,128)S(1)}, u32[]{:S(2)}, u32[]{:S(2)}) async-start(f32[16,32,256]{2,1,0:T(8,128)} %bitcast.19), calls=%async_computation.2 | async-start | bytes 1048576 | tf_op jit(solution)/shard_map/all_to_all | solution.py:100
  83.8 4.4 %collective-permute-start.9 = (f32[32,256]{1,0:T(8,128)S(1)}, f32[32,256]{1,0:T(8,128)S(1)}, u32[]{:S(2)}, u32[]{:S(2)}) collective-permute-start(f32[32,256]{1,0:T(8,128)S(1)} %get-tuple-element.6), channel_id=1, source_target_pairs={{0,64},{64,128},{128,192},{192,0},{1,65},{65,129},{129,193},{193,1... | collective-permute-start | bytes 98312 | tf_op jit(solution)/shard_map/ppermute | solution.py:115
  85.2 4.8 %collective-permute-start.11 = (f32[32,256]{1,0:T(8,128)S(1)}, f32[32,256]{1,0:T(8,128)S(1)}, u32[]{:S(2)}, u32[]{:S(2)}) collective-permute-start(f32[32,256]{1,0:T(8,128)S(1)} %get-tuple-element.7), channel_id=1, source_target_pairs={{0,192},{64,0},{128,64},{192,128},{1,193},{65,1},{129,65},{193,129... | collective-permute-start | bytes 98312 | tf_op jit(solution)/shard_map/ppermute | solution.py:115
  86.6 5.7 %collective-permute-start.10 = (f32[32,256]{1,0:T(8,128)S(1)}, f32[32,256]{1,0:T(8,128)S(1)}, u32[]{:S(2)}, u32[]{:S(2)}) collective-permute-start(f32[32,256]{1,0:T(8,128)S(1)} %get-tuple-element.8), channel_id=1, source_target_pairs={{0,128},{64,192},{128,0},{192,64},{1,129},{65,193},{129,1},{193,65... | collective-permute-start | bytes 98312 | tf_op jit(solution)/shard_map/ppermute | solution.py:115
  92.2 5.7 %collective-permute-start.14 = (f32[32,256]{1,0:T(8,128)S(1)}, f32[32,256]{1,0:T(8,128)S(1)}, u32[]{:S(2)}, u32[]{:S(2)}) collective-permute-start(f32[32,256]{1,0:T(8,128)S(1)} %fusion.7), channel_id=1, source_target_pairs={{0,48},{16,0},{32,16},{48,32},{1,49},{17,1},{33,17},{49,33},{2,50}... | collective-permute-start | bytes 98312 | tf_op jit(solution)/shard_map/ppermute | solution.py:115
  96.9 3.7 %collective-permute-start.13 = (f32[32,256]{1,0:T(8,128)S(1)}, f32[32,256]{1,0:T(8,128)S(1)}, u32[]{:S(2)}, u32[]{:S(2)}) collective-permute-start(f32[32,256]{1,0:T(8,128)S(1)} %fusion.7), channel_id=1, source_target_pairs={{0,32},{16,48},{32,0},{48,16},{1,33},{17,49},{33,1},{49,17},{2,34}... | collective-permute-start | bytes 98312 | tf_op jit(solution)/shard_map/ppermute | solution.py:115
  96.9 4.6 %collective-permute-start.12 = (f32[32,256]{1,0:T(8,128)S(1)}, f32[32,256]{1,0:T(8,128)S(1)}, u32[]{:S(2)}, u32[]{:S(2)}) collective-permute-start(f32[32,256]{1,0:T(8,128)S(1)} %fusion.7), channel_id=1, source_target_pairs={{0,16},{16,32},{32,48},{48,0},{1,17},{17,33},{33,49},{49,1},{2,18}... | collective-permute-start | bytes 98312 | tf_op jit(solution)/shard_map/ppermute | solution.py:115
  101.5 6.0 %collective-permute-start.17 = (f32[32,256]{1,0:T(8,128)S(1)}, f32[32,256]{1,0:T(8,128)S(1)}, u32[]{:S(2)}, u32[]{:S(2)}) collective-permute-start(f32[32,256]{1,0:T(8,128)S(1)} %add_add_fusion.refs_0_), channel_id=1, source_target_pairs={{0,192},{64,0},{128,64},{192,128},{1,193},{65,1},{129,65},{193,129... | collective-permute-start | bytes 98312 | tf_op jit(solution)/shard_map/ppermute | solution.py:115
  102.3 5.8 %collective-permute-start.16 = (f32[32,256]{1,0:T(8,128)S(1)}, f32[32,256]{1,0:T(8,128)S(1)}, u32[]{:S(2)}, u32[]{:S(2)}) collective-permute-start(f32[32,256]{1,0:T(8,128)S(1)} %add_add_fusion.refs_0_), channel_id=1, source_target_pairs={{0,128},{64,192},{128,0},{192,64},{1,129},{65,193},{129,1},{193,65... | collective-permute-start | bytes 98312 | tf_op jit(solution)/shard_map/ppermute | solution.py:115
  103.0 9.0 %collective-permute-start.15 = (f32[32,256]{1,0:T(8,128)S(1)}, f32[32,256]{1,0:T(8,128)S(1)}, u32[]{:S(2)}, u32[]{:S(2)}) collective-permute-start(f32[32,256]{1,0:T(8,128)S(1)} %add_add_fusion.refs_0_), channel_id=1, source_target_pairs={{0,64},{64,128},{128,192},{192,0},{1,65},{65,129},{129,193},{193,1... | collective-permute-start | bytes 98312 | tf_op jit(solution)/shard_map/ppermute | solution.py:115
  103.8 8.3 %collective-permute-start.18 = (f32[32,256]{1,0:T(8,128)S(1)}, f32[32,256]{1,0:T(8,128)S(1)}, u32[]{:S(2)}, u32[]{:S(2)}) collective-permute-start(f32[32,256]{1,0:T(8,128)S(1)} %add_add_fusion.refs_0_), channel_id=1, source_target_pairs={{0,8},{8,0},{1,9},{9,1},{2,10},{10,2},{3,11},{11,3},{4,12},{12,4},... | collective-permute-start | bytes 98312 | tf_op jit(solution)/shard_map/ppermute | solution.py:115
  107.5 4.5 %collective-permute-start.21 = (f32[32,256]{1,0:T(8,128)S(1)}, f32[32,256]{1,0:T(8,128)S(1)}, u32[]{:S(2)}, u32[]{:S(2)}) collective-permute-start(f32[32,256]{1,0:T(8,128)S(1)} %collective-permute-done.17.refs_3_), channel_id=1, source_target_pairs={{0,8},{8,0},{1,9},{9,1},{2,10},{10,2},{3,11},{11,3},{4,12},{12,4},... | collective-permute-start | bytes 98312 | tf_op jit(solution)/shard_map/ppermute | solution.py:115
  108.1 4.7 %collective-permute-start.20 = (f32[32,256]{1,0:T(8,128)S(1)}, f32[32,256]{1,0:T(8,128)S(1)}, u32[]{:S(2)}, u32[]{:S(2)}) collective-permute-start(f32[32,256]{1,0:T(8,128)S(1)} %collective-permute-done.16.refs_2_), channel_id=1, source_target_pairs={{0,8},{8,0},{1,9},{9,1},{2,10},{10,2},{3,11},{11,3},{4,12},{12,4},... | collective-permute-start | bytes 98312 | tf_op jit(solution)/shard_map/ppermute | solution.py:115
  112.0 1.2 collective-permute-start.19
  135.5 3.1 %collective-permute-start.22 = (bf16[512,256]{1,0:T(8,128)(2,1)S(1)}, bf16[512,256]{1,0:T(8,128)(2,1)S(1)}, u32[]{:S(2)}, u32[]{:S(2)}) collective-permute-start(bf16[512,256]{1,0:T(8,128)(2,1)S(1)} %bitcast.78), channel_id=1, source_target_pairs={{0,8},{8,0},{1,9},{9,1},{2,10},{10,2},{3,11},{11,3},{4,12},{12,4},... | collective-permute-start | bytes 786440 | tf_op jit(solution)/shard_map/ppermute | solution.py:115
  138.8 28.7 %copy-start.2 = (bf16[1024,256]{1,0:T(8,128)(2,1)}, bf16[1024,256]{1,0:T(8,128)(2,1)S(1)}, u32[]{:S(2)}) copy-start(bf16[1024,256]{1,0:T(8,128)(2,1)S(1)} %maximum_select_fusion) | copy-start | bytes 1572868
  145.5 1.3 collective-permute-start.23
  146.8 2.6 %collective-permute-start.26 = (f32[16,256]{1,0:T(8,128)S(1)}, f32[16,256]{1,0:T(8,128)S(1)}, u32[]{:S(2)}, u32[]{:S(2)}) collective-permute-start(f32[16,256]{1,0:T(8,128)S(1)} %bitcast_add_fusion.2), channel_id=1, source_target_pairs={{0,192},{64,0},{128,64},{192,128},{1,193},{65,1},{129,65},{193,129... | collective-permute-start | bytes 49160 | tf_op jit(solution)/shard_map/ppermute | solution.py:115
  147.3 4.1 %collective-permute-start.25 = (f32[16,256]{1,0:T(8,128)S(1)}, f32[16,256]{1,0:T(8,128)S(1)}, u32[]{:S(2)}, u32[]{:S(2)}) collective-permute-start(f32[16,256]{1,0:T(8,128)S(1)} %bitcast_add_fusion.2), channel_id=1, source_target_pairs={{0,128},{64,192},{128,0},{192,64},{1,129},{65,193},{129,1},{193,65... | collective-permute-start | bytes 49160 | tf_op jit(solution)/shard_map/ppermute | solution.py:115
  147.6 4.1 %collective-permute-start.24 = (f32[16,256]{1,0:T(8,128)S(1)}, f32[16,256]{1,0:T(8,128)S(1)}, u32[]{:S(2)}, u32[]{:S(2)}) collective-permute-start(f32[16,256]{1,0:T(8,128)S(1)} %bitcast_add_fusion.2), channel_id=1, source_target_pairs={{0,64},{64,128},{128,192},{192,0},{1,65},{65,129},{129,193},{193,1... | collective-permute-start | bytes 49160 | tf_op jit(solution)/shard_map/ppermute | solution.py:115

commit v3 on v2

--- a/solution.py
+++ b/solution.py
@@ -22,6 +22,19 @@
     middle = rest.astype(jnp.bfloat16)
     low = (rest - middle.astype(jnp.float32)).astype(jnp.bfloat16)
     return high, middle, low
+
+
+def split_pair(a, b):
+    ah, am, al = pieces(a)
+    bh, bm, bl = pieces(b)
+    left = jnp.concatenate([ah, ah, am, ah, al, am], axis=0)
+    return left, jnp.concatenate([bh, bm, bh, bl, bh, bm], axis=0)
+
+
+def cross(a, b, **kw):
+    return lax.dot_general(
+        a, b, (((0,), (0,)), ((), ())), preferred_element_type=jnp.float32, **kw
+    )
 
 
 def inverse_kernel(places, total, *refs):
@@ -42,8 +55,10 @@
     whole_lane = lax.broadcasted_iota(jnp.int32, (n, n), 1)
 
     def step(k, carry):
+        panel, left, right = carry
         o = pl.multiple_of(k * B, B)
-        panel = m_ref[pl.ds(o, B), :]
+        cleared = (whole_row >= o) & (whole_lane >= o - B) & (whole_lane < o)
+        m_ref[...] = jnp.where(cleared, 0.0, m_ref[...]) - cross(left, right)
         front = pltpu.roll(panel, n - o, 1)
         cols = [jnp.broadcast_to(front[:, j:j + 1], (B, 128)) for j in range(B)]
         inside = (lane >= o) & (lane < o + B)
@@ -61,25 +76,17 @@
                 pivot = cols[m][j:j + 1, :] * scale
                 cols[m] = jnp.where(other, cols[m] - col * pivot, pivot)
         solved = jnp.concatenate(parts, axis=1)
-        below = jnp.where(lane >= o + B, panel, 0.0)
-        uh, um, ul = pieces(below)
-        wh, wm, wl = pieces(solved)
-        left = jnp.concatenate([uh, uh, um, uh, ul, um], axis=0)
-        right = jnp.concatenate([wh, wm, wh, wl, wh, wm], axis=0)
-        update = lax.dot_general(
-            left, right, (((0,), (0,)), ((), ())), preferred_element_type=jnp.float32
-        )
-        cleared = (whole_row >= o + B) & (whole_lane >= o) & (whole_lane < o + B)
-        m_ref[...] = jnp.where(cleared, 0.0, m_ref[...]) - update
+        left, right = split_pair(jnp.where(lane >= o + B, panel, 0.0), solved)
+        ahead = split_pair(front[:, :128], front[:, :128])[0][:, B:2 * B]
+        following = pl.multiple_of(jnp.minimum(o + B, n - B), B)
+        panel_next = jnp.where(inside, 0.0, m_ref[pl.ds(following, B), :]) - cross(ahead, right)
         m_ref[pl.ds(o, B), :] = jnp.where(lane < o, panel, jnp.where(inside, unit, 0.0))
         w_ref[pl.ds(o, B), :] = jnp.where(lane < o + B, solved, 0.0)
-        return carry
-
-    lax.fori_loop(0, n // B, step, 0)
-    x_ref[...] = lax.dot_general(
-        m_ref[...], w_ref[...], (((0,), (0,)), ((), ())),
-        precision=lax.Precision.HIGHEST, preferred_element_type=jnp.float32,
-    )
+        return panel_next, left, right
+
+    nothing = jnp.zeros((6 * B, n), jnp.bfloat16)
+    lax.fori_loop(0, n // B, step, (m_ref[0:B, :], nothing, nothing))
+    x_ref[...] = cross(m_ref[...], w_ref[...], precision=HIGHEST)
 
 
 def inverse(parts, places, gram_first, total):
@@ -132,6 +139,24 @@
     return [x] + [shift(x, axis, d) for d in range(1, lax.axis_size(axis))]
 
 
+def pair(x, axis, d):
+    return lax.ppermute(x, axis, [(s, s ^ d) for s in range(lax.axis_size(axis))])
+
+
+def quad_gather(x, axis):
+    return [x] + [pair(x, axis, d) for d in (1, 2, 3)]
+
+
+def ordered(parts, me):
+    odd = lax.rem(me, 2) == 1
+    low = [jnp.where(odd, parts[1], parts[0]), jnp.where(odd, parts[0], parts[1])]
+    high = [jnp.where(odd, parts[3], parts[2]), jnp.where(odd, parts[2], parts[3])]
+    up = me >= 2
+    first = [jnp.where(up, h, l) for l, h in zip(low, high)]
+    last = [jnp.where(up, l, h) for l, h in zip(low, high)]
+    return jnp.concatenate(first + last, axis=0)
+
+
 def keep(x, bit):
     half = x.shape[0] // 2
     low, high = x[:half], x[half:]
@@ -197,7 +222,10 @@
     mine = mine + shift(other, "core", 1)
     mttkrp_third = scatter_sum(mine, CHIP)
     third_solution = jnp.dot(mttkrp_third, inverse_third, precision=HIGHEST)
-    mine = gather(third_solution.astype(jnp.bfloat16), CHIP)
+    parts = quad_gather(third_solution.astype(jnp.bfloat16), "zl")
+    block = ordered(parts, lax.axis_index("zl"))
+    parts = quad_gather(block, "x")
+    mine = ordered(parts, lax.axis_index("x"))
     third_new = join(mine, shift(mine, "core", 1), core)
 
     back = jnp.einsum("ijk,kr->ijr", tensor, third_new, preferred_element_type=jnp.float32)
@@ -205,12 +233,12 @@
         "ijr,jr->ir", back, second_factor.astype(jnp.float32), precision=HIGHEST
     )
     partial_first = partial_first + shift(partial_first, "core", 1)
-    partial_first = ring_sum(partial_first, "x").astype(jnp.bfloat16)
+    scale = 1.0 / math.sqrt(second_total * third_total)
+    partial_first = (ring_sum(partial_first, "x") * scale).astype(jnp.bfloat16)
     axes = ("zl",) + NARROW
     n = lax.axis_size(axes)
     copies = jnp.broadcast_to(partial_first[None], (n,) + partial_first.shape)
     first_mode = jnp.sum(exchange(copies, axes), axis=0, dtype=jnp.float32)
-    first_mode = first_mode / math.sqrt(second_total * third_total)
     return (second_factor, third_new, first_mode)
 
 

time: 170 us -> 170 us (level)
  blocking collectives: 28.1 us -> 16.9 us
  starting transfers between devices: 65.8 us -> 72.8 us
  waiting for transfers between devices: 29.5 us -> 35.3 us
    all_to_all x2 -> x1, blocking collectives: 28.1 us -> 16.9 us  [exchange(): return lax.all_to_all(x, axes, 0, 0, tiled=True)]
    ppermute x0 -> x6, starting transfers between devices: none -> 7.33 us  [pair(): lax.ppermute(x, axis, [(s, s ^ d) for s in range(lax.axis_size(axis))])]
    ppermute x0 -> x6, waiting for transfers between devices: none -> 5.77 us  [pair(): lax.ppermute(x, axis, [(s, s ^ d) for s in range(lax.axis_size(axis))])]
  transfers between devices with their start and end apart: 30 -> 36, of which waited for: 17 -> 20; matrix products, arithmetic and copies ran while one was open for 2% -> 2% of each run, Pallas kernels for 11% -> 10%
where the time goes in v3:
time: 170 us; the launch traced here: 168 us
  starting transfers between devices  72.8 us (43%)
  waiting for transfers between devices  35.3 us (21%)
  matrix products  21 us (12%)
  blocking collectives  16.9 us (10%)
  Pallas kernels  16.4 us (10%)
  other arithmetic  2.79 us (2%)
    ppermute x27, starting transfers between devices, shift(): return lax.ppermute(x, axis, [(s, (s + d) % n) for s in range(n)])  43.9 us
    ppermute x27, waiting for transfers between devices, shift(): return lax.ppermute(x, axis, [(s, (s + d) % n) for s in range(n)])  23.5 us
    all_to_all x3, starting transfers between devices, exchange(): return lax.all_to_all(x, axes, 0, 0, tiled=True)  21.5 us
    all_to_all x1, blocking collectives, exchange(): return lax.all_to_all(x, axes, 0, 0, tiled=True)  16.9 us
    pallas_call x2, Pallas kernels, inverse(): pl.pallas_call(functools.partial(inverse_kernel, places, total), out_shap...  16.4 us
    ppermute x6, starting transfers between devices, pair(): lax.ppermute(x, axis, [(s, s ^ d) for s in range(lax.axis_size(axis))])  7.33 us
    dot_general x1, matrix products, on_device(): jnp.einsum('ijk,kr->ijr', tensor, third_new, preferred_element_type=jnp.f...  6.63 us
    dot_general x1, matrix products, on_device(): jnp.einsum('ijk,jr->ikr', tensor, second_factor, preferred_element_type=j...  6.56 us
  transfers between devices with their start and end apart: 36, of which 20 were waited for; matrix products, arithmetic and copies ran while one was open for 2% of the time, Pallas kernels for 10%

profile of v3, /device:TPU:1, one launch (start us, length us, event | category | flops | bytes accessed | tf_op | source)
XLA Modules:
  0.0 167.9 jit_solution(17608424840430229766)
XLA Ops:
  0.6 0.8 multiply_bitcast_fusion
  1.7 6.5 %multiply_reduce_fusion.1 = f32[256,256]{0,1:T(8,128)} fusion(bf16[16,256,1024]{2,1,0:T(8,128)(2,1)} %param.3, f32[256,16]{0,1:T(8,128)S(1)} %multiply_bitcast_fusion, bf16[1024,256]{1,0:T(8,128)(2,1)S(1)} %copy-done), kind=kOutput, calls=%fused_computation.3 | convolution fusion | flops 2149515264 | bytes 9191424 | tf_op jit(solution)/shard_map/ijk,kr->ijr/dot_general | solution.py:200
  8.1 11.6 %all-to-all-start = ((f32[8,32,256]{2,1,0:T(8,128)}), f32[8,32,256]{2,1,0:T(8,128)S(1)}, u32[]{:S(2)}, u32[]{:S(2)}) async-start(f32[8,32,256]{2,1,0:T(8,128)} %bitcast.8), calls=%async_computation | async-start | bytes 524288 | tf_op jit(solution)/shard_map/all_to_all | solution.py:107
  20.2 2.8 %collective-permute-start.2 = (f32[64,256]{1,0:T(8,128)S(1)}, f32[64,256]{1,0:T(8,128)S(1)}, u32[]{:S(2)}, u32[]{:S(2)}) collective-permute-start(f32[64,256]{1,0:T(8,128)S(1)} %get-tuple-element.14), channel_id=1, source_target_pairs={{0,3},{1,0},{2,1},{3,2},{4,7},{5,4},{6,5},{7,6},{8,11},{9,8},{10,9... | collective-permute-start | bytes 196616 | tf_op jit(solution)/shard_map/ppermute | solution.py:122
  24.1 6.0 %all-to-all-done = f32[8,32,256]{2,1,0:T(8,128)S(1)} async-done(((f32[8,32,256]{2,1,0:T(8,128)}), f32[8,32,256]{2,1,0:T(8,128)S(1)}, u32[]{:S(2)}, u32[]{:S(2)}) %all-to-all-start) | async-done | bytes 262176 | tf_op jit(solution)/shard_map/all_to_all | solution.py:107
  30.8 3.4 %all-to-all-start.1 = ((f32[8,32,256]{2,1,0:T(8,128)}), f32[8,32,256]{2,1,0:T(8,128)S(1)}, u32[]{:S(2)}, u32[]{:S(2)}) async-start(f32[8,32,256]{2,1,0:T(8,128)} %broadcast_in_dim.4), calls=%async_computation.1 | async-start | bytes 524288 | tf_op jit(solution)/shard_map/all_to_all | solution.py:107
  34.3 5.4 %collective-permute-start.3 = (f32[64,256]{1,0:T(8,128)S(1)}, f32[64,256]{1,0:T(8,128)S(1)}, u32[]{:S(2)}, u32[]{:S(2)}) collective-permute-start(f32[64,256]{1,0:T(8,128)S(1)} %fusion.5), channel_id=1, source_target_pairs={{0,4},{4,0},{1,5},{5,1},{2,6},{6,2},{3,7},{7,3},{8,12},{12,8},{9,1... | collective-permute-start | bytes 196616 | tf_op jit(solution)/shard_map/ppermute | solution.py:122
  39.6 4.6 %collective-permute-done.3 = f32[64,256]{1,0:T(8,128)S(1)} collective-permute-done((f32[64,256]{1,0:T(8,128)S(1)}, f32[64,256]{1,0:T(8,128)S(1)}, u32[]{:S(2)}, u32[]{:S(2)}) %collective-permute-start.3) | collective-permute-done | bytes 65568 | tf_op jit(solution)/shard_map/ppermute | solution.py:122
  44.2 1.9 %collective-permute-start.4 = (f32[64,256]{1,0:T(8,128)S(1)}, f32[64,256]{1,0:T(8,128)S(1)}, u32[]{:S(2)}, u32[]{:S(2)}) collective-permute-start(f32[64,256]{1,0:T(8,128)S(1)} %add.102.refs_0_), channel_id=1, source_target_pairs={{0,1},{1,2},{2,3},{3,0},{4,5},{5,6},{6,7},{7,4},{8,9},{9,10},{10,1... | collective-permute-start | bytes 196616 | tf_op jit(solution)/shard_map/ppermute | solution.py:122
  46.1 2.4 %collective-permute-start.5 = (f32[64,256]{1,0:T(8,128)S(1)}, f32[64,256]{1,0:T(8,128)S(1)}, u32[]{:S(2)}, u32[]{:S(2)}) collective-permute-start(f32[64,256]{1,0:T(8,128)S(1)} %add.102.refs_0_), channel_id=1, source_target_pairs={{0,2},{1,3},{2,0},{3,1},{4,6},{5,7},{6,4},{7,5},{8,10},{9,11},{10,... | collective-permute-start | bytes 196616 | tf_op jit(solution)/shard_map/ppermute | solution.py:122
  48.5 1.2 collective-permute-start.6
  49.9 0.9 collective-permute-done.5.refs_2_
  50.9 0.8 collective-permute-done.6.refs_3_
  51.6 8.2 %inverse.2 = f32[256,256]{1,0:T(8,128)S(1)} custom-call(f32[64,256]{1,0:T(8,128)S(1)} %add.102.refs_0_, f32[64,256]{1,0:T(8,128)S(1)} %collective-permute-done.4.refs_1_, f32[64,256]{1,0:T(8,128)S(1)} %collective-permute-done.5.refs_2_, f32[64,256]{1,0:T(8,128)S(1)} %collective-permute-done.6.refs_3_, f32[256,256]{1,0:T(8,128)S(1)} %convolution_multiply_fusion.refs_4_.refs_8_), custom_call_target="tpu_custom_call" | custom-call | flops 201326592 | bytes 524288 | tf_op jit(solution)/shard_map/inverse/pallas_call | solution.py:94
  60.3 6.6 %multiply_reduce_fusion = f32[256,1024]{1,0:T(8,128)S(1)} fusion(bf16[16,256,1024]{2,1,0:T(8,128)(2,1)} %param.3, f32[256,16]{0,1:T(8,128)S(1)} %multiply_bitcast_fusion, bf16[256,256]{1,0:T(8,128)(2,1)S(1)} %get-tuple-element.24), kind=kOutput, calls=%fused_computation | convolution fusion | flops 2155610112 | bytes 9584640 | tf_op jit(solution)/shard_map/ijk,jr->ikr/dot_general | solution.py:217
  67.2 6.2 %collective-permute-start.7 = (f32[512,256]{1,0:T(8,128)S(1)}, f32[512,256]{1,0:T(8,128)S(1)}, u32[]{:S(2)}, u32[]{:S(2)}) collective-permute-start(f32[512,256]{1,0:T(8,128)S(1)} %slice_select_fusion), channel_id=1, source_target_pairs={{0,8},{8,0},{1,9},{9,1},{2,10},{10,2},{3,11},{11,3},{4,12},{12,4},... | collective-permute-start | bytes 1572872 | tf_op jit(solution)/shard_map/ppermute | solution.py:122
  74.0 1.0 collective-permute-done.7
  75.0 0.9 select_add_fusion
  75.9 6.5 %all-to-all-start.2 = ((f32[16,32,256]{2,1,0:T(8,128)}), f32[16,32,256]{2,1,0:T(8,128)S(1)}, u32[]{:S(2)}, u32[]{:S(2)}) async-start(f32[16,32,256]{2,1,0:T(8,128)} %bitcast.19), calls=%async_computation.2 | async-start | bytes 1048576 | tf_op jit(solution)/shard_map/all_to_all | solution.py:107
  82.4 2.6 %collective-permute-start.11 = (f32[32,256]{1,0:T(8,128)S(1)}, f32[32,256]{1,0:T(8,128)S(1)}, u32[]{:S(2)}, u32[]{:S(2)}) collective-permute-start(f32[32,256]{1,0:T(8,128)S(1)} %get-tuple-element.17), channel_id=1, source_target_pairs={{0,192},{64,0},{128,64},{192,128},{1,193},{65,1},{129,65},{193,129... | collective-permute-start | bytes 98312 | tf_op jit(solution)/shard_map/ppermute | solution.py:122
  87.0 2.8 %collective-permute-done.10 = f32[32,256]{1,0:T(8,128)S(1)} collective-permute-done((f32[32,256]{1,0:T(8,128)S(1)}, f32[32,256]{1,0:T(8,128)S(1)}, u32[]{:S(2)}, u32[]{:S(2)}) %collective-permute-start.10) | collective-permute-done | bytes 32800 | tf_op jit(solution)/shard_map/ppermute | solution.py:122
  89.8 1.4 collective-permute-done.9
  91.2 5.1 %collective-permute-start.14 = (f32[32,256]{1,0:T(8,128)S(1)}, f32[32,256]{1,0:T(8,128)S(1)}, u32[]{:S(2)}, u32[]{:S(2)}) collective-permute-start(f32[32,256]{1,0:T(8,128)S(1)} %fusion.7), channel_id=1, source_target_pairs={{0,48},{16,0},{32,16},{48,32},{1,49},{17,1},{33,17},{49,33},{2,50}... | collective-permute-start | bytes 98312 | tf_op jit(solution)/shard_map/ppermute | solution.py:122
  97.4 2.9 %collective-permute-done.13 = f32[32,256]{1,0:T(8,128)S(1)} collective-permute-done((f32[32,256]{1,0:T(8,128)S(1)}, f32[32,256]{1,0:T(8,128)S(1)}, u32[]{:S(2)}, u32[]{:S(2)}) %collective-permute-start.13) | collective-permute-done | bytes 32800 | tf_op jit(solution)/shard_map/ppermute | solution.py:122
  100.3 0.9 collective-permute-done.12
  101.3 1.0 collective-permute-start.16
  102.3 1.6 collective-permute-start.17
  103.9 2.6 %collective-permute-start.18 = (f32[32,256]{1,0:T(8,128)S(1)}, f32[32,256]{1,0:T(8,128)S(1)}, u32[]{:S(2)}, u32[]{:S(2)}) collective-permute-start(f32[32,256]{1,0:T(8,128)S(1)} %add_add_fusion.refs_0_), channel_id=1, source_target_pairs={{0,8},{8,0},{1,9},{9,1},{2,10},{10,2},{3,11},{11,3},{4,12},{12,4},... | collective-permute-start | bytes 98312 | tf_op jit(solution)/shard_map/ppermute | solution.py:122
  106.5 1.4 collective-permute-start.19
  108.3 0.8 collective-permute-start.21
  109.2 0.8 collective-permute-done.21.refs_7_
  110.0 8.2 %inverse.3 = f32[256,256]{1,0:T(8,128)S(1)} custom-call(f32[32,256]{1,0:T(8,128)S(1)} %add_add_fusion.refs_0_, f32[32,256]{1,0:T(8,128)S(1)} %collective-permute-done.15.refs_1_, f32[32,256]{1,0:T(8,128)S(1)} %collective-permute-done.16.refs_2_, f32[32,256]{1,0:T(8,128)S(1)} %collective-permute-done.17.refs_3_, ...), custom_call_target="tpu_custom_call" | custom-call | flops 201326592 | bytes 524288 | tf_op jit(solution)/shard_map/inverse/pallas_call | solution.py:94
  119.6 2.6 %collective-permute-start.24 = (bf16[32,256]{1,0:T(8,128)(2,1)S(1)}, bf16[32,256]{1,0:T(8,128)(2,1)S(1)}, u32[]{:S(2)}, u32[]{:S(2)}) collective-permute-start(bf16[32,256]{1,0:T(8,128)(2,1)S(1)} %convolution_convert_fusion.1), channel_id=1, source_target_pairs={{0,16},{16,0},{32,48},{48,32},{1,17},{17,1},{33,49},{49,33},{2,18}... | collective-permute-start | bytes 49160 | tf_op jit(solution)/shard_map/ppermute | solution.py:143
  122.2 0.8 collective-permute-done.22
  123.6 1.5 collective-permute-start.27
  125.1 1.4 collective-permute-start.25
  126.5 0.9 collective-permute-start.26
  127.3 2.1 %collective-permute-done.25 = bf16[128,256]{1,0:T(8,128)(2,1)S(1)} collective-permute-done((bf16[128,256]{1,0:T(8,128)(2,1)S(1)}, bf16[128,256]{1,0:T(8,128)(2,1)S(1)}, u32[]{:S(2)}, u32[]{:S(2)}) %collective-permute-start.25) | collective-permute-done | bytes 65568 | tf_op jit(solution)/shard_map/ppermute | solution.py:143
  129.4 2.2 %collective-permute-done.26 = bf16[128,256]{1,0:T(8,128)(2,1)S(1)} collective-permute-done((bf16[128,256]{1,0:T(8,128)(2,1)S(1)}, bf16[128,256]{1,0:T(8,128)(2,1)S(1)}, u32[]{:S(2)}, u32[]{:S(2)}) %collective-permute-start.26) | collective-permute-done | bytes 65568 | tf_op jit(solution)/shard_map/ppermute | solution.py:143
  131.9 2.4 %collective-permute-start.28 = (bf16[512,256]{1,0:T(8,128)(2,1)S(1)}, bf16[512,256]{1,0:T(8,128)(2,1)S(1)}, u32[]{:S(2)}, u32[]{:S(2)}) collective-permute-start(bf16[512,256]{1,0:T(8,128)(2,1)S(1)} %pad_maximum_fusion), channel_id=1, source_target_pairs={{0,8},{8,0},{1,9},{9,1},{2,10},{10,2},{3,11},{11,3},{4,12},{12,4},... | collective-permute-start | bytes 786440 | tf_op jit(solution)/shard_map/ppermute | solution.py:122
  134.4 1.0 collective-permute-done.28
  135.6 6.6 %fusion = f32[256,16]{0,1:T(8,128)S(1)} fusion(bf16[16,256,1024]{2,1,0:T(8,128)(2,1)} %param.3, f32[256,256]{1,0:T(8,128)S(1)} %copy.34, bf16[1024,256]{1,0:T(8,128)(2,1)S(1)} %broadcast_select_fusion), kind=kOutput, calls=%fused_computation.2 | convolution fusion | flops 2149576704 | bytes 9191424 | tf_op jit(solution)/shard_map/ijk,kr->ijr/dot_general | solution.py:231
  142.7 0.8 collective-permute-done.29
  143.5 1.6 collective-permute-start.32
  145.2 1.0 collective-permute-start.31
  146.2 3.1 %collective-permute-done.31 = f32[16,256]{1,0:T(8,128)S(1)} collective-permute-done((f32[16,256]{1,0:T(8,128)S(1)}, f32[16,256]{1,0:T(8,128)S(1)}, u32[]{:S(2)}, u32[]{:S(2)}) %collective-permute-start.31) | collective-permute-done | bytes 16416 | tf_op jit(solution)/shard_map/ppermute | solution.py:122
  149.3 1.0 collective-permute-done.30
  150.3 16.9 %all_to_all.20 = bf16[32,16,256]{2,1,0:T(8,128)(2,1)S(1)} all-to-all(bf16[32,16,256]{2,1,0:T(8,128)(2,1)S(1)} %broadcast_in_dim.5), channel_id=1, replica_groups=mesh['x'=4,'zl'=4,'core'=2,'zh'=2,'y'=4] {'zl','zh','y'}, dimensions={0} | all-to-all | bytes 524288 | tf_op jit(solution)/shard_map/all_to_all | solution.py:107
  (76 shorter events, 11.1 us)
Async XLA Ops:
  0.6 1.1 copy-start
  1.7 48.0 %copy-start.3 = (bf16[16,256]{1,0:T(8,128)(2,1)S(1)}, bf16[16,256]{1,0:T(8,128)(2,1)}, u32[]{:S(2)}) copy-start(bf16[16,256]{1,0:T(8,128)(2,1)} %param.4) | copy-start | bytes 24580
  8.1 21.9 %all-to-all-start = ((f32[8,32,256]{2,1,0:T(8,128)}), f32[8,32,256]{2,1,0:T(8,128)S(1)}, u32[]{:S(2)}, u32[]{:S(2)}) async-start(f32[8,32,256]{2,1,0:T(8,128)} %bitcast.8), calls=%async_computation | async-start | bytes 524288 | tf_op jit(solution)/shard_map/all_to_all | solution.py:107
  20.2 14.0 %collective-permute-start.2 = (f32[64,256]{1,0:T(8,128)S(1)}, f32[64,256]{1,0:T(8,128)S(1)}, u32[]{:S(2)}, u32[]{:S(2)}) collective-permute-start(f32[64,256]{1,0:T(8,128)S(1)} %get-tuple-element.14), channel_id=1, source_target_pairs={{0,3},{1,0},{2,1},{3,2},{4,7},{5,4},{6,5},{7,6},{8,11},{9,8},{10,9... | collective-permute-start | bytes 196616 | tf_op jit(solution)/shard_map/ppermute | solution.py:122
  22.9 11.3 %collective-permute-start.1 = (f32[64,256]{1,0:T(8,128)S(1)}, f32[64,256]{1,0:T(8,128)S(1)}, u32[]{:S(2)}, u32[]{:S(2)}) collective-permute-start(f32[64,256]{1,0:T(8,128)S(1)} %get-tuple-element.15), channel_id=1, source_target_pairs={{0,2},{1,3},{2,0},{3,1},{4,6},{5,7},{6,4},{7,5},{8,10},{9,11},{10,... | collective-permute-start | bytes 196616 | tf_op jit(solution)/shard_map/ppermute | solution.py:122
  23.5 10.7 %collective-permute-start = (f32[64,256]{1,0:T(8,128)S(1)}, f32[64,256]{1,0:T(8,128)S(1)}, u32[]{:S(2)}, u32[]{:S(2)}) collective-permute-start(f32[64,256]{1,0:T(8,128)S(1)} %get-tuple-element.13), channel_id=1, source_target_pairs={{0,1},{1,2},{2,3},{3,0},{4,5},{5,6},{6,7},{7,4},{8,9},{9,10},{10,1... | collective-permute-start | bytes 196616 | tf_op jit(solution)/shard_map/ppermute | solution.py:122
  30.8 29.1 %all-to-all-start.1 = ((f32[8,32,256]{2,1,0:T(8,128)}), f32[8,32,256]{2,1,0:T(8,128)S(1)}, u32[]{:S(2)}, u32[]{:S(2)}) async-start(f32[8,32,256]{2,1,0:T(8,128)} %broadcast_in_dim.4), calls=%async_computation.1 | async-start | bytes 524288 | tf_op jit(solution)/shard_map/all_to_all | solution.py:107
  34.3 9.9 %collective-permute-start.3 = (f32[64,256]{1,0:T(8,128)S(1)}, f32[64,256]{1,0:T(8,128)S(1)}, u32[]{:S(2)}, u32[]{:S(2)}) collective-permute-start(f32[64,256]{1,0:T(8,128)S(1)} %fusion.5), channel_id=1, source_target_pairs={{0,4},{4,0},{1,5},{5,1},{2,6},{6,2},{3,7},{7,3},{8,12},{12,8},{9,1... | collective-permute-start | bytes 196616 | tf_op jit(solution)/shard_map/ppermute | solution.py:122
  44.2 5.7 %collective-permute-start.4 = (f32[64,256]{1,0:T(8,128)S(1)}, f32[64,256]{1,0:T(8,128)S(1)}, u32[]{:S(2)}, u32[]{:S(2)}) collective-permute-start(f32[64,256]{1,0:T(8,128)S(1)} %add.102.refs_0_), channel_id=1, source_target_pairs={{0,1},{1,2},{2,3},{3,0},{4,5},{5,6},{6,7},{7,4},{8,9},{9,10},{10,1... | collective-permute-start | bytes 196616 | tf_op jit(solution)/shard_map/ppermute | solution.py:122
  46.1 4.7 %collective-permute-start.5 = (f32[64,256]{1,0:T(8,128)S(1)}, f32[64,256]{1,0:T(8,128)S(1)}, u32[]{:S(2)}, u32[]{:S(2)}) collective-permute-start(f32[64,256]{1,0:T(8,128)S(1)} %add.102.refs_0_), channel_id=1, source_target_pairs={{0,2},{1,3},{2,0},{3,1},{4,6},{5,7},{6,4},{7,5},{8,10},{9,11},{10,... | collective-permute-start | bytes 196616 | tf_op jit(solution)/shard_map/ppermute | solution.py:122
  48.5 3.1 %collective-permute-start.6 = (f32[64,256]{1,0:T(8,128)S(1)}, f32[64,256]{1,0:T(8,128)S(1)}, u32[]{:S(2)}, u32[]{:S(2)}) collective-permute-start(f32[64,256]{1,0:T(8,128)S(1)} %add.102.refs_0_), channel_id=1, source_target_pairs={{0,3},{1,0},{2,1},{3,2},{4,7},{5,4},{6,5},{7,6},{8,11},{9,8},{10,9... | collective-permute-start | bytes 196616 | tf_op jit(solution)/shard_map/ppermute | solution.py:122
  60.2 13.2 %copy-start.1 = (bf16[256,256]{1,0:T(8,128)(2,1)}, bf16[256,256]{1,0:T(8,128)(2,1)S(1)}, u32[]{:S(2)}) copy-start(bf16[256,256]{1,0:T(8,128)(2,1)S(1)} %get-tuple-element.24) | copy-start | bytes 393220
  67.2 7.7 %collective-permute-start.7 = (f32[512,256]{1,0:T(8,128)S(1)}, f32[512,256]{1,0:T(8,128)S(1)}, u32[]{:S(2)}, u32[]{:S(2)}) collective-permute-start(f32[512,256]{1,0:T(8,128)S(1)} %slice_select_fusion), channel_id=1, source_target_pairs={{0,8},{8,0},{1,9},{9,1},{2,10},{10,2},{3,11},{11,3},{4,12},{12,4},... | collective-permute-start | bytes 1572872 | tf_op jit(solution)/shard_map/ppermute | solution.py:122
  73.7 8.7 %collective-permute-start.8 = (f32[128,256]{1,0:T(8,128)S(1)}, f32[128,256]{1,0:T(8,128)S(1)}, u32[]{:S(2)}, u32[]{:S(2)}) collective-permute-start(f32[128,256]{1,0:T(8,128)S(1)} %slice_select_fusion.1), channel_id=1, source_target_pairs={{0,8},{8,0},{1,9},{9,1},{2,10},{10,2},{3,11},{11,3},{4,12},{12,4},... | collective-permute-start | bytes 393224 | tf_op jit(solution)/shard_map/ppermute | solution.py:122
  75.9 42.4 %all-to-all-start.2 = ((f32[16,32,256]{2,1,0:T(8,128)}), f32[16,32,256]{2,1,0:T(8,128)S(1)}, u32[]{:S(2)}, u32[]{:S(2)}) async-start(f32[16,32,256]{2,1,0:T(8,128)} %bitcast.19), calls=%async_computation.2 | async-start | bytes 1048576 | tf_op jit(solution)/shard_map/all_to_all | solution.py:107
  82.4 4.5 %collective-permute-start.11 = (f32[32,256]{1,0:T(8,128)S(1)}, f32[32,256]{1,0:T(8,128)S(1)}, u32[]{:S(2)}, u32[]{:S(2)}) collective-permute-start(f32[32,256]{1,0:T(8,128)S(1)} %get-tuple-element.17), channel_id=1, source_target_pairs={{0,192},{64,0},{128,64},{192,128},{1,193},{65,1},{129,65},{193,129... | collective-permute-start | bytes 98312 | tf_op jit(solution)/shard_map/ppermute | solution.py:122
  85.1 4.7 %collective-permute-start.10 = (f32[32,256]{1,0:T(8,128)S(1)}, f32[32,256]{1,0:T(8,128)S(1)}, u32[]{:S(2)}, u32[]{:S(2)}) collective-permute-start(f32[32,256]{1,0:T(8,128)S(1)} %get-tuple-element.18), channel_id=1, source_target_pairs={{0,128},{64,192},{128,0},{192,64},{1,129},{65,193},{129,1},{193,65... | collective-permute-start | bytes 98312 | tf_op jit(solution)/shard_map/ppermute | solution.py:122
  85.7 5.5 %collective-permute-start.9 = (f32[32,256]{1,0:T(8,128)S(1)}, f32[32,256]{1,0:T(8,128)S(1)}, u32[]{:S(2)}, u32[]{:S(2)}) collective-permute-start(f32[32,256]{1,0:T(8,128)S(1)} %get-tuple-element.16), channel_id=1, source_target_pairs={{0,64},{64,128},{128,192},{192,0},{1,65},{65,129},{129,193},{193,1... | collective-permute-start | bytes 98312 | tf_op jit(solution)/shard_map/ppermute | solution.py:122
  91.2 6.1 %collective-permute-start.14 = (f32[32,256]{1,0:T(8,128)S(1)}, f32[32,256]{1,0:T(8,128)S(1)}, u32[]{:S(2)}, u32[]{:S(2)}) collective-permute-start(f32[32,256]{1,0:T(8,128)S(1)} %fusion.7), channel_id=1, source_target_pairs={{0,48},{16,0},{32,16},{48,32},{1,49},{17,1},{33,17},{49,33},{2,50}... | collective-permute-start | bytes 98312 | tf_op jit(solution)/shard_map/ppermute | solution.py:122
  96.3 4.0 %collective-permute-start.13 = (f32[32,256]{1,0:T(8,128)S(1)}, f32[32,256]{1,0:T(8,128)S(1)}, u32[]{:S(2)}, u32[]{:S(2)}) collective-permute-start(f32[32,256]{1,0:T(8,128)S(1)} %fusion.7), channel_id=1, source_target_pairs={{0,32},{16,48},{32,0},{48,16},{1,33},{17,49},{33,1},{49,17},{2,34}... | collective-permute-start | bytes 98312 | tf_op jit(solution)/shard_map/ppermute | solution.py:122
  96.3 4.8 %collective-permute-start.12 = (f32[32,256]{1,0:T(8,128)S(1)}, f32[32,256]{1,0:T(8,128)S(1)}, u32[]{:S(2)}, u32[]{:S(2)}) collective-permute-start(f32[32,256]{1,0:T(8,128)S(1)} %fusion.7), channel_id=1, source_target_pairs={{0,16},{16,32},{32,48},{48,0},{1,17},{17,33},{33,49},{49,1},{2,18}... | collective-permute-start | bytes 98312 | tf_op jit(solution)/shard_map/ppermute | solution.py:122
  101.2 5.3 %collective-permute-start.15 = (f32[32,256]{1,0:T(8,128)S(1)}, f32[32,256]{1,0:T(8,128)S(1)}, u32[]{:S(2)}, u32[]{:S(2)}) collective-permute-start(f32[32,256]{1,0:T(8,128)S(1)} %add_add_fusion.refs_0_), channel_id=1, source_target_pairs={{0,64},{64,128},{128,192},{192,0},{1,65},{65,129},{129,193},{193,1... | collective-permute-start | bytes 98312 | tf_op jit(solution)/shard_map/ppermute | solution.py:122
  101.3 6.7 %collective-permute-start.16 = (f32[32,256]{1,0:T(8,128)S(1)}, f32[32,256]{1,0:T(8,128)S(1)}, u32[]{:S(2)}, u32[]{:S(2)}) collective-permute-start(f32[32,256]{1,0:T(8,128)S(1)} %add_add_fusion.refs_0_), channel_id=1, source_target_pairs={{0,128},{64,192},{128,0},{192,64},{1,129},{65,193},{129,1},{193,65... | collective-permute-start | bytes 98312 | tf_op jit(solution)/shard_map/ppermute | solution.py:122
  102.3 6.0 %collective-permute-start.17 = (f32[32,256]{1,0:T(8,128)S(1)}, f32[32,256]{1,0:T(8,128)S(1)}, u32[]{:S(2)}, u32[]{:S(2)}) collective-permute-start(f32[32,256]{1,0:T(8,128)S(1)} %add_add_fusion.refs_0_), channel_id=1, source_target_pairs={{0,192},{64,0},{128,64},{192,128},{1,193},{65,1},{129,65},{193,129... | collective-permute-start | bytes 98312 | tf_op jit(solution)/shard_map/ppermute | solution.py:122
  103.9 5.2 %collective-permute-start.18 = (f32[32,256]{1,0:T(8,128)S(1)}, f32[32,256]{1,0:T(8,128)S(1)}, u32[]{:S(2)}, u32[]{:S(2)}) collective-permute-start(f32[32,256]{1,0:T(8,128)S(1)} %add_add_fusion.refs_0_), channel_id=1, source_target_pairs={{0,8},{8,0},{1,9},{9,1},{2,10},{10,2},{3,11},{11,3},{4,12},{12,4},... | collective-permute-start | bytes 98312 | tf_op jit(solution)/shard_map/ppermute | solution.py:122
  106.5 2.7 %collective-permute-start.19 = (f32[32,256]{1,0:T(8,128)S(1)}, f32[32,256]{1,0:T(8,128)S(1)}, u32[]{:S(2)}, u32[]{:S(2)}) collective-permute-start(f32[32,256]{1,0:T(8,128)S(1)} %collective-permute-done.15.refs_1_), channel_id=1, source_target_pairs={{0,8},{8,0},{1,9},{9,1},{2,10},{10,2},{3,11},{11,3},{4,12},{12,4},... | collective-permute-start | bytes 98312 | tf_op jit(solution)/shard_map/ppermute | solution.py:122
  108.0 1.3 collective-permute-start.20
  108.3 1.7 collective-permute-start.21
  118.5 4.5 %collective-permute-start.22 = (bf16[32,256]{1,0:T(8,128)(2,1)S(1)}, bf16[32,256]{1,0:T(8,128)(2,1)S(1)}, u32[]{:S(2)}, u32[]{:S(2)}) collective-permute-start(bf16[32,256]{1,0:T(8,128)(2,1)S(1)} %convolution_convert_fusion.1), channel_id=1, source_target_pairs={{0,48},{16,32},{32,16},{48,0},{1,49},{17,33},{33,17},{49,1},{2,50}... | collective-permute-start | bytes 49160 | tf_op jit(solution)/shard_map/ppermute | solution.py:143
  118.9 4.1 %collective-permute-start.23 = (bf16[32,256]{1,0:T(8,128)(2,1)S(1)}, bf16[32,256]{1,0:T(8,128)(2,1)S(1)}, u32[]{:S(2)}, u32[]{:S(2)}) collective-permute-start(bf16[32,256]{1,0:T(8,128)(2,1)S(1)} %convolution_convert_fusion.1), channel_id=1, source_target_pairs={{0,32},{16,48},{32,0},{48,16},{1,33},{17,49},{33,1},{49,17},{2,34}... | collective-permute-start | bytes 49160 | tf_op jit(solution)/shard_map/ppermute | solution.py:143
  119.6 4.0 %collective-permute-start.24 = (bf16[32,256]{1,0:T(8,128)(2,1)S(1)}, bf16[32,256]{1,0:T(8,128)(2,1)S(1)}, u32[]{:S(2)}, u32[]{:S(2)}) collective-permute-start(bf16[32,256]{1,0:T(8,128)(2,1)S(1)} %convolution_convert_fusion.1), channel_id=1, source_target_pairs={{0,16},{16,0},{32,48},{48,32},{1,17},{17,1},{33,49},{49,33},{2,18}... | collective-permute-start | bytes 49160 | tf_op jit(solution)/shard_map/ppermute | solution.py:143
  123.6 3.7 %collective-permute-start.27 = (bf16[128,256]{1,0:T(8,128)(2,1)S(1)}, bf16[128,256]{1,0:T(8,128)(2,1)S(1)}, u32[]{:S(2)}, u32[]{:S(2)}) collective-permute-start(bf16[128,256]{1,0:T(8,128)(2,1)S(1)} %pad_maximum_fusion.1), channel_id=1, source_target_pairs={{0,64},{64,0},{128,192},{192,128},{1,65},{65,1},{129,193},{193,129... | collective-permute-start | bytes 196616 | tf_op jit(solution)/shard_map/ppermute | solution.py:143
  125.1 4.3 %collective-permute-start.25 = (bf16[128,256]{1,0:T(8,128)(2,1)S(1)}, bf16[128,256]{1,0:T(8,128)(2,1)S(1)}, u32[]{:S(2)}, u32[]{:S(2)}) collective-permute-start(bf16[128,256]{1,0:T(8,128)(2,1)S(1)} %pad_maximum_fusion.1), channel_id=1, source_target_pairs={{0,192},{64,128},{128,64},{192,0},{1,193},{65,129},{129,65},{193,1... | collective-permute-start | bytes 196616 | tf_op jit(solution)/shard_map/ppermute | solution.py:143
  126.5 5.2 %collective-permute-start.26 = (bf16[128,256]{1,0:T(8,128)(2,1)S(1)}, bf16[128,256]{1,0:T(8,128)(2,1)S(1)}, u32[]{:S(2)}, u32[]{:S(2)}) collective-permute-start(bf16[128,256]{1,0:T(8,128)(2,1)S(1)} %pad_maximum_fusion.1), channel_id=1, source_target_pairs={{0,128},{64,192},{128,0},{192,64},{1,129},{65,193},{129,1},{193,65... | collective-permute-start | bytes 196616 | tf_op jit(solution)/shard_map/ppermute | solution.py:143
  131.9 3.5 %collective-permute-start.28 = (bf16[512,256]{1,0:T(8,128)(2,1)S(1)}, bf16[512,256]{1,0:T(8,128)(2,1)S(1)}, u32[]{:S(2)}, u32[]{:S(2)}) collective-permute-start(bf16[512,256]{1,0:T(8,128)(2,1)S(1)} %pad_maximum_fusion), channel_id=1, source_target_pairs={{0,8},{8,0},{1,9},{9,1},{2,10},{10,2},{3,11},{11,3},{4,12},{12,4},... | collective-permute-start | bytes 786440 | tf_op jit(solution)/shard_map/ppermute | solution.py:122
  135.6 32.3 %copy-start.2 = (bf16[1024,256]{1,0:T(8,128)(2,1)}, bf16[1024,256]{1,0:T(8,128)(2,1)S(1)}, u32[]{:S(2)}) copy-start(bf16[1024,256]{1,0:T(8,128)(2,1)S(1)} %broadcast_select_fusion) | copy-start | bytes 1572868
  142.2 1.3 collective-permute-start.29
  143.5 2.6 %collective-permute-start.32 = (f32[16,256]{1,0:T(8,128)S(1)}, f32[16,256]{1,0:T(8,128)S(1)}, u32[]{:S(2)}, u32[]{:S(2)}) collective-permute-start(f32[16,256]{1,0:T(8,128)S(1)} %bitcast_add_fusion.2), channel_id=1, source_target_pairs={{0,192},{64,0},{128,64},{192,128},{1,193},{65,1},{129,65},{193,129... | collective-permute-start | bytes 49160 | tf_op jit(solution)/shard_map/ppermute | solution.py:122
  145.2 4.1 %collective-permute-start.31 = (f32[16,256]{1,0:T(8,128)S(1)}, f32[16,256]{1,0:T(8,128)S(1)}, u32[]{:S(2)}, u32[]{:S(2)}) collective-permute-start(f32[16,256]{1,0:T(8,128)S(1)} %bitcast_add_fusion.2), channel_id=1, source_target_pairs={{0,128},{64,192},{128,0},{192,64},{1,129},{65,193},{129,1},{193,65... | collective-permute-start | bytes 49160 | tf_op jit(solution)/shard_map/ppermute | solution.py:122
  146.1 4.1 %collective-permute-start.30 = (f32[16,256]{1,0:T(8,128)S(1)}, f32[16,256]{1,0:T(8,128)S(1)}, u32[]{:S(2)}, u32[]{:S(2)}) collective-permute-start(f32[16,256]{1,0:T(8,128)S(1)} %bitcast_add_fusion.2), channel_id=1, source_target_pairs={{0,64},{64,128},{128,192},{192,0},{1,65},{65,129},{129,193},{193,1... | collective-permute-start | bytes 49160 | tf_op jit(solution)/shard_map/ppermute | solution.py:122

commit v4 on v3

--- a/solution.py
+++ b/solution.py
@@ -169,16 +169,15 @@
     )
 
 
-def narrow_places():
+def quad_places():
+    me = lax.axis_index("x")
+    odd = lax.rem(me, 2)
+    return [me, me + 1 - 2 * odd, lax.rem(me + 2, 4), 3 - me]
+
+
+def ring_places():
     me = lax.axis_index("y")
     return [lax.rem(me + 4 - d, 4) for d in range(4)]
-
-
-def wide_places():
-    me = lax.axis_index("x")
-    core = lax.axis_index("core")
-    ring = [lax.rem(me + 4 - d, 4) for d in range(4)]
-    return [core * 4 + r for r in ring] + [(1 - core) * 4 + r for r in ring]
 
 
 def on_device(tensor, first_factor, third_factor):
@@ -195,7 +194,7 @@
     gram_part = ring_scatter(gram_part, "y")
     gram_part = ring_sum(gram_part, "zh")
     parts = ring_gather(gram_part, "y")
-    inverse_second = inverse(parts, narrow_places, gram_first, third_total)
+    inverse_second = inverse(parts, ring_places, gram_first, third_total)
 
     contracted = jnp.einsum("ijk,kr->ijr", tensor, third_factor, preferred_element_type=jnp.float32)
     partial_second = jnp.einsum(
@@ -206,13 +205,12 @@
     second_factor = jnp.dot(mttkrp_second, inverse_second, precision=HIGHEST).astype(jnp.bfloat16)
 
     gram_local = jnp.dot(second_factor.T, second_factor, preferred_element_type=jnp.float32)
-    mine, other = keep(gram_local, core)
-    mine = mine + shift(other, "core", 1)
-    mine = ring_scatter(mine, "x")
-    mine = ring_sum(mine, "zl")
-    parts = ring_gather(mine, "x")
-    parts = parts + [shift(part, "core", 1) for part in parts]
-    inverse_third = inverse(parts, wide_places, gram_first, second_total)
+    mine = scatter_sum(gram_local, WIDE)
+    mine = join(mine, shift(mine, "core", 1), core)
+    parts = quad_gather(mine, "zl")
+    mine = ordered(parts, lax.axis_index("zl"))
+    parts = quad_gather(mine, "x")
+    inverse_third = inverse(parts, quad_places, gram_first, second_total)
 
     middle = jnp.einsum("ijk,jr->ikr", tensor, second_factor, preferred_element_type=jnp.float32)
     partial_third = jnp.einsum(
@@ -222,10 +220,7 @@
     mine = mine + shift(other, "core", 1)
     mttkrp_third = scatter_sum(mine, CHIP)
     third_solution = jnp.dot(mttkrp_third, inverse_third, precision=HIGHEST)
-    parts = quad_gather(third_solution.astype(jnp.bfloat16), "zl")
-    block = ordered(parts, lax.axis_index("zl"))
-    parts = quad_gather(block, "x")
-    mine = ordered(parts, lax.axis_index("x"))
+    mine = gather(third_solution.astype(jnp.bfloat16), CHIP)
     third_new = join(mine, shift(mine, "core", 1), core)
 
     back = jnp.einsum("ijk,kr->ijr", tensor, third_new, preferred_element_type=jnp.float32)

time: 170 us -> 177 us (1.041)
  starting transfers between devices: 72.8 us -> 57.9 us
  blocking collectives: 16.9 us -> 28.6 us
  waiting for transfers between devices: 35.3 us -> 44.7 us
    ppermute x27 -> x14, starting transfers between devices: 43.9 us -> 25.4 us  [shift(): return lax.ppermute(x, axis, [(s, (s + d) % n) for s in range(n)])]
    all_to_all x1 -> x2, blocking collectives: 16.9 us -> 28.6 us  [exchange(): return lax.all_to_all(x, axes, 0, 0, tiled=True)]
    all_to_all x3 -> x4, waiting for transfers between devices: 5.98 us -> 15.6 us  [exchange(): return lax.all_to_all(x, axes, 0, 0, tiled=True)]
    ppermute x27 -> x14, waiting for transfers between devices: 23.5 us -> 14.9 us  [shift(): return lax.ppermute(x, axis, [(s, (s + d) % n) for s in range(n)])]
    ppermute x6, waiting for transfers between devices: 5.77 us -> 14.1 us  [pair(): lax.ppermute(x, axis, [(s, s ^ d) for s in range(lax.axis_size(axis))])]
    all_to_all x3 -> x4, starting transfers between devices: 21.5 us -> 25.6 us  [exchange(): return lax.all_to_all(x, axes, 0, 0, tiled=True)]
  transfers between devices with their start and end apart: 36 -> 24, of which waited for: 20 -> 15; matrix products, arithmetic and copies ran while one was open for 2% -> 2% of each run, Pallas kernels for 10% -> 9%
where the time goes in v4:
time: 177 us; the launch traced here: 175 us
  starting transfers between devices  57.9 us (33%)
  waiting for transfers between devices  44.7 us (25%)
  blocking collectives  28.6 us (16%)
  matrix products  21.8 us (12%)
  Pallas kernels  16.4 us (9%)
  other arithmetic  2.76 us (2%)
    all_to_all x2, blocking collectives, exchange(): return lax.all_to_all(x, axes, 0, 0, tiled=True)  28.6 us
    all_to_all x4, starting transfers between devices, exchange(): return lax.all_to_all(x, axes, 0, 0, tiled=True)  25.6 us
    ppermute x14, starting transfers between devices, shift(): return lax.ppermute(x, axis, [(s, (s + d) % n) for s in range(n)])  25.4 us
    pallas_call x2, Pallas kernels, inverse(): pl.pallas_call(functools.partial(inverse_kernel, places, total), out_shap...  16.4 us
    all_to_all x4, waiting for transfers between devices, exchange(): return lax.all_to_all(x, axes, 0, 0, tiled=True)  15.6 us
    ppermute x14, waiting for transfers between devices, shift(): return lax.ppermute(x, axis, [(s, (s + d) % n) for s in range(n)])  14.9 us
    ppermute x6, waiting for transfers between devices, pair(): lax.ppermute(x, axis, [(s, s ^ d) for s in range(lax.axis_size(axis))])  14.1 us
    ppermute x6, starting transfers between devices, pair(): lax.ppermute(x, axis, [(s, s ^ d) for s in range(lax.axis_size(axis))])  6.95 us
  transfers between devices with their start and end apart: 24, of which 15 were waited for; matrix products, arithmetic and copies ran while one was open for 2% of the time, Pallas kernels for 9%

profile of v4, /device:TPU:1, one launch (start us, length us, event | category | flops | bytes accessed | tf_op | source)
XLA Modules:
  0.0 174.8 jit_solution(7166827261601478610)
XLA Ops:
  0.6 0.8 multiply_bitcast_fusion
  1.7 6.4 %multiply_reduce_fusion.1 = f32[256,256]{0,1:T(8,128)} fusion(bf16[16,256,1024]{2,1,0:T(8,128)(2,1)} %param.3, f32[256,16]{0,1:T(8,128)S(1)} %multiply_bitcast_fusion, bf16[1024,256]{1,0:T(8,128)(2,1)S(1)} %copy-done), kind=kOutput, calls=%fused_computation.3 | convolution fusion | flops 2149515264 | bytes 9191424 | tf_op jit(solution)/shard_map/ijk,kr->ijr/dot_general | solution.py:199
  8.1 11.6 %all-to-all-start = ((f32[8,32,256]{2,1,0:T(8,128)}), f32[8,32,256]{2,1,0:T(8,128)S(1)}, u32[]{:S(2)}, u32[]{:S(2)}) async-start(f32[8,32,256]{2,1,0:T(8,128)} %bitcast.8), calls=%async_computation | async-start | bytes 524288 | tf_op jit(solution)/shard_map/all_to_all | solution.py:107
  20.2 1.5 collective-permute-start
  21.7 1.3 collective-permute-start.2
  23.0 1.7 collective-permute-start.1
  24.7 5.3 %all-to-all-done = f32[8,32,256]{2,1,0:T(8,128)S(1)} async-done(((f32[8,32,256]{2,1,0:T(8,128)}), f32[8,32,256]{2,1,0:T(8,128)S(1)}, u32[]{:S(2)}, u32[]{:S(2)}) %all-to-all-start) | async-done | bytes 262176 | tf_op jit(solution)/shard_map/all_to_all | solution.py:107
  30.0 0.7 broadcast_in_dim.6
  30.7 3.4 %all-to-all-start.1 = ((f32[8,32,256]{2,1,0:T(8,128)}), f32[8,32,256]{2,1,0:T(8,128)S(1)}, u32[]{:S(2)}, u32[]{:S(2)}) async-start(f32[8,32,256]{2,1,0:T(8,128)} %broadcast_in_dim.6), calls=%async_computation.1 | async-start | bytes 524288 | tf_op jit(solution)/shard_map/all_to_all | solution.py:107
  34.2 5.4 %collective-permute-start.3 = (f32[64,256]{1,0:T(8,128)S(1)}, f32[64,256]{1,0:T(8,128)S(1)}, u32[]{:S(2)}, u32[]{:S(2)}) collective-permute-start(f32[64,256]{1,0:T(8,128)S(1)} %fusion.5), channel_id=1, source_target_pairs={{0,4},{4,0},{1,5},{5,1},{2,6},{6,2},{3,7},{7,3},{8,12},{12,8},{9,1... | collective-permute-start | bytes 196616 | tf_op jit(solution)/shard_map/ppermute | solution.py:122
  39.6 4.5 %collective-permute-done.3 = f32[64,256]{1,0:T(8,128)S(1)} collective-permute-done((f32[64,256]{1,0:T(8,128)S(1)}, f32[64,256]{1,0:T(8,128)S(1)}, u32[]{:S(2)}, u32[]{:S(2)}) %collective-permute-start.3) | collective-permute-done | bytes 65568 | tf_op jit(solution)/shard_map/ppermute | solution.py:122
  44.0 3.1 %collective-permute-start.6 = (f32[64,256]{1,0:T(8,128)S(1)}, f32[64,256]{1,0:T(8,128)S(1)}, u32[]{:S(2)}, u32[]{:S(2)}) collective-permute-start(f32[64,256]{1,0:T(8,128)S(1)} %add.59.refs_0_), channel_id=1, source_target_pairs={{0,3},{1,0},{2,1},{3,2},{4,7},{5,4},{6,5},{7,6},{8,11},{9,8},{10,9... | collective-permute-start | bytes 196616 | tf_op jit(solution)/shard_map/ppermute | solution.py:122
  47.1 0.6 collective-permute-start.5
  47.7 0.6 collective-permute-start.4
  48.5 3.3 %collective-permute-done.5.refs_2_ = f32[64,256]{1,0:T(8,128)S(1)} collective-permute-done((f32[64,256]{1,0:T(8,128)S(1)}, f32[64,256]{1,0:T(8,128)S(1)}, u32[]{:S(2)}, u32[]{:S(2)}) %collective-permute-start.5) | collective-permute-done | bytes 65568 | tf_op jit(solution)/shard_map/ppermute | solution.py:122
  51.8 0.7 collective-permute-done.4.refs_1_
  52.4 8.2 %inverse.2 = f32[256,256]{1,0:T(8,128)S(1)} custom-call(f32[64,256]{1,0:T(8,128)S(1)} %add.59.refs_0_, f32[64,256]{1,0:T(8,128)S(1)} %collective-permute-done.4.refs_1_, f32[64,256]{1,0:T(8,128)S(1)} %collective-permute-done.5.refs_2_, f32[64,256]{1,0:T(8,128)S(1)} %collective-permute-done.6.refs_3_, f32[256,256]{1,0:T(8,128)S(1)} %convolution_multiply_fusion.refs_4_), custom_call_target="tpu_custom_call" | custom-call | flops 201326592 | bytes 524288 | tf_op jit(solution)/shard_map/inverse/pallas_call | solution.py:94
  60.7 0.4 bitcast_convert_fusion
  61.1 6.6 %multiply_reduce_fusion = f32[256,1024]{1,0:T(8,128)S(1)} fusion(bf16[16,256,1024]{2,1,0:T(8,128)(2,1)} %param.3, f32[256,16]{0,1:T(8,128)S(1)} %multiply_bitcast_fusion, bf16[256,256]{1,0:T(8,128)(2,1)S(1)} %get-tuple-element.11), kind=kOutput, calls=%fused_computation | convolution fusion | flops 2155610112 | bytes 9584640 | tf_op jit(solution)/shard_map/ijk,jr->ikr/dot_general | solution.py:215
  68.1 6.0 %collective-permute-start.7 = (f32[512,256]{1,0:T(8,128)S(1)}, f32[512,256]{1,0:T(8,128)S(1)}, u32[]{:S(2)}, u32[]{:S(2)}) collective-permute-start(f32[512,256]{1,0:T(8,128)S(1)} %slice_select_fusion), channel_id=1, source_target_pairs={{0,8},{8,0},{1,9},{9,1},{2,10},{10,2},{3,11},{11,3},{4,12},{12,4},... | collective-permute-start | bytes 1572872 | tf_op jit(solution)/shard_map/ppermute | solution.py:122
  74.1 0.9 convolution_bitcast_fusion
  75.1 6.9 %all-to-all-start.3 = ((f32[32,8,256]{2,1,0:T(8,128)}), f32[32,8,256]{2,1,0:T(8,128)S(1)}, u32[]{:S(2)}, u32[]{:S(2)}) async-start(f32[32,8,256]{2,1,0:T(8,128)} %convolution_bitcast_fusion), calls=%async_computation.3 | async-start | bytes 524288 | tf_op jit(solution)/shard_map/all_to_all | solution.py:107
  82.0 0.9 select_add_fusion
  82.9 10.3 %all-to-all-done.3 = f32[32,8,256]{2,1,0:T(8,128)S(1)} async-done(((f32[32,8,256]{2,1,0:T(8,128)}), f32[32,8,256]{2,1,0:T(8,128)S(1)}, u32[]{:S(2)}, u32[]{:S(2)}) %all-to-all-start.3) | async-done | bytes 262176 | tf_op jit(solution)/shard_map/all_to_all | solution.py:107
  93.2 3.6 %all-to-all-start.2 = ((f32[16,32,256]{2,1,0:T(8,128)}), f32[16,32,256]{2,1,0:T(8,128)S(1)}, u32[]{:S(2)}, u32[]{:S(2)}) async-start(f32[16,32,256]{2,1,0:T(8,128)} %bitcast.19), calls=%async_computation.2 | async-start | bytes 1048576 | tf_op jit(solution)/shard_map/all_to_all | solution.py:107
  97.0 1.2 collective-permute-done.8
  98.1 1.2 collective-permute-start.11
  99.4 2.1 %collective-permute-start.10 = (f32[16,256]{1,0:T(8,128)S(1)}, f32[16,256]{1,0:T(8,128)S(1)}, u32[]{:S(2)}, u32[]{:S(2)}) collective-permute-start(f32[16,256]{1,0:T(8,128)S(1)} %maximum_select_fusion.1), channel_id=1, source_target_pairs={{0,32},{16,48},{32,0},{48,16},{1,33},{17,49},{33,1},{49,17},{2,34}... | collective-permute-start | bytes 49160 | tf_op jit(solution)/shard_map/ppermute | solution.py:143
  101.7 4.5 %collective-permute-done.11 = f32[16,256]{1,0:T(8,128)S(1)} collective-permute-done((f32[16,256]{1,0:T(8,128)S(1)}, f32[16,256]{1,0:T(8,128)S(1)}, u32[]{:S(2)}, u32[]{:S(2)}) %collective-permute-start.11) | collective-permute-done | bytes 16416 | tf_op jit(solution)/shard_map/ppermute | solution.py:143
  106.2 5.8 %collective-permute-done.10 = f32[16,256]{1,0:T(8,128)S(1)} collective-permute-done((f32[16,256]{1,0:T(8,128)S(1)}, f32[16,256]{1,0:T(8,128)S(1)}, u32[]{:S(2)}, u32[]{:S(2)}) %collective-permute-start.10) | collective-permute-done | bytes 16416 | tf_op jit(solution)/shard_map/ppermute | solution.py:143
  112.0 2.6 %collective-permute-start.14 = (f32[64,256]{1,0:T(8,128)S(1)}, f32[64,256]{1,0:T(8,128)S(1)}, u32[]{:S(2)}, u32[]{:S(2)}) collective-permute-start(f32[64,256]{1,0:T(8,128)S(1)} %pad_maximum_fusion.refs_0_), channel_id=1, source_target_pairs={{0,192},{64,128},{128,64},{192,0},{1,193},{65,129},{129,65},{193,1... | collective-permute-start | bytes 196616 | tf_op jit(solution)/shard_map/ppermute | solution.py:143
  114.6 0.8 collective-permute-start.13
  115.4 1.0 collective-permute-done.14.refs_3_
  116.4 2.8 %collective-permute-done.13.refs_2_ = f32[64,256]{1,0:T(8,128)S(1)} collective-permute-done((f32[64,256]{1,0:T(8,128)S(1)}, f32[64,256]{1,0:T(8,128)S(1)}, u32[]{:S(2)}, u32[]{:S(2)}) %collective-permute-start.13) | collective-permute-done | bytes 65568 | tf_op jit(solution)/shard_map/ppermute | solution.py:143
  119.2 8.2 %inverse.3 = f32[256,256]{1,0:T(8,128)S(1)} custom-call(f32[64,256]{1,0:T(8,128)S(1)} %pad_maximum_fusion.refs_0_, f32[64,256]{1,0:T(8,128)S(1)} %collective-permute-done.12.refs_1_, f32[64,256]{1,0:T(8,128)S(1)} %collective-permute-done.13.refs_2_, f32[64,256]{1,0:T(8,128)S(1)} %collective-permute-done.14.refs_3_, ...), custom_call_target="tpu_custom_call" | custom-call | flops 201326592 | bytes 524288 | tf_op jit(solution)/shard_map/inverse/pallas_call | solution.py:94
  127.8 13.5 %all_to_all.30 = bf16[16,32,256]{2,1,0:T(8,128)(2,1)S(1)} all-to-all(bf16[16,32,256]{2,1,0:T(8,128)(2,1)S(1)} %broadcast_in_dim.7), channel_id=1, replica_groups=mesh['x'=4,'zl'=4,'core'=2,'zh'=2,'y'=4] {'x','zl'}, dimensions={0} | all-to-all | bytes 524288 | tf_op jit(solution)/shard_map/all_to_all | solution.py:107
  141.3 3.2 %collective-permute-start.15 = (bf16[512,256]{1,0:T(8,128)(2,1)S(1)}, bf16[512,256]{1,0:T(8,128)(2,1)S(1)}, u32[]{:S(2)}, u32[]{:S(2)}) collective-permute-start(bf16[512,256]{1,0:T(8,128)(2,1)S(1)} %bitcast.67), channel_id=1, source_target_pairs={{0,8},{8,0},{1,9},{9,1},{2,10},{10,2},{3,11},{11,3},{4,12},{12,4},... | collective-permute-start | bytes 786440 | tf_op jit(solution)/shard_map/ppermute | solution.py:122
  144.7 1.0 collective-permute-done.15
  146.0 6.7 %fusion = f32[256,16]{0,1:T(8,128)S(1)} fusion(bf16[16,256,1024]{2,1,0:T(8,128)(2,1)} %param.3, f32[256,256]{1,0:T(8,128)S(1)} %copy.34, bf16[1024,256]{1,0:T(8,128)(2,1)S(1)} %maximum_select_fusion), kind=kOutput, calls=%fused_computation.2 | convolution fusion | flops 2149576704 | bytes 9191424 | tf_op jit(solution)/shard_map/ijk,kr->ijr/dot_general | solution.py:226
  152.7 0.5 collective-permute-start.16
  153.2 0.8 collective-permute-done.16
  154.0 0.6 collective-permute-start.19
  154.6 0.3 collective-permute-start.18
  154.9 0.6 collective-permute-start.17
  155.5 1.1 collective-permute-done.19
  156.6 2.1 %collective-permute-done.18 = f32[16,256]{1,0:T(8,128)S(1)} collective-permute-done((f32[16,256]{1,0:T(8,128)S(1)}, f32[16,256]{1,0:T(8,128)S(1)}, u32[]{:S(2)}, u32[]{:S(2)}) %collective-permute-start.18) | collective-permute-done | bytes 16416 | tf_op jit(solution)/shard_map/ppermute | solution.py:122
  159.0 15.1 %all_to_all.31 = bf16[32,16,256]{2,1,0:T(8,128)(2,1)S(1)} all-to-all(bf16[32,16,256]{2,1,0:T(8,128)(2,1)S(1)} %broadcast_in_dim.8), channel_id=1, replica_groups=mesh['x'=4,'zl'=4,'core'=2,'zh'=2,'y'=4] {'zl','zh','y'}, dimensions={0} | all-to-all | bytes 524288 | tf_op jit(solution)/shard_map/all_to_all | solution.py:107
  174.1 0.7 convert_reduce_fusion
  (41 shorter events, 2.7 us)
Async XLA Ops:
  0.6 1.1 copy-start
  1.7 46.6 %copy-start.3 = (bf16[16,256]{1,0:T(8,128)(2,1)S(1)}, bf16[16,256]{1,0:T(8,128)(2,1)}, u32[]{:S(2)}) copy-start(bf16[16,256]{1,0:T(8,128)(2,1)} %param.4) | copy-start | bytes 24580
  8.1 21.8 %all-to-all-start = ((f32[8,32,256]{2,1,0:T(8,128)}), f32[8,32,256]{2,1,0:T(8,128)S(1)}, u32[]{:S(2)}, u32[]{:S(2)}) async-start(f32[8,32,256]{2,1,0:T(8,128)} %bitcast.8), calls=%async_computation | async-start | bytes 524288 | tf_op jit(solution)/shard_map/all_to_all | solution.py:107
  20.2 14.0 %collective-permute-start = (f32[64,256]{1,0:T(8,128)S(1)}, f32[64,256]{1,0:T(8,128)S(1)}, u32[]{:S(2)}, u32[]{:S(2)}) collective-permute-start(f32[64,256]{1,0:T(8,128)S(1)} %get-tuple-element.3), channel_id=1, source_target_pairs={{0,1},{1,2},{2,3},{3,0},{4,5},{5,6},{6,7},{7,4},{8,9},{9,10},{10,1... | collective-permute-start | bytes 196616 | tf_op jit(solution)/shard_map/ppermute | solution.py:122
  21.7 12.5 %collective-permute-start.2 = (f32[64,256]{1,0:T(8,128)S(1)}, f32[64,256]{1,0:T(8,128)S(1)}, u32[]{:S(2)}, u32[]{:S(2)}) collective-permute-start(f32[64,256]{1,0:T(8,128)S(1)} %get-tuple-element.4), channel_id=1, source_target_pairs={{0,3},{1,0},{2,1},{3,2},{4,7},{5,4},{6,5},{7,6},{8,11},{9,8},{10,9... | collective-permute-start | bytes 196616 | tf_op jit(solution)/shard_map/ppermute | solution.py:122
  23.0 11.2 %collective-permute-start.1 = (f32[64,256]{1,0:T(8,128)S(1)}, f32[64,256]{1,0:T(8,128)S(1)}, u32[]{:S(2)}, u32[]{:S(2)}) collective-permute-start(f32[64,256]{1,0:T(8,128)S(1)} %get-tuple-element.5), channel_id=1, source_target_pairs={{0,2},{1,3},{2,0},{3,1},{4,6},{5,7},{6,4},{7,5},{8,10},{9,11},{10,... | collective-permute-start | bytes 196616 | tf_op jit(solution)/shard_map/ppermute | solution.py:122
  30.7 30.0 %all-to-all-start.1 = ((f32[8,32,256]{2,1,0:T(8,128)}), f32[8,32,256]{2,1,0:T(8,128)S(1)}, u32[]{:S(2)}, u32[]{:S(2)}) async-start(f32[8,32,256]{2,1,0:T(8,128)} %broadcast_in_dim.6), calls=%async_computation.1 | async-start | bytes 524288 | tf_op jit(solution)/shard_map/all_to_all | solution.py:107
  34.2 9.8 %collective-permute-start.3 = (f32[64,256]{1,0:T(8,128)S(1)}, f32[64,256]{1,0:T(8,128)S(1)}, u32[]{:S(2)}, u32[]{:S(2)}) collective-permute-start(f32[64,256]{1,0:T(8,128)S(1)} %fusion.5), channel_id=1, source_target_pairs={{0,4},{4,0},{1,5},{5,1},{2,6},{6,2},{3,7},{7,3},{8,12},{12,8},{9,1... | collective-permute-start | bytes 196616 | tf_op jit(solution)/shard_map/ppermute | solution.py:122
  44.0 4.5 %collective-permute-start.6 = (f32[64,256]{1,0:T(8,128)S(1)}, f32[64,256]{1,0:T(8,128)S(1)}, u32[]{:S(2)}, u32[]{:S(2)}) collective-permute-start(f32[64,256]{1,0:T(8,128)S(1)} %add.59.refs_0_), channel_id=1, source_target_pairs={{0,3},{1,0},{2,1},{3,2},{4,7},{5,4},{6,5},{7,6},{8,11},{9,8},{10,9... | collective-permute-start | bytes 196616 | tf_op jit(solution)/shard_map/ppermute | solution.py:122
  47.1 4.7 %collective-permute-start.5 = (f32[64,256]{1,0:T(8,128)S(1)}, f32[64,256]{1,0:T(8,128)S(1)}, u32[]{:S(2)}, u32[]{:S(2)}) collective-permute-start(f32[64,256]{1,0:T(8,128)S(1)} %add.59.refs_0_), channel_id=1, source_target_pairs={{0,2},{1,3},{2,0},{3,1},{4,6},{5,7},{6,4},{7,5},{8,10},{9,11},{10,... | collective-permute-start | bytes 196616 | tf_op jit(solution)/shard_map/ppermute | solution.py:122
  47.7 4.8 %collective-permute-start.4 = (f32[64,256]{1,0:T(8,128)S(1)}, f32[64,256]{1,0:T(8,128)S(1)}, u32[]{:S(2)}, u32[]{:S(2)}) collective-permute-start(f32[64,256]{1,0:T(8,128)S(1)} %add.59.refs_0_), channel_id=1, source_target_pairs={{0,1},{1,2},{2,3},{3,0},{4,5},{5,6},{6,7},{7,4},{8,9},{9,10},{10,1... | collective-permute-start | bytes 196616 | tf_op jit(solution)/shard_map/ppermute | solution.py:122
  61.1 13.1 %copy-start.1 = (bf16[256,256]{1,0:T(8,128)(2,1)}, bf16[256,256]{1,0:T(8,128)(2,1)S(1)}, u32[]{:S(2)}) copy-start(bf16[256,256]{1,0:T(8,128)(2,1)S(1)} %get-tuple-element.11) | copy-start | bytes 393220
  68.1 13.9 %collective-permute-start.7 = (f32[512,256]{1,0:T(8,128)S(1)}, f32[512,256]{1,0:T(8,128)S(1)}, u32[]{:S(2)}, u32[]{:S(2)}) collective-permute-start(f32[512,256]{1,0:T(8,128)S(1)} %slice_select_fusion), channel_id=1, source_target_pairs={{0,8},{8,0},{1,9},{9,1},{2,10},{10,2},{3,11},{11,3},{4,12},{12,4},... | collective-permute-start | bytes 1572872 | tf_op jit(solution)/shard_map/ppermute | solution.py:122
  75.1 18.2 %all-to-all-start.3 = ((f32[32,8,256]{2,1,0:T(8,128)}), f32[32,8,256]{2,1,0:T(8,128)S(1)}, u32[]{:S(2)}, u32[]{:S(2)}) async-start(f32[32,8,256]{2,1,0:T(8,128)} %convolution_bitcast_fusion), calls=%async_computation.3 | async-start | bytes 524288 | tf_op jit(solution)/shard_map/all_to_all | solution.py:107
  93.2 34.2 %all-to-all-start.2 = ((f32[16,32,256]{2,1,0:T(8,128)}), f32[16,32,256]{2,1,0:T(8,128)S(1)}, u32[]{:S(2)}, u32[]{:S(2)}) async-start(f32[16,32,256]{2,1,0:T(8,128)} %bitcast.19), calls=%async_computation.2 | async-start | bytes 1048576 | tf_op jit(solution)/shard_map/all_to_all | solution.py:107
  96.9 1.3 collective-permute-start.8
  98.1 8.0 %collective-permute-start.11 = (f32[16,256]{1,0:T(8,128)S(1)}, f32[16,256]{1,0:T(8,128)S(1)}, u32[]{:S(2)}, u32[]{:S(2)}) collective-permute-start(f32[16,256]{1,0:T(8,128)S(1)} %maximum_select_fusion.1), channel_id=1, source_target_pairs={{0,16},{16,0},{32,48},{48,32},{1,17},{17,1},{33,49},{49,33},{2,18}... | collective-permute-start | bytes 49160 | tf_op jit(solution)/shard_map/ppermute | solution.py:143
  99.4 12.6 %collective-permute-start.10 = (f32[16,256]{1,0:T(8,128)S(1)}, f32[16,256]{1,0:T(8,128)S(1)}, u32[]{:S(2)}, u32[]{:S(2)}) collective-permute-start(f32[16,256]{1,0:T(8,128)S(1)} %maximum_select_fusion.1), channel_id=1, source_target_pairs={{0,32},{16,48},{32,0},{48,16},{1,33},{17,49},{33,1},{49,17},{2,34}... | collective-permute-start | bytes 49160 | tf_op jit(solution)/shard_map/ppermute | solution.py:143
  101.5 10.5 %collective-permute-start.9 = (f32[16,256]{1,0:T(8,128)S(1)}, f32[16,256]{1,0:T(8,128)S(1)}, u32[]{:S(2)}, u32[]{:S(2)}) collective-permute-start(f32[16,256]{1,0:T(8,128)S(1)} %maximum_select_fusion.1), channel_id=1, source_target_pairs={{0,48},{16,32},{32,16},{48,0},{1,49},{17,33},{33,17},{49,1},{2,50}... | collective-permute-start | bytes 49160 | tf_op jit(solution)/shard_map/ppermute | solution.py:143
  112.0 4.4 %collective-permute-start.14 = (f32[64,256]{1,0:T(8,128)S(1)}, f32[64,256]{1,0:T(8,128)S(1)}, u32[]{:S(2)}, u32[]{:S(2)}) collective-permute-start(f32[64,256]{1,0:T(8,128)S(1)} %pad_maximum_fusion.refs_0_), channel_id=1, source_target_pairs={{0,192},{64,128},{128,64},{192,0},{1,193},{65,129},{129,65},{193,1... | collective-permute-start | bytes 196616 | tf_op jit(solution)/shard_map/ppermute | solution.py:143
  114.6 4.6 %collective-permute-start.13 = (f32[64,256]{1,0:T(8,128)S(1)}, f32[64,256]{1,0:T(8,128)S(1)}, u32[]{:S(2)}, u32[]{:S(2)}) collective-permute-start(f32[64,256]{1,0:T(8,128)S(1)} %pad_maximum_fusion.refs_0_), channel_id=1, source_target_pairs={{0,128},{64,192},{128,0},{192,64},{1,129},{65,193},{129,1},{193,65... | collective-permute-start | bytes 196616 | tf_op jit(solution)/shard_map/ppermute | solution.py:143
  115.4 3.9 %collective-permute-start.12 = (f32[64,256]{1,0:T(8,128)S(1)}, f32[64,256]{1,0:T(8,128)S(1)}, u32[]{:S(2)}, u32[]{:S(2)}) collective-permute-start(f32[64,256]{1,0:T(8,128)S(1)} %pad_maximum_fusion.refs_0_), channel_id=1, source_target_pairs={{0,64},{64,0},{128,192},{192,128},{1,65},{65,1},{129,193},{193,129... | collective-permute-start | bytes 196616 | tf_op jit(solution)/shard_map/ppermute | solution.py:143
  141.3 4.4 %collective-permute-start.15 = (bf16[512,256]{1,0:T(8,128)(2,1)S(1)}, bf16[512,256]{1,0:T(8,128)(2,1)S(1)}, u32[]{:S(2)}, u32[]{:S(2)}) collective-permute-start(bf16[512,256]{1,0:T(8,128)(2,1)S(1)} %bitcast.67), channel_id=1, source_target_pairs={{0,8},{8,0},{1,9},{9,1},{2,10},{10,2},{3,11},{11,3},{4,12},{12,4},... | collective-permute-start | bytes 786440 | tf_op jit(solution)/shard_map/ppermute | solution.py:122
  146.0 28.8 %copy-start.2 = (bf16[1024,256]{1,0:T(8,128)(2,1)}, bf16[1024,256]{1,0:T(8,128)(2,1)S(1)}, u32[]{:S(2)}) copy-start(bf16[1024,256]{1,0:T(8,128)(2,1)S(1)} %maximum_select_fusion) | copy-start | bytes 1572868
  152.7 1.3 collective-permute-start.16
  154.0 2.6 %collective-permute-start.19 = (f32[16,256]{1,0:T(8,128)S(1)}, f32[16,256]{1,0:T(8,128)S(1)}, u32[]{:S(2)}, u32[]{:S(2)}) collective-permute-start(f32[16,256]{1,0:T(8,128)S(1)} %bitcast_add_fusion.1), channel_id=1, source_target_pairs={{0,192},{64,0},{128,64},{192,128},{1,193},{65,1},{129,65},{193,129... | collective-permute-start | bytes 49160 | tf_op jit(solution)/shard_map/ppermute | solution.py:122
  154.6 4.1 %collective-permute-start.18 = (f32[16,256]{1,0:T(8,128)S(1)}, f32[16,256]{1,0:T(8,128)S(1)}, u32[]{:S(2)}, u32[]{:S(2)}) collective-permute-start(f32[16,256]{1,0:T(8,128)S(1)} %bitcast_add_fusion.1), channel_id=1, source_target_pairs={{0,128},{64,192},{128,0},{192,64},{1,129},{65,193},{129,1},{193,65... | collective-permute-start | bytes 49160 | tf_op jit(solution)/shard_map/ppermute | solution.py:122
  154.9 4.1 %collective-permute-start.17 = (f32[16,256]{1,0:T(8,128)S(1)}, f32[16,256]{1,0:T(8,128)S(1)}, u32[]{:S(2)}, u32[]{:S(2)}) collective-permute-start(f32[16,256]{1,0:T(8,128)S(1)} %bitcast_add_fusion.1), channel_id=1, source_target_pairs={{0,64},{64,128},{128,192},{192,0},{1,65},{65,129},{129,193},{193,1... | collective-permute-start | bytes 49160 | tf_op jit(solution)/shard_map/ppermute | solution.py:122

commit v5 on v3

--- a/solution.py
+++ b/solution.py
@@ -201,9 +201,12 @@
     partial_second = jnp.einsum(
         "ijr,ir->jr", contracted, first_second, precision=HIGHEST
     )
-    row = scatter_sum(partial_second, NARROW)
-    mttkrp_second = gather(row, NARROW)
+    row = ring_scatter(partial_second, "y")
+    row = ring_sum(row, "zh")
+    parts = quad_gather(row, "y")
+    mttkrp_second = jnp.concatenate(parts, axis=0)
     second_factor = jnp.dot(mttkrp_second, inverse_second, precision=HIGHEST).astype(jnp.bfloat16)
+    second_factor = ordered(jnp.split(second_factor, 4, axis=0), lax.axis_index("y"))
 
     gram_local = jnp.dot(second_factor.T, second_factor, preferred_element_type=jnp.float32)
     mine, other = keep(gram_local, core)
@@ -222,10 +225,7 @@
     mine = mine + shift(other, "core", 1)
     mttkrp_third = scatter_sum(mine, CHIP)
     third_solution = jnp.dot(mttkrp_third, inverse_third, precision=HIGHEST)
-    parts = quad_gather(third_solution.astype(jnp.bfloat16), "zl")
-    block = ordered(parts, lax.axis_index("zl"))
-    parts = quad_gather(block, "x")
-    mine = ordered(parts, lax.axis_index("x"))
+    mine = gather(third_solution.astype(jnp.bfloat16), CHIP)
     third_new = join(mine, shift(mine, "core", 1), core)
 
     back = jnp.einsum("ijk,kr->ijr", tensor, third_new, preferred_element_type=jnp.float32)

time: 170 us -> 157 us (0.924)
  waiting for transfers between devices: 35.3 us -> 22.5 us
  blocking collectives: 16.9 us -> 28.6 us
  starting transfers between devices: 72.8 us -> 61.2 us
    all_to_all x3 -> x1, starting transfers between devices: 21.5 us -> 5.7 us  [exchange(): return lax.all_to_all(x, axes, 0, 0, tiled=True)]
    all_to_all x1 -> x2, blocking collectives: 16.9 us -> 28.6 us  [exchange(): return lax.all_to_all(x, axes, 0, 0, tiled=True)]
    ppermute x27 -> x31, starting transfers between devices: 43.9 us -> 52.2 us  [shift(): return lax.ppermute(x, axis, [(s, (s + d) % n) for s in range(n)])]
    all_to_all x3 -> x1, waiting for transfers between devices: 5.98 us -> 0.01 us  [exchange(): return lax.all_to_all(x, axes, 0, 0, tiled=True)]
    ppermute x6 -> x3, waiting for transfers between devices: 5.77 us -> 0.01 us  [pair(): lax.ppermute(x, axis, [(s, s ^ d) for s in range(lax.axis_size(axis))])]
    ppermute x6 -> x3, starting transfers between devices: 7.33 us -> 3.34 us  [pair(): lax.ppermute(x, axis, [(s, s ^ d) for s in range(lax.axis_size(axis))])]
    ppermute x27 -> x31, waiting for transfers between devices: 23.5 us -> 22.4 us  [shift(): return lax.ppermute(x, axis, [(s, (s + d) % n) for s in range(n)])]
  transfers between devices with their start and end apart: 36 -> 35, of which waited for: 20 -> 16; matrix products, arithmetic and copies ran while one was open for 2% -> 6% of each run, Pallas kernels for 10% -> 11%
where the time goes in v5:
time: 157 us; the launch traced here: 155 us
  starting transfers between devices  61.2 us (39%)
  blocking collectives  28.6 us (18%)
  waiting for transfers between devices  22.5 us (14%)
  matrix products  20.3 us (13%)
  Pallas kernels  16.4 us (10%)
  other arithmetic  3.42 us (2%)
  local copies, waits for them, and re-layouts  1.6 us (1%)
    ppermute x31, starting transfers between devices, shift(): return lax.ppermute(x, axis, [(s, (s + d) % n) for s in range(n)])  52.2 us
    all_to_all x2, blocking collectives, exchange(): return lax.all_to_all(x, axes, 0, 0, tiled=True)  28.6 us
    ppermute x31, waiting for transfers between devices, shift(): return lax.ppermute(x, axis, [(s, (s + d) % n) for s in range(n)])  22.4 us
    pallas_call x2, Pallas kernels, inverse(): pl.pallas_call(functools.partial(inverse_kernel, places, total), out_shap...  16.4 us
    dot_general x1, matrix products, on_device(): jnp.einsum('ijk,kr->ijr', tensor, third_new, preferred_element_type=jnp.f...  6.63 us
    dot_general x1, matrix products, on_device(): jnp.einsum('ijk,jr->ikr', tensor, second_factor, preferred_element_type=j...  6.56 us
    dot_general x1, matrix products, on_device(): jnp.einsum('ijk,kr->ijr', tensor, third_factor, preferred_element_type=jn...  5.75 us
    all_to_all x1, starting transfers between devices, exchange(): return lax.all_to_all(x, axes, 0, 0, tiled=True)  5.7 us
  transfers between devices with their start and end apart: 35, of which 16 were waited for; matrix products, arithmetic and copies ran while one was open for 6% of the time, Pallas kernels for 11%

profile of v5, /device:TPU:1, one launch (start us, length us, event | category | flops | bytes accessed | tf_op | source)
XLA Modules:
  0.0 155.0 jit_solution(12039223615730804844)
XLA Ops:
  0.7 1.0 copy-done
  2.1 2.2 %collective-permute-start.7 = (f32[64,256]{1,0:T(8,128)S(1)}, f32[64,256]{1,0:T(8,128)S(1)}, u32[]{:S(2)}, u32[]{:S(2)}) collective-permute-start(f32[64,256]{1,0:T(8,128)S(1)} %get-tuple-element.8), channel_id=1, source_target_pairs={{0,1},{1,2},{2,3},{3,0},{4,5},{5,6},{6,7},{7,4},{8,9},{9,10},{10,1... | collective-permute-start | bytes 196616 | tf_op jit(solution)/shard_map/ppermute | solution.py:122
  4.3 1.5 collective-permute-start.9
  5.8 1.6 %collective-permute-start.8 = (f32[64,256]{1,0:T(8,128)S(1)}, f32[64,256]{1,0:T(8,128)S(1)}, u32[]{:S(2)}, u32[]{:S(2)}) collective-permute-start(f32[64,256]{1,0:T(8,128)S(1)} %get-tuple-element.10), channel_id=1, source_target_pairs={{0,2},{1,3},{2,0},{3,1},{4,6},{5,7},{6,4},{7,5},{8,10},{9,11},{10,... | collective-permute-start | bytes 196616 | tf_op jit(solution)/shard_map/ppermute | solution.py:122
  7.3 0.7 multiply_bitcast_fusion
  8.0 5.7 %multiply_reduce_fusion.1 = f32[256,256]{0,1:T(8,128)S(1)} fusion(bf16[16,256,1024]{2,1,0:T(8,128)(2,1)} %param.3, f32[256,16]{0,1:T(8,128)S(1)} %multiply_bitcast_fusion, bf16[1024,256]{1,0:T(8,128)(2,1)S(1)} %copy-done), kind=kOutput, calls=%fused_computation.3 | convolution fusion | flops 2149515264 | bytes 9191424 | tf_op jit(solution)/shard_map/ijk,kr->ijr/dot_general | solution.py:200
  14.3 2.3 %collective-permute-start.2 = (f32[64,256]{1,0:T(8,128)S(1)}, f32[64,256]{1,0:T(8,128)S(1)}, u32[]{:S(2)}, u32[]{:S(2)}) collective-permute-start(f32[64,256]{1,0:T(8,128)S(1)} %get-tuple-element.6), channel_id=1, source_target_pairs={{0,3},{1,0},{2,1},{3,2},{4,7},{5,4},{6,5},{7,6},{8,11},{9,8},{10,9... | collective-permute-start | bytes 196616 | tf_op jit(solution)/shard_map/ppermute | solution.py:122
  16.8 7.0 %collective-permute-start.10 = (f32[64,256]{1,0:T(8,128)S(1)}, f32[64,256]{1,0:T(8,128)S(1)}, u32[]{:S(2)}, u32[]{:S(2)}) collective-permute-start(f32[64,256]{1,0:T(8,128)S(1)} %fusion.12), channel_id=1, source_target_pairs={{0,4},{4,0},{1,5},{5,1},{2,6},{6,2},{3,7},{7,3},{8,12},{12,8},{9,1... | collective-permute-start | bytes 196616 | tf_op jit(solution)/shard_map/ppermute | solution.py:122
  23.9 4.4 %collective-permute-start.3 = (f32[64,256]{1,0:T(8,128)S(1)}, f32[64,256]{1,0:T(8,128)S(1)}, u32[]{:S(2)}, u32[]{:S(2)}) collective-permute-start(f32[64,256]{1,0:T(8,128)S(1)} %fusion.14), channel_id=1, source_target_pairs={{0,4},{4,0},{1,5},{5,1},{2,6},{6,2},{3,7},{7,3},{8,12},{12,8},{9,1... | collective-permute-start | bytes 196616 | tf_op jit(solution)/shard_map/ppermute | solution.py:122
  28.7 2.2 %collective-permute-done.3 = f32[64,256]{1,0:T(8,128)S(1)} collective-permute-done((f32[64,256]{1,0:T(8,128)S(1)}, f32[64,256]{1,0:T(8,128)S(1)}, u32[]{:S(2)}, u32[]{:S(2)}) %collective-permute-start.3) | collective-permute-done | bytes 65568 | tf_op jit(solution)/shard_map/ppermute | solution.py:122
  31.0 1.5 collective-permute-start.6
  32.4 1.5 collective-permute-start.5
  34.3 2.8 %collective-permute-start.12 = (f32[64,256]{1,0:T(8,128)S(1)}, f32[64,256]{1,0:T(8,128)S(1)}, u32[]{:S(2)}, u32[]{:S(2)}) collective-permute-start(f32[64,256]{1,0:T(8,128)S(1)} %add.125.refs_0_), channel_id=1, source_target_pairs={{0,2},{1,3},{2,0},{3,1},{4,6},{5,7},{6,4},{7,5},{8,10},{9,11},{10,... | collective-permute-start | bytes 196616 | tf_op jit(solution)/shard_map/ppermute | solution.py:122
  37.3 2.1 %collective-permute-done.12.refs_2_ = f32[64,256]{1,0:T(8,128)S(1)} collective-permute-done((f32[64,256]{1,0:T(8,128)S(1)}, f32[64,256]{1,0:T(8,128)S(1)}, u32[]{:S(2)}, u32[]{:S(2)}) %collective-permute-start.12) | collective-permute-done | bytes 65568 | tf_op jit(solution)/shard_map/ppermute | solution.py:122
  39.4 2.7 %collective-permute-done.11.refs_1_ = f32[64,256]{1,0:T(8,128)S(1)} collective-permute-done((f32[64,256]{1,0:T(8,128)S(1)}, f32[64,256]{1,0:T(8,128)S(1)}, u32[]{:S(2)}, u32[]{:S(2)}) %collective-permute-start.11) | collective-permute-done | bytes 65568 | tf_op jit(solution)/shard_map/ppermute | solution.py:122
  42.1 8.2 %inverse.2 = f32[256,256]{1,0:T(8,128)S(1)} custom-call(f32[64,256]{1,0:T(8,128)S(1)} %add.125.refs_0_, f32[64,256]{1,0:T(8,128)S(1)} %collective-permute-done.11.refs_1_, f32[64,256]{1,0:T(8,128)S(1)} %collective-permute-done.12.refs_2_, f32[64,256]{1,0:T(8,128)S(1)} %collective-permute-done.13.refs_3_, f32[256,256]{1,0:T(8,128)S(1)} %convolution_multiply_fusion.refs_4_.refs_8_), custom_call_target="tpu_custom_call" | custom-call | flops 201326592 | bytes 524288 | tf_op jit(solution)/shard_map/inverse/pallas_call | solution.py:94
  50.9 6.6 %multiply_reduce_fusion = f32[256,1024]{1,0:T(8,128)S(1)} fusion(bf16[16,256,1024]{2,1,0:T(8,128)(2,1)} %param.3, f32[256,16]{0,1:T(8,128)S(1)} %multiply_bitcast_fusion, bf16[256,256]{1,0:T(8,128)(2,1)S(1)} %get-tuple-element.4), kind=kOutput, calls=%fused_computation | convolution fusion | flops 2155610112 | bytes 9584640 | tf_op jit(solution)/shard_map/ijk,jr->ikr/dot_general | solution.py:220
  57.8 5.5 %collective-permute-start.14 = (f32[512,256]{1,0:T(8,128)S(1)}, f32[512,256]{1,0:T(8,128)S(1)}, u32[]{:S(2)}, u32[]{:S(2)}) collective-permute-start(f32[512,256]{1,0:T(8,128)S(1)} %slice_select_fusion), channel_id=1, source_target_pairs={{0,8},{8,0},{1,9},{9,1},{2,10},{10,2},{3,11},{11,3},{4,12},{12,4},... | collective-permute-start | bytes 1572872 | tf_op jit(solution)/shard_map/ppermute | solution.py:122
  63.5 0.7 slice_select_fusion.1
  64.2 0.6 collective-permute-done.14
  64.8 0.9 select_add_fusion
  65.7 5.7 %all-to-all-start = ((f32[16,32,256]{2,1,0:T(8,128)}), f32[16,32,256]{2,1,0:T(8,128)S(1)}, u32[]{:S(2)}, u32[]{:S(2)}) async-start(f32[16,32,256]{2,1,0:T(8,128)} %bitcast.23), calls=%async_computation | async-start | bytes 1048576 | tf_op jit(solution)/shard_map/all_to_all | solution.py:107
  71.5 1.4 collective-permute-start.16
  72.9 1.3 collective-permute-start.18
  74.3 1.6 %collective-permute-start.17 = (f32[32,256]{1,0:T(8,128)S(1)}, f32[32,256]{1,0:T(8,128)S(1)}, u32[]{:S(2)}, u32[]{:S(2)}) collective-permute-start(f32[32,256]{1,0:T(8,128)S(1)} %get-tuple-element.13), channel_id=1, source_target_pairs={{0,128},{64,192},{128,0},{192,64},{1,129},{65,193},{129,1},{193,65... | collective-permute-start | bytes 98312 | tf_op jit(solution)/shard_map/ppermute | solution.py:122
  75.9 1.8 %collective-permute-done.18 = f32[32,256]{1,0:T(8,128)S(1)} collective-permute-done((f32[32,256]{1,0:T(8,128)S(1)}, f32[32,256]{1,0:T(8,128)S(1)}, u32[]{:S(2)}, u32[]{:S(2)}) %collective-permute-start.18) | collective-permute-done | bytes 32800 | tf_op jit(solution)/shard_map/ppermute | solution.py:122
  77.7 2.2 %collective-permute-done.17 = f32[32,256]{1,0:T(8,128)S(1)} collective-permute-done((f32[32,256]{1,0:T(8,128)S(1)}, f32[32,256]{1,0:T(8,128)S(1)}, u32[]{:S(2)}, u32[]{:S(2)}) %collective-permute-start.17) | collective-permute-done | bytes 32800 | tf_op jit(solution)/shard_map/ppermute | solution.py:122
  79.9 4.7 %collective-permute-start.21 = (f32[32,256]{1,0:T(8,128)S(1)}, f32[32,256]{1,0:T(8,128)S(1)}, u32[]{:S(2)}, u32[]{:S(2)}) collective-permute-start(f32[32,256]{1,0:T(8,128)S(1)} %fusion.16), channel_id=1, source_target_pairs={{0,48},{16,0},{32,16},{48,32},{1,49},{17,1},{33,17},{49,33},{2,50}... | collective-permute-start | bytes 98312 | tf_op jit(solution)/shard_map/ppermute | solution.py:122
  85.0 0.6 collective-permute-done.21
  85.7 2.6 %collective-permute-done.20 = f32[32,256]{1,0:T(8,128)S(1)} collective-permute-done((f32[32,256]{1,0:T(8,128)S(1)}, f32[32,256]{1,0:T(8,128)S(1)}, u32[]{:S(2)}, u32[]{:S(2)}) %collective-permute-start.20) | collective-permute-done | bytes 32800 | tf_op jit(solution)/shard_map/ppermute | solution.py:122
  88.3 0.9 collective-permute-done.19
  89.2 0.8 collective-permute-start.24
  90.0 0.7 collective-permute-start.23
  90.7 0.8 collective-permute-start.22
  91.5 3.7 %collective-permute-start.25 = (f32[32,256]{1,0:T(8,128)S(1)}, f32[32,256]{1,0:T(8,128)S(1)}, u32[]{:S(2)}, u32[]{:S(2)}) collective-permute-start(f32[32,256]{1,0:T(8,128)S(1)} %add_add_fusion.refs_0_), channel_id=1, source_target_pairs={{0,8},{8,0},{1,9},{9,1},{2,10},{10,2},{3,11},{11,3},{4,12},{12,4},... | collective-permute-start | bytes 98312 | tf_op jit(solution)/shard_map/ppermute | solution.py:122
  95.2 0.6 collective-permute-start.28
  95.9 3.9 %collective-permute-start.27 = (f32[32,256]{1,0:T(8,128)S(1)}, f32[32,256]{1,0:T(8,128)S(1)}, u32[]{:S(2)}, u32[]{:S(2)}) collective-permute-start(f32[32,256]{1,0:T(8,128)S(1)} %collective-permute-done.23.refs_2_), channel_id=1, source_target_pairs={{0,8},{8,0},{1,9},{9,1},{2,10},{10,2},{3,11},{11,3},{4,12},{12,4},... | collective-permute-start | bytes 98312 | tf_op jit(solution)/shard_map/ppermute | solution.py:122
  99.8 0.8 collective-permute-done.27.refs_6_
  101.0 8.2 %inverse.3 = f32[256,256]{1,0:T(8,128)S(1)} custom-call(f32[32,256]{1,0:T(8,128)S(1)} %add_add_fusion.refs_0_, f32[32,256]{1,0:T(8,128)S(1)} %collective-permute-done.22.refs_1_, f32[32,256]{1,0:T(8,128)S(1)} %collective-permute-done.23.refs_2_, f32[32,256]{1,0:T(8,128)S(1)} %collective-permute-done.24.refs_3_, ...), custom_call_target="tpu_custom_call" | custom-call | flops 201326592 | bytes 524288 | tf_op jit(solution)/shard_map/inverse/pallas_call | solution.py:94
  109.5 13.0 %all_to_all.15 = bf16[16,32,256]{2,1,0:T(8,128)(2,1)S(1)} all-to-all(bf16[16,32,256]{2,1,0:T(8,128)(2,1)S(1)} %broadcast_in_dim.4), channel_id=1, replica_groups=mesh['x'=4,'zl'=4,'core'=2,'zh'=2,'y'=4] {'x','zl'}, dimensions={0} | all-to-all | bytes 524288 | tf_op jit(solution)/shard_map/all_to_all | solution.py:107
  122.5 1.9 %collective-permute-start.29 = (bf16[512,256]{1,0:T(8,128)(2,1)S(1)}, bf16[512,256]{1,0:T(8,128)(2,1)S(1)}, u32[]{:S(2)}, u32[]{:S(2)}) collective-permute-start(bf16[512,256]{1,0:T(8,128)(2,1)S(1)} %bitcast.87), channel_id=1, source_target_pairs={{0,8},{8,0},{1,9},{9,1},{2,10},{10,2},{3,11},{11,3},{4,12},{12,4},... | collective-permute-start | bytes 786440 | tf_op jit(solution)/shard_map/ppermute | solution.py:122
  124.6 1.0 collective-permute-done.29
  125.8 6.6 %fusion = f32[256,16]{0,1:T(8,128)S(1)} fusion(bf16[16,256,1024]{2,1,0:T(8,128)(2,1)} %param.3, f32[256,256]{1,0:T(8,128)S(1)} %copy.34, bf16[1024,256]{1,0:T(8,128)(2,1)S(1)} %maximum_select_fusion), kind=kOutput, calls=%fused_computation.2 | convolution fusion | flops 2149576704 | bytes 9191424 | tf_op jit(solution)/shard_map/ijk,kr->ijr/dot_general | solution.py:231
  132.9 0.8 collective-permute-done.30
  135.2 1.1 collective-permute-done.33
  136.4 2.1 %collective-permute-done.32 = f32[16,256]{1,0:T(8,128)S(1)} collective-permute-done((f32[16,256]{1,0:T(8,128)S(1)}, f32[16,256]{1,0:T(8,128)S(1)}, u32[]{:S(2)}, u32[]{:S(2)}) %collective-permute-start.32) | collective-permute-done | bytes 16416 | tf_op jit(solution)/shard_map/ppermute | solution.py:122
  138.8 15.6 %all_to_all.16 = bf16[32,16,256]{2,1,0:T(8,128)(2,1)S(1)} all-to-all(bf16[32,16,256]{2,1,0:T(8,128)(2,1)S(1)} %broadcast_in_dim.5), channel_id=1, replica_groups=mesh['x'=4,'zl'=4,'core'=2,'zh'=2,'y'=4] {'zl','zh','y'}, dimensions={0} | all-to-all | bytes 524288 | tf_op jit(solution)/shard_map/all_to_all | solution.py:107
  154.4 0.7 convert_reduce_fusion
  (67 shorter events, 7.1 us)
Async XLA Ops:
  0.6 1.0 copy-start
  2.1 14.5 %collective-permute-start.7 = (f32[64,256]{1,0:T(8,128)S(1)}, f32[64,256]{1,0:T(8,128)S(1)}, u32[]{:S(2)}, u32[]{:S(2)}) collective-permute-start(f32[64,256]{1,0:T(8,128)S(1)} %get-tuple-element.8), channel_id=1, source_target_pairs={{0,1},{1,2},{2,3},{3,0},{4,5},{5,6},{6,7},{7,4},{8,9},{9,10},{10,1... | collective-permute-start | bytes 196616 | tf_op jit(solution)/shard_map/ppermute | solution.py:122
  4.3 12.5 %collective-permute-start.9 = (f32[64,256]{1,0:T(8,128)S(1)}, f32[64,256]{1,0:T(8,128)S(1)}, u32[]{:S(2)}, u32[]{:S(2)}) collective-permute-start(f32[64,256]{1,0:T(8,128)S(1)} %get-tuple-element.9), channel_id=1, source_target_pairs={{0,3},{1,0},{2,1},{3,2},{4,7},{5,4},{6,5},{7,6},{8,11},{9,8},{10,9... | collective-permute-start | bytes 196616 | tf_op jit(solution)/shard_map/ppermute | solution.py:122
  5.8 11.0 %collective-permute-start.8 = (f32[64,256]{1,0:T(8,128)S(1)}, f32[64,256]{1,0:T(8,128)S(1)}, u32[]{:S(2)}, u32[]{:S(2)}) collective-permute-start(f32[64,256]{1,0:T(8,128)S(1)} %get-tuple-element.10), channel_id=1, source_target_pairs={{0,2},{1,3},{2,0},{3,1},{4,6},{5,7},{6,4},{7,5},{8,10},{9,11},{10,... | collective-permute-start | bytes 196616 | tf_op jit(solution)/shard_map/ppermute | solution.py:122
  8.0 29.1 %copy-start.3 = (bf16[16,256]{1,0:T(8,128)(2,1)S(1)}, bf16[16,256]{1,0:T(8,128)(2,1)}, u32[]{:S(2)}) copy-start(bf16[16,256]{1,0:T(8,128)(2,1)} %param.4) | copy-start | bytes 24580
  13.8 10.0 %collective-permute-start = (f32[64,256]{1,0:T(8,128)S(1)}, f32[64,256]{1,0:T(8,128)S(1)}, u32[]{:S(2)}, u32[]{:S(2)}) collective-permute-start(f32[64,256]{1,0:T(8,128)S(1)} %get-tuple-element.5), channel_id=1, source_target_pairs={{0,1},{1,2},{2,3},{3,0},{4,5},{5,6},{6,7},{7,4},{8,9},{9,10},{10,1... | collective-permute-start | bytes 196616 | tf_op jit(solution)/shard_map/ppermute | solution.py:122
  14.3 9.5 %collective-permute-start.2 = (f32[64,256]{1,0:T(8,128)S(1)}, f32[64,256]{1,0:T(8,128)S(1)}, u32[]{:S(2)}, u32[]{:S(2)}) collective-permute-start(f32[64,256]{1,0:T(8,128)S(1)} %get-tuple-element.6), channel_id=1, source_target_pairs={{0,3},{1,0},{2,1},{3,2},{4,7},{5,4},{6,5},{7,6},{8,11},{9,8},{10,9... | collective-permute-start | bytes 196616 | tf_op jit(solution)/shard_map/ppermute | solution.py:122
  16.6 7.2 %collective-permute-start.1 = (f32[64,256]{1,0:T(8,128)S(1)}, f32[64,256]{1,0:T(8,128)S(1)}, u32[]{:S(2)}, u32[]{:S(2)}) collective-permute-start(f32[64,256]{1,0:T(8,128)S(1)} %get-tuple-element.7), channel_id=1, source_target_pairs={{0,2},{1,3},{2,0},{3,1},{4,6},{5,7},{6,4},{7,5},{8,10},{9,11},{10,... | collective-permute-start | bytes 196616 | tf_op jit(solution)/shard_map/ppermute | solution.py:122
  16.8 11.4 %collective-permute-start.10 = (f32[64,256]{1,0:T(8,128)S(1)}, f32[64,256]{1,0:T(8,128)S(1)}, u32[]{:S(2)}, u32[]{:S(2)}) collective-permute-start(f32[64,256]{1,0:T(8,128)S(1)} %fusion.12), channel_id=1, source_target_pairs={{0,4},{4,0},{1,5},{5,1},{2,6},{6,2},{3,7},{7,3},{8,12},{12,8},{9,1... | collective-permute-start | bytes 196616 | tf_op jit(solution)/shard_map/ppermute | solution.py:122
  23.9 7.1 %collective-permute-start.3 = (f32[64,256]{1,0:T(8,128)S(1)}, f32[64,256]{1,0:T(8,128)S(1)}, u32[]{:S(2)}, u32[]{:S(2)}) collective-permute-start(f32[64,256]{1,0:T(8,128)S(1)} %fusion.14), channel_id=1, source_target_pairs={{0,4},{4,0},{1,5},{5,1},{2,6},{6,2},{3,7},{7,3},{8,12},{12,8},{9,1... | collective-permute-start | bytes 196616 | tf_op jit(solution)/shard_map/ppermute | solution.py:122
  28.2 8.9 %collective-permute-start.13 = (f32[64,256]{1,0:T(8,128)S(1)}, f32[64,256]{1,0:T(8,128)S(1)}, u32[]{:S(2)}, u32[]{:S(2)}) collective-permute-start(f32[64,256]{1,0:T(8,128)S(1)} %add.125.refs_0_), channel_id=1, source_target_pairs={{0,3},{1,0},{2,1},{3,2},{4,7},{5,4},{6,5},{7,6},{8,11},{9,8},{10,9... | collective-permute-start | bytes 196616 | tf_op jit(solution)/shard_map/ppermute | solution.py:122
  31.0 19.4 %collective-permute-start.6 = (f32[64,256]{1,0:T(8,128)S(1)}, f32[64,256]{1,0:T(8,128)S(1)}, u32[]{:S(2)}, u32[]{:S(2)}) collective-permute-start(f32[64,256]{1,0:T(8,128)S(1)} %add.121), channel_id=1, source_target_pairs={{0,3},{1,2},{2,1},{3,0},{4,7},{5,6},{6,5},{7,4},{8,11},{9,10},{10,... | collective-permute-start | bytes 196616 | tf_op jit(solution)/shard_map/ppermute | solution.py:143
  32.4 17.9 %collective-permute-start.5 = (f32[64,256]{1,0:T(8,128)S(1)}, f32[64,256]{1,0:T(8,128)S(1)}, u32[]{:S(2)}, u32[]{:S(2)}) collective-permute-start(f32[64,256]{1,0:T(8,128)S(1)} %add.121), channel_id=1, source_target_pairs={{0,2},{1,3},{2,0},{3,1},{4,6},{5,7},{6,4},{7,5},{8,10},{9,11},{10,... | collective-permute-start | bytes 196616 | tf_op jit(solution)/shard_map/ppermute | solution.py:143
  33.9 16.4 %collective-permute-start.4 = (f32[64,256]{1,0:T(8,128)S(1)}, f32[64,256]{1,0:T(8,128)S(1)}, u32[]{:S(2)}, u32[]{:S(2)}) collective-permute-start(f32[64,256]{1,0:T(8,128)S(1)} %add.121), channel_id=1, source_target_pairs={{0,1},{1,0},{2,3},{3,2},{4,5},{5,4},{6,7},{7,6},{8,9},{9,8},{10,11... | collective-permute-start | bytes 196616 | tf_op jit(solution)/shard_map/ppermute | solution.py:143
  34.3 5.1 %collective-permute-start.12 = (f32[64,256]{1,0:T(8,128)S(1)}, f32[64,256]{1,0:T(8,128)S(1)}, u32[]{:S(2)}, u32[]{:S(2)}) collective-permute-start(f32[64,256]{1,0:T(8,128)S(1)} %add.125.refs_0_), channel_id=1, source_target_pairs={{0,2},{1,3},{2,0},{3,1},{4,6},{5,7},{6,4},{7,5},{8,10},{9,11},{10,... | collective-permute-start | bytes 196616 | tf_op jit(solution)/shard_map/ppermute | solution.py:122
  37.1 5.0 %collective-permute-start.11 = (f32[64,256]{1,0:T(8,128)S(1)}, f32[64,256]{1,0:T(8,128)S(1)}, u32[]{:S(2)}, u32[]{:S(2)}) collective-permute-start(f32[64,256]{1,0:T(8,128)S(1)} %add.125.refs_0_), channel_id=1, source_target_pairs={{0,1},{1,2},{2,3},{3,0},{4,5},{5,6},{6,7},{7,4},{8,9},{9,10},{10,1... | collective-permute-start | bytes 196616 | tf_op jit(solution)/shard_map/ppermute | solution.py:122
  50.8 12.5 %copy-start.1 = (bf16[256,256]{1,0:T(8,128)(2,1)}, bf16[256,256]{1,0:T(8,128)(2,1)S(1)}, u32[]{:S(2)}) copy-start(bf16[256,256]{1,0:T(8,128)(2,1)S(1)} %get-tuple-element.4) | copy-start | bytes 393220
  57.8 7.0 %collective-permute-start.14 = (f32[512,256]{1,0:T(8,128)S(1)}, f32[512,256]{1,0:T(8,128)S(1)}, u32[]{:S(2)}, u32[]{:S(2)}) collective-permute-start(f32[512,256]{1,0:T(8,128)S(1)} %slice_select_fusion), channel_id=1, source_target_pairs={{0,8},{8,0},{1,9},{9,1},{2,10},{10,2},{3,11},{11,3},{4,12},{12,4},... | collective-permute-start | bytes 1572872 | tf_op jit(solution)/shard_map/ppermute | solution.py:122
  64.2 7.3 %collective-permute-start.15 = (f32[128,256]{1,0:T(8,128)}, f32[128,256]{1,0:T(8,128)S(1)}, u32[]{:S(2)}, u32[]{:S(2)}) collective-permute-start(f32[128,256]{1,0:T(8,128)} %slice_select_fusion.1), channel_id=1, source_target_pairs={{0,8},{8,0},{1,9},{9,1},{2,10},{10,2},{3,11},{11,3},{4,12},{12,4},... | collective-permute-start | bytes 393224 | tf_op jit(solution)/shard_map/ppermute | solution.py:122
  65.7 43.5 %all-to-all-start = ((f32[16,32,256]{2,1,0:T(8,128)}), f32[16,32,256]{2,1,0:T(8,128)S(1)}, u32[]{:S(2)}, u32[]{:S(2)}) async-start(f32[16,32,256]{2,1,0:T(8,128)} %bitcast.23), calls=%async_computation | async-start | bytes 1048576 | tf_op jit(solution)/shard_map/all_to_all | solution.py:107
  71.5 4.4 %collective-permute-start.16 = (f32[32,256]{1,0:T(8,128)S(1)}, f32[32,256]{1,0:T(8,128)S(1)}, u32[]{:S(2)}, u32[]{:S(2)}) collective-permute-start(f32[32,256]{1,0:T(8,128)S(1)} %get-tuple-element.11), channel_id=1, source_target_pairs={{0,64},{64,128},{128,192},{192,0},{1,65},{65,129},{129,193},{193,1... | collective-permute-start | bytes 98312 | tf_op jit(solution)/shard_map/ppermute | solution.py:122
  72.9 4.8 %collective-permute-start.18 = (f32[32,256]{1,0:T(8,128)S(1)}, f32[32,256]{1,0:T(8,128)S(1)}, u32[]{:S(2)}, u32[]{:S(2)}) collective-permute-start(f32[32,256]{1,0:T(8,128)S(1)} %get-tuple-element.12), channel_id=1, source_target_pairs={{0,192},{64,0},{128,64},{192,128},{1,193},{65,1},{129,65},{193,129... | collective-permute-start | bytes 98312 | tf_op jit(solution)/shard_map/ppermute | solution.py:122
  74.3 5.7 %collective-permute-start.17 = (f32[32,256]{1,0:T(8,128)S(1)}, f32[32,256]{1,0:T(8,128)S(1)}, u32[]{:S(2)}, u32[]{:S(2)}) collective-permute-start(f32[32,256]{1,0:T(8,128)S(1)} %get-tuple-element.13), channel_id=1, source_target_pairs={{0,128},{64,192},{128,0},{192,64},{1,129},{65,193},{129,1},{193,65... | collective-permute-start | bytes 98312 | tf_op jit(solution)/shard_map/ppermute | solution.py:122
  79.9 5.7 %collective-permute-start.21 = (f32[32,256]{1,0:T(8,128)S(1)}, f32[32,256]{1,0:T(8,128)S(1)}, u32[]{:S(2)}, u32[]{:S(2)}) collective-permute-start(f32[32,256]{1,0:T(8,128)S(1)} %fusion.16), channel_id=1, source_target_pairs={{0,48},{16,0},{32,16},{48,32},{1,49},{17,1},{33,17},{49,33},{2,50}... | collective-permute-start | bytes 98312 | tf_op jit(solution)/shard_map/ppermute | solution.py:122
  84.7 3.7 %collective-permute-start.20 = (f32[32,256]{1,0:T(8,128)S(1)}, f32[32,256]{1,0:T(8,128)S(1)}, u32[]{:S(2)}, u32[]{:S(2)}) collective-permute-start(f32[32,256]{1,0:T(8,128)S(1)} %fusion.16), channel_id=1, source_target_pairs={{0,32},{16,48},{32,0},{48,16},{1,33},{17,49},{33,1},{49,17},{2,34}... | collective-permute-start | bytes 98312 | tf_op jit(solution)/shard_map/ppermute | solution.py:122
  84.7 4.6 %collective-permute-start.19 = (f32[32,256]{1,0:T(8,128)S(1)}, f32[32,256]{1,0:T(8,128)S(1)}, u32[]{:S(2)}, u32[]{:S(2)}) collective-permute-start(f32[32,256]{1,0:T(8,128)S(1)} %fusion.16), channel_id=1, source_target_pairs={{0,16},{16,32},{32,48},{48,0},{1,17},{17,33},{33,49},{49,1},{2,18}... | collective-permute-start | bytes 98312 | tf_op jit(solution)/shard_map/ppermute | solution.py:122
  89.2 6.0 %collective-permute-start.24 = (f32[32,256]{1,0:T(8,128)S(1)}, f32[32,256]{1,0:T(8,128)S(1)}, u32[]{:S(2)}, u32[]{:S(2)}) collective-permute-start(f32[32,256]{1,0:T(8,128)S(1)} %add_add_fusion.refs_0_), channel_id=1, source_target_pairs={{0,192},{64,0},{128,64},{192,128},{1,193},{65,1},{129,65},{193,129... | collective-permute-start | bytes 98312 | tf_op jit(solution)/shard_map/ppermute | solution.py:122
  90.0 5.8 %collective-permute-start.23 = (f32[32,256]{1,0:T(8,128)S(1)}, f32[32,256]{1,0:T(8,128)S(1)}, u32[]{:S(2)}, u32[]{:S(2)}) collective-permute-start(f32[32,256]{1,0:T(8,128)S(1)} %add_add_fusion.refs_0_), channel_id=1, source_target_pairs={{0,128},{64,192},{128,0},{192,64},{1,129},{65,193},{129,1},{193,65... | collective-permute-start | bytes 98312 | tf_op jit(solution)/shard_map/ppermute | solution.py:122
  90.7 9.0 %collective-permute-start.22 = (f32[32,256]{1,0:T(8,128)S(1)}, f32[32,256]{1,0:T(8,128)S(1)}, u32[]{:S(2)}, u32[]{:S(2)}) collective-permute-start(f32[32,256]{1,0:T(8,128)S(1)} %add_add_fusion.refs_0_), channel_id=1, source_target_pairs={{0,64},{64,128},{128,192},{192,0},{1,65},{65,129},{129,193},{193,1... | collective-permute-start | bytes 98312 | tf_op jit(solution)/shard_map/ppermute | solution.py:122
  91.5 8.3 %collective-permute-start.25 = (f32[32,256]{1,0:T(8,128)S(1)}, f32[32,256]{1,0:T(8,128)S(1)}, u32[]{:S(2)}, u32[]{:S(2)}) collective-permute-start(f32[32,256]{1,0:T(8,128)S(1)} %add_add_fusion.refs_0_), channel_id=1, source_target_pairs={{0,8},{8,0},{1,9},{9,1},{2,10},{10,2},{3,11},{11,3},{4,12},{12,4},... | collective-permute-start | bytes 98312 | tf_op jit(solution)/shard_map/ppermute | solution.py:122
  95.2 4.5 %collective-permute-start.28 = (f32[32,256]{1,0:T(8,128)S(1)}, f32[32,256]{1,0:T(8,128)S(1)}, u32[]{:S(2)}, u32[]{:S(2)}) collective-permute-start(f32[32,256]{1,0:T(8,128)S(1)} %collective-permute-done.24.refs_3_), channel_id=1, source_target_pairs={{0,8},{8,0},{1,9},{9,1},{2,10},{10,2},{3,11},{11,3},{4,12},{12,4},... | collective-permute-start | bytes 98312 | tf_op jit(solution)/shard_map/ppermute | solution.py:122
  95.9 4.7 %collective-permute-start.27 = (f32[32,256]{1,0:T(8,128)S(1)}, f32[32,256]{1,0:T(8,128)S(1)}, u32[]{:S(2)}, u32[]{:S(2)}) collective-permute-start(f32[32,256]{1,0:T(8,128)S(1)} %collective-permute-done.23.refs_2_), channel_id=1, source_target_pairs={{0,8},{8,0},{1,9},{9,1},{2,10},{10,2},{3,11},{11,3},{4,12},{12,4},... | collective-permute-start | bytes 98312 | tf_op jit(solution)/shard_map/ppermute | solution.py:122
  99.7 1.2 collective-permute-start.26
  122.5 3.1 %collective-permute-start.29 = (bf16[512,256]{1,0:T(8,128)(2,1)S(1)}, bf16[512,256]{1,0:T(8,128)(2,1)S(1)}, u32[]{:S(2)}, u32[]{:S(2)}) collective-permute-start(bf16[512,256]{1,0:T(8,128)(2,1)S(1)} %bitcast.87), channel_id=1, source_target_pairs={{0,8},{8,0},{1,9},{9,1},{2,10},{10,2},{3,11},{11,3},{4,12},{12,4},... | collective-permute-start | bytes 786440 | tf_op jit(solution)/shard_map/ppermute | solution.py:122
  125.8 29.2 %copy-start.2 = (bf16[1024,256]{1,0:T(8,128)(2,1)}, bf16[1024,256]{1,0:T(8,128)(2,1)S(1)}, u32[]{:S(2)}) copy-start(bf16[1024,256]{1,0:T(8,128)(2,1)S(1)} %maximum_select_fusion) | copy-start | bytes 1572868
  132.5 1.3 collective-permute-start.30
  133.8 2.6 %collective-permute-start.33 = (f32[16,256]{1,0:T(8,128)S(1)}, f32[16,256]{1,0:T(8,128)S(1)}, u32[]{:S(2)}, u32[]{:S(2)}) collective-permute-start(f32[16,256]{1,0:T(8,128)S(1)} %bitcast_add_fusion.3), channel_id=1, source_target_pairs={{0,192},{64,0},{128,64},{192,128},{1,193},{65,1},{129,65},{193,129... | collective-permute-start | bytes 49160 | tf_op jit(solution)/shard_map/ppermute | solution.py:122
  134.3 4.1 %collective-permute-start.32 = (f32[16,256]{1,0:T(8,128)S(1)}, f32[16,256]{1,0:T(8,128)S(1)}, u32[]{:S(2)}, u32[]{:S(2)}) collective-permute-start(f32[16,256]{1,0:T(8,128)S(1)} %bitcast_add_fusion.3), channel_id=1, source_target_pairs={{0,128},{64,192},{128,0},{192,64},{1,129},{65,193},{129,1},{193,65... | collective-permute-start | bytes 49160 | tf_op jit(solution)/shard_map/ppermute | solution.py:122
  134.6 4.1 %collective-permute-start.31 = (f32[16,256]{1,0:T(8,128)S(1)}, f32[16,256]{1,0:T(8,128)S(1)}, u32[]{:S(2)}, u32[]{:S(2)}) collective-permute-start(f32[16,256]{1,0:T(8,128)S(1)} %bitcast_add_fusion.3), channel_id=1, source_target_pairs={{0,64},{64,128},{128,192},{192,0},{1,65},{65,129},{129,193},{193,1... | collective-permute-start | bytes 49160 | tf_op jit(solution)/shard_map/ppermute | solution.py:122

commit v6 on v5

--- a/solution.py
+++ b/solution.py
@@ -203,10 +203,8 @@
     )
     row = ring_scatter(partial_second, "y")
     row = ring_sum(row, "zh")
-    parts = quad_gather(row, "y")
-    mttkrp_second = jnp.concatenate(parts, axis=0)
-    second_factor = jnp.dot(mttkrp_second, inverse_second, precision=HIGHEST).astype(jnp.bfloat16)
-    second_factor = ordered(jnp.split(second_factor, 4, axis=0), lax.axis_index("y"))
+    row = jnp.dot(row, inverse_second, precision=HIGHEST).astype(jnp.bfloat16)
+    second_factor = ordered(quad_gather(row, "y"), lax.axis_index("y"))
 
     gram_local = jnp.dot(second_factor.T, second_factor, preferred_element_type=jnp.float32)
     mine, other = keep(gram_local, core)

time: 157 us -> 159 us (1.013)
  blocking collectives: 28.6 us -> 31.2 us
    ppermute x31, waiting for transfers between devices: 22.4 us -> 19.7 us  [shift(): return lax.ppermute(x, axis, [(s, (s + d) % n) for s in range(n)])]
    all_to_all x2, blocking collectives: 28.6 us -> 31.2 us  [exchange(): return lax.all_to_all(x, axes, 0, 0, tiled=True)]
    ppermute x3, waiting for transfers between devices: 0.01 us -> 2.54 us  [pair(): lax.ppermute(x, axis, [(s, s ^ d) for s in range(lax.axis_size(axis))])]
  transfers between devices with their start and end apart: 35 -> 35, of which waited for: 16 -> 18; matrix products, arithmetic and copies ran while one was open for 6% -> 6% of each run, Pallas kernels for 11% -> 10%
where the time goes in v6:
time: 159 us; the launch traced here: 157 us
  starting transfers between devices  61.1 us (38%)
  blocking collectives  31.2 us (20%)
  waiting for transfers between devices  22.3 us (14%)
  matrix products  20.2 us (13%)
  Pallas kernels  16.4 us (10%)
  other arithmetic  3.41 us (2%)
  local copies, waits for them, and re-layouts  1.6 us (1%)
    ppermute x31, starting transfers between devices, shift(): return lax.ppermute(x, axis, [(s, (s + d) % n) for s in range(n)])  51.7 us
    all_to_all x2, blocking collectives, exchange(): return lax.all_to_all(x, axes, 0, 0, tiled=True)  31.2 us
    ppermute x31, waiting for transfers between devices, shift(): return lax.ppermute(x, axis, [(s, (s + d) % n) for s in range(n)])  19.7 us
    pallas_call x2, Pallas kernels, inverse(): pl.pallas_call(functools.partial(inverse_kernel, places, total), out_shap...  16.4 us
    dot_general x1, matrix products, on_device(): jnp.einsum('ijk,kr->ijr', tensor, third_new, preferred_element_type=jnp.f...  6.63 us
    dot_general x1, matrix products, on_device(): jnp.einsum('ijk,jr->ikr', tensor, second_factor, preferred_element_type=j...  6.56 us
    dot_general x1, matrix products, on_device(): jnp.einsum('ijk,kr->ijr', tensor, third_factor, preferred_element_type=jn...  5.75 us
    all_to_all x1, starting transfers between devices, exchange(): return lax.all_to_all(x, axes, 0, 0, tiled=True)  5.48 us
  transfers between devices with their start and end apart: 35, of which 18 were waited for; matrix products, arithmetic and copies ran while one was open for 6% of the time, Pallas kernels for 10%

profile of v6, /device:TPU:1, one launch (start us, length us, event | category | flops | bytes accessed | tf_op | source)
XLA Modules:
  0.0 157.2 jit_solution(579231095209998675)
XLA Ops:
  0.7 1.0 copy-done
  2.1 2.2 %collective-permute-start.4 = (f32[64,256]{1,0:T(8,128)S(1)}, f32[64,256]{1,0:T(8,128)S(1)}, u32[]{:S(2)}, u32[]{:S(2)}) collective-permute-start(f32[64,256]{1,0:T(8,128)S(1)} %get-tuple-element.8), channel_id=1, source_target_pairs={{0,1},{1,2},{2,3},{3,0},{4,5},{5,6},{6,7},{7,4},{8,9},{9,10},{10,1... | collective-permute-start | bytes 196616 | tf_op jit(solution)/shard_map/ppermute | solution.py:122
  4.3 1.5 collective-permute-start.6
  5.8 1.6 collective-permute-start.5
  7.3 0.7 multiply_bitcast_fusion
  8.0 5.7 %multiply_reduce_fusion.1 = f32[256,256]{0,1:T(8,128)S(1)} fusion(bf16[16,256,1024]{2,1,0:T(8,128)(2,1)} %param.3, f32[256,16]{0,1:T(8,128)S(1)} %multiply_bitcast_fusion, bf16[1024,256]{1,0:T(8,128)(2,1)S(1)} %copy-done), kind=kOutput, calls=%fused_computation.3 | convolution fusion | flops 2149515264 | bytes 9191424 | tf_op jit(solution)/shard_map/ijk,kr->ijr/dot_general | solution.py:200
  14.3 2.3 %collective-permute-start.2 = (f32[64,256]{1,0:T(8,128)S(1)}, f32[64,256]{1,0:T(8,128)S(1)}, u32[]{:S(2)}, u32[]{:S(2)}) collective-permute-start(f32[64,256]{1,0:T(8,128)S(1)} %get-tuple-element.6), channel_id=1, source_target_pairs={{0,3},{1,0},{2,1},{3,2},{4,7},{5,4},{6,5},{7,6},{8,11},{9,8},{10,9... | collective-permute-start | bytes 196616 | tf_op jit(solution)/shard_map/ppermute | solution.py:122
  16.8 7.0 %collective-permute-start.7 = (f32[64,256]{1,0:T(8,128)S(1)}, f32[64,256]{1,0:T(8,128)S(1)}, u32[]{:S(2)}, u32[]{:S(2)}) collective-permute-start(f32[64,256]{1,0:T(8,128)S(1)} %fusion.5), channel_id=1, source_target_pairs={{0,4},{4,0},{1,5},{5,1},{2,6},{6,2},{3,7},{7,3},{8,12},{12,8},{9,1... | collective-permute-start | bytes 196616 | tf_op jit(solution)/shard_map/ppermute | solution.py:122
  23.9 4.4 %collective-permute-start.3 = (f32[64,256]{1,0:T(8,128)S(1)}, f32[64,256]{1,0:T(8,128)S(1)}, u32[]{:S(2)}, u32[]{:S(2)}) collective-permute-start(f32[64,256]{1,0:T(8,128)S(1)} %fusion.7), channel_id=1, source_target_pairs={{0,4},{4,0},{1,5},{5,1},{2,6},{6,2},{3,7},{7,3},{8,12},{12,8},{9,1... | collective-permute-start | bytes 196616 | tf_op jit(solution)/shard_map/ppermute | solution.py:122
  28.7 0.9 collective-permute-start.9
  30.0 1.4 collective-permute-done.10.refs_3_
  31.4 2.2 %collective-permute-done.9.refs_2_ = f32[64,256]{1,0:T(8,128)S(1)} collective-permute-done((f32[64,256]{1,0:T(8,128)S(1)}, f32[64,256]{1,0:T(8,128)S(1)}, u32[]{:S(2)}, u32[]{:S(2)}) %collective-permute-start.9) | collective-permute-done | bytes 65568 | tf_op jit(solution)/shard_map/ppermute | solution.py:122
  33.6 0.7 collective-permute-done.8.refs_1_
  34.3 8.2 %inverse.2 = f32[256,256]{1,0:T(8,128)S(1)} custom-call(f32[64,256]{1,0:T(8,128)S(1)} %add.125.refs_0_, f32[64,256]{1,0:T(8,128)S(1)} %collective-permute-done.8.refs_1_, f32[64,256]{1,0:T(8,128)S(1)} %collective-permute-done.9.refs_2_, f32[64,256]{1,0:T(8,128)S(1)} %collective-permute-done.10.refs_3_, f32[256,256]{1,0:T(8,128)S(1)} %convolution_multiply_fusion.refs_4_.refs_8_), custom_call_target="tpu_custom_call" | custom-call | flops 201326592 | bytes 524288 | tf_op jit(solution)/shard_map/inverse/pallas_call | solution.py:94
  43.2 2.1 %collective-permute-start.12 = (bf16[64,256]{1,0:T(8,128)(2,1)S(1)}, bf16[64,256]{1,0:T(8,128)(2,1)S(1)}, u32[]{:S(2)}, u32[]{:S(2)}) collective-permute-start(bf16[64,256]{1,0:T(8,128)(2,1)S(1)} %convolution_convert_fusion), channel_id=1, source_target_pairs={{0,2},{1,3},{2,0},{3,1},{4,6},{5,7},{6,4},{7,5},{8,10},{9,11},{10,... | collective-permute-start | bytes 98312 | tf_op jit(solution)/shard_map/ppermute | solution.py:143
  45.4 1.4 collective-permute-start.11
  46.8 0.7 collective-permute-done.12
  47.5 1.8 %collective-permute-done.11 = bf16[64,256]{1,0:T(8,128)(2,1)S(1)} collective-permute-done((bf16[64,256]{1,0:T(8,128)(2,1)S(1)}, bf16[64,256]{1,0:T(8,128)(2,1)S(1)}, u32[]{:S(2)}, u32[]{:S(2)}) %collective-permute-start.11) | collective-permute-done | bytes 32800 | tf_op jit(solution)/shard_map/ppermute | solution.py:143
  49.4 6.6 %multiply_reduce_fusion = f32[256,1024]{1,0:T(8,128)S(1)} fusion(bf16[16,256,1024]{2,1,0:T(8,128)(2,1)} %param.3, f32[256,16]{0,1:T(8,128)S(1)} %multiply_bitcast_fusion, bf16[256,256]{1,0:T(8,128)(2,1)S(1)} %get-tuple-element.4), kind=kOutput, calls=%fused_computation | convolution fusion | flops 2155610112 | bytes 9584640 | tf_op jit(solution)/shard_map/ijk,jr->ikr/dot_general | solution.py:218
  56.4 6.7 %collective-permute-start.14 = (f32[512,256]{1,0:T(8,128)S(1)}, f32[512,256]{1,0:T(8,128)S(1)}, u32[]{:S(2)}, u32[]{:S(2)}) collective-permute-start(f32[512,256]{1,0:T(8,128)S(1)} %slice_select_fusion), channel_id=1, source_target_pairs={{0,8},{8,0},{1,9},{9,1},{2,10},{10,2},{3,11},{11,3},{4,12},{12,4},... | collective-permute-start | bytes 1572872 | tf_op jit(solution)/shard_map/ppermute | solution.py:122
  63.3 0.7 slice_select_fusion.1
  64.6 0.9 select_add_fusion
  65.5 5.5 %all-to-all-start = ((f32[16,32,256]{2,1,0:T(8,128)}), f32[16,32,256]{2,1,0:T(8,128)S(1)}, u32[]{:S(2)}, u32[]{:S(2)}) async-start(f32[16,32,256]{2,1,0:T(8,128)} %bitcast.23), calls=%async_computation | async-start | bytes 1048576 | tf_op jit(solution)/shard_map/all_to_all | solution.py:107
  71.1 1.4 collective-permute-start.16
  72.5 1.3 collective-permute-start.18
  73.9 1.6 %collective-permute-start.17 = (f32[32,256]{1,0:T(8,128)S(1)}, f32[32,256]{1,0:T(8,128)S(1)}, u32[]{:S(2)}, u32[]{:S(2)}) collective-permute-start(f32[32,256]{1,0:T(8,128)S(1)} %get-tuple-element.13), channel_id=1, source_target_pairs={{0,128},{64,192},{128,0},{192,64},{1,129},{65,193},{129,1},{193,65... | collective-permute-start | bytes 98312 | tf_op jit(solution)/shard_map/ppermute | solution.py:122
  75.5 1.8 %collective-permute-done.18 = f32[32,256]{1,0:T(8,128)S(1)} collective-permute-done((f32[32,256]{1,0:T(8,128)S(1)}, f32[32,256]{1,0:T(8,128)S(1)}, u32[]{:S(2)}, u32[]{:S(2)}) %collective-permute-start.18) | collective-permute-done | bytes 32800 | tf_op jit(solution)/shard_map/ppermute | solution.py:122
  77.3 2.2 %collective-permute-done.17 = f32[32,256]{1,0:T(8,128)S(1)} collective-permute-done((f32[32,256]{1,0:T(8,128)S(1)}, f32[32,256]{1,0:T(8,128)S(1)}, u32[]{:S(2)}, u32[]{:S(2)}) %collective-permute-start.17) | collective-permute-done | bytes 32800 | tf_op jit(solution)/shard_map/ppermute | solution.py:122
  79.5 4.7 %collective-permute-start.21 = (f32[32,256]{1,0:T(8,128)S(1)}, f32[32,256]{1,0:T(8,128)S(1)}, u32[]{:S(2)}, u32[]{:S(2)}) collective-permute-start(f32[32,256]{1,0:T(8,128)S(1)} %fusion.10), channel_id=1, source_target_pairs={{0,48},{16,0},{32,16},{48,32},{1,49},{17,1},{33,17},{49,33},{2,50}... | collective-permute-start | bytes 98312 | tf_op jit(solution)/shard_map/ppermute | solution.py:122
  84.6 0.6 collective-permute-done.21
  85.3 2.6 %collective-permute-done.20 = f32[32,256]{1,0:T(8,128)S(1)} collective-permute-done((f32[32,256]{1,0:T(8,128)S(1)}, f32[32,256]{1,0:T(8,128)S(1)}, u32[]{:S(2)}, u32[]{:S(2)}) %collective-permute-start.20) | collective-permute-done | bytes 32800 | tf_op jit(solution)/shard_map/ppermute | solution.py:122
  87.9 0.9 collective-permute-done.19
  88.8 0.8 collective-permute-start.24
  89.6 0.7 collective-permute-start.23
  90.3 0.8 collective-permute-start.22
  91.1 3.7 %collective-permute-start.25 = (f32[32,256]{1,0:T(8,128)S(1)}, f32[32,256]{1,0:T(8,128)S(1)}, u32[]{:S(2)}, u32[]{:S(2)}) collective-permute-start(f32[32,256]{1,0:T(8,128)S(1)} %add_add_fusion.refs_0_), channel_id=1, source_target_pairs={{0,8},{8,0},{1,9},{9,1},{2,10},{10,2},{3,11},{11,3},{4,12},{12,4},... | collective-permute-start | bytes 98312 | tf_op jit(solution)/shard_map/ppermute | solution.py:122
  95.5 3.9 %collective-permute-start.27 = (f32[32,256]{1,0:T(8,128)S(1)}, f32[32,256]{1,0:T(8,128)S(1)}, u32[]{:S(2)}, u32[]{:S(2)}) collective-permute-start(f32[32,256]{1,0:T(8,128)S(1)} %collective-permute-done.23.refs_2_), channel_id=1, source_target_pairs={{0,8},{8,0},{1,9},{9,1},{2,10},{10,2},{3,11},{11,3},{4,12},{12,4},... | collective-permute-start | bytes 98312 | tf_op jit(solution)/shard_map/ppermute | solution.py:122
  99.4 0.8 collective-permute-done.27.refs_6_
  100.5 8.2 %inverse.3 = f32[256,256]{1,0:T(8,128)S(1)} custom-call(f32[32,256]{1,0:T(8,128)S(1)} %add_add_fusion.refs_0_, f32[32,256]{1,0:T(8,128)S(1)} %collective-permute-done.22.refs_1_, f32[32,256]{1,0:T(8,128)S(1)} %collective-permute-done.23.refs_2_, f32[32,256]{1,0:T(8,128)S(1)} %collective-permute-done.24.refs_3_, ...), custom_call_target="tpu_custom_call" | custom-call | flops 201326592 | bytes 524288 | tf_op jit(solution)/shard_map/inverse/pallas_call | solution.py:94
  109.1 13.0 %all_to_all.15 = bf16[16,32,256]{2,1,0:T(8,128)(2,1)S(1)} all-to-all(bf16[16,32,256]{2,1,0:T(8,128)(2,1)S(1)} %broadcast_in_dim.4), channel_id=1, replica_groups=mesh['x'=4,'zl'=4,'core'=2,'zh'=2,'y'=4] {'x','zl'}, dimensions={0} | all-to-all | bytes 524288 | tf_op jit(solution)/shard_map/all_to_all | solution.py:107
  122.1 1.9 %collective-permute-start.29 = (bf16[512,256]{1,0:T(8,128)(2,1)S(1)}, bf16[512,256]{1,0:T(8,128)(2,1)S(1)}, u32[]{:S(2)}, u32[]{:S(2)}) collective-permute-start(bf16[512,256]{1,0:T(8,128)(2,1)S(1)} %bitcast.87), channel_id=1, source_target_pairs={{0,8},{8,0},{1,9},{9,1},{2,10},{10,2},{3,11},{11,3},{4,12},{12,4},... | collective-permute-start | bytes 786440 | tf_op jit(solution)/shard_map/ppermute | solution.py:122
  124.2 1.0 collective-permute-done.29
  125.4 6.6 %fusion = f32[256,16]{0,1:T(8,128)S(1)} fusion(bf16[16,256,1024]{2,1,0:T(8,128)(2,1)} %param.3, f32[256,256]{1,0:T(8,128)S(1)} %copy.34, bf16[1024,256]{1,0:T(8,128)(2,1)S(1)} %maximum_select_fusion), kind=kOutput, calls=%fused_computation.2 | convolution fusion | flops 2149576704 | bytes 9191424 | tf_op jit(solution)/shard_map/ijk,kr->ijr/dot_general | solution.py:229
  132.5 0.8 collective-permute-done.30
  134.8 1.1 collective-permute-done.33
  136.0 2.1 %collective-permute-done.32 = f32[16,256]{1,0:T(8,128)S(1)} collective-permute-done((f32[16,256]{1,0:T(8,128)S(1)}, f32[16,256]{1,0:T(8,128)S(1)}, u32[]{:S(2)}, u32[]{:S(2)}) %collective-permute-start.32) | collective-permute-done | bytes 16416 | tf_op jit(solution)/shard_map/ppermute | solution.py:122
  138.4 18.2 %all_to_all.16 = bf16[32,16,256]{2,1,0:T(8,128)(2,1)S(1)} all-to-all(bf16[32,16,256]{2,1,0:T(8,128)(2,1)S(1)} %broadcast_in_dim.5), channel_id=1, replica_groups=mesh['x'=4,'zl'=4,'core'=2,'zh'=2,'y'=4] {'zl','zh','y'}, dimensions={0} | all-to-all | bytes 524288 | tf_op jit(solution)/shard_map/all_to_all | solution.py:107
  156.6 0.7 convert_reduce_fusion
  (66 shorter events, 8.4 us)
Async XLA Ops:
  0.6 1.0 copy-start
  2.1 14.5 %collective-permute-start.4 = (f32[64,256]{1,0:T(8,128)S(1)}, f32[64,256]{1,0:T(8,128)S(1)}, u32[]{:S(2)}, u32[]{:S(2)}) collective-permute-start(f32[64,256]{1,0:T(8,128)S(1)} %get-tuple-element.8), channel_id=1, source_target_pairs={{0,1},{1,2},{2,3},{3,0},{4,5},{5,6},{6,7},{7,4},{8,9},{9,10},{10,1... | collective-permute-start | bytes 196616 | tf_op jit(solution)/shard_map/ppermute | solution.py:122
  4.3 12.5 %collective-permute-start.6 = (f32[64,256]{1,0:T(8,128)S(1)}, f32[64,256]{1,0:T(8,128)S(1)}, u32[]{:S(2)}, u32[]{:S(2)}) collective-permute-start(f32[64,256]{1,0:T(8,128)S(1)} %get-tuple-element.9), channel_id=1, source_target_pairs={{0,3},{1,0},{2,1},{3,2},{4,7},{5,4},{6,5},{7,6},{8,11},{9,8},{10,9... | collective-permute-start | bytes 196616 | tf_op jit(solution)/shard_map/ppermute | solution.py:122
  5.8 11.0 %collective-permute-start.5 = (f32[64,256]{1,0:T(8,128)S(1)}, f32[64,256]{1,0:T(8,128)S(1)}, u32[]{:S(2)}, u32[]{:S(2)}) collective-permute-start(f32[64,256]{1,0:T(8,128)S(1)} %get-tuple-element.10), channel_id=1, source_target_pairs={{0,2},{1,3},{2,0},{3,1},{4,6},{5,7},{6,4},{7,5},{8,10},{9,11},{10,... | collective-permute-start | bytes 196616 | tf_op jit(solution)/shard_map/ppermute | solution.py:122
  8.0 21.8 %copy-start.3 = (bf16[16,256]{1,0:T(8,128)(2,1)S(1)}, bf16[16,256]{1,0:T(8,128)(2,1)}, u32[]{:S(2)}) copy-start(bf16[16,256]{1,0:T(8,128)(2,1)} %param.4) | copy-start | bytes 24580
  13.8 10.0 %collective-permute-start = (f32[64,256]{1,0:T(8,128)S(1)}, f32[64,256]{1,0:T(8,128)S(1)}, u32[]{:S(2)}, u32[]{:S(2)}) collective-permute-start(f32[64,256]{1,0:T(8,128)S(1)} %get-tuple-element.5), channel_id=1, source_target_pairs={{0,1},{1,2},{2,3},{3,0},{4,5},{5,6},{6,7},{7,4},{8,9},{9,10},{10,1... | collective-permute-start | bytes 196616 | tf_op jit(solution)/shard_map/ppermute | solution.py:122
  14.3 9.5 %collective-permute-start.2 = (f32[64,256]{1,0:T(8,128)S(1)}, f32[64,256]{1,0:T(8,128)S(1)}, u32[]{:S(2)}, u32[]{:S(2)}) collective-permute-start(f32[64,256]{1,0:T(8,128)S(1)} %get-tuple-element.6), channel_id=1, source_target_pairs={{0,3},{1,0},{2,1},{3,2},{4,7},{5,4},{6,5},{7,6},{8,11},{9,8},{10,9... | collective-permute-start | bytes 196616 | tf_op jit(solution)/shard_map/ppermute | solution.py:122
  16.6 7.2 %collective-permute-start.1 = (f32[64,256]{1,0:T(8,128)S(1)}, f32[64,256]{1,0:T(8,128)S(1)}, u32[]{:S(2)}, u32[]{:S(2)}) collective-permute-start(f32[64,256]{1,0:T(8,128)S(1)} %get-tuple-element.7), channel_id=1, source_target_pairs={{0,2},{1,3},{2,0},{3,1},{4,6},{5,7},{6,4},{7,5},{8,10},{9,11},{10,... | collective-permute-start | bytes 196616 | tf_op jit(solution)/shard_map/ppermute | solution.py:122
  16.8 11.4 %collective-permute-start.7 = (f32[64,256]{1,0:T(8,128)S(1)}, f32[64,256]{1,0:T(8,128)S(1)}, u32[]{:S(2)}, u32[]{:S(2)}) collective-permute-start(f32[64,256]{1,0:T(8,128)S(1)} %fusion.5), channel_id=1, source_target_pairs={{0,4},{4,0},{1,5},{5,1},{2,6},{6,2},{3,7},{7,3},{8,12},{12,8},{9,1... | collective-permute-start | bytes 196616 | tf_op jit(solution)/shard_map/ppermute | solution.py:122
  23.9 18.7 %collective-permute-start.3 = (f32[64,256]{1,0:T(8,128)S(1)}, f32[64,256]{1,0:T(8,128)S(1)}, u32[]{:S(2)}, u32[]{:S(2)}) collective-permute-start(f32[64,256]{1,0:T(8,128)S(1)} %fusion.7), channel_id=1, source_target_pairs={{0,4},{4,0},{1,5},{5,1},{2,6},{6,2},{3,7},{7,3},{8,12},{12,8},{9,1... | collective-permute-start | bytes 196616 | tf_op jit(solution)/shard_map/ppermute | solution.py:122
  28.2 3.2 %collective-permute-start.10 = (f32[64,256]{1,0:T(8,128)S(1)}, f32[64,256]{1,0:T(8,128)S(1)}, u32[]{:S(2)}, u32[]{:S(2)}) collective-permute-start(f32[64,256]{1,0:T(8,128)S(1)} %add.125.refs_0_), channel_id=1, source_target_pairs={{0,3},{1,0},{2,1},{3,2},{4,7},{5,4},{6,5},{7,6},{8,11},{9,8},{10,9... | collective-permute-start | bytes 196616 | tf_op jit(solution)/shard_map/ppermute | solution.py:122
  28.7 4.9 %collective-permute-start.9 = (f32[64,256]{1,0:T(8,128)S(1)}, f32[64,256]{1,0:T(8,128)S(1)}, u32[]{:S(2)}, u32[]{:S(2)}) collective-permute-start(f32[64,256]{1,0:T(8,128)S(1)} %add.125.refs_0_), channel_id=1, source_target_pairs={{0,2},{1,3},{2,0},{3,1},{4,6},{5,7},{6,4},{7,5},{8,10},{9,11},{10,... | collective-permute-start | bytes 196616 | tf_op jit(solution)/shard_map/ppermute | solution.py:122
  29.6 4.7 %collective-permute-start.8 = (f32[64,256]{1,0:T(8,128)S(1)}, f32[64,256]{1,0:T(8,128)S(1)}, u32[]{:S(2)}, u32[]{:S(2)}) collective-permute-start(f32[64,256]{1,0:T(8,128)S(1)} %add.125.refs_0_), channel_id=1, source_target_pairs={{0,1},{1,2},{2,3},{3,0},{4,5},{5,6},{6,7},{7,4},{8,9},{9,10},{10,1... | collective-permute-start | bytes 196616 | tf_op jit(solution)/shard_map/ppermute | solution.py:122
  42.8 4.0 %collective-permute-start.13 = (bf16[64,256]{1,0:T(8,128)(2,1)S(1)}, bf16[64,256]{1,0:T(8,128)(2,1)S(1)}, u32[]{:S(2)}, u32[]{:S(2)}) collective-permute-start(bf16[64,256]{1,0:T(8,128)(2,1)S(1)} %convolution_convert_fusion), channel_id=1, source_target_pairs={{0,1},{1,0},{2,3},{3,2},{4,5},{5,4},{6,7},{7,6},{8,9},{9,8},{10,11... | collective-permute-start | bytes 98312 | tf_op jit(solution)/shard_map/ppermute | solution.py:143
  43.2 4.3 %collective-permute-start.12 = (bf16[64,256]{1,0:T(8,128)(2,1)S(1)}, bf16[64,256]{1,0:T(8,128)(2,1)S(1)}, u32[]{:S(2)}, u32[]{:S(2)}) collective-permute-start(bf16[64,256]{1,0:T(8,128)(2,1)S(1)} %convolution_convert_fusion), channel_id=1, source_target_pairs={{0,2},{1,3},{2,0},{3,1},{4,6},{5,7},{6,4},{7,5},{8,10},{9,11},{10,... | collective-permute-start | bytes 98312 | tf_op jit(solution)/shard_map/ppermute | solution.py:143
  45.4 4.0 %collective-permute-start.11 = (bf16[64,256]{1,0:T(8,128)(2,1)S(1)}, bf16[64,256]{1,0:T(8,128)(2,1)S(1)}, u32[]{:S(2)}, u32[]{:S(2)}) collective-permute-start(bf16[64,256]{1,0:T(8,128)(2,1)S(1)} %convolution_convert_fusion), channel_id=1, source_target_pairs={{0,3},{1,2},{2,1},{3,0},{4,7},{5,6},{6,5},{7,4},{8,11},{9,10},{10,... | collective-permute-start | bytes 98312 | tf_op jit(solution)/shard_map/ppermute | solution.py:143
  49.4 13.7 %copy-start.1 = (bf16[256,256]{1,0:T(8,128)(2,1)}, bf16[256,256]{1,0:T(8,128)(2,1)S(1)}, u32[]{:S(2)}) copy-start(bf16[256,256]{1,0:T(8,128)(2,1)S(1)} %get-tuple-element.4) | copy-start | bytes 393220
  56.4 8.3 %collective-permute-start.14 = (f32[512,256]{1,0:T(8,128)S(1)}, f32[512,256]{1,0:T(8,128)S(1)}, u32[]{:S(2)}, u32[]{:S(2)}) collective-permute-start(f32[512,256]{1,0:T(8,128)S(1)} %slice_select_fusion), channel_id=1, source_target_pairs={{0,8},{8,0},{1,9},{9,1},{2,10},{10,2},{3,11},{11,3},{4,12},{12,4},... | collective-permute-start | bytes 1572872 | tf_op jit(solution)/shard_map/ppermute | solution.py:122
  64.0 7.1 %collective-permute-start.15 = (f32[128,256]{1,0:T(8,128)}, f32[128,256]{1,0:T(8,128)S(1)}, u32[]{:S(2)}, u32[]{:S(2)}) collective-permute-start(f32[128,256]{1,0:T(8,128)} %slice_select_fusion.1), channel_id=1, source_target_pairs={{0,8},{8,0},{1,9},{9,1},{2,10},{10,2},{3,11},{11,3},{4,12},{12,4},... | collective-permute-start | bytes 393224 | tf_op jit(solution)/shard_map/ppermute | solution.py:122
  65.5 43.2 %all-to-all-start = ((f32[16,32,256]{2,1,0:T(8,128)}), f32[16,32,256]{2,1,0:T(8,128)S(1)}, u32[]{:S(2)}, u32[]{:S(2)}) async-start(f32[16,32,256]{2,1,0:T(8,128)} %bitcast.23), calls=%async_computation | async-start | bytes 1048576 | tf_op jit(solution)/shard_map/all_to_all | solution.py:107
  71.1 4.4 %collective-permute-start.16 = (f32[32,256]{1,0:T(8,128)S(1)}, f32[32,256]{1,0:T(8,128)S(1)}, u32[]{:S(2)}, u32[]{:S(2)}) collective-permute-start(f32[32,256]{1,0:T(8,128)S(1)} %get-tuple-element.11), channel_id=1, source_target_pairs={{0,64},{64,128},{128,192},{192,0},{1,65},{65,129},{129,193},{193,1... | collective-permute-start | bytes 98312 | tf_op jit(solution)/shard_map/ppermute | solution.py:122
  72.5 4.8 %collective-permute-start.18 = (f32[32,256]{1,0:T(8,128)S(1)}, f32[32,256]{1,0:T(8,128)S(1)}, u32[]{:S(2)}, u32[]{:S(2)}) collective-permute-start(f32[32,256]{1,0:T(8,128)S(1)} %get-tuple-element.12), channel_id=1, source_target_pairs={{0,192},{64,0},{128,64},{192,128},{1,193},{65,1},{129,65},{193,129... | collective-permute-start | bytes 98312 | tf_op jit(solution)/shard_map/ppermute | solution.py:122
  73.9 5.7 %collective-permute-start.17 = (f32[32,256]{1,0:T(8,128)S(1)}, f32[32,256]{1,0:T(8,128)S(1)}, u32[]{:S(2)}, u32[]{:S(2)}) collective-permute-start(f32[32,256]{1,0:T(8,128)S(1)} %get-tuple-element.13), channel_id=1, source_target_pairs={{0,128},{64,192},{128,0},{192,64},{1,129},{65,193},{129,1},{193,65... | collective-permute-start | bytes 98312 | tf_op jit(solution)/shard_map/ppermute | solution.py:122
  79.5 5.7 %collective-permute-start.21 = (f32[32,256]{1,0:T(8,128)S(1)}, f32[32,256]{1,0:T(8,128)S(1)}, u32[]{:S(2)}, u32[]{:S(2)}) collective-permute-start(f32[32,256]{1,0:T(8,128)S(1)} %fusion.10), channel_id=1, source_target_pairs={{0,48},{16,0},{32,16},{48,32},{1,49},{17,1},{33,17},{49,33},{2,50}... | collective-permute-start | bytes 98312 | tf_op jit(solution)/shard_map/ppermute | solution.py:122
  84.3 3.7 %collective-permute-start.20 = (f32[32,256]{1,0:T(8,128)S(1)}, f32[32,256]{1,0:T(8,128)S(1)}, u32[]{:S(2)}, u32[]{:S(2)}) collective-permute-start(f32[32,256]{1,0:T(8,128)S(1)} %fusion.10), channel_id=1, source_target_pairs={{0,32},{16,48},{32,0},{48,16},{1,33},{17,49},{33,1},{49,17},{2,34}... | collective-permute-start | bytes 98312 | tf_op jit(solution)/shard_map/ppermute | solution.py:122
  84.3 4.6 %collective-permute-start.19 = (f32[32,256]{1,0:T(8,128)S(1)}, f32[32,256]{1,0:T(8,128)S(1)}, u32[]{:S(2)}, u32[]{:S(2)}) collective-permute-start(f32[32,256]{1,0:T(8,128)S(1)} %fusion.10), channel_id=1, source_target_pairs={{0,16},{16,32},{32,48},{48,0},{1,17},{17,33},{33,49},{49,1},{2,18}... | collective-permute-start | bytes 98312 | tf_op jit(solution)/shard_map/ppermute | solution.py:122
  88.8 6.0 %collective-permute-start.24 = (f32[32,256]{1,0:T(8,128)S(1)}, f32[32,256]{1,0:T(8,128)S(1)}, u32[]{:S(2)}, u32[]{:S(2)}) collective-permute-start(f32[32,256]{1,0:T(8,128)S(1)} %add_add_fusion.refs_0_), channel_id=1, source_target_pairs={{0,192},{64,0},{128,64},{192,128},{1,193},{65,1},{129,65},{193,129... | collective-permute-start | bytes 98312 | tf_op jit(solution)/shard_map/ppermute | solution.py:122
  89.6 5.8 %collective-permute-start.23 = (f32[32,256]{1,0:T(8,128)S(1)}, f32[32,256]{1,0:T(8,128)S(1)}, u32[]{:S(2)}, u32[]{:S(2)}) collective-permute-start(f32[32,256]{1,0:T(8,128)S(1)} %add_add_fusion.refs_0_), channel_id=1, source_target_pairs={{0,128},{64,192},{128,0},{192,64},{1,129},{65,193},{129,1},{193,65... | collective-permute-start | bytes 98312 | tf_op jit(solution)/shard_map/ppermute | solution.py:122
  90.3 9.0 %collective-permute-start.22 = (f32[32,256]{1,0:T(8,128)S(1)}, f32[32,256]{1,0:T(8,128)S(1)}, u32[]{:S(2)}, u32[]{:S(2)}) collective-permute-start(f32[32,256]{1,0:T(8,128)S(1)} %add_add_fusion.refs_0_), channel_id=1, source_target_pairs={{0,64},{64,128},{128,192},{192,0},{1,65},{65,129},{129,193},{193,1... | collective-permute-start | bytes 98312 | tf_op jit(solution)/shard_map/ppermute | solution.py:122
  91.1 8.3 %collective-permute-start.25 = (f32[32,256]{1,0:T(8,128)S(1)}, f32[32,256]{1,0:T(8,128)S(1)}, u32[]{:S(2)}, u32[]{:S(2)}) collective-permute-start(f32[32,256]{1,0:T(8,128)S(1)} %add_add_fusion.refs_0_), channel_id=1, source_target_pairs={{0,8},{8,0},{1,9},{9,1},{2,10},{10,2},{3,11},{11,3},{4,12},{12,4},... | collective-permute-start | bytes 98312 | tf_op jit(solution)/shard_map/ppermute | solution.py:122
  94.8 4.5 %collective-permute-start.28 = (f32[32,256]{1,0:T(8,128)S(1)}, f32[32,256]{1,0:T(8,128)S(1)}, u32[]{:S(2)}, u32[]{:S(2)}) collective-permute-start(f32[32,256]{1,0:T(8,128)S(1)} %collective-permute-done.24.refs_3_), channel_id=1, source_target_pairs={{0,8},{8,0},{1,9},{9,1},{2,10},{10,2},{3,11},{11,3},{4,12},{12,4},... | collective-permute-start | bytes 98312 | tf_op jit(solution)/shard_map/ppermute | solution.py:122
  95.5 4.7 %collective-permute-start.27 = (f32[32,256]{1,0:T(8,128)S(1)}, f32[32,256]{1,0:T(8,128)S(1)}, u32[]{:S(2)}, u32[]{:S(2)}) collective-permute-start(f32[32,256]{1,0:T(8,128)S(1)} %collective-permute-done.23.refs_2_), channel_id=1, source_target_pairs={{0,8},{8,0},{1,9},{9,1},{2,10},{10,2},{3,11},{11,3},{4,12},{12,4},... | collective-permute-start | bytes 98312 | tf_op jit(solution)/shard_map/ppermute | solution.py:122
  99.3 1.2 collective-permute-start.26
  122.1 3.1 %collective-permute-start.29 = (bf16[512,256]{1,0:T(8,128)(2,1)S(1)}, bf16[512,256]{1,0:T(8,128)(2,1)S(1)}, u32[]{:S(2)}, u32[]{:S(2)}) collective-permute-start(bf16[512,256]{1,0:T(8,128)(2,1)S(1)} %bitcast.87), channel_id=1, source_target_pairs={{0,8},{8,0},{1,9},{9,1},{2,10},{10,2},{3,11},{11,3},{4,12},{12,4},... | collective-permute-start | bytes 786440 | tf_op jit(solution)/shard_map/ppermute | solution.py:122
  125.4 31.8 %copy-start.2 = (bf16[1024,256]{1,0:T(8,128)(2,1)}, bf16[1024,256]{1,0:T(8,128)(2,1)S(1)}, u32[]{:S(2)}) copy-start(bf16[1024,256]{1,0:T(8,128)(2,1)S(1)} %maximum_select_fusion) | copy-start | bytes 1572868
  132.1 1.3 collective-permute-start.30
  133.4 2.6 %collective-permute-start.33 = (f32[16,256]{1,0:T(8,128)S(1)}, f32[16,256]{1,0:T(8,128)S(1)}, u32[]{:S(2)}, u32[]{:S(2)}) collective-permute-start(f32[16,256]{1,0:T(8,128)S(1)} %bitcast_add_fusion.3), channel_id=1, source_target_pairs={{0,192},{64,0},{128,64},{192,128},{1,193},{65,1},{129,65},{193,129... | collective-permute-start | bytes 49160 | tf_op jit(solution)/shard_map/ppermute | solution.py:122
  133.9 4.1 %collective-permute-start.32 = (f32[16,256]{1,0:T(8,128)S(1)}, f32[16,256]{1,0:T(8,128)S(1)}, u32[]{:S(2)}, u32[]{:S(2)}) collective-permute-start(f32[16,256]{1,0:T(8,128)S(1)} %bitcast_add_fusion.3), channel_id=1, source_target_pairs={{0,128},{64,192},{128,0},{192,64},{1,129},{65,193},{129,1},{193,65... | collective-permute-start | bytes 49160 | tf_op jit(solution)/shard_map/ppermute | solution.py:122
  134.2 4.1 %collective-permute-start.31 = (f32[16,256]{1,0:T(8,128)S(1)}, f32[16,256]{1,0:T(8,128)S(1)}, u32[]{:S(2)}, u32[]{:S(2)}) collective-permute-start(f32[16,256]{1,0:T(8,128)S(1)} %bitcast_add_fusion.3), channel_id=1, source_target_pairs={{0,64},{64,128},{128,192},{192,0},{1,65},{65,129},{129,193},{193,1... | collective-permute-start | bytes 49160 | tf_op jit(solution)/shard_map/ppermute | solution.py:122

commit v7 on v4

--- a/solution.py
+++ b/solution.py
@@ -117,44 +117,8 @@
     return exchange(jnp.broadcast_to(x[None], (n,) + x.shape), axes).reshape(n * x.shape[0], x.shape[1])
 
 
-def shift(x, axis, d):
-    n = lax.axis_size(axis)
-    return lax.ppermute(x, axis, [(s, (s + d) % n) for s in range(n)])
-
-
-def ring_scatter(x, axis):
-    n = lax.axis_size(axis)
-    me = lax.axis_index(axis)
-    blocks = x.reshape(n, x.shape[0] // n, x.shape[1])
-    take = lambda d: lax.dynamic_index_in_dim(blocks, lax.rem(me + d, n), 0, keepdims=False)
-    arrived = [shift(take(d), axis, d) for d in range(1, n)]
-    return sum(arrived, take(0))
-
-
-def ring_sum(x, axis):
-    return sum([shift(x, axis, d) for d in range(1, lax.axis_size(axis))], x)
-
-
-def ring_gather(x, axis):
-    return [x] + [shift(x, axis, d) for d in range(1, lax.axis_size(axis))]
-
-
 def pair(x, axis, d):
-    return lax.ppermute(x, axis, [(s, s ^ d) for s in range(lax.axis_size(axis))])
-
-
-def quad_gather(x, axis):
-    return [x] + [pair(x, axis, d) for d in (1, 2, 3)]
-
-
-def ordered(parts, me):
-    odd = lax.rem(me, 2) == 1
-    low = [jnp.where(odd, parts[1], parts[0]), jnp.where(odd, parts[0], parts[1])]
-    high = [jnp.where(odd, parts[3], parts[2]), jnp.where(odd, parts[2], parts[3])]
-    up = me >= 2
-    first = [jnp.where(up, h, l) for l, h in zip(low, high)]
-    last = [jnp.where(up, l, h) for l, h in zip(low, high)]
-    return jnp.concatenate(first + last, axis=0)
+    return lax.ppermute(x, axis, [(i, i ^ d) for i in range(lax.axis_size(axis))])
 
 
 def keep(x, bit):
@@ -169,15 +133,24 @@
     )
 
 
-def quad_places():
-    me = lax.axis_index("x")
-    odd = lax.rem(me, 2)
-    return [me, me + 1 - 2 * odd, lax.rem(me + 2, 4), 3 - me]
-
-
-def ring_places():
-    me = lax.axis_index("y")
-    return [lax.rem(me + 4 - d, 4) for d in range(4)]
+def quarter_bits(axis):
+    me = lax.axis_index(axis)
+    high = me // 2
+    low = lax.rem(me, 2)
+    return lax.rem(low + high, 2), high
+
+
+def halve(x, axis, d, bit):
+    mine, other = keep(x, bit)
+    return mine + pair(other, axis, d)
+
+
+def grow(x, axis, d, bit):
+    return join(x, pair(x, axis, d), bit)
+
+
+def whole():
+    return [0]
 
 
 def on_device(tensor, first_factor, third_factor):
@@ -191,45 +164,51 @@
     gram_first = jnp.dot(first_factor.T, first_factor, preferred_element_type=jnp.float32) / window
 
     gram_part = jnp.dot(third_factor.T, third_factor, preferred_element_type=jnp.float32)
-    gram_part = ring_scatter(gram_part, "y")
-    gram_part = ring_sum(gram_part, "zh")
-    parts = ring_gather(gram_part, "y")
-    inverse_second = inverse(parts, ring_places, gram_first, third_total)
+    near, far = quarter_bits("y")
+    gram_part = halve(gram_part, "y", 1, near)
+    gram_part = halve(gram_part, "y", 3, far)
+    gram_part = gram_part + pair(gram_part, "zh", 1)
+    gram_part = grow(gram_part, "y", 3, far)
+    gram_third = grow(gram_part, "y", 1, near)
+    inverse_second = inverse([gram_third], whole, gram_first, third_total)
 
     contracted = jnp.einsum("ijk,kr->ijr", tensor, third_factor, preferred_element_type=jnp.float32)
-    partial_second = jnp.einsum(
-        "ijr,ir->jr", contracted, first_second, precision=HIGHEST
-    )
-    row = scatter_sum(partial_second, NARROW)
-    mttkrp_second = gather(row, NARROW)
-    second_factor = jnp.dot(mttkrp_second, inverse_second, precision=HIGHEST).astype(jnp.bfloat16)
-
+    partial_second = jnp.sum(contracted * first_second[:, None, :], axis=0)
+    row = halve(partial_second, "y", 1, near)
+    row = halve(row, "y", 3, far)
+    row = row + pair(row, "zh", 1)
+    row = jnp.dot(row, inverse_second, precision=HIGHEST).astype(jnp.bfloat16)
+    row = grow(row, "y", 3, far)
+    second_factor = grow(row, "y", 1, near)
+
+    first_third, tensor = lax.optimization_barrier((first_third, tensor))
     gram_local = jnp.dot(second_factor.T, second_factor, preferred_element_type=jnp.float32)
-    mine = scatter_sum(gram_local, WIDE)
-    mine = join(mine, shift(mine, "core", 1), core)
-    parts = quad_gather(mine, "zl")
-    mine = ordered(parts, lax.axis_index("zl"))
-    parts = quad_gather(mine, "x")
-    inverse_third = inverse(parts, quad_places, gram_first, second_total)
+    near, far = quarter_bits("x")
+    mine = halve(gram_local, "core", 1, core)
+    mine = halve(mine, "x", 1, near)
+    mine = halve(mine, "x", 3, far)
+    mine = mine + pair(mine, "zl", 1)
+    mine = mine + pair(mine, "zl", 2)
+    mine = grow(mine, "x", 3, far)
+    mine = grow(mine, "x", 1, near)
+    gram_second = grow(mine, "core", 1, core)
+    inverse_third = inverse([gram_second], whole, gram_first, second_total)
 
     middle = jnp.einsum("ijk,jr->ikr", tensor, second_factor, preferred_element_type=jnp.float32)
-    partial_third = jnp.einsum(
-        "ikr,ir->kr", middle, first_third, precision=HIGHEST
-    )
-    mine, other = keep(partial_third, core)
-    mine = mine + shift(other, "core", 1)
+    partial_third = jnp.sum(middle * first_third[:, None, :], axis=0)
+    mine = halve(partial_third, "core", 1, core)
     mttkrp_third = scatter_sum(mine, CHIP)
     third_solution = jnp.dot(mttkrp_third, inverse_third, precision=HIGHEST)
     mine = gather(third_solution.astype(jnp.bfloat16), CHIP)
-    third_new = join(mine, shift(mine, "core", 1), core)
+    third_new = grow(mine, "core", 1, core)
 
     back = jnp.einsum("ijk,kr->ijr", tensor, third_new, preferred_element_type=jnp.float32)
-    partial_first = jnp.einsum(
-        "ijr,jr->ir", back, second_factor.astype(jnp.float32), precision=HIGHEST
-    )
-    partial_first = partial_first + shift(partial_first, "core", 1)
+    partial_first = jnp.sum(back * second_factor.astype(jnp.float32)[None], axis=1)
+    partial_first = partial_first + pair(partial_first, "core", 1)
+    partial_first = partial_first + pair(partial_first, "x", 1)
+    partial_first = partial_first + pair(partial_first, "x", 3)
     scale = 1.0 / math.sqrt(second_total * third_total)
-    partial_first = (ring_sum(partial_first, "x") * scale).astype(jnp.bfloat16)
+    partial_first = (partial_first * scale).astype(jnp.bfloat16)
     axes = ("zl",) + NARROW
     n = lax.axis_size(axes)
     copies = jnp.broadcast_to(partial_first[None], (n,) + partial_first.shape)

time: 177 us -> 164 us (0.927)
  waiting for transfers between devices: 44.7 us -> 37.3 us
  starting transfers between devices: 57.9 us -> 53.9 us
  matrix products: 21.8 us -> 18.8 us
  blocking collectives: 28.6 us -> 30.9 us
    all_to_all x4 -> x1, starting transfers between devices: 25.6 us -> 5.23 us  [exchange(): return lax.all_to_all(x, axes, 0, 0, tiled=True)]
    ppermute x20 -> x23, starting transfers between devices: 32.3 us -> 48.6 us  [pair(): lax.ppermute(x, axis, [(i, i ^ d) for i in range(lax.axis_size(axis))])]
    all_to_all x4 -> x1, waiting for transfers between devices: 15.6 us -> 0.01 us  [exchange(): return lax.all_to_all(x, axes, 0, 0, tiled=True)]
    ppermute x20 -> x23, waiting for transfers between devices: 29.1 us -> 37.3 us  [pair(): lax.ppermute(x, axis, [(i, i ^ d) for i in range(lax.axis_size(axis))])]
    all_to_all x2, blocking collectives: 28.6 us -> 30.9 us  [exchange(): return lax.all_to_all(x, axes, 0, 0, tiled=True)]
  transfers between devices with their start and end apart: 24 -> 24, of which waited for: 15 -> 17; matrix products, arithmetic and copies ran while one was open for 2% -> 8% of each run, Pallas kernels for 9% -> 10%
where the time goes in v7:
time: 164 us; the launch traced here: 162 us
  starting transfers between devices  53.9 us (33%)
  waiting for transfers between devices  37.3 us (23%)
  blocking collectives  30.9 us (19%)
  matrix products  18.8 us (11%)
  Pallas kernels  16.4 us (10%)
  other arithmetic  2.95 us (2%)
    ppermute x23, starting transfers between devices, pair(): lax.ppermute(x, axis, [(i, i ^ d) for i in range(lax.axis_size(axis))])  48.6 us
    ppermute x23, waiting for transfers between devices, pair(): lax.ppermute(x, axis, [(i, i ^ d) for i in range(lax.axis_size(axis))])  37.3 us
    all_to_all x2, blocking collectives, exchange(): return lax.all_to_all(x, axes, 0, 0, tiled=True)  30.9 us
    pallas_call x2, Pallas kernels, inverse(): pl.pallas_call(functools.partial(inverse_kernel, places, total), out_shap...  16.4 us
    dot_general x1, matrix products, on_device(): jnp.einsum('ijk,kr->ijr', tensor, third_new, preferred_element_type=jnp.f...  5.92 us
    dot_general x1, matrix products, on_device(): jnp.einsum('ijk,jr->ikr', tensor, second_factor, preferred_element_type=j...  5.86 us
    dot_general x1, matrix products, on_device(): jnp.einsum('ijk,kr->ijr', tensor, third_factor, preferred_element_type=jn...  5.74 us
    all_to_all x1, starting transfers between devices, exchange(): return lax.all_to_all(x, axes, 0, 0, tiled=True)  5.23 us
  transfers between devices with their start and end apart: 24, of which 17 were waited for; matrix products, arithmetic and copies ran while one was open for 8% of the time, Pallas kernels for 10%

profile of v7, /device:TPU:1, one launch (start us, length us, event | category | flops | bytes accessed | tf_op | source)
XLA Modules:
  0.0 162.3 jit_solution(13501269479597844472)
XLA Ops:
  0.7 1.0 copy-done
  1.7 0.3 fusion.5
  2.0 2.2 %collective-permute-start.3 = (f32[128,256]{1,0:T(8,128)S(1)}, f32[128,256]{1,0:T(8,128)S(1)}, u32[]{:S(2)}, u32[]{:S(2)}) collective-permute-start(f32[128,256]{1,0:T(8,128)S(1)} %slice_select_fusion.2), channel_id=1, source_target_pairs={{0,1},{1,0},{2,3},{3,2},{4,5},{5,4},{6,7},{7,6},{8,9},{9,8},{10,11... | collective-permute-start | bytes 393224 | tf_op jit(solution)/shard_map/ppermute | solution.py:121
  4.2 0.7 convert_multiply_fusion
  5.0 5.7 %multiply_reduce_fusion.2 = f32[256,256]{1,0:T(8,128)S(1)} fusion(bf16[16,256,1024]{2,1,0:T(8,128)(2,1)} %param.3, f32[16,256]{1,0:T(8,128)S(1)} %convert_multiply_fusion, bf16[1024,256]{1,0:T(8,128)(2,1)S(1)} %copy-done), kind=kOutput, calls=%fused_computation.2 | convolution fusion | flops 2149515264 | bytes 9191424 | tf_op jit(solution)/shard_map/ijk,kr->ijr/dot_general | solution.py:175
  10.9 3.0 %collective-permute-start.4 = (f32[64,256]{1,0:T(8,128)S(1)}, f32[64,256]{1,0:T(8,128)S(1)}, u32[]{:S(2)}, u32[]{:S(2)}) collective-permute-start(f32[64,256]{1,0:T(8,128)S(1)} %slice_select_fusion.5), channel_id=1, source_target_pairs={{0,3},{1,2},{2,1},{3,0},{4,7},{5,6},{6,5},{7,4},{8,11},{9,10},{10,... | collective-permute-start | bytes 196616 | tf_op jit(solution)/shard_map/ppermute | solution.py:121
  14.1 1.4 collective-permute-done.4
  15.5 7.0 %collective-permute-start.5 = (f32[64,256]{1,0:T(8,128)S(1)}, f32[64,256]{1,0:T(8,128)S(1)}, u32[]{:S(2)}, u32[]{:S(2)}) collective-permute-start(f32[64,256]{1,0:T(8,128)S(1)} %select_add_fusion.5), channel_id=1, source_target_pairs={{0,4},{4,0},{1,5},{5,1},{2,6},{6,2},{3,7},{7,3},{8,12},{12,8},{9,1... | collective-permute-start | bytes 196616 | tf_op jit(solution)/shard_map/ppermute | solution.py:121
  22.6 1.7 %collective-permute-done.5 = f32[64,256]{1,0:T(8,128)S(1)} collective-permute-done((f32[64,256]{1,0:T(8,128)S(1)}, f32[64,256]{1,0:T(8,128)S(1)}, u32[]{:S(2)}, u32[]{:S(2)}) %collective-permute-start.5) | collective-permute-done | bytes 65568 | tf_op jit(solution)/shard_map/ppermute | solution.py:121
  24.3 2.8 %collective-permute-start.6 = (f32[64,256]{1,0:T(8,128)S(1)}, f32[64,256]{1,0:T(8,128)S(1)}, u32[]{:S(2)}, u32[]{:S(2)}) collective-permute-start(f32[64,256]{1,0:T(8,128)S(1)} %add.59), channel_id=1, source_target_pairs={{0,3},{1,2},{2,1},{3,0},{4,7},{5,6},{6,5},{7,4},{8,11},{9,10},{10,... | collective-permute-start | bytes 196616 | tf_op jit(solution)/shard_map/ppermute | solution.py:121
  27.1 1.5 collective-permute-done.6
  28.8 2.7 %collective-permute-done.1 = f32[64,256]{1,0:T(8,128)S(1)} collective-permute-done((f32[64,256]{1,0:T(8,128)S(1)}, f32[64,256]{1,0:T(8,128)S(1)}, u32[]{:S(2)}, u32[]{:S(2)}) %collective-permute-start.1) | collective-permute-done | bytes 65568 | tf_op jit(solution)/shard_map/ppermute | solution.py:121
  31.5 5.4 %collective-permute-start.2 = (f32[64,256]{1,0:T(8,128)S(1)}, f32[64,256]{1,0:T(8,128)S(1)}, u32[]{:S(2)}, u32[]{:S(2)}) collective-permute-start(f32[64,256]{1,0:T(8,128)S(1)} %select_add_fusion.6), channel_id=1, source_target_pairs={{0,4},{4,0},{1,5},{5,1},{2,6},{6,2},{3,7},{7,3},{8,12},{12,8},{9,1... | collective-permute-start | bytes 196616 | tf_op jit(solution)/shard_map/ppermute | solution.py:121
  36.9 8.2 %inverse.2 = f32[256,256]{1,0:T(8,128)S(1)} custom-call(f32[256,256]{1,0:T(8,128)S(1)} %maximum_select_fusion.1.refs_0_, f32[256,256]{1,0:T(8,128)S(1)} %convolution_multiply_fusion.refs_1_), custom_call_target="tpu_custom_call" | custom-call | flops 201326592 | bytes 524288 | tf_op jit(solution)/shard_map/inverse/pallas_call | solution.py:94
  45.1 0.2 convolution_convert_fusion
  45.4 0.7 collective-permute-start.8
  46.0 3.4 %collective-permute-done.8 = bf16[64,256]{1,0:T(8,128)(2,1)S(1)} collective-permute-done((bf16[64,256]{1,0:T(8,128)(2,1)S(1)}, bf16[64,256]{1,0:T(8,128)(2,1)S(1)}, u32[]{:S(2)}, u32[]{:S(2)}) %collective-permute-start.8) | collective-permute-done | bytes 32800 | tf_op jit(solution)/shard_map/ppermute | solution.py:121
  49.6 3.1 %collective-permute-done.9 = bf16[128,256]{1,0:T(8,128)(2,1)S(1)} collective-permute-done((bf16[128,256]{1,0:T(8,128)(2,1)S(1)}, bf16[128,256]{1,0:T(8,128)(2,1)S(1)}, u32[]{:S(2)}, u32[]{:S(2)}) %collective-permute-start.9) | collective-permute-done | bytes 65568 | tf_op jit(solution)/shard_map/ppermute | solution.py:121
  52.9 8.1 %collective-permute-start.11 = (f32[128,256]{1,0:T(8,128)S(1)}, f32[128,256]{1,0:T(8,128)S(1)}, u32[]{:S(2)}, u32[]{:S(2)}) collective-permute-start(f32[128,256]{1,0:T(8,128)S(1)} %slice_select_fusion.1), channel_id=1, source_target_pairs={{0,8},{8,0},{1,9},{9,1},{2,10},{10,2},{3,11},{11,3},{4,12},{12,4},... | collective-permute-start | bytes 393224 | tf_op jit(solution)/shard_map/ppermute | solution.py:121
  61.0 5.9 %multiply_reduce_fusion = f32[1024,256]{1,0:T(8,128)S(1)} fusion(bf16[16,256,1024]{2,1,0:T(8,128)(2,1)} %param.3, f32[16,256]{1,0:T(8,128)S(1)} %convert_multiply_fusion, bf16[256,256]{1,0:T(8,128)(2,1)S(1)} %get-tuple-element.8), kind=kOutput, calls=%fused_computation | convolution fusion | flops 2155610112 | bytes 9584640 | tf_op jit(solution)/shard_map/ijk,jr->ikr/dot_general | solution.py:197
  67.1 1.3 collective-permute-start.12
  68.4 1.9 %collective-permute-done.12 = f32[64,256]{1,0:T(8,128)S(1)} collective-permute-done((f32[64,256]{1,0:T(8,128)S(1)}, f32[64,256]{1,0:T(8,128)S(1)}, u32[]{:S(2)}, u32[]{:S(2)}) %collective-permute-start.12) | collective-permute-done | bytes 65568 | tf_op jit(solution)/shard_map/ppermute | solution.py:121
  70.4 0.9 select_add_fusion
  71.3 5.2 %all-to-all-start = ((f32[16,32,256]{2,1,0:T(8,128)}), f32[16,32,256]{2,1,0:T(8,128)S(1)}, u32[]{:S(2)}, u32[]{:S(2)}) async-start(f32[16,32,256]{2,1,0:T(8,128)} %bitcast.2), calls=%async_computation | async-start | bytes 1048576 | tf_op jit(solution)/shard_map/all_to_all | solution.py:107
  76.5 2.7 %collective-permute-start.13 = (f32[32,256]{1,0:T(8,128)S(1)}, f32[32,256]{1,0:T(8,128)S(1)}, u32[]{:S(2)}, u32[]{:S(2)}) collective-permute-start(f32[32,256]{1,0:T(8,128)S(1)} %slice_select_fusion.7), channel_id=1, source_target_pairs={{0,192},{64,128},{128,64},{192,0},{1,193},{65,129},{129,65},{193,1... | collective-permute-start | bytes 98312 | tf_op jit(solution)/shard_map/ppermute | solution.py:121
  79.2 2.2 %collective-permute-done.13 = f32[32,256]{1,0:T(8,128)S(1)} collective-permute-done((f32[32,256]{1,0:T(8,128)S(1)}, f32[32,256]{1,0:T(8,128)S(1)}, u32[]{:S(2)}, u32[]{:S(2)}) %collective-permute-start.13) | collective-permute-done | bytes 32800 | tf_op jit(solution)/shard_map/ppermute | solution.py:121
  81.4 0.7 collective-permute-start.14
  82.1 2.9 %collective-permute-done.14 = f32[32,256]{1,0:T(8,128)S(1)} collective-permute-done((f32[32,256]{1,0:T(8,128)S(1)}, f32[32,256]{1,0:T(8,128)S(1)}, u32[]{:S(2)}, u32[]{:S(2)}) %collective-permute-start.14) | collective-permute-done | bytes 32800 | tf_op jit(solution)/shard_map/ppermute | solution.py:121
  85.1 3.2 %collective-permute-start.15 = (f32[32,256]{1,0:T(8,128)S(1)}, f32[32,256]{1,0:T(8,128)S(1)}, u32[]{:S(2)}, u32[]{:S(2)}) collective-permute-start(f32[32,256]{1,0:T(8,128)S(1)} %add.65), channel_id=1, source_target_pairs={{0,32},{16,48},{32,0},{48,16},{1,33},{17,49},{33,1},{49,17},{2,34}... | collective-permute-start | bytes 98312 | tf_op jit(solution)/shard_map/ppermute | solution.py:121
  88.2 3.0 %collective-permute-done.15 = f32[32,256]{1,0:T(8,128)S(1)} collective-permute-done((f32[32,256]{1,0:T(8,128)S(1)}, f32[32,256]{1,0:T(8,128)S(1)}, u32[]{:S(2)}, u32[]{:S(2)}) %collective-permute-start.15) | collective-permute-done | bytes 32800 | tf_op jit(solution)/shard_map/ppermute | solution.py:121
  91.2 2.4 %collective-permute-start.16 = (f32[32,256]{1,0:T(8,128)S(1)}, f32[32,256]{1,0:T(8,128)S(1)}, u32[]{:S(2)}, u32[]{:S(2)}) collective-permute-start(f32[32,256]{1,0:T(8,128)S(1)} %add.66), channel_id=1, source_target_pairs={{0,192},{64,128},{128,64},{192,0},{1,193},{65,129},{129,65},{193,1... | collective-permute-start | bytes 98312 | tf_op jit(solution)/shard_map/ppermute | solution.py:121
  93.6 1.6 collective-permute-done.16
  95.3 3.1 %collective-permute-done.17 = f32[64,256]{1,0:T(8,128)S(1)} collective-permute-done((f32[64,256]{1,0:T(8,128)S(1)}, f32[64,256]{1,0:T(8,128)S(1)}, u32[]{:S(2)}, u32[]{:S(2)}) %collective-permute-start.17) | collective-permute-done | bytes 65568 | tf_op jit(solution)/shard_map/ppermute | solution.py:121
  98.4 5.8 %collective-permute-start.18 = (f32[128,256]{1,0:T(8,128)S(1)}, f32[128,256]{1,0:T(8,128)S(1)}, u32[]{:S(2)}, u32[]{:S(2)}) collective-permute-start(f32[128,256]{1,0:T(8,128)S(1)} %maximum_select_fusion.5), channel_id=1, source_target_pairs={{0,8},{8,0},{1,9},{9,1},{2,10},{10,2},{3,11},{11,3},{4,12},{12,4},... | collective-permute-start | bytes 393224 | tf_op jit(solution)/shard_map/ppermute | solution.py:121
  104.2 1.0 collective-permute-done.18
  105.2 8.2 %inverse.3 = f32[256,256]{1,0:T(8,128)S(1)} custom-call(f32[256,256]{1,0:T(8,128)S(1)} %maximum_select_fusion.2.refs_0_, f32[256,256]{1,0:T(8,128)S(1)} %convolution_multiply_fusion.refs_1_), custom_call_target="tpu_custom_call" | custom-call | flops 201326592 | bytes 524288 | tf_op jit(solution)/shard_map/inverse/pallas_call | solution.py:94
  113.5 0.2 convolution_convert_fusion.1
  113.8 14.7 %all_to_all.15 = bf16[16,32,256]{2,1,0:T(8,128)(2,1)S(1)} all-to-all(bf16[16,32,256]{2,1,0:T(8,128)(2,1)S(1)} %broadcast_in_dim.4), channel_id=1, replica_groups=mesh['x'=4,'zl'=4,'core'=2,'zh'=2,'y'=4] {'x','zl'}, dimensions={0} | all-to-all | bytes 524288 | tf_op jit(solution)/shard_map/all_to_all | solution.py:107
  128.5 1.9 %collective-permute-start.19 = (bf16[512,256]{1,0:T(8,128)(2,1)S(1)}, bf16[512,256]{1,0:T(8,128)(2,1)S(1)}, u32[]{:S(2)}, u32[]{:S(2)}) collective-permute-start(bf16[512,256]{1,0:T(8,128)(2,1)S(1)} %bitcast.23), channel_id=1, source_target_pairs={{0,8},{8,0},{1,9},{9,1},{2,10},{10,2},{3,11},{11,3},{4,12},{12,4},... | collective-permute-start | bytes 786440 | tf_op jit(solution)/shard_map/ppermute | solution.py:121
  130.4 1.2 collective-permute-done.19
  131.8 5.9 %multiply_reduce_fusion.1 = f32[16,256]{1,0:T(8,128)S(1)} fusion(bf16[16,256,1024]{2,1,0:T(8,128)(2,1)} %param.3, f32[256,256]{1,0:T(8,128)S(1)} %get-tuple-element.7, bf16[1024,256]{1,0:T(8,128)(2,1)S(1)} %maximum_select_fusion), kind=kOutput, calls=%fused_computation.1 | convolution fusion | flops 2149576704 | bytes 9191424 | tf_op jit(solution)/shard_map/ijk,kr->ijr/dot_general | solution.py:205
  137.7 0.5 collective-permute-start.20
  138.2 0.8 collective-permute-done.20
  139.0 2.6 %collective-permute-done.21 = f32[16,256]{1,0:T(8,128)S(1)} collective-permute-done((f32[16,256]{1,0:T(8,128)S(1)}, f32[16,256]{1,0:T(8,128)S(1)}, u32[]{:S(2)}, u32[]{:S(2)}) %collective-permute-start.21) | collective-permute-done | bytes 16416 | tf_op jit(solution)/shard_map/ppermute | solution.py:121
  141.6 0.6 collective-permute-start.22
  142.2 3.2 %collective-permute-done.22 = f32[16,256]{1,0:T(8,128)S(1)} collective-permute-done((f32[16,256]{1,0:T(8,128)S(1)}, f32[16,256]{1,0:T(8,128)S(1)}, u32[]{:S(2)}, u32[]{:S(2)}) %collective-permute-start.22) | collective-permute-done | bytes 16416 | tf_op jit(solution)/shard_map/ppermute | solution.py:121
  145.5 16.2 %all_to_all.16 = bf16[32,16,256]{2,1,0:T(8,128)(2,1)S(1)} all-to-all(bf16[32,16,256]{2,1,0:T(8,128)(2,1)S(1)} %broadcast_in_dim.5), channel_id=1, replica_groups=mesh['x'=4,'zl'=4,'core'=2,'zh'=2,'y'=4] {'zl','zh','y'}, dimensions={0} | all-to-all | bytes 524288 | tf_op jit(solution)/shard_map/all_to_all | solution.py:107
  161.7 0.7 convert_reduce_fusion
  (55 shorter events, 1.8 us)
Async XLA Ops:
  0.6 1.0 copy-start
  2.0 8.8 %collective-permute-start.3 = (f32[128,256]{1,0:T(8,128)S(1)}, f32[128,256]{1,0:T(8,128)S(1)}, u32[]{:S(2)}, u32[]{:S(2)}) collective-permute-start(f32[128,256]{1,0:T(8,128)S(1)} %slice_select_fusion.2), channel_id=1, source_target_pairs={{0,1},{1,0},{2,3},{3,2},{4,5},{5,4},{6,7},{7,6},{8,9},{9,8},{10,11... | collective-permute-start | bytes 393224 | tf_op jit(solution)/shard_map/ppermute | solution.py:121
  4.9 8.9 %copy-start.3 = (bf16[16,256]{1,0:T(8,128)(2,1)S(1)}, bf16[16,256]{1,0:T(8,128)(2,1)}, u32[]{:S(2)}) copy-start(bf16[16,256]{1,0:T(8,128)(2,1)} %param.4) | copy-start | bytes 24580
  10.7 11.8 %collective-permute-start = (f32[128,256]{1,0:T(8,128)S(1)}, f32[128,256]{1,0:T(8,128)S(1)}, u32[]{:S(2)}, u32[]{:S(2)}) collective-permute-start(f32[128,256]{1,0:T(8,128)S(1)} %slice_select_fusion.3), channel_id=1, source_target_pairs={{0,1},{1,0},{2,3},{3,2},{4,5},{5,4},{6,7},{7,6},{8,9},{9,8},{10,11... | collective-permute-start | bytes 393224 | tf_op jit(solution)/shard_map/ppermute | solution.py:121
  10.9 4.6 %collective-permute-start.4 = (f32[64,256]{1,0:T(8,128)S(1)}, f32[64,256]{1,0:T(8,128)S(1)}, u32[]{:S(2)}, u32[]{:S(2)}) collective-permute-start(f32[64,256]{1,0:T(8,128)S(1)} %slice_select_fusion.5), channel_id=1, source_target_pairs={{0,3},{1,2},{2,1},{3,0},{4,7},{5,6},{6,5},{7,4},{8,11},{9,10},{10,... | collective-permute-start | bytes 196616 | tf_op jit(solution)/shard_map/ppermute | solution.py:121
  15.5 8.7 %collective-permute-start.5 = (f32[64,256]{1,0:T(8,128)S(1)}, f32[64,256]{1,0:T(8,128)S(1)}, u32[]{:S(2)}, u32[]{:S(2)}) collective-permute-start(f32[64,256]{1,0:T(8,128)S(1)} %select_add_fusion.5), channel_id=1, source_target_pairs={{0,4},{4,0},{1,5},{5,1},{2,6},{6,2},{3,7},{7,3},{8,12},{12,8},{9,1... | collective-permute-start | bytes 196616 | tf_op jit(solution)/shard_map/ppermute | solution.py:121
  24.3 4.4 %collective-permute-start.6 = (f32[64,256]{1,0:T(8,128)S(1)}, f32[64,256]{1,0:T(8,128)S(1)}, u32[]{:S(2)}, u32[]{:S(2)}) collective-permute-start(f32[64,256]{1,0:T(8,128)S(1)} %add.59), channel_id=1, source_target_pairs={{0,3},{1,2},{2,1},{3,0},{4,7},{5,6},{6,5},{7,4},{8,11},{9,10},{10,... | collective-permute-start | bytes 196616 | tf_op jit(solution)/shard_map/ppermute | solution.py:121
  27.0 4.4 %collective-permute-start.1 = (f32[64,256]{1,0:T(8,128)S(1)}, f32[64,256]{1,0:T(8,128)S(1)}, u32[]{:S(2)}, u32[]{:S(2)}) collective-permute-start(f32[64,256]{1,0:T(8,128)S(1)} %slice_select_fusion.6), channel_id=1, source_target_pairs={{0,3},{1,2},{2,1},{3,0},{4,7},{5,6},{6,5},{7,4},{8,11},{9,10},{10,... | collective-permute-start | bytes 196616 | tf_op jit(solution)/shard_map/ppermute | solution.py:121
  28.7 8.2 %collective-permute-start.7 = (f32[128,256]{1,0:T(8,128)S(1)}, f32[128,256]{1,0:T(8,128)S(1)}, u32[]{:S(2)}, u32[]{:S(2)}) collective-permute-start(f32[128,256]{1,0:T(8,128)S(1)} %maximum_select_fusion.3), channel_id=1, source_target_pairs={{0,1},{1,0},{2,3},{3,2},{4,5},{5,4},{6,7},{7,6},{8,9},{9,8},{10,11... | collective-permute-start | bytes 393224 | tf_op jit(solution)/shard_map/ppermute | solution.py:121
  31.5 13.6 %collective-permute-start.2 = (f32[64,256]{1,0:T(8,128)S(1)}, f32[64,256]{1,0:T(8,128)S(1)}, u32[]{:S(2)}, u32[]{:S(2)}) collective-permute-start(f32[64,256]{1,0:T(8,128)S(1)} %select_add_fusion.6), channel_id=1, source_target_pairs={{0,4},{4,0},{1,5},{5,1},{2,6},{6,2},{3,7},{7,3},{8,12},{12,8},{9,1... | collective-permute-start | bytes 196616 | tf_op jit(solution)/shard_map/ppermute | solution.py:121
  45.4 4.1 %collective-permute-start.8 = (bf16[64,256]{1,0:T(8,128)(2,1)S(1)}, bf16[64,256]{1,0:T(8,128)(2,1)S(1)}, u32[]{:S(2)}, u32[]{:S(2)}) collective-permute-start(bf16[64,256]{1,0:T(8,128)(2,1)S(1)} %convolution_convert_fusion), channel_id=1, source_target_pairs={{0,3},{1,2},{2,1},{3,0},{4,7},{5,6},{6,5},{7,4},{8,11},{9,10},{10,... | collective-permute-start | bytes 98312 | tf_op jit(solution)/shard_map/ppermute | solution.py:121
  49.4 3.2 %collective-permute-start.9 = (bf16[128,256]{1,0:T(8,128)(2,1)S(1)}, bf16[128,256]{1,0:T(8,128)(2,1)S(1)}, u32[]{:S(2)}, u32[]{:S(2)}) collective-permute-start(bf16[128,256]{1,0:T(8,128)(2,1)S(1)} %maximum_select_fusion.6), channel_id=1, source_target_pairs={{0,1},{1,0},{2,3},{3,2},{4,5},{5,4},{6,7},{7,6},{8,9},{9,8},{10,11... | collective-permute-start | bytes 196616 | tf_op jit(solution)/shard_map/ppermute | solution.py:121
  52.7 14.2 %copy-start.1 = (bf16[256,256]{1,0:T(8,128)(2,1)}, bf16[256,256]{1,0:T(8,128)(2,1)S(1)}, u32[]{:S(2)}) copy-start(bf16[256,256]{1,0:T(8,128)(2,1)S(1)} %get-tuple-element.8) | copy-start | bytes 393220
  52.9 14.1 %collective-permute-start.11 = (f32[128,256]{1,0:T(8,128)S(1)}, f32[128,256]{1,0:T(8,128)S(1)}, u32[]{:S(2)}, u32[]{:S(2)}) collective-permute-start(f32[128,256]{1,0:T(8,128)S(1)} %slice_select_fusion.1), channel_id=1, source_target_pairs={{0,8},{8,0},{1,9},{9,1},{2,10},{10,2},{3,11},{11,3},{4,12},{12,4},... | collective-permute-start | bytes 393224 | tf_op jit(solution)/shard_map/ppermute | solution.py:121
  67.0 3.4 %collective-permute-start.10 = (f32[512,256]{1,0:T(8,128)S(1)}, f32[512,256]{1,0:T(8,128)S(1)}, u32[]{:S(2)}, u32[]{:S(2)}) collective-permute-start(f32[512,256]{1,0:T(8,128)S(1)} %slice_select_fusion), channel_id=1, source_target_pairs={{0,8},{8,0},{1,9},{9,1},{2,10},{10,2},{3,11},{11,3},{4,12},{12,4},... | collective-permute-start | bytes 1572872 | tf_op jit(solution)/shard_map/ppermute | solution.py:121
  67.1 3.2 %collective-permute-start.12 = (f32[64,256]{1,0:T(8,128)S(1)}, f32[64,256]{1,0:T(8,128)S(1)}, u32[]{:S(2)}, u32[]{:S(2)}) collective-permute-start(f32[64,256]{1,0:T(8,128)S(1)} %slice_select_fusion.4), channel_id=1, source_target_pairs={{0,64},{64,0},{128,192},{192,128},{1,65},{65,1},{129,193},{193,129... | collective-permute-start | bytes 196616 | tf_op jit(solution)/shard_map/ppermute | solution.py:121
  71.3 42.2 %all-to-all-start = ((f32[16,32,256]{2,1,0:T(8,128)}), f32[16,32,256]{2,1,0:T(8,128)S(1)}, u32[]{:S(2)}, u32[]{:S(2)}) async-start(f32[16,32,256]{2,1,0:T(8,128)} %bitcast.2), calls=%async_computation | async-start | bytes 1048576 | tf_op jit(solution)/shard_map/all_to_all | solution.py:107
  76.5 4.9 %collective-permute-start.13 = (f32[32,256]{1,0:T(8,128)S(1)}, f32[32,256]{1,0:T(8,128)S(1)}, u32[]{:S(2)}, u32[]{:S(2)}) collective-permute-start(f32[32,256]{1,0:T(8,128)S(1)} %slice_select_fusion.7), channel_id=1, source_target_pairs={{0,192},{64,128},{128,64},{192,0},{1,193},{65,129},{129,65},{193,1... | collective-permute-start | bytes 98312 | tf_op jit(solution)/shard_map/ppermute | solution.py:121
  81.4 3.6 %collective-permute-start.14 = (f32[32,256]{1,0:T(8,128)S(1)}, f32[32,256]{1,0:T(8,128)S(1)}, u32[]{:S(2)}, u32[]{:S(2)}) collective-permute-start(f32[32,256]{1,0:T(8,128)S(1)} %select_add_fusion.7), channel_id=1, source_target_pairs={{0,16},{16,0},{32,48},{48,32},{1,17},{17,1},{33,49},{49,33},{2,18}... | collective-permute-start | bytes 98312 | tf_op jit(solution)/shard_map/ppermute | solution.py:121
  85.1 6.1 %collective-permute-start.15 = (f32[32,256]{1,0:T(8,128)S(1)}, f32[32,256]{1,0:T(8,128)S(1)}, u32[]{:S(2)}, u32[]{:S(2)}) collective-permute-start(f32[32,256]{1,0:T(8,128)S(1)} %add.65), channel_id=1, source_target_pairs={{0,32},{16,48},{32,0},{48,16},{1,33},{17,49},{33,1},{49,17},{2,34}... | collective-permute-start | bytes 98312 | tf_op jit(solution)/shard_map/ppermute | solution.py:121
  91.2 4.0 %collective-permute-start.16 = (f32[32,256]{1,0:T(8,128)S(1)}, f32[32,256]{1,0:T(8,128)S(1)}, u32[]{:S(2)}, u32[]{:S(2)}) collective-permute-start(f32[32,256]{1,0:T(8,128)S(1)} %add.66), channel_id=1, source_target_pairs={{0,192},{64,128},{128,64},{192,0},{1,193},{65,129},{129,65},{193,1... | collective-permute-start | bytes 98312 | tf_op jit(solution)/shard_map/ppermute | solution.py:121
  95.2 3.2 %collective-permute-start.17 = (f32[64,256]{1,0:T(8,128)S(1)}, f32[64,256]{1,0:T(8,128)S(1)}, u32[]{:S(2)}, u32[]{:S(2)}) collective-permute-start(f32[64,256]{1,0:T(8,128)S(1)} %maximum_select_fusion.7), channel_id=1, source_target_pairs={{0,64},{64,0},{128,192},{192,128},{1,65},{65,1},{129,193},{193,129... | collective-permute-start | bytes 196616 | tf_op jit(solution)/shard_map/ppermute | solution.py:121
  98.4 6.8 %collective-permute-start.18 = (f32[128,256]{1,0:T(8,128)S(1)}, f32[128,256]{1,0:T(8,128)S(1)}, u32[]{:S(2)}, u32[]{:S(2)}) collective-permute-start(f32[128,256]{1,0:T(8,128)S(1)} %maximum_select_fusion.5), channel_id=1, source_target_pairs={{0,8},{8,0},{1,9},{9,1},{2,10},{10,2},{3,11},{11,3},{4,12},{12,4},... | collective-permute-start | bytes 393224 | tf_op jit(solution)/shard_map/ppermute | solution.py:121
  128.5 3.1 %collective-permute-start.19 = (bf16[512,256]{1,0:T(8,128)(2,1)S(1)}, bf16[512,256]{1,0:T(8,128)(2,1)S(1)}, u32[]{:S(2)}, u32[]{:S(2)}) collective-permute-start(bf16[512,256]{1,0:T(8,128)(2,1)S(1)} %bitcast.23), channel_id=1, source_target_pairs={{0,8},{8,0},{1,9},{9,1},{2,10},{10,2},{3,11},{11,3},{4,12},{12,4},... | collective-permute-start | bytes 786440 | tf_op jit(solution)/shard_map/ppermute | solution.py:121
  131.8 5.9 %copy-start.2 = (bf16[1024,256]{1,0:T(8,128)(2,1)}, bf16[1024,256]{1,0:T(8,128)(2,1)S(1)}, u32[]{:S(2)}) copy-start(bf16[1024,256]{1,0:T(8,128)(2,1)S(1)} %maximum_select_fusion) | copy-start | bytes 1572868
  137.7 1.3 collective-permute-start.20
  139.0 2.6 %collective-permute-start.21 = (f32[16,256]{1,0:T(8,128)S(1)}, f32[16,256]{1,0:T(8,128)S(1)}, u32[]{:S(2)}, u32[]{:S(2)}) collective-permute-start(f32[16,256]{1,0:T(8,128)S(1)} %add.67), channel_id=1, source_target_pairs={{0,64},{64,0},{128,192},{192,128},{1,65},{65,1},{129,193},{193,129... | collective-permute-start | bytes 49160 | tf_op jit(solution)/shard_map/ppermute | solution.py:121
  141.6 3.8 %collective-permute-start.22 = (f32[16,256]{1,0:T(8,128)S(1)}, f32[16,256]{1,0:T(8,128)S(1)}, u32[]{:S(2)}, u32[]{:S(2)}) collective-permute-start(f32[16,256]{1,0:T(8,128)S(1)} %add.68), channel_id=1, source_target_pairs={{0,192},{64,128},{128,64},{192,0},{1,193},{65,129},{129,65},{193,1... | collective-permute-start | bytes 49160 | tf_op jit(solution)/shard_map/ppermute | solution.py:121

commit v8 on v6

--- a/solution.py
+++ b/solution.py
@@ -40,13 +40,14 @@
 def inverse_kernel(places, total, *refs):
     part_refs, (f_ref, x_ref, m_ref, w_ref) = refs[:-4], refs[-4:]
     n = f_ref.shape[0]
-    depth = part_refs[0].shape[0]
-    for place, part_ref in zip(places(), part_refs):
+    blocks = [(ref, t, len(group), place) for ref, group in zip(part_refs, places()) for t, place in enumerate(group)]
+    for part_ref, t, count, place in blocks:
+        depth = part_ref.shape[0] // count
         base = pl.multiple_of(place * depth, depth)
         here = (depth, n)
         diagonal = lax.broadcasted_iota(jnp.int32, here, 0) + base == lax.broadcasted_iota(jnp.int32, here, 1)
         m_ref[pl.ds(base, depth), :] = f_ref[pl.ds(base, depth), :] * (
-            part_ref[...] * (1.0 / total)
+            part_ref[t * depth:(t + 1) * depth, :] * (1.0 / total)
         ) + jnp.where(diagonal, ridge, 0.0)
     row = lax.broadcasted_iota(jnp.int32, (B, n), 0)
     lane = lax.broadcasted_iota(jnp.int32, (B, n), 1)
@@ -171,14 +172,13 @@
 
 def narrow_places():
     me = lax.axis_index("y")
-    return [lax.rem(me + 4 - d, 4) for d in range(4)]
+    return [(lax.rem(me + 4 - d, 4),) for d in range(4)]
 
 
 def wide_places():
     me = lax.axis_index("x")
-    core = lax.axis_index("core")
     ring = [lax.rem(me + 4 - d, 4) for d in range(4)]
-    return [core * 4 + r for r in ring] + [(1 - core) * 4 + r for r in ring]
+    return [(r, r + 4) for r in ring]
 
 
 def on_device(tensor, first_factor, third_factor):
@@ -198,27 +198,24 @@
     inverse_second = inverse(parts, narrow_places, gram_first, third_total)
 
     contracted = jnp.einsum("ijk,kr->ijr", tensor, third_factor, preferred_element_type=jnp.float32)
-    partial_second = jnp.einsum(
-        "ijr,ir->jr", contracted, first_second, precision=HIGHEST
-    )
+    partial_second = jnp.sum(contracted * first_second[:, None, :], axis=0)
     row = ring_scatter(partial_second, "y")
     row = ring_sum(row, "zh")
     row = jnp.dot(row, inverse_second, precision=HIGHEST).astype(jnp.bfloat16)
     second_factor = ordered(quad_gather(row, "y"), lax.axis_index("y"))
 
+    first_third, tensor = lax.optimization_barrier((first_third, tensor))
     gram_local = jnp.dot(second_factor.T, second_factor, preferred_element_type=jnp.float32)
     mine, other = keep(gram_local, core)
     mine = mine + shift(other, "core", 1)
     mine = ring_scatter(mine, "x")
     mine = ring_sum(mine, "zl")
+    mine = join(mine, shift(mine, "core", 1), core)
     parts = ring_gather(mine, "x")
-    parts = parts + [shift(part, "core", 1) for part in parts]
     inverse_third = inverse(parts, wide_places, gram_first, second_total)
 
     middle = jnp.einsum("ijk,jr->ikr", tensor, second_factor, preferred_element_type=jnp.float32)
-    partial_third = jnp.einsum(
-        "ikr,ir->kr", middle, first_third, precision=HIGHEST
-    )
+    partial_third = jnp.sum(middle * first_third[:, None, :], axis=0)
     mine, other = keep(partial_third, core)
     mine = mine + shift(other, "core", 1)
     mttkrp_third = scatter_sum(mine, CHIP)
@@ -227,9 +224,7 @@
     third_new = join(mine, shift(mine, "core", 1), core)
 
     back = jnp.einsum("ijk,kr->ijr", tensor, third_new, preferred_element_type=jnp.float32)
-    partial_first = jnp.einsum(
-        "ijr,jr->ir", back, second_factor.astype(jnp.float32), precision=HIGHEST
-    )
+    partial_first = jnp.sum(back * second_factor.astype(jnp.float32)[None], axis=1)
     partial_first = partial_first + shift(partial_first, "core", 1)
     scale = 1.0 / math.sqrt(second_total * third_total)
     partial_first = (ring_sum(partial_first, "x") * scale).astype(jnp.bfloat16)

time: 159 us -> 157 us (0.987)
  waiting for transfers between devices: 22.3 us -> 27.2 us
  starting transfers between devices: 61.1 us -> 57.5 us
  blocking collectives: 31.2 us -> 29.4 us
    ppermute x31 -> x28, waiting for transfers between devices: 19.7 us -> 24.7 us  [shift(): return lax.ppermute(x, axis, [(s, (s + d) % n) for s in range(n)])]
    ppermute x31 -> x28, starting transfers between devices: 51.7 us -> 48 us  [shift(): return lax.ppermute(x, axis, [(s, (s + d) % n) for s in range(n)])]
    all_to_all x2, blocking collectives: 31.2 us -> 29.4 us  [exchange(): return lax.all_to_all(x, axes, 0, 0, tiled=True)]
  transfers between devices with their start and end apart: 35 -> 32, of which waited for: 18 -> 20; matrix products, arithmetic and copies ran while one was open for 6% -> 6% of each run, Pallas kernels for 10% -> 11%
where the time goes in v8:
time: 157 us; the launch traced here: 155 us
  starting transfers between devices  57.5 us (37%)
  blocking collectives  29.4 us (19%)
  waiting for transfers between devices  27.2 us (17%)
  matrix products  18.8 us (12%)
  Pallas kernels  16.4 us (10%)
  other arithmetic  3.41 us (2%)
    ppermute x28, starting transfers between devices, shift(): return lax.ppermute(x, axis, [(s, (s + d) % n) for s in range(n)])  48 us
    all_to_all x2, blocking collectives, exchange(): return lax.all_to_all(x, axes, 0, 0, tiled=True)  29.4 us
    ppermute x28, waiting for transfers between devices, shift(): return lax.ppermute(x, axis, [(s, (s + d) % n) for s in range(n)])  24.7 us
    pallas_call x2, Pallas kernels, inverse(): pl.pallas_call(functools.partial(inverse_kernel, places, total), out_shap...  16.4 us
    dot_general x1, matrix products, on_device(): jnp.einsum('ijk,kr->ijr', tensor, third_new, preferred_element_type=jnp.f...  5.93 us
    dot_general x1, matrix products, on_device(): jnp.einsum('ijk,jr->ikr', tensor, second_factor, preferred_element_type=j...  5.87 us
    dot_general x1, matrix products, on_device(): jnp.einsum('ijk,kr->ijr', tensor, third_factor, preferred_element_type=jn...  5.75 us
    all_to_all x1, starting transfers between devices, exchange(): return lax.all_to_all(x, axes, 0, 0, tiled=True)  5.48 us
  transfers between devices with their start and end apart: 32, of which 20 were waited for; matrix products, arithmetic and copies ran while one was open for 6% of the time, Pallas kernels for 11%

profile of v8, /device:TPU:1, one launch (start us, length us, event | category | flops | bytes accessed | tf_op | source)
XLA Modules:
  0.0 154.8 jit_solution(1693476928458734603)
XLA Ops:
  0.7 1.0 copy-done
  2.1 2.2 %collective-permute-start.4 = (f32[64,256]{1,0:T(8,128)S(1)}, f32[64,256]{1,0:T(8,128)S(1)}, u32[]{:S(2)}, u32[]{:S(2)}) collective-permute-start(f32[64,256]{1,0:T(8,128)S(1)} %get-tuple-element.12), channel_id=1, source_target_pairs={{0,1},{1,2},{2,3},{3,0},{4,5},{5,6},{6,7},{7,4},{8,9},{9,10},{10,1... | collective-permute-start | bytes 196616 | tf_op jit(solution)/shard_map/ppermute | solution.py:123
  4.3 1.5 collective-permute-start.6
  5.8 1.6 %collective-permute-start.5 = (f32[64,256]{1,0:T(8,128)S(1)}, f32[64,256]{1,0:T(8,128)S(1)}, u32[]{:S(2)}, u32[]{:S(2)}) collective-permute-start(f32[64,256]{1,0:T(8,128)S(1)} %get-tuple-element.14), channel_id=1, source_target_pairs={{0,2},{1,3},{2,0},{3,1},{4,6},{5,7},{6,4},{7,5},{8,10},{9,11},{10,... | collective-permute-start | bytes 196616 | tf_op jit(solution)/shard_map/ppermute | solution.py:123
  7.3 0.7 convert_multiply_fusion
  8.0 5.7 %multiply_reduce_fusion.2 = f32[256,256]{1,0:T(8,128)S(1)} fusion(bf16[16,256,1024]{2,1,0:T(8,128)(2,1)} %param.3, f32[16,256]{1,0:T(8,128)S(1)} %convert_multiply_fusion, bf16[1024,256]{1,0:T(8,128)(2,1)S(1)} %copy-done), kind=kOutput, calls=%fused_computation.2 | convolution fusion | flops 2149515264 | bytes 9191424 | tf_op jit(solution)/shard_map/ijk,kr->ijr/dot_general | solution.py:200
  14.3 2.3 %collective-permute-start.2 = (f32[64,256]{1,0:T(8,128)S(1)}, f32[64,256]{1,0:T(8,128)S(1)}, u32[]{:S(2)}, u32[]{:S(2)}) collective-permute-start(f32[64,256]{1,0:T(8,128)S(1)} %get-tuple-element.10), channel_id=1, source_target_pairs={{0,3},{1,0},{2,1},{3,2},{4,7},{5,4},{6,5},{7,6},{8,11},{9,8},{10,9... | collective-permute-start | bytes 196616 | tf_op jit(solution)/shard_map/ppermute | solution.py:123
  16.8 7.0 %collective-permute-start.7 = (f32[64,256]{1,0:T(8,128)S(1)}, f32[64,256]{1,0:T(8,128)S(1)}, u32[]{:S(2)}, u32[]{:S(2)}) collective-permute-start(f32[64,256]{1,0:T(8,128)S(1)} %fusion.4), channel_id=1, source_target_pairs={{0,4},{4,0},{1,5},{5,1},{2,6},{6,2},{3,7},{7,3},{8,12},{12,8},{9,1... | collective-permute-start | bytes 196616 | tf_op jit(solution)/shard_map/ppermute | solution.py:123
  23.9 4.4 %collective-permute-start.3 = (f32[64,256]{1,0:T(8,128)S(1)}, f32[64,256]{1,0:T(8,128)S(1)}, u32[]{:S(2)}, u32[]{:S(2)}) collective-permute-start(f32[64,256]{1,0:T(8,128)S(1)} %fusion.6), channel_id=1, source_target_pairs={{0,4},{4,0},{1,5},{5,1},{2,6},{6,2},{3,7},{7,3},{8,12},{12,8},{9,1... | collective-permute-start | bytes 196616 | tf_op jit(solution)/shard_map/ppermute | solution.py:123
  28.7 0.9 collective-permute-start.9
  30.0 1.4 collective-permute-done.10.refs_3_
  31.4 2.2 %collective-permute-done.9.refs_2_ = f32[64,256]{1,0:T(8,128)S(1)} collective-permute-done((f32[64,256]{1,0:T(8,128)S(1)}, f32[64,256]{1,0:T(8,128)S(1)}, u32[]{:S(2)}, u32[]{:S(2)}) %collective-permute-start.9) | collective-permute-done | bytes 65568 | tf_op jit(solution)/shard_map/ppermute | solution.py:123
  33.6 0.7 collective-permute-done.8.refs_1_
  34.3 8.2 %inverse.2 = f32[256,256]{1,0:T(8,128)S(1)} custom-call(f32[64,256]{1,0:T(8,128)S(1)} %add.125.refs_0_, f32[64,256]{1,0:T(8,128)S(1)} %collective-permute-done.8.refs_1_, f32[64,256]{1,0:T(8,128)S(1)} %collective-permute-done.9.refs_2_, f32[64,256]{1,0:T(8,128)S(1)} %collective-permute-done.10.refs_3_, f32[256,256]{1,0:T(8,128)S(1)} %convolution_multiply_fusion.refs_4_), custom_call_target="tpu_custom_call" | custom-call | flops 201326592 | bytes 524288 | tf_op jit(solution)/shard_map/inverse/pallas_call | solution.py:95
  43.2 2.1 %collective-permute-start.12 = (bf16[64,256]{1,0:T(8,128)(2,1)S(1)}, bf16[64,256]{1,0:T(8,128)(2,1)S(1)}, u32[]{:S(2)}, u32[]{:S(2)}) collective-permute-start(bf16[64,256]{1,0:T(8,128)(2,1)S(1)} %convolution_convert_fusion), channel_id=1, source_target_pairs={{0,2},{1,3},{2,0},{3,1},{4,6},{5,7},{6,4},{7,5},{8,10},{9,11},{10,... | collective-permute-start | bytes 98312 | tf_op jit(solution)/shard_map/ppermute | solution.py:144
  45.4 1.4 collective-permute-start.11
  46.8 0.7 collective-permute-done.12
  47.5 1.8 %collective-permute-done.11 = bf16[64,256]{1,0:T(8,128)(2,1)S(1)} collective-permute-done((bf16[64,256]{1,0:T(8,128)(2,1)S(1)}, bf16[64,256]{1,0:T(8,128)(2,1)S(1)}, u32[]{:S(2)}, u32[]{:S(2)}) %collective-permute-start.11) | collective-permute-done | bytes 32800 | tf_op jit(solution)/shard_map/ppermute | solution.py:144
  49.4 5.9 %multiply_reduce_fusion = f32[1024,256]{1,0:T(8,128)S(1)} fusion(bf16[16,256,1024]{2,1,0:T(8,128)(2,1)} %param.3, f32[16,256]{1,0:T(8,128)S(1)} %convert_multiply_fusion, bf16[256,256]{1,0:T(8,128)(2,1)S(1)} %get-tuple-element.8), kind=kOutput, calls=%fused_computation | convolution fusion | flops 2155610112 | bytes 9584640 | tf_op jit(solution)/shard_map/ijk,jr->ikr/dot_general | solution.py:217
  55.4 6.7 %collective-permute-start.14 = (f32[512,256]{1,0:T(8,128)S(1)}, f32[512,256]{1,0:T(8,128)S(1)}, u32[]{:S(2)}, u32[]{:S(2)}) collective-permute-start(f32[512,256]{1,0:T(8,128)S(1)} %slice_select_fusion), channel_id=1, source_target_pairs={{0,8},{8,0},{1,9},{9,1},{2,10},{10,2},{3,11},{11,3},{4,12},{12,4},... | collective-permute-start | bytes 1572872 | tf_op jit(solution)/shard_map/ppermute | solution.py:123
  62.3 0.7 slice_select_fusion.1
  63.6 0.9 select_add_fusion
  64.5 5.5 %all-to-all-start = ((f32[16,32,256]{2,1,0:T(8,128)}), f32[16,32,256]{2,1,0:T(8,128)S(1)}, u32[]{:S(2)}, u32[]{:S(2)}) async-start(f32[16,32,256]{2,1,0:T(8,128)} %bitcast.12), calls=%async_computation | async-start | bytes 1048576 | tf_op jit(solution)/shard_map/all_to_all | solution.py:108
  70.1 1.4 collective-permute-start.16
  71.5 1.3 collective-permute-start.18
  72.8 1.7 %collective-permute-start.17 = (f32[32,256]{1,0:T(8,128)S(1)}, f32[32,256]{1,0:T(8,128)S(1)}, u32[]{:S(2)}, u32[]{:S(2)}) collective-permute-start(f32[32,256]{1,0:T(8,128)S(1)} %get-tuple-element.17), channel_id=1, source_target_pairs={{0,128},{64,192},{128,0},{192,64},{1,129},{65,193},{129,1},{193,65... | collective-permute-start | bytes 98312 | tf_op jit(solution)/shard_map/ppermute | solution.py:123
  74.5 1.8 %collective-permute-done.18 = f32[32,256]{1,0:T(8,128)S(1)} collective-permute-done((f32[32,256]{1,0:T(8,128)S(1)}, f32[32,256]{1,0:T(8,128)S(1)}, u32[]{:S(2)}, u32[]{:S(2)}) %collective-permute-start.18) | collective-permute-done | bytes 32800 | tf_op jit(solution)/shard_map/ppermute | solution.py:123
  76.3 2.2 %collective-permute-done.17 = f32[32,256]{1,0:T(8,128)S(1)} collective-permute-done((f32[32,256]{1,0:T(8,128)S(1)}, f32[32,256]{1,0:T(8,128)S(1)}, u32[]{:S(2)}, u32[]{:S(2)}) %collective-permute-start.17) | collective-permute-done | bytes 32800 | tf_op jit(solution)/shard_map/ppermute | solution.py:123
  78.5 4.7 %collective-permute-start.21 = (f32[32,256]{1,0:T(8,128)S(1)}, f32[32,256]{1,0:T(8,128)S(1)}, u32[]{:S(2)}, u32[]{:S(2)}) collective-permute-start(f32[32,256]{1,0:T(8,128)S(1)} %fusion.9), channel_id=1, source_target_pairs={{0,48},{16,0},{32,16},{48,32},{1,49},{17,1},{33,17},{49,33},{2,50}... | collective-permute-start | bytes 98312 | tf_op jit(solution)/shard_map/ppermute | solution.py:123
  84.2 2.6 %collective-permute-done.20 = f32[32,256]{1,0:T(8,128)S(1)} collective-permute-done((f32[32,256]{1,0:T(8,128)S(1)}, f32[32,256]{1,0:T(8,128)S(1)}, u32[]{:S(2)}, u32[]{:S(2)}) %collective-permute-start.20) | collective-permute-done | bytes 32800 | tf_op jit(solution)/shard_map/ppermute | solution.py:123
  86.9 0.9 collective-permute-done.19
  87.8 2.7 %collective-permute-start.22 = (f32[32,256]{1,0:T(8,128)S(1)}, f32[32,256]{1,0:T(8,128)S(1)}, u32[]{:S(2)}, u32[]{:S(2)}) collective-permute-start(f32[32,256]{1,0:T(8,128)S(1)} %add_add_fusion), channel_id=1, source_target_pairs={{0,8},{8,0},{1,9},{9,1},{2,10},{10,2},{3,11},{11,3},{4,12},{12,4},... | collective-permute-start | bytes 98312 | tf_op jit(solution)/shard_map/ppermute | solution.py:123
  90.5 0.9 collective-permute-done.22
  91.3 2.1 %collective-permute-start.25 = (f32[64,256]{1,0:T(8,128)S(1)}, f32[64,256]{1,0:T(8,128)S(1)}, u32[]{:S(2)}, u32[]{:S(2)}) collective-permute-start(f32[64,256]{1,0:T(8,128)S(1)} %maximum_select_fusion.1.refs_0_), channel_id=1, source_target_pairs={{0,192},{64,0},{128,64},{192,128},{1,193},{65,1},{129,65},{193,129... | collective-permute-start | bytes 196616 | tf_op jit(solution)/shard_map/ppermute | solution.py:123
  93.5 0.7 collective-permute-start.23
  94.1 0.7 collective-permute-done.25.refs_3_
  94.8 3.4 %collective-permute-done.24.refs_2_ = f32[64,256]{1,0:T(8,128)S(1)} collective-permute-done((f32[64,256]{1,0:T(8,128)S(1)}, f32[64,256]{1,0:T(8,128)S(1)}, u32[]{:S(2)}, u32[]{:S(2)}) %collective-permute-start.24) | collective-permute-done | bytes 65568 | tf_op jit(solution)/shard_map/ppermute | solution.py:123
  98.2 1.1 collective-permute-done.23.refs_1_
  99.3 8.2 %inverse.3 = f32[256,256]{1,0:T(8,128)S(1)} custom-call(f32[64,256]{1,0:T(8,128)S(1)} %maximum_select_fusion.1.refs_0_, f32[64,256]{1,0:T(8,128)S(1)} %collective-permute-done.23.refs_1_, f32[64,256]{1,0:T(8,128)S(1)} %collective-permute-done.24.refs_2_, f32[64,256]{1,0:T(8,128)S(1)} %collective-permute-done.25.refs_3_, ...), custom_call_target="tpu_custom_call" | custom-call | flops 201326592 | bytes 524288 | tf_op jit(solution)/shard_map/inverse/pallas_call | solution.py:95
  107.8 11.2 %all_to_all.15 = bf16[16,32,256]{2,1,0:T(8,128)(2,1)S(1)} all-to-all(bf16[16,32,256]{2,1,0:T(8,128)(2,1)S(1)} %broadcast_in_dim.4), channel_id=1, replica_groups=mesh['x'=4,'zl'=4,'core'=2,'zh'=2,'y'=4] {'x','zl'}, dimensions={0} | all-to-all | bytes 524288 | tf_op jit(solution)/shard_map/all_to_all | solution.py:108
  119.0 3.2 %collective-permute-start.26 = (bf16[512,256]{1,0:T(8,128)(2,1)S(1)}, bf16[512,256]{1,0:T(8,128)(2,1)S(1)}, u32[]{:S(2)}, u32[]{:S(2)}) collective-permute-start(bf16[512,256]{1,0:T(8,128)(2,1)S(1)} %bitcast.64), channel_id=1, source_target_pairs={{0,8},{8,0},{1,9},{9,1},{2,10},{10,2},{3,11},{11,3},{4,12},{12,4},... | collective-permute-start | bytes 786440 | tf_op jit(solution)/shard_map/ppermute | solution.py:123
  122.3 1.2 collective-permute-done.26
  123.7 5.9 %multiply_reduce_fusion.1 = f32[16,256]{1,0:T(8,128)S(1)} fusion(bf16[16,256,1024]{2,1,0:T(8,128)(2,1)} %param.3, f32[256,256]{1,0:T(8,128)S(1)} %get-tuple-element.7, bf16[1024,256]{1,0:T(8,128)(2,1)S(1)} %maximum_select_fusion), kind=kOutput, calls=%fused_computation.1 | convolution fusion | flops 2149576704 | bytes 9191424 | tf_op jit(solution)/shard_map/ijk,kr->ijr/dot_general | solution.py:226
  130.1 0.8 collective-permute-done.27
  132.4 1.1 collective-permute-done.30
  133.5 2.1 %collective-permute-done.29 = f32[16,256]{1,0:T(8,128)S(1)} collective-permute-done((f32[16,256]{1,0:T(8,128)S(1)}, f32[16,256]{1,0:T(8,128)S(1)}, u32[]{:S(2)}, u32[]{:S(2)}) %collective-permute-start.29) | collective-permute-done | bytes 16416 | tf_op jit(solution)/shard_map/ppermute | solution.py:123
  136.0 18.2 %all_to_all.16 = bf16[32,16,256]{2,1,0:T(8,128)(2,1)S(1)} all-to-all(bf16[32,16,256]{2,1,0:T(8,128)(2,1)S(1)} %broadcast_in_dim.5), channel_id=1, replica_groups=mesh['x'=4,'zl'=4,'core'=2,'zh'=2,'y'=4] {'zl','zh','y'}, dimensions={0} | all-to-all | bytes 524288 | tf_op jit(solution)/shard_map/all_to_all | solution.py:108
  154.2 0.7 convert_reduce_fusion
  (59 shorter events, 7.6 us)
Async XLA Ops:
  0.6 1.0 copy-start
  2.1 14.5 %collective-permute-start.4 = (f32[64,256]{1,0:T(8,128)S(1)}, f32[64,256]{1,0:T(8,128)S(1)}, u32[]{:S(2)}, u32[]{:S(2)}) collective-permute-start(f32[64,256]{1,0:T(8,128)S(1)} %get-tuple-element.12), channel_id=1, source_target_pairs={{0,1},{1,2},{2,3},{3,0},{4,5},{5,6},{6,7},{7,4},{8,9},{9,10},{10,1... | collective-permute-start | bytes 196616 | tf_op jit(solution)/shard_map/ppermute | solution.py:123
  4.3 12.5 %collective-permute-start.6 = (f32[64,256]{1,0:T(8,128)S(1)}, f32[64,256]{1,0:T(8,128)S(1)}, u32[]{:S(2)}, u32[]{:S(2)}) collective-permute-start(f32[64,256]{1,0:T(8,128)S(1)} %get-tuple-element.13), channel_id=1, source_target_pairs={{0,3},{1,0},{2,1},{3,2},{4,7},{5,4},{6,5},{7,6},{8,11},{9,8},{10,9... | collective-permute-start | bytes 196616 | tf_op jit(solution)/shard_map/ppermute | solution.py:123
  5.8 11.0 %collective-permute-start.5 = (f32[64,256]{1,0:T(8,128)S(1)}, f32[64,256]{1,0:T(8,128)S(1)}, u32[]{:S(2)}, u32[]{:S(2)}) collective-permute-start(f32[64,256]{1,0:T(8,128)S(1)} %get-tuple-element.14), channel_id=1, source_target_pairs={{0,2},{1,3},{2,0},{3,1},{4,6},{5,7},{6,4},{7,5},{8,10},{9,11},{10,... | collective-permute-start | bytes 196616 | tf_op jit(solution)/shard_map/ppermute | solution.py:123
  8.0 21.7 %copy-start.3 = (bf16[16,256]{1,0:T(8,128)(2,1)S(1)}, bf16[16,256]{1,0:T(8,128)(2,1)}, u32[]{:S(2)}) copy-start(bf16[16,256]{1,0:T(8,128)(2,1)} %param.4) | copy-start | bytes 24580
  13.8 10.0 %collective-permute-start = (f32[64,256]{1,0:T(8,128)S(1)}, f32[64,256]{1,0:T(8,128)S(1)}, u32[]{:S(2)}, u32[]{:S(2)}) collective-permute-start(f32[64,256]{1,0:T(8,128)S(1)} %get-tuple-element.9), channel_id=1, source_target_pairs={{0,1},{1,2},{2,3},{3,0},{4,5},{5,6},{6,7},{7,4},{8,9},{9,10},{10,1... | collective-permute-start | bytes 196616 | tf_op jit(solution)/shard_map/ppermute | solution.py:123
  14.3 9.5 %collective-permute-start.2 = (f32[64,256]{1,0:T(8,128)S(1)}, f32[64,256]{1,0:T(8,128)S(1)}, u32[]{:S(2)}, u32[]{:S(2)}) collective-permute-start(f32[64,256]{1,0:T(8,128)S(1)} %get-tuple-element.10), channel_id=1, source_target_pairs={{0,3},{1,0},{2,1},{3,2},{4,7},{5,4},{6,5},{7,6},{8,11},{9,8},{10,9... | collective-permute-start | bytes 196616 | tf_op jit(solution)/shard_map/ppermute | solution.py:123
  16.6 7.2 %collective-permute-start.1 = (f32[64,256]{1,0:T(8,128)S(1)}, f32[64,256]{1,0:T(8,128)S(1)}, u32[]{:S(2)}, u32[]{:S(2)}) collective-permute-start(f32[64,256]{1,0:T(8,128)S(1)} %get-tuple-element.11), channel_id=1, source_target_pairs={{0,2},{1,3},{2,0},{3,1},{4,6},{5,7},{6,4},{7,5},{8,10},{9,11},{10,... | collective-permute-start | bytes 196616 | tf_op jit(solution)/shard_map/ppermute | solution.py:123
  16.8 11.4 %collective-permute-start.7 = (f32[64,256]{1,0:T(8,128)S(1)}, f32[64,256]{1,0:T(8,128)S(1)}, u32[]{:S(2)}, u32[]{:S(2)}) collective-permute-start(f32[64,256]{1,0:T(8,128)S(1)} %fusion.4), channel_id=1, source_target_pairs={{0,4},{4,0},{1,5},{5,1},{2,6},{6,2},{3,7},{7,3},{8,12},{12,8},{9,1... | collective-permute-start | bytes 196616 | tf_op jit(solution)/shard_map/ppermute | solution.py:123
  23.9 18.7 %collective-permute-start.3 = (f32[64,256]{1,0:T(8,128)S(1)}, f32[64,256]{1,0:T(8,128)S(1)}, u32[]{:S(2)}, u32[]{:S(2)}) collective-permute-start(f32[64,256]{1,0:T(8,128)S(1)} %fusion.6), channel_id=1, source_target_pairs={{0,4},{4,0},{1,5},{5,1},{2,6},{6,2},{3,7},{7,3},{8,12},{12,8},{9,1... | collective-permute-start | bytes 196616 | tf_op jit(solution)/shard_map/ppermute | solution.py:123
  28.2 3.2 %collective-permute-start.10 = (f32[64,256]{1,0:T(8,128)S(1)}, f32[64,256]{1,0:T(8,128)S(1)}, u32[]{:S(2)}, u32[]{:S(2)}) collective-permute-start(f32[64,256]{1,0:T(8,128)S(1)} %add.125.refs_0_), channel_id=1, source_target_pairs={{0,3},{1,0},{2,1},{3,2},{4,7},{5,4},{6,5},{7,6},{8,11},{9,8},{10,9... | collective-permute-start | bytes 196616 | tf_op jit(solution)/shard_map/ppermute | solution.py:123
  28.7 4.9 %collective-permute-start.9 = (f32[64,256]{1,0:T(8,128)S(1)}, f32[64,256]{1,0:T(8,128)S(1)}, u32[]{:S(2)}, u32[]{:S(2)}) collective-permute-start(f32[64,256]{1,0:T(8,128)S(1)} %add.125.refs_0_), channel_id=1, source_target_pairs={{0,2},{1,3},{2,0},{3,1},{4,6},{5,7},{6,4},{7,5},{8,10},{9,11},{10,... | collective-permute-start | bytes 196616 | tf_op jit(solution)/shard_map/ppermute | solution.py:123
  29.6 4.7 %collective-permute-start.8 = (f32[64,256]{1,0:T(8,128)S(1)}, f32[64,256]{1,0:T(8,128)S(1)}, u32[]{:S(2)}, u32[]{:S(2)}) collective-permute-start(f32[64,256]{1,0:T(8,128)S(1)} %add.125.refs_0_), channel_id=1, source_target_pairs={{0,1},{1,2},{2,3},{3,0},{4,5},{5,6},{6,7},{7,4},{8,9},{9,10},{10,1... | collective-permute-start | bytes 196616 | tf_op jit(solution)/shard_map/ppermute | solution.py:123
  42.8 4.0 %collective-permute-start.13 = (bf16[64,256]{1,0:T(8,128)(2,1)S(1)}, bf16[64,256]{1,0:T(8,128)(2,1)S(1)}, u32[]{:S(2)}, u32[]{:S(2)}) collective-permute-start(bf16[64,256]{1,0:T(8,128)(2,1)S(1)} %convolution_convert_fusion), channel_id=1, source_target_pairs={{0,1},{1,0},{2,3},{3,2},{4,5},{5,4},{6,7},{7,6},{8,9},{9,8},{10,11... | collective-permute-start | bytes 98312 | tf_op jit(solution)/shard_map/ppermute | solution.py:144
  43.2 4.3 %collective-permute-start.12 = (bf16[64,256]{1,0:T(8,128)(2,1)S(1)}, bf16[64,256]{1,0:T(8,128)(2,1)S(1)}, u32[]{:S(2)}, u32[]{:S(2)}) collective-permute-start(bf16[64,256]{1,0:T(8,128)(2,1)S(1)} %convolution_convert_fusion), channel_id=1, source_target_pairs={{0,2},{1,3},{2,0},{3,1},{4,6},{5,7},{6,4},{7,5},{8,10},{9,11},{10,... | collective-permute-start | bytes 98312 | tf_op jit(solution)/shard_map/ppermute | solution.py:144
  45.4 4.0 %collective-permute-start.11 = (bf16[64,256]{1,0:T(8,128)(2,1)S(1)}, bf16[64,256]{1,0:T(8,128)(2,1)S(1)}, u32[]{:S(2)}, u32[]{:S(2)}) collective-permute-start(bf16[64,256]{1,0:T(8,128)(2,1)S(1)} %convolution_convert_fusion), channel_id=1, source_target_pairs={{0,3},{1,2},{2,1},{3,0},{4,7},{5,6},{6,5},{7,4},{8,11},{9,10},{10,... | collective-permute-start | bytes 98312 | tf_op jit(solution)/shard_map/ppermute | solution.py:144
  49.4 12.7 %copy-start.1 = (bf16[256,256]{1,0:T(8,128)(2,1)}, bf16[256,256]{1,0:T(8,128)(2,1)S(1)}, u32[]{:S(2)}) copy-start(bf16[256,256]{1,0:T(8,128)(2,1)S(1)} %get-tuple-element.8) | copy-start | bytes 393220
  55.4 8.3 %collective-permute-start.14 = (f32[512,256]{1,0:T(8,128)S(1)}, f32[512,256]{1,0:T(8,128)S(1)}, u32[]{:S(2)}, u32[]{:S(2)}) collective-permute-start(f32[512,256]{1,0:T(8,128)S(1)} %slice_select_fusion), channel_id=1, source_target_pairs={{0,8},{8,0},{1,9},{9,1},{2,10},{10,2},{3,11},{11,3},{4,12},{12,4},... | collective-permute-start | bytes 1572872 | tf_op jit(solution)/shard_map/ppermute | solution.py:123
  63.0 7.0 %collective-permute-start.15 = (f32[128,256]{1,0:T(8,128)}, f32[128,256]{1,0:T(8,128)S(1)}, u32[]{:S(2)}, u32[]{:S(2)}) collective-permute-start(f32[128,256]{1,0:T(8,128)} %slice_select_fusion.1), channel_id=1, source_target_pairs={{0,8},{8,0},{1,9},{9,1},{2,10},{10,2},{3,11},{11,3},{4,12},{12,4},... | collective-permute-start | bytes 393224 | tf_op jit(solution)/shard_map/ppermute | solution.py:123
  64.5 43.0 %all-to-all-start = ((f32[16,32,256]{2,1,0:T(8,128)}), f32[16,32,256]{2,1,0:T(8,128)S(1)}, u32[]{:S(2)}, u32[]{:S(2)}) async-start(f32[16,32,256]{2,1,0:T(8,128)} %bitcast.12), calls=%async_computation | async-start | bytes 1048576 | tf_op jit(solution)/shard_map/all_to_all | solution.py:108
  70.1 4.4 %collective-permute-start.16 = (f32[32,256]{1,0:T(8,128)S(1)}, f32[32,256]{1,0:T(8,128)S(1)}, u32[]{:S(2)}, u32[]{:S(2)}) collective-permute-start(f32[32,256]{1,0:T(8,128)S(1)} %get-tuple-element.15), channel_id=1, source_target_pairs={{0,64},{64,128},{128,192},{192,0},{1,65},{65,129},{129,193},{193,1... | collective-permute-start | bytes 98312 | tf_op jit(solution)/shard_map/ppermute | solution.py:123
  71.5 4.8 %collective-permute-start.18 = (f32[32,256]{1,0:T(8,128)S(1)}, f32[32,256]{1,0:T(8,128)S(1)}, u32[]{:S(2)}, u32[]{:S(2)}) collective-permute-start(f32[32,256]{1,0:T(8,128)S(1)} %get-tuple-element.16), channel_id=1, source_target_pairs={{0,192},{64,0},{128,64},{192,128},{1,193},{65,1},{129,65},{193,129... | collective-permute-start | bytes 98312 | tf_op jit(solution)/shard_map/ppermute | solution.py:123
  72.8 5.7 %collective-permute-start.17 = (f32[32,256]{1,0:T(8,128)S(1)}, f32[32,256]{1,0:T(8,128)S(1)}, u32[]{:S(2)}, u32[]{:S(2)}) collective-permute-start(f32[32,256]{1,0:T(8,128)S(1)} %get-tuple-element.17), channel_id=1, source_target_pairs={{0,128},{64,192},{128,0},{192,64},{1,129},{65,193},{129,1},{193,65... | collective-permute-start | bytes 98312 | tf_op jit(solution)/shard_map/ppermute | solution.py:123
  78.5 5.7 %collective-permute-start.21 = (f32[32,256]{1,0:T(8,128)S(1)}, f32[32,256]{1,0:T(8,128)S(1)}, u32[]{:S(2)}, u32[]{:S(2)}) collective-permute-start(f32[32,256]{1,0:T(8,128)S(1)} %fusion.9), channel_id=1, source_target_pairs={{0,48},{16,0},{32,16},{48,32},{1,49},{17,1},{33,17},{49,33},{2,50}... | collective-permute-start | bytes 98312 | tf_op jit(solution)/shard_map/ppermute | solution.py:123
  83.2 3.7 %collective-permute-start.20 = (f32[32,256]{1,0:T(8,128)S(1)}, f32[32,256]{1,0:T(8,128)S(1)}, u32[]{:S(2)}, u32[]{:S(2)}) collective-permute-start(f32[32,256]{1,0:T(8,128)S(1)} %fusion.9), channel_id=1, source_target_pairs={{0,32},{16,48},{32,0},{48,16},{1,33},{17,49},{33,1},{49,17},{2,34}... | collective-permute-start | bytes 98312 | tf_op jit(solution)/shard_map/ppermute | solution.py:123
  83.2 4.6 %collective-permute-start.19 = (f32[32,256]{1,0:T(8,128)S(1)}, f32[32,256]{1,0:T(8,128)S(1)}, u32[]{:S(2)}, u32[]{:S(2)}) collective-permute-start(f32[32,256]{1,0:T(8,128)S(1)} %fusion.9), channel_id=1, source_target_pairs={{0,16},{16,32},{32,48},{48,0},{1,17},{17,33},{33,49},{49,1},{2,18}... | collective-permute-start | bytes 98312 | tf_op jit(solution)/shard_map/ppermute | solution.py:123
  87.8 3.5 %collective-permute-start.22 = (f32[32,256]{1,0:T(8,128)S(1)}, f32[32,256]{1,0:T(8,128)S(1)}, u32[]{:S(2)}, u32[]{:S(2)}) collective-permute-start(f32[32,256]{1,0:T(8,128)S(1)} %add_add_fusion), channel_id=1, source_target_pairs={{0,8},{8,0},{1,9},{9,1},{2,10},{10,2},{3,11},{11,3},{4,12},{12,4},... | collective-permute-start | bytes 98312 | tf_op jit(solution)/shard_map/ppermute | solution.py:123
  91.3 3.5 %collective-permute-start.25 = (f32[64,256]{1,0:T(8,128)S(1)}, f32[64,256]{1,0:T(8,128)S(1)}, u32[]{:S(2)}, u32[]{:S(2)}) collective-permute-start(f32[64,256]{1,0:T(8,128)S(1)} %maximum_select_fusion.1.refs_0_), channel_id=1, source_target_pairs={{0,192},{64,0},{128,64},{192,128},{1,193},{65,1},{129,65},{193,129... | collective-permute-start | bytes 196616 | tf_op jit(solution)/shard_map/ppermute | solution.py:123
  93.5 4.7 %collective-permute-start.24 = (f32[64,256]{1,0:T(8,128)S(1)}, f32[64,256]{1,0:T(8,128)S(1)}, u32[]{:S(2)}, u32[]{:S(2)}) collective-permute-start(f32[64,256]{1,0:T(8,128)S(1)} %maximum_select_fusion.1.refs_0_), channel_id=1, source_target_pairs={{0,128},{64,192},{128,0},{192,64},{1,129},{65,193},{129,1},{193,65... | collective-permute-start | bytes 196616 | tf_op jit(solution)/shard_map/ppermute | solution.py:123
  93.5 5.8 %collective-permute-start.23 = (f32[64,256]{1,0:T(8,128)S(1)}, f32[64,256]{1,0:T(8,128)S(1)}, u32[]{:S(2)}, u32[]{:S(2)}) collective-permute-start(f32[64,256]{1,0:T(8,128)S(1)} %maximum_select_fusion.1.refs_0_), channel_id=1, source_target_pairs={{0,64},{64,128},{128,192},{192,0},{1,65},{65,129},{129,193},{193,1... | collective-permute-start | bytes 196616 | tf_op jit(solution)/shard_map/ppermute | solution.py:123
  119.0 4.4 %collective-permute-start.26 = (bf16[512,256]{1,0:T(8,128)(2,1)S(1)}, bf16[512,256]{1,0:T(8,128)(2,1)S(1)}, u32[]{:S(2)}, u32[]{:S(2)}) collective-permute-start(bf16[512,256]{1,0:T(8,128)(2,1)S(1)} %bitcast.64), channel_id=1, source_target_pairs={{0,8},{8,0},{1,9},{9,1},{2,10},{10,2},{3,11},{11,3},{4,12},{12,4},... | collective-permute-start | bytes 786440 | tf_op jit(solution)/shard_map/ppermute | solution.py:123
  123.7 5.9 %copy-start.2 = (bf16[1024,256]{1,0:T(8,128)(2,1)}, bf16[1024,256]{1,0:T(8,128)(2,1)S(1)}, u32[]{:S(2)}) copy-start(bf16[1024,256]{1,0:T(8,128)(2,1)S(1)} %maximum_select_fusion) | copy-start | bytes 1572868
  129.6 1.3 collective-permute-start.27
  130.9 2.6 %collective-permute-start.30 = (f32[16,256]{1,0:T(8,128)S(1)}, f32[16,256]{1,0:T(8,128)S(1)}, u32[]{:S(2)}, u32[]{:S(2)}) collective-permute-start(f32[16,256]{1,0:T(8,128)S(1)} %add.141), channel_id=1, source_target_pairs={{0,192},{64,0},{128,64},{192,128},{1,193},{65,1},{129,65},{193,129... | collective-permute-start | bytes 49160 | tf_op jit(solution)/shard_map/ppermute | solution.py:123
  131.5 4.1 %collective-permute-start.29 = (f32[16,256]{1,0:T(8,128)S(1)}, f32[16,256]{1,0:T(8,128)S(1)}, u32[]{:S(2)}, u32[]{:S(2)}) collective-permute-start(f32[16,256]{1,0:T(8,128)S(1)} %add.141), channel_id=1, source_target_pairs={{0,128},{64,192},{128,0},{192,64},{1,129},{65,193},{129,1},{193,65... | collective-permute-start | bytes 49160 | tf_op jit(solution)/shard_map/ppermute | solution.py:123
  131.9 4.1 %collective-permute-start.28 = (f32[16,256]{1,0:T(8,128)S(1)}, f32[16,256]{1,0:T(8,128)S(1)}, u32[]{:S(2)}, u32[]{:S(2)}) collective-permute-start(f32[16,256]{1,0:T(8,128)S(1)} %add.141), channel_id=1, source_target_pairs={{0,64},{64,128},{128,192},{192,0},{1,65},{65,129},{129,193},{193,1... | collective-permute-start | bytes 49160 | tf_op jit(solution)/shard_map/ppermute | solution.py:123

commit v9 on v8

--- a/solution.py
+++ b/solution.py
@@ -108,11 +108,6 @@
     return lax.all_to_all(x, axes, 0, 0, tiled=True)
 
 
-def scatter_sum(x, axes):
-    n = lax.axis_size(axes)
-    return jnp.sum(exchange(x.reshape(n, x.shape[0] // n, x.shape[1]), axes), axis=0)
-
-
 def gather(x, axes):
     n = lax.axis_size(axes)
     return exchange(jnp.broadcast_to(x[None], (n,) + x.shape), axes).reshape(n * x.shape[0], x.shape[1])
@@ -218,7 +213,8 @@
     partial_third = jnp.sum(middle * first_third[:, None, :], axis=0)
     mine, other = keep(partial_third, core)
     mine = mine + shift(other, "core", 1)
-    mttkrp_third = scatter_sum(mine, CHIP)
+    mine = ring_scatter(mine, "x")
+    mttkrp_third = ring_scatter(mine, "zl")
     third_solution = jnp.dot(mttkrp_third, inverse_third, precision=HIGHEST)
     mine = gather(third_solution.astype(jnp.bfloat16), CHIP)
     third_new = join(mine, shift(mine, "core", 1), core)

time: 157 us -> 152 us (0.968)
  waiting for transfers between devices: 27.2 us -> 17.6 us
  starting transfers between devices: 57.5 us -> 60.9 us
  blocking collectives: 29.4 us -> 31.1 us
    ppermute x28 -> x34, waiting for transfers between devices: 24.7 us -> 14.2 us  [shift(): return lax.ppermute(x, axis, [(s, (s + d) % n) for s in range(n)])]
    ppermute x28 -> x34, starting transfers between devices: 48 us -> 57.5 us  [shift(): return lax.ppermute(x, axis, [(s, (s + d) % n) for s in range(n)])]
    all_to_all x1 -> x0, starting transfers between devices: 5.48 us -> none  [exchange(): return lax.all_to_all(x, axes, 0, 0, tiled=True)]
    all_to_all x2, blocking collectives: 29.4 us -> 31.1 us  [exchange(): return lax.all_to_all(x, axes, 0, 0, tiled=True)]
  transfers between devices with their start and end apart: 32 -> 37, of which waited for: 20 -> 14; matrix products, arithmetic and copies ran while one was open for 6% -> 9% of each run, Pallas kernels for 11% -> 11%
where the time goes in v9:
time: 152 us; the launch traced here: 149 us
  starting transfers between devices  60.9 us (40%)
  blocking collectives  31.1 us (20%)
  matrix products  18.8 us (12%)
  waiting for transfers between devices  17.6 us (12%)
  Pallas kernels  16.4 us (11%)
  other arithmetic  1.97 us (1%)
    ppermute x34, starting transfers between devices, shift(): return lax.ppermute(x, axis, [(s, (s + d) % n) for s in range(n)])  57.5 us
    all_to_all x2, blocking collectives, exchange(): return lax.all_to_all(x, axes, 0, 0, tiled=True)  31.1 us
    pallas_call x2, Pallas kernels, inverse(): pl.pallas_call(functools.partial(inverse_kernel, places, total), out_shap...  16.4 us
    ppermute x34, waiting for transfers between devices, shift(): return lax.ppermute(x, axis, [(s, (s + d) % n) for s in range(n)])  14.2 us
    dot_general x1, matrix products, on_device(): jnp.einsum('ijk,kr->ijr', tensor, third_new, preferred_element_type=jnp.f...  5.92 us
    dot_general x1, matrix products, on_device(): jnp.einsum('ijk,jr->ikr', tensor, second_factor, preferred_element_type=j...  5.87 us
    dot_general x1, matrix products, on_device(): jnp.einsum('ijk,kr->ijr', tensor, third_factor, preferred_element_type=jn...  5.74 us
    ppermute x3, waiting for transfers between devices, pair(): lax.ppermute(x, axis, [(s, s ^ d) for s in range(lax.axis_size(axis))])  3.41 us
  transfers between devices with their start and end apart: 37, of which 14 were waited for; matrix products, arithmetic and copies ran while one was open for 9% of the time, Pallas kernels for 11%

profile of v9, /device:TPU:1, one launch (start us, length us, event | category | flops | bytes accessed | tf_op | source)
XLA Modules:
  0.0 149.0 jit_solution(18210795614068903855)
XLA Ops:
  0.7 1.0 copy-done
  2.1 2.2 %collective-permute-start.4 = (f32[64,256]{1,0:T(8,128)S(1)}, f32[64,256]{1,0:T(8,128)S(1)}, u32[]{:S(2)}, u32[]{:S(2)}) collective-permute-start(f32[64,256]{1,0:T(8,128)S(1)} %get-tuple-element.15), channel_id=1, source_target_pairs={{0,1},{1,2},{2,3},{3,0},{4,5},{5,6},{6,7},{7,4},{8,9},{9,10},{10,1... | collective-permute-start | bytes 196616 | tf_op jit(solution)/shard_map/ppermute | solution.py:118
  4.3 2.6 %collective-permute-start.5 = (f32[64,256]{1,0:T(8,128)S(1)}, f32[64,256]{1,0:T(8,128)S(1)}, u32[]{:S(2)}, u32[]{:S(2)}) collective-permute-start(f32[64,256]{1,0:T(8,128)S(1)} %get-tuple-element.17), channel_id=1, source_target_pairs={{0,2},{1,3},{2,0},{3,1},{4,6},{5,7},{6,4},{7,5},{8,10},{9,11},{10,... | collective-permute-start | bytes 196616 | tf_op jit(solution)/shard_map/ppermute | solution.py:118
  6.9 1.1 collective-permute-start.6
  7.9 0.7 convert_multiply_fusion
  8.7 5.7 %multiply_reduce_fusion.2 = f32[256,256]{1,0:T(8,128)S(1)} fusion(bf16[16,256,1024]{2,1,0:T(8,128)(2,1)} %param.3, f32[16,256]{1,0:T(8,128)S(1)} %convert_multiply_fusion, bf16[1024,256]{1,0:T(8,128)(2,1)S(1)} %copy-done), kind=kOutput, calls=%fused_computation.2 | convolution fusion | flops 2149515264 | bytes 9191424 | tf_op jit(solution)/shard_map/ijk,kr->ijr/dot_general | solution.py:195
  14.9 0.8 collective-permute-start.1
  15.7 1.7 %collective-permute-start.2 = (f32[64,256]{1,0:T(8,128)S(1)}, f32[64,256]{1,0:T(8,128)S(1)}, u32[]{:S(2)}, u32[]{:S(2)}) collective-permute-start(f32[64,256]{1,0:T(8,128)S(1)} %get-tuple-element.13), channel_id=1, source_target_pairs={{0,3},{1,0},{2,1},{3,2},{4,7},{5,4},{6,5},{7,6},{8,11},{9,8},{10,9... | collective-permute-start | bytes 196616 | tf_op jit(solution)/shard_map/ppermute | solution.py:118
  17.4 7.0 %collective-permute-start.7 = (f32[64,256]{1,0:T(8,128)S(1)}, f32[64,256]{1,0:T(8,128)S(1)}, u32[]{:S(2)}, u32[]{:S(2)}) collective-permute-start(f32[64,256]{1,0:T(8,128)S(1)} %fusion.6), channel_id=1, source_target_pairs={{0,4},{4,0},{1,5},{5,1},{2,6},{6,2},{3,7},{7,3},{8,12},{12,8},{9,1... | collective-permute-start | bytes 196616 | tf_op jit(solution)/shard_map/ppermute | solution.py:118
  24.5 3.0 %collective-permute-start.3 = (f32[64,256]{1,0:T(8,128)S(1)}, f32[64,256]{1,0:T(8,128)S(1)}, u32[]{:S(2)}, u32[]{:S(2)}) collective-permute-start(f32[64,256]{1,0:T(8,128)S(1)} %fusion.8), channel_id=1, source_target_pairs={{0,4},{4,0},{1,5},{5,1},{2,6},{6,2},{3,7},{7,3},{8,12},{12,8},{9,1... | collective-permute-start | bytes 196616 | tf_op jit(solution)/shard_map/ppermute | solution.py:118
  27.4 2.1 %collective-permute-start.10 = (f32[64,256]{1,0:T(8,128)S(1)}, f32[64,256]{1,0:T(8,128)S(1)}, u32[]{:S(2)}, u32[]{:S(2)}) collective-permute-start(f32[64,256]{1,0:T(8,128)S(1)} %add.172.refs_0_), channel_id=1, source_target_pairs={{0,3},{1,0},{2,1},{3,2},{4,7},{5,4},{6,5},{7,6},{8,11},{9,8},{10,9... | collective-permute-start | bytes 196616 | tf_op jit(solution)/shard_map/ppermute | solution.py:118
  29.6 1.3 collective-permute-start.9
  31.1 3.6 %collective-permute-done.8.refs_1_ = f32[64,256]{1,0:T(8,128)S(1)} collective-permute-done((f32[64,256]{1,0:T(8,128)S(1)}, f32[64,256]{1,0:T(8,128)S(1)}, u32[]{:S(2)}, u32[]{:S(2)}) %collective-permute-start.8) | collective-permute-done | bytes 65568 | tf_op jit(solution)/shard_map/ppermute | solution.py:118
  34.7 8.2 %inverse.2 = f32[256,256]{1,0:T(8,128)S(1)} custom-call(f32[64,256]{1,0:T(8,128)S(1)} %add.172.refs_0_, f32[64,256]{1,0:T(8,128)S(1)} %collective-permute-done.8.refs_1_, f32[64,256]{1,0:T(8,128)S(1)} %collective-permute-done.9.refs_2_, f32[64,256]{1,0:T(8,128)S(1)} %collective-permute-done.10.refs_3_, f32[256,256]{1,0:T(8,128)S(1)} %convolution_multiply_fusion.refs_4_), custom_call_target="tpu_custom_call" | custom-call | flops 201326592 | bytes 524288 | tf_op jit(solution)/shard_map/inverse/pallas_call | solution.py:95
  43.2 2.5 %collective-permute-start.11 = (bf16[64,256]{1,0:T(8,128)(2,1)S(1)}, bf16[64,256]{1,0:T(8,128)(2,1)S(1)}, u32[]{:S(2)}, u32[]{:S(2)}) collective-permute-start(bf16[64,256]{1,0:T(8,128)(2,1)S(1)} %convolution_convert_fusion), channel_id=1, source_target_pairs={{0,3},{1,2},{2,1},{3,0},{4,7},{5,6},{6,5},{7,4},{8,11},{9,10},{10,... | collective-permute-start | bytes 98312 | tf_op jit(solution)/shard_map/ppermute | solution.py:139
  45.7 0.9 collective-permute-start.13
  46.6 0.7 collective-permute-done.11
  47.3 2.8 %collective-permute-done.12 = bf16[64,256]{1,0:T(8,128)(2,1)S(1)} collective-permute-done((bf16[64,256]{1,0:T(8,128)(2,1)S(1)}, bf16[64,256]{1,0:T(8,128)(2,1)S(1)}, u32[]{:S(2)}, u32[]{:S(2)}) %collective-permute-start.12) | collective-permute-done | bytes 32800 | tf_op jit(solution)/shard_map/ppermute | solution.py:139
  50.3 6.1 %collective-permute-start.21 = (f32[128,256]{1,0:T(8,128)S(1)}, f32[128,256]{1,0:T(8,128)S(1)}, u32[]{:S(2)}, u32[]{:S(2)}) collective-permute-start(f32[128,256]{1,0:T(8,128)S(1)} %slice_select_fusion.1), channel_id=1, source_target_pairs={{0,8},{8,0},{1,9},{9,1},{2,10},{10,2},{3,11},{11,3},{4,12},{12,4},... | collective-permute-start | bytes 393224 | tf_op jit(solution)/shard_map/ppermute | solution.py:118
  56.5 5.9 %multiply_reduce_fusion = f32[1024,256]{1,0:T(8,128)S(1)} fusion(bf16[16,256,1024]{2,1,0:T(8,128)(2,1)} %param.3, f32[16,256]{1,0:T(8,128)S(1)} %convert_multiply_fusion, bf16[256,256]{1,0:T(8,128)(2,1)S(1)} %get-tuple-element.8), kind=kOutput, calls=%fused_computation | convolution fusion | flops 2155610112 | bytes 9584640 | tf_op jit(solution)/shard_map/ijk,jr->ikr/dot_general | solution.py:212
  62.6 1.3 collective-permute-start.22
  63.9 2.5 %collective-permute-start.23 = (f32[32,256]{1,0:T(8,128)S(1)}, f32[32,256]{1,0:T(8,128)S(1)}, u32[]{:S(2)}, u32[]{:S(2)}) collective-permute-start(f32[32,256]{1,0:T(8,128)S(1)} %get-tuple-element.23), channel_id=1, source_target_pairs={{0,128},{64,192},{128,0},{192,64},{1,129},{65,193},{129,1},{193,65... | collective-permute-start | bytes 98312 | tf_op jit(solution)/shard_map/ppermute | solution.py:118
  66.3 1.2 collective-permute-start.24
  68.2 1.2 collective-permute-done.24
  69.4 0.8 collective-permute-start.25
  70.2 1.2 collective-permute-start.26
  71.4 1.6 %collective-permute-start.27 = (f32[32,256]{1,0:T(8,128)S(1)}, f32[32,256]{1,0:T(8,128)S(1)}, u32[]{:S(2)}, u32[]{:S(2)}) collective-permute-start(f32[32,256]{1,0:T(8,128)S(1)} %fusion.11), channel_id=1, source_target_pairs={{0,48},{16,0},{32,16},{48,32},{1,49},{17,1},{33,17},{49,33},{2,50}... | collective-permute-start | bytes 98312 | tf_op jit(solution)/shard_map/ppermute | solution.py:118
  73.1 1.1 collective-permute-done.25
  74.6 3.4 %collective-permute-start.28 = (f32[32,256]{1,0:T(8,128)S(1)}, f32[32,256]{1,0:T(8,128)S(1)}, u32[]{:S(2)}, u32[]{:S(2)}) collective-permute-start(f32[32,256]{1,0:T(8,128)S(1)} %add_add_fusion), channel_id=1, source_target_pairs={{0,8},{8,0},{1,9},{9,1},{2,10},{10,2},{3,11},{11,3},{4,12},{12,4},... | collective-permute-start | bytes 98312 | tf_op jit(solution)/shard_map/ppermute | solution.py:118
  78.3 3.5 %collective-permute-start.16 = (f32[128,256]{1,0:T(8,128)S(1)}, f32[128,256]{1,0:T(8,128)S(1)}, u32[]{:S(2)}, u32[]{:S(2)}) collective-permute-start(f32[128,256]{1,0:T(8,128)S(1)} %get-tuple-element.11), channel_id=1, source_target_pairs={{0,128},{64,192},{128,0},{192,64},{1,129},{65,193},{129,1},{193,65... | collective-permute-start | bytes 393224 | tf_op jit(solution)/shard_map/ppermute | solution.py:118
  81.8 1.8 %collective-permute-start.29 = (f32[64,256]{1,0:T(8,128)S(1)}, f32[64,256]{1,0:T(8,128)S(1)}, u32[]{:S(2)}, u32[]{:S(2)}) collective-permute-start(f32[64,256]{1,0:T(8,128)S(1)} %maximum_select_fusion.1.refs_0_), channel_id=1, source_target_pairs={{0,64},{64,128},{128,192},{192,0},{1,65},{65,129},{129,193},{193,1... | collective-permute-start | bytes 196616 | tf_op jit(solution)/shard_map/ppermute | solution.py:118
  83.7 0.8 collective-permute-done.15
  84.5 1.6 %collective-permute-start.31 = (f32[64,256]{1,0:T(8,128)S(1)}, f32[64,256]{1,0:T(8,128)S(1)}, u32[]{:S(2)}, u32[]{:S(2)}) collective-permute-start(f32[64,256]{1,0:T(8,128)S(1)} %maximum_select_fusion.1.refs_0_), channel_id=1, source_target_pairs={{0,192},{64,0},{128,64},{192,128},{1,193},{65,1},{129,65},{193,129... | collective-permute-start | bytes 196616 | tf_op jit(solution)/shard_map/ppermute | solution.py:118
  86.1 2.1 %collective-permute-done.16 = f32[128,256]{1,0:T(8,128)S(1)} collective-permute-done((f32[128,256]{1,0:T(8,128)S(1)}, f32[128,256]{1,0:T(8,128)S(1)}, u32[]{:S(2)}, u32[]{:S(2)}) %collective-permute-start.16) | collective-permute-done | bytes 131104 | tf_op jit(solution)/shard_map/ppermute | solution.py:118
  88.3 1.6 %collective-permute-start.18 = (f32[32,256]{1,0:T(8,128)S(1)}, f32[32,256]{1,0:T(8,128)S(1)}, u32[]{:S(2)}, u32[]{:S(2)}) collective-permute-start(f32[32,256]{1,0:T(8,128)S(1)} %get-tuple-element.18), channel_id=1, source_target_pairs={{0,16},{16,32},{32,48},{48,0},{1,17},{17,33},{33,49},{49,1},{2,18}... | collective-permute-start | bytes 98312 | tf_op jit(solution)/shard_map/ppermute | solution.py:118
  89.9 2.1 %collective-permute-start.19 = (f32[32,256]{1,0:T(8,128)S(1)}, f32[32,256]{1,0:T(8,128)S(1)}, u32[]{:S(2)}, u32[]{:S(2)}) collective-permute-start(f32[32,256]{1,0:T(8,128)S(1)} %get-tuple-element.20), channel_id=1, source_target_pairs={{0,32},{16,48},{32,0},{48,16},{1,33},{17,49},{33,1},{49,17},{2,34}... | collective-permute-start | bytes 98312 | tf_op jit(solution)/shard_map/ppermute | solution.py:118
  91.9 1.0 collective-permute-start.20
  93.0 8.2 %inverse.3 = f32[256,256]{1,0:T(8,128)S(1)} custom-call(f32[64,256]{1,0:T(8,128)S(1)} %maximum_select_fusion.1.refs_0_, f32[64,256]{1,0:T(8,128)S(1)} %collective-permute-done.29.refs_1_, f32[64,256]{1,0:T(8,128)S(1)} %collective-permute-done.30.refs_2_, f32[64,256]{1,0:T(8,128)S(1)} %collective-permute-done.31.refs_3_, ...), custom_call_target="tpu_custom_call" | custom-call | flops 201326592 | bytes 524288 | tf_op jit(solution)/shard_map/inverse/pallas_call | solution.py:95
  101.5 14.3 %all_to_all.10 = bf16[16,32,256]{2,1,0:T(8,128)(2,1)S(1)} all-to-all(bf16[16,32,256]{2,1,0:T(8,128)(2,1)S(1)} %broadcast_in_dim.4), channel_id=1, replica_groups=mesh['x'=4,'zl'=4,'core'=2,'zh'=2,'y'=4] {'x','zl'}, dimensions={0} | all-to-all | bytes 524288 | tf_op jit(solution)/shard_map/all_to_all | solution.py:108
  115.9 2.2 %collective-permute-start.32 = (bf16[512,256]{1,0:T(8,128)(2,1)S(1)}, bf16[512,256]{1,0:T(8,128)(2,1)S(1)}, u32[]{:S(2)}, u32[]{:S(2)}) collective-permute-start(bf16[512,256]{1,0:T(8,128)(2,1)S(1)} %bitcast.91), channel_id=1, source_target_pairs={{0,8},{8,0},{1,9},{9,1},{2,10},{10,2},{3,11},{11,3},{4,12},{12,4},... | collective-permute-start | bytes 786440 | tf_op jit(solution)/shard_map/ppermute | solution.py:118
  118.0 1.2 collective-permute-done.32
  119.4 5.9 %multiply_reduce_fusion.1 = f32[16,256]{1,0:T(8,128)S(1)} fusion(bf16[16,256,1024]{2,1,0:T(8,128)(2,1)} %param.3, f32[256,256]{1,0:T(8,128)S(1)} %get-tuple-element.7, bf16[1024,256]{1,0:T(8,128)(2,1)S(1)} %maximum_select_fusion), kind=kOutput, calls=%fused_computation.1 | convolution fusion | flops 2149576704 | bytes 9191424 | tf_op jit(solution)/shard_map/ijk,kr->ijr/dot_general | solution.py:222
  125.9 0.8 collective-permute-done.33
  126.7 1.8 %collective-permute-start.35 = (f32[16,256]{1,0:T(8,128)S(1)}, f32[16,256]{1,0:T(8,128)S(1)}, u32[]{:S(2)}, u32[]{:S(2)}) collective-permute-start(f32[16,256]{1,0:T(8,128)S(1)} %add.201), channel_id=1, source_target_pairs={{0,128},{64,192},{128,0},{192,64},{1,129},{65,193},{129,1},{193,65... | collective-permute-start | bytes 49160 | tf_op jit(solution)/shard_map/ppermute | solution.py:118
  128.5 0.9 collective-permute-start.36
  129.4 1.1 collective-permute-done.34
  130.9 0.7 collective-permute-done.36
  131.6 16.7 %all_to_all.11 = bf16[32,16,256]{2,1,0:T(8,128)(2,1)S(1)} all-to-all(bf16[32,16,256]{2,1,0:T(8,128)(2,1)S(1)} %broadcast_in_dim.5), channel_id=1, replica_groups=mesh['x'=4,'zl'=4,'core'=2,'zh'=2,'y'=4] {'zl','zh','y'}, dimensions={0} | all-to-all | bytes 524288 | tf_op jit(solution)/shard_map/all_to_all | solution.py:108
  (71 shorter events, 5.5 us)
Async XLA Ops:
  0.6 1.0 copy-start
  2.1 13.6 %collective-permute-start.4 = (f32[64,256]{1,0:T(8,128)S(1)}, f32[64,256]{1,0:T(8,128)S(1)}, u32[]{:S(2)}, u32[]{:S(2)}) collective-permute-start(f32[64,256]{1,0:T(8,128)S(1)} %get-tuple-element.15), channel_id=1, source_target_pairs={{0,1},{1,2},{2,3},{3,0},{4,5},{5,6},{6,7},{7,4},{8,9},{9,10},{10,1... | collective-permute-start | bytes 196616 | tf_op jit(solution)/shard_map/ppermute | solution.py:118
  4.3 13.1 %collective-permute-start.5 = (f32[64,256]{1,0:T(8,128)S(1)}, f32[64,256]{1,0:T(8,128)S(1)}, u32[]{:S(2)}, u32[]{:S(2)}) collective-permute-start(f32[64,256]{1,0:T(8,128)S(1)} %get-tuple-element.17), channel_id=1, source_target_pairs={{0,2},{1,3},{2,0},{3,1},{4,6},{5,7},{6,4},{7,5},{8,10},{9,11},{10,... | collective-permute-start | bytes 196616 | tf_op jit(solution)/shard_map/ppermute | solution.py:118
  6.9 10.5 %collective-permute-start.6 = (f32[64,256]{1,0:T(8,128)S(1)}, f32[64,256]{1,0:T(8,128)S(1)}, u32[]{:S(2)}, u32[]{:S(2)}) collective-permute-start(f32[64,256]{1,0:T(8,128)S(1)} %get-tuple-element.16), channel_id=1, source_target_pairs={{0,3},{1,0},{2,1},{3,2},{4,7},{5,4},{6,5},{7,6},{8,11},{9,8},{10,9... | collective-permute-start | bytes 196616 | tf_op jit(solution)/shard_map/ppermute | solution.py:118
  8.6 22.2 %copy-start.3 = (bf16[16,256]{1,0:T(8,128)(2,1)S(1)}, bf16[16,256]{1,0:T(8,128)(2,1)}, u32[]{:S(2)}) copy-start(bf16[16,256]{1,0:T(8,128)(2,1)} %param.4) | copy-start | bytes 24580
  14.4 10.0 %collective-permute-start = (f32[64,256]{1,0:T(8,128)S(1)}, f32[64,256]{1,0:T(8,128)S(1)}, u32[]{:S(2)}, u32[]{:S(2)}) collective-permute-start(f32[64,256]{1,0:T(8,128)S(1)} %get-tuple-element.12), channel_id=1, source_target_pairs={{0,1},{1,2},{2,3},{3,0},{4,5},{5,6},{6,7},{7,4},{8,9},{9,10},{10,1... | collective-permute-start | bytes 196616 | tf_op jit(solution)/shard_map/ppermute | solution.py:118
  14.9 9.5 %collective-permute-start.1 = (f32[64,256]{1,0:T(8,128)S(1)}, f32[64,256]{1,0:T(8,128)S(1)}, u32[]{:S(2)}, u32[]{:S(2)}) collective-permute-start(f32[64,256]{1,0:T(8,128)S(1)} %get-tuple-element.14), channel_id=1, source_target_pairs={{0,2},{1,3},{2,0},{3,1},{4,6},{5,7},{6,4},{7,5},{8,10},{9,11},{10,... | collective-permute-start | bytes 196616 | tf_op jit(solution)/shard_map/ppermute | solution.py:118
  15.7 8.7 %collective-permute-start.2 = (f32[64,256]{1,0:T(8,128)S(1)}, f32[64,256]{1,0:T(8,128)S(1)}, u32[]{:S(2)}, u32[]{:S(2)}) collective-permute-start(f32[64,256]{1,0:T(8,128)S(1)} %get-tuple-element.13), channel_id=1, source_target_pairs={{0,3},{1,0},{2,1},{3,2},{4,7},{5,4},{6,5},{7,6},{8,11},{9,8},{10,9... | collective-permute-start | bytes 196616 | tf_op jit(solution)/shard_map/ppermute | solution.py:118
  17.4 10.0 %collective-permute-start.7 = (f32[64,256]{1,0:T(8,128)S(1)}, f32[64,256]{1,0:T(8,128)S(1)}, u32[]{:S(2)}, u32[]{:S(2)}) collective-permute-start(f32[64,256]{1,0:T(8,128)S(1)} %fusion.6), channel_id=1, source_target_pairs={{0,4},{4,0},{1,5},{5,1},{2,6},{6,2},{3,7},{7,3},{8,12},{12,8},{9,1... | collective-permute-start | bytes 196616 | tf_op jit(solution)/shard_map/ppermute | solution.py:118
  24.5 18.5 %collective-permute-start.3 = (f32[64,256]{1,0:T(8,128)S(1)}, f32[64,256]{1,0:T(8,128)S(1)}, u32[]{:S(2)}, u32[]{:S(2)}) collective-permute-start(f32[64,256]{1,0:T(8,128)S(1)} %fusion.8), channel_id=1, source_target_pairs={{0,4},{4,0},{1,5},{5,1},{2,6},{6,2},{3,7},{7,3},{8,12},{12,8},{9,1... | collective-permute-start | bytes 196616 | tf_op jit(solution)/shard_map/ppermute | solution.py:118
  27.4 3.6 %collective-permute-start.10 = (f32[64,256]{1,0:T(8,128)S(1)}, f32[64,256]{1,0:T(8,128)S(1)}, u32[]{:S(2)}, u32[]{:S(2)}) collective-permute-start(f32[64,256]{1,0:T(8,128)S(1)} %add.172.refs_0_), channel_id=1, source_target_pairs={{0,3},{1,0},{2,1},{3,2},{4,7},{5,4},{6,5},{7,6},{8,11},{9,8},{10,9... | collective-permute-start | bytes 196616 | tf_op jit(solution)/shard_map/ppermute | solution.py:118
  29.5 5.1 %collective-permute-start.8 = (f32[64,256]{1,0:T(8,128)S(1)}, f32[64,256]{1,0:T(8,128)S(1)}, u32[]{:S(2)}, u32[]{:S(2)}) collective-permute-start(f32[64,256]{1,0:T(8,128)S(1)} %add.172.refs_0_), channel_id=1, source_target_pairs={{0,1},{1,2},{2,3},{3,0},{4,5},{5,6},{6,7},{7,4},{8,9},{9,10},{10,1... | collective-permute-start | bytes 196616 | tf_op jit(solution)/shard_map/ppermute | solution.py:118
  29.6 5.1 %collective-permute-start.9 = (f32[64,256]{1,0:T(8,128)S(1)}, f32[64,256]{1,0:T(8,128)S(1)}, u32[]{:S(2)}, u32[]{:S(2)}) collective-permute-start(f32[64,256]{1,0:T(8,128)S(1)} %add.172.refs_0_), channel_id=1, source_target_pairs={{0,2},{1,3},{2,0},{3,1},{4,6},{5,7},{6,4},{7,5},{8,10},{9,11},{10,... | collective-permute-start | bytes 196616 | tf_op jit(solution)/shard_map/ppermute | solution.py:118
  43.2 4.1 %collective-permute-start.11 = (bf16[64,256]{1,0:T(8,128)(2,1)S(1)}, bf16[64,256]{1,0:T(8,128)(2,1)S(1)}, u32[]{:S(2)}, u32[]{:S(2)}) collective-permute-start(bf16[64,256]{1,0:T(8,128)(2,1)S(1)} %convolution_convert_fusion), channel_id=1, source_target_pairs={{0,3},{1,2},{2,1},{3,0},{4,7},{5,6},{6,5},{7,4},{8,11},{9,10},{10,... | collective-permute-start | bytes 98312 | tf_op jit(solution)/shard_map/ppermute | solution.py:139
  45.7 4.3 %collective-permute-start.12 = (bf16[64,256]{1,0:T(8,128)(2,1)S(1)}, bf16[64,256]{1,0:T(8,128)(2,1)S(1)}, u32[]{:S(2)}, u32[]{:S(2)}) collective-permute-start(bf16[64,256]{1,0:T(8,128)(2,1)S(1)} %convolution_convert_fusion), channel_id=1, source_target_pairs={{0,2},{1,3},{2,0},{3,1},{4,6},{5,7},{6,4},{7,5},{8,10},{9,11},{10,... | collective-permute-start | bytes 98312 | tf_op jit(solution)/shard_map/ppermute | solution.py:139
  45.7 4.3 %collective-permute-start.13 = (bf16[64,256]{1,0:T(8,128)(2,1)S(1)}, bf16[64,256]{1,0:T(8,128)(2,1)S(1)}, u32[]{:S(2)}, u32[]{:S(2)}) collective-permute-start(bf16[64,256]{1,0:T(8,128)(2,1)S(1)} %convolution_convert_fusion), channel_id=1, source_target_pairs={{0,1},{1,0},{2,3},{3,2},{4,5},{5,4},{6,7},{7,6},{8,9},{9,8},{10,11... | collective-permute-start | bytes 98312 | tf_op jit(solution)/shard_map/ppermute | solution.py:139
  50.1 12.3 %copy-start.1 = (bf16[256,256]{1,0:T(8,128)(2,1)}, bf16[256,256]{1,0:T(8,128)(2,1)S(1)}, u32[]{:S(2)}) copy-start(bf16[256,256]{1,0:T(8,128)(2,1)S(1)} %get-tuple-element.8) | copy-start | bytes 393220
  50.3 12.2 %collective-permute-start.21 = (f32[128,256]{1,0:T(8,128)S(1)}, f32[128,256]{1,0:T(8,128)S(1)}, u32[]{:S(2)}, u32[]{:S(2)}) collective-permute-start(f32[128,256]{1,0:T(8,128)S(1)} %slice_select_fusion.1), channel_id=1, source_target_pairs={{0,8},{8,0},{1,9},{9,1},{2,10},{10,2},{3,11},{11,3},{4,12},{12,4},... | collective-permute-start | bytes 393224 | tf_op jit(solution)/shard_map/ppermute | solution.py:118
  62.4 15.6 %collective-permute-start.14 = (f32[512,256]{1,0:T(8,128)S(1)}, f32[512,256]{1,0:T(8,128)S(1)}, u32[]{:S(2)}, u32[]{:S(2)}) collective-permute-start(f32[512,256]{1,0:T(8,128)S(1)} %slice_select_fusion), channel_id=1, source_target_pairs={{0,8},{8,0},{1,9},{9,1},{2,10},{10,2},{3,11},{11,3},{4,12},{12,4},... | collective-permute-start | bytes 1572872 | tf_op jit(solution)/shard_map/ppermute | solution.py:118
  62.6 4.9 %collective-permute-start.22 = (f32[32,256]{1,0:T(8,128)S(1)}, f32[32,256]{1,0:T(8,128)S(1)}, u32[]{:S(2)}, u32[]{:S(2)}) collective-permute-start(f32[32,256]{1,0:T(8,128)S(1)} %get-tuple-element.21), channel_id=1, source_target_pairs={{0,64},{64,128},{128,192},{192,0},{1,65},{65,129},{129,193},{193,1... | collective-permute-start | bytes 98312 | tf_op jit(solution)/shard_map/ppermute | solution.py:118
  63.9 4.3 %collective-permute-start.23 = (f32[32,256]{1,0:T(8,128)S(1)}, f32[32,256]{1,0:T(8,128)S(1)}, u32[]{:S(2)}, u32[]{:S(2)}) collective-permute-start(f32[32,256]{1,0:T(8,128)S(1)} %get-tuple-element.23), channel_id=1, source_target_pairs={{0,128},{64,192},{128,0},{192,64},{1,129},{65,193},{129,1},{193,65... | collective-permute-start | bytes 98312 | tf_op jit(solution)/shard_map/ppermute | solution.py:118
  66.3 3.1 %collective-permute-start.24 = (f32[32,256]{1,0:T(8,128)S(1)}, f32[32,256]{1,0:T(8,128)S(1)}, u32[]{:S(2)}, u32[]{:S(2)}) collective-permute-start(f32[32,256]{1,0:T(8,128)S(1)} %get-tuple-element.22), channel_id=1, source_target_pairs={{0,192},{64,0},{128,64},{192,128},{1,193},{65,1},{129,65},{193,129... | collective-permute-start | bytes 98312 | tf_op jit(solution)/shard_map/ppermute | solution.py:118
  69.4 4.8 %collective-permute-start.25 = (f32[32,256]{1,0:T(8,128)S(1)}, f32[32,256]{1,0:T(8,128)S(1)}, u32[]{:S(2)}, u32[]{:S(2)}) collective-permute-start(f32[32,256]{1,0:T(8,128)S(1)} %fusion.11), channel_id=1, source_target_pairs={{0,16},{16,32},{32,48},{48,0},{1,17},{17,33},{33,49},{49,1},{2,18}... | collective-permute-start | bytes 98312 | tf_op jit(solution)/shard_map/ppermute | solution.py:118
  70.2 4.4 %collective-permute-start.26 = (f32[32,256]{1,0:T(8,128)S(1)}, f32[32,256]{1,0:T(8,128)S(1)}, u32[]{:S(2)}, u32[]{:S(2)}) collective-permute-start(f32[32,256]{1,0:T(8,128)S(1)} %fusion.11), channel_id=1, source_target_pairs={{0,32},{16,48},{32,0},{48,16},{1,33},{17,49},{33,1},{49,17},{2,34}... | collective-permute-start | bytes 98312 | tf_op jit(solution)/shard_map/ppermute | solution.py:118
  71.4 3.2 %collective-permute-start.27 = (f32[32,256]{1,0:T(8,128)S(1)}, f32[32,256]{1,0:T(8,128)S(1)}, u32[]{:S(2)}, u32[]{:S(2)}) collective-permute-start(f32[32,256]{1,0:T(8,128)S(1)} %fusion.11), channel_id=1, source_target_pairs={{0,48},{16,0},{32,16},{48,32},{1,49},{17,1},{33,17},{49,33},{2,50}... | collective-permute-start | bytes 98312 | tf_op jit(solution)/shard_map/ppermute | solution.py:118
  74.6 7.2 %collective-permute-start.28 = (f32[32,256]{1,0:T(8,128)S(1)}, f32[32,256]{1,0:T(8,128)S(1)}, u32[]{:S(2)}, u32[]{:S(2)}) collective-permute-start(f32[32,256]{1,0:T(8,128)S(1)} %add_add_fusion), channel_id=1, source_target_pairs={{0,8},{8,0},{1,9},{9,1},{2,10},{10,2},{3,11},{11,3},{4,12},{12,4},... | collective-permute-start | bytes 98312 | tf_op jit(solution)/shard_map/ppermute | solution.py:118
  78.2 6.3 %collective-permute-start.15 = (f32[128,256]{1,0:T(8,128)S(1)}, f32[128,256]{1,0:T(8,128)S(1)}, u32[]{:S(2)}, u32[]{:S(2)}) collective-permute-start(f32[128,256]{1,0:T(8,128)S(1)} %get-tuple-element.9), channel_id=1, source_target_pairs={{0,64},{64,128},{128,192},{192,0},{1,65},{65,129},{129,193},{193,1... | collective-permute-start | bytes 393224 | tf_op jit(solution)/shard_map/ppermute | solution.py:118
  78.3 10.0 %collective-permute-start.16 = (f32[128,256]{1,0:T(8,128)S(1)}, f32[128,256]{1,0:T(8,128)S(1)}, u32[]{:S(2)}, u32[]{:S(2)}) collective-permute-start(f32[128,256]{1,0:T(8,128)S(1)} %get-tuple-element.11), channel_id=1, source_target_pairs={{0,128},{64,192},{128,0},{192,64},{1,129},{65,193},{129,1},{193,65... | collective-permute-start | bytes 393224 | tf_op jit(solution)/shard_map/ppermute | solution.py:118
  81.8 6.4 %collective-permute-start.17 = (f32[128,256]{1,0:T(8,128)S(1)}, f32[128,256]{1,0:T(8,128)S(1)}, u32[]{:S(2)}, u32[]{:S(2)}) collective-permute-start(f32[128,256]{1,0:T(8,128)S(1)} %get-tuple-element.10), channel_id=1, source_target_pairs={{0,192},{64,0},{128,64},{192,128},{1,193},{65,1},{129,65},{193,129... | collective-permute-start | bytes 393224 | tf_op jit(solution)/shard_map/ppermute | solution.py:118
  81.8 10.1 %collective-permute-start.29 = (f32[64,256]{1,0:T(8,128)S(1)}, f32[64,256]{1,0:T(8,128)S(1)}, u32[]{:S(2)}, u32[]{:S(2)}) collective-permute-start(f32[64,256]{1,0:T(8,128)S(1)} %maximum_select_fusion.1.refs_0_), channel_id=1, source_target_pairs={{0,64},{64,128},{128,192},{192,0},{1,65},{65,129},{129,193},{193,1... | collective-permute-start | bytes 196616 | tf_op jit(solution)/shard_map/ppermute | solution.py:118
  83.6 9.4 %collective-permute-start.30 = (f32[64,256]{1,0:T(8,128)S(1)}, f32[64,256]{1,0:T(8,128)S(1)}, u32[]{:S(2)}, u32[]{:S(2)}) collective-permute-start(f32[64,256]{1,0:T(8,128)S(1)} %maximum_select_fusion.1.refs_0_), channel_id=1, source_target_pairs={{0,128},{64,192},{128,0},{192,64},{1,129},{65,193},{129,1},{193,65... | collective-permute-start | bytes 196616 | tf_op jit(solution)/shard_map/ppermute | solution.py:118
  84.5 8.5 %collective-permute-start.31 = (f32[64,256]{1,0:T(8,128)S(1)}, f32[64,256]{1,0:T(8,128)S(1)}, u32[]{:S(2)}, u32[]{:S(2)}) collective-permute-start(f32[64,256]{1,0:T(8,128)S(1)} %maximum_select_fusion.1.refs_0_), channel_id=1, source_target_pairs={{0,192},{64,0},{128,64},{192,128},{1,193},{65,1},{129,65},{193,129... | collective-permute-start | bytes 196616 | tf_op jit(solution)/shard_map/ppermute | solution.py:118
  88.3 12.9 %collective-permute-start.18 = (f32[32,256]{1,0:T(8,128)S(1)}, f32[32,256]{1,0:T(8,128)S(1)}, u32[]{:S(2)}, u32[]{:S(2)}) collective-permute-start(f32[32,256]{1,0:T(8,128)S(1)} %get-tuple-element.18), channel_id=1, source_target_pairs={{0,16},{16,32},{32,48},{48,0},{1,17},{17,33},{33,49},{49,1},{2,18}... | collective-permute-start | bytes 98312 | tf_op jit(solution)/shard_map/ppermute | solution.py:118
  89.9 11.4 %collective-permute-start.19 = (f32[32,256]{1,0:T(8,128)S(1)}, f32[32,256]{1,0:T(8,128)S(1)}, u32[]{:S(2)}, u32[]{:S(2)}) collective-permute-start(f32[32,256]{1,0:T(8,128)S(1)} %get-tuple-element.20), channel_id=1, source_target_pairs={{0,32},{16,48},{32,0},{48,16},{1,33},{17,49},{33,1},{49,17},{2,34}... | collective-permute-start | bytes 98312 | tf_op jit(solution)/shard_map/ppermute | solution.py:118
  91.9 9.3 %collective-permute-start.20 = (f32[32,256]{1,0:T(8,128)S(1)}, f32[32,256]{1,0:T(8,128)S(1)}, u32[]{:S(2)}, u32[]{:S(2)}) collective-permute-start(f32[32,256]{1,0:T(8,128)S(1)} %get-tuple-element.19), channel_id=1, source_target_pairs={{0,48},{16,0},{32,16},{48,32},{1,49},{17,1},{33,17},{49,33},{2,50}... | collective-permute-start | bytes 98312 | tf_op jit(solution)/shard_map/ppermute | solution.py:118
  115.9 3.3 %collective-permute-start.32 = (bf16[512,256]{1,0:T(8,128)(2,1)S(1)}, bf16[512,256]{1,0:T(8,128)(2,1)S(1)}, u32[]{:S(2)}, u32[]{:S(2)}) collective-permute-start(bf16[512,256]{1,0:T(8,128)(2,1)S(1)} %bitcast.91), channel_id=1, source_target_pairs={{0,8},{8,0},{1,9},{9,1},{2,10},{10,2},{3,11},{11,3},{4,12},{12,4},... | collective-permute-start | bytes 786440 | tf_op jit(solution)/shard_map/ppermute | solution.py:118
  119.4 5.9 %copy-start.2 = (bf16[1024,256]{1,0:T(8,128)(2,1)}, bf16[1024,256]{1,0:T(8,128)(2,1)S(1)}, u32[]{:S(2)}) copy-start(bf16[1024,256]{1,0:T(8,128)(2,1)S(1)} %maximum_select_fusion) | copy-start | bytes 1572868
  125.4 1.3 collective-permute-start.33
  126.7 3.8 %collective-permute-start.34 = (f32[16,256]{1,0:T(8,128)S(1)}, f32[16,256]{1,0:T(8,128)S(1)}, u32[]{:S(2)}, u32[]{:S(2)}) collective-permute-start(f32[16,256]{1,0:T(8,128)S(1)} %add.201), channel_id=1, source_target_pairs={{0,64},{64,128},{128,192},{192,0},{1,65},{65,129},{129,193},{193,1... | collective-permute-start | bytes 49160 | tf_op jit(solution)/shard_map/ppermute | solution.py:118
  126.7 4.2 %collective-permute-start.35 = (f32[16,256]{1,0:T(8,128)S(1)}, f32[16,256]{1,0:T(8,128)S(1)}, u32[]{:S(2)}, u32[]{:S(2)}) collective-permute-start(f32[16,256]{1,0:T(8,128)S(1)} %add.201), channel_id=1, source_target_pairs={{0,128},{64,192},{128,0},{192,64},{1,129},{65,193},{129,1},{193,65... | collective-permute-start | bytes 49160 | tf_op jit(solution)/shard_map/ppermute | solution.py:118
  128.5 3.1 %collective-permute-start.36 = (f32[16,256]{1,0:T(8,128)S(1)}, f32[16,256]{1,0:T(8,128)S(1)}, u32[]{:S(2)}, u32[]{:S(2)}) collective-permute-start(f32[16,256]{1,0:T(8,128)S(1)} %add.201), channel_id=1, source_target_pairs={{0,192},{64,0},{128,64},{192,128},{1,193},{65,1},{129,65},{193,129... | collective-permute-start | bytes 49160 | tf_op jit(solution)/shard_map/ppermute | solution.py:118

commit v10 on v9

--- a/solution.py
+++ b/solution.py
@@ -11,7 +11,6 @@
 ridge = 0.5
 B = 16
 WIDE = ("x", "zl", "core")
-CHIP = ("x", "zl")
 NARROW = ("zh", "y")
 HIGHEST = lax.Precision.HIGHEST
 
@@ -108,11 +107,6 @@
     return lax.all_to_all(x, axes, 0, 0, tiled=True)
 
 
-def gather(x, axes):
-    n = lax.axis_size(axes)
-    return exchange(jnp.broadcast_to(x[None], (n,) + x.shape), axes).reshape(n * x.shape[0], x.shape[1])
-
-
 def shift(x, axis, d):
     n = lax.axis_size(axis)
     return lax.ppermute(x, axis, [(s, (s + d) % n) for s in range(n)])
@@ -122,9 +116,11 @@
     n = lax.axis_size(axis)
     me = lax.axis_index(axis)
     blocks = x.reshape(n, x.shape[0] // n, x.shape[1])
-    take = lambda d: lax.dynamic_index_in_dim(blocks, lax.rem(me + d, n), 0, keepdims=False)
-    arrived = [shift(take(d), axis, d) for d in range(1, n)]
-    return sum(arrived, take(0))
+    own, *sent = [
+        lax.dynamic_index_in_dim(blocks, lax.rem(me + d, n), 0, keepdims=False) for d in range(n)
+    ]
+    arrived = [shift(block, axis, d + 1) for d, block in enumerate(sent)]
+    return sum(arrived, own)
 
 
 def ring_sum(x, axis):
@@ -214,9 +210,11 @@
     mine, other = keep(partial_third, core)
     mine = mine + shift(other, "core", 1)
     mine = ring_scatter(mine, "x")
-    mttkrp_third = ring_scatter(mine, "zl")
+    mttkrp_third = ring_sum(mine, "zl")
     third_solution = jnp.dot(mttkrp_third, inverse_third, precision=HIGHEST)
-    mine = gather(third_solution.astype(jnp.bfloat16), CHIP)
+    block = third_solution.astype(jnp.bfloat16)
+    copies = jnp.broadcast_to(block[None], (lax.axis_size("x"),) + block.shape)
+    mine = exchange(copies, "x").reshape(-1, block.shape[1])
     third_new = join(mine, shift(mine, "core", 1), core)
 
     back = jnp.einsum("ijk,kr->ijr", tensor, third_new, preferred_element_type=jnp.float32)

time: 152 us -> 153 us (level)
  blocking collectives: 31.1 us -> 26 us
  waiting for transfers between devices: 17.6 us -> 22 us
  starting transfers between devices: 60.9 us -> 62.8 us
    all_to_all x2, blocking collectives: 31.1 us -> 26 us  [exchange(): return lax.all_to_all(x, axes, 0, 0, tiled=True)]
    ppermute x34, waiting for transfers between devices: 14.2 us -> 18.6 us  [shift(): return lax.ppermute(x, axis, [(s, (s + d) % n) for s in range(n)])]
    ppermute x34, starting transfers between devices: 57.5 us -> 59.4 us  [shift(): return lax.ppermute(x, axis, [(s, (s + d) % n) for s in range(n)])]
  transfers between devices with their start and end apart: 37 -> 37, of which waited for: 14 -> 16; matrix products, arithmetic and copies ran while one was open for 9% -> 9% of each run, Pallas kernels for 11% -> 11%
where the time goes in v10:
time: 153 us; the launch traced here: 150 us
  starting transfers between devices  62.8 us (41%)
  blocking collectives  26 us (17%)
  waiting for transfers between devices  22 us (14%)
  matrix products  18.8 us (12%)
  Pallas kernels  16.4 us (11%)
  other arithmetic  1.96 us (1%)
    ppermute x34, starting transfers between devices, shift(): return lax.ppermute(x, axis, [(s, (s + d) % n) for s in range(n)])  59.4 us
    all_to_all x2, blocking collectives, exchange(): return lax.all_to_all(x, axes, 0, 0, tiled=True)  26 us
    ppermute x34, waiting for transfers between devices, shift(): return lax.ppermute(x, axis, [(s, (s + d) % n) for s in range(n)])  18.6 us
    pallas_call x2, Pallas kernels, inverse(): pl.pallas_call(functools.partial(inverse_kernel, places, total), out_shap...  16.4 us
    dot_general x1, matrix products, on_device(): jnp.einsum('ijk,kr->ijr', tensor, third_new, preferred_element_type=jnp.f...  5.92 us
    dot_general x1, matrix products, on_device(): jnp.einsum('ijk,jr->ikr', tensor, second_factor, preferred_element_type=j...  5.87 us
    dot_general x1, matrix products, on_device(): jnp.einsum('ijk,kr->ijr', tensor, third_factor, preferred_element_type=jn...  5.75 us
    ppermute x3, waiting for transfers between devices, pair(): lax.ppermute(x, axis, [(s, s ^ d) for s in range(lax.axis_size(axis))])  3.41 us
  transfers between devices with their start and end apart: 37, of which 16 were waited for; matrix products, arithmetic and copies ran while one was open for 9% of the time, Pallas kernels for 11%

profile of v10, /device:TPU:1, one launch (start us, length us, event | category | flops | bytes accessed | tf_op | source)
XLA Modules:
  0.0 150.2 jit_solution(14038224255574183099)
XLA Ops:
  0.7 1.0 copy-done
  2.1 2.2 %collective-permute-start.4 = (f32[64,256]{1,0:T(8,128)S(1)}, f32[64,256]{1,0:T(8,128)S(1)}, u32[]{:S(2)}, u32[]{:S(2)}) collective-permute-start(f32[64,256]{1,0:T(8,128)S(1)} %get-tuple-element.15), channel_id=1, source_target_pairs={{0,1},{1,2},{2,3},{3,0},{4,5},{5,6},{6,7},{7,4},{8,9},{9,10},{10,1... | collective-permute-start | bytes 196616 | tf_op jit(solution)/shard_map/ppermute | solution.py:112
  4.3 2.6 %collective-permute-start.5 = (f32[64,256]{1,0:T(8,128)S(1)}, f32[64,256]{1,0:T(8,128)S(1)}, u32[]{:S(2)}, u32[]{:S(2)}) collective-permute-start(f32[64,256]{1,0:T(8,128)S(1)} %get-tuple-element.17), channel_id=1, source_target_pairs={{0,2},{1,3},{2,0},{3,1},{4,6},{5,7},{6,4},{7,5},{8,10},{9,11},{10,... | collective-permute-start | bytes 196616 | tf_op jit(solution)/shard_map/ppermute | solution.py:112
  6.9 1.1 collective-permute-start.6
  7.9 0.7 convert_multiply_fusion
  8.7 5.7 %multiply_reduce_fusion.2 = f32[256,256]{1,0:T(8,128)S(1)} fusion(bf16[16,256,1024]{2,1,0:T(8,128)(2,1)} %param.3, f32[16,256]{1,0:T(8,128)S(1)} %convert_multiply_fusion, bf16[1024,256]{1,0:T(8,128)(2,1)S(1)} %copy-done), kind=kOutput, calls=%fused_computation.2 | convolution fusion | flops 2149515264 | bytes 9191424 | tf_op jit(solution)/shard_map/ijk,kr->ijr/dot_general | solution.py:191
  14.9 0.8 collective-permute-start.1
  15.7 1.7 %collective-permute-start.2 = (f32[64,256]{1,0:T(8,128)S(1)}, f32[64,256]{1,0:T(8,128)S(1)}, u32[]{:S(2)}, u32[]{:S(2)}) collective-permute-start(f32[64,256]{1,0:T(8,128)S(1)} %get-tuple-element.13), channel_id=1, source_target_pairs={{0,3},{1,0},{2,1},{3,2},{4,7},{5,4},{6,5},{7,6},{8,11},{9,8},{10,9... | collective-permute-start | bytes 196616 | tf_op jit(solution)/shard_map/ppermute | solution.py:112
  17.4 7.0 %collective-permute-start.7 = (f32[64,256]{1,0:T(8,128)S(1)}, f32[64,256]{1,0:T(8,128)S(1)}, u32[]{:S(2)}, u32[]{:S(2)}) collective-permute-start(f32[64,256]{1,0:T(8,128)S(1)} %fusion.9), channel_id=1, source_target_pairs={{0,4},{4,0},{1,5},{5,1},{2,6},{6,2},{3,7},{7,3},{8,12},{12,8},{9,1... | collective-permute-start | bytes 196616 | tf_op jit(solution)/shard_map/ppermute | solution.py:112
  24.5 3.0 %collective-permute-start.3 = (f32[64,256]{1,0:T(8,128)S(1)}, f32[64,256]{1,0:T(8,128)S(1)}, u32[]{:S(2)}, u32[]{:S(2)}) collective-permute-start(f32[64,256]{1,0:T(8,128)S(1)} %fusion.11), channel_id=1, source_target_pairs={{0,4},{4,0},{1,5},{5,1},{2,6},{6,2},{3,7},{7,3},{8,12},{12,8},{9,1... | collective-permute-start | bytes 196616 | tf_op jit(solution)/shard_map/ppermute | solution.py:112
  27.5 2.1 %collective-permute-start.10 = (f32[64,256]{1,0:T(8,128)S(1)}, f32[64,256]{1,0:T(8,128)S(1)}, u32[]{:S(2)}, u32[]{:S(2)}) collective-permute-start(f32[64,256]{1,0:T(8,128)S(1)} %add.151.refs_0_), channel_id=1, source_target_pairs={{0,3},{1,0},{2,1},{3,2},{4,7},{5,4},{6,5},{7,6},{8,11},{9,8},{10,9... | collective-permute-start | bytes 196616 | tf_op jit(solution)/shard_map/ppermute | solution.py:112
  29.6 1.3 collective-permute-start.9
  31.1 3.6 %collective-permute-done.8.refs_1_ = f32[64,256]{1,0:T(8,128)S(1)} collective-permute-done((f32[64,256]{1,0:T(8,128)S(1)}, f32[64,256]{1,0:T(8,128)S(1)}, u32[]{:S(2)}, u32[]{:S(2)}) %collective-permute-start.8) | collective-permute-done | bytes 65568 | tf_op jit(solution)/shard_map/ppermute | solution.py:112
  34.7 8.2 %inverse.2 = f32[256,256]{1,0:T(8,128)S(1)} custom-call(f32[64,256]{1,0:T(8,128)S(1)} %add.151.refs_0_, f32[64,256]{1,0:T(8,128)S(1)} %collective-permute-done.8.refs_1_, f32[64,256]{1,0:T(8,128)S(1)} %collective-permute-done.9.refs_2_, f32[64,256]{1,0:T(8,128)S(1)} %collective-permute-done.10.refs_3_, f32[256,256]{1,0:T(8,128)S(1)} %convolution_multiply_fusion.refs_4_), custom_call_target="tpu_custom_call" | custom-call | flops 201326592 | bytes 524288 | tf_op jit(solution)/shard_map/inverse/pallas_call | solution.py:94
  43.2 2.5 %collective-permute-start.11 = (bf16[64,256]{1,0:T(8,128)(2,1)S(1)}, bf16[64,256]{1,0:T(8,128)(2,1)S(1)}, u32[]{:S(2)}, u32[]{:S(2)}) collective-permute-start(bf16[64,256]{1,0:T(8,128)(2,1)S(1)} %convolution_convert_fusion.1), channel_id=1, source_target_pairs={{0,3},{1,2},{2,1},{3,0},{4,7},{5,6},{6,5},{7,4},{8,11},{9,10},{10,... | collective-permute-start | bytes 98312 | tf_op jit(solution)/shard_map/ppermute | solution.py:135
  45.7 0.9 collective-permute-start.13
  46.6 0.7 collective-permute-done.11
  47.3 2.8 %collective-permute-done.12 = bf16[64,256]{1,0:T(8,128)(2,1)S(1)} collective-permute-done((bf16[64,256]{1,0:T(8,128)(2,1)S(1)}, bf16[64,256]{1,0:T(8,128)(2,1)S(1)}, u32[]{:S(2)}, u32[]{:S(2)}) %collective-permute-start.12) | collective-permute-done | bytes 32800 | tf_op jit(solution)/shard_map/ppermute | solution.py:135
  50.3 6.1 %collective-permute-start.21 = (f32[128,256]{1,0:T(8,128)S(1)}, f32[128,256]{1,0:T(8,128)S(1)}, u32[]{:S(2)}, u32[]{:S(2)}) collective-permute-start(f32[128,256]{1,0:T(8,128)S(1)} %slice_select_fusion.1), channel_id=1, source_target_pairs={{0,8},{8,0},{1,9},{9,1},{2,10},{10,2},{3,11},{11,3},{4,12},{12,4},... | collective-permute-start | bytes 393224 | tf_op jit(solution)/shard_map/ppermute | solution.py:112
  56.5 5.9 %multiply_reduce_fusion = f32[1024,256]{1,0:T(8,128)S(1)} fusion(bf16[16,256,1024]{2,1,0:T(8,128)(2,1)} %param.3, f32[16,256]{1,0:T(8,128)S(1)} %convert_multiply_fusion, bf16[256,256]{1,0:T(8,128)(2,1)S(1)} %get-tuple-element.8), kind=kOutput, calls=%fused_computation | convolution fusion | flops 2155610112 | bytes 9584640 | tf_op jit(solution)/shard_map/ijk,jr->ikr/dot_general | solution.py:208
  62.6 1.3 collective-permute-start.22
  63.9 2.5 %collective-permute-start.23 = (f32[32,256]{1,0:T(8,128)S(1)}, f32[32,256]{1,0:T(8,128)S(1)}, u32[]{:S(2)}, u32[]{:S(2)}) collective-permute-start(f32[32,256]{1,0:T(8,128)S(1)} %get-tuple-element.20), channel_id=1, source_target_pairs={{0,128},{64,192},{128,0},{192,64},{1,129},{65,193},{129,1},{193,65... | collective-permute-start | bytes 98312 | tf_op jit(solution)/shard_map/ppermute | solution.py:112
  66.3 1.2 collective-permute-start.24
  68.2 1.2 collective-permute-done.24
  69.4 0.8 collective-permute-start.25
  70.2 1.2 collective-permute-start.26
  71.4 1.6 %collective-permute-start.27 = (f32[32,256]{1,0:T(8,128)S(1)}, f32[32,256]{1,0:T(8,128)S(1)}, u32[]{:S(2)}, u32[]{:S(2)}) collective-permute-start(f32[32,256]{1,0:T(8,128)S(1)} %fusion.14), channel_id=1, source_target_pairs={{0,48},{16,0},{32,16},{48,32},{1,49},{17,1},{33,17},{49,33},{2,50}... | collective-permute-start | bytes 98312 | tf_op jit(solution)/shard_map/ppermute | solution.py:112
  73.1 1.1 collective-permute-done.25
  74.6 3.4 %collective-permute-start.28 = (f32[32,256]{1,0:T(8,128)S(1)}, f32[32,256]{1,0:T(8,128)S(1)}, u32[]{:S(2)}, u32[]{:S(2)}) collective-permute-start(f32[32,256]{1,0:T(8,128)S(1)} %add_add_fusion), channel_id=1, source_target_pairs={{0,8},{8,0},{1,9},{9,1},{2,10},{10,2},{3,11},{11,3},{4,12},{12,4},... | collective-permute-start | bytes 98312 | tf_op jit(solution)/shard_map/ppermute | solution.py:112
  78.3 3.5 %collective-permute-start.16 = (f32[128,256]{1,0:T(8,128)S(1)}, f32[128,256]{1,0:T(8,128)S(1)}, u32[]{:S(2)}, u32[]{:S(2)}) collective-permute-start(f32[128,256]{1,0:T(8,128)S(1)} %get-tuple-element.11), channel_id=1, source_target_pairs={{0,128},{64,192},{128,0},{192,64},{1,129},{65,193},{129,1},{193,65... | collective-permute-start | bytes 393224 | tf_op jit(solution)/shard_map/ppermute | solution.py:112
  81.8 1.8 %collective-permute-start.29 = (f32[64,256]{1,0:T(8,128)S(1)}, f32[64,256]{1,0:T(8,128)S(1)}, u32[]{:S(2)}, u32[]{:S(2)}) collective-permute-start(f32[64,256]{1,0:T(8,128)S(1)} %maximum_select_fusion.1.refs_0_), channel_id=1, source_target_pairs={{0,64},{64,128},{128,192},{192,0},{1,65},{65,129},{129,193},{193,1... | collective-permute-start | bytes 196616 | tf_op jit(solution)/shard_map/ppermute | solution.py:112
  83.6 0.9 collective-permute-done.15
  84.5 3.7 %collective-permute-done.16 = f32[128,256]{1,0:T(8,128)S(1)} collective-permute-done((f32[128,256]{1,0:T(8,128)S(1)}, f32[128,256]{1,0:T(8,128)S(1)}, u32[]{:S(2)}, u32[]{:S(2)}) %collective-permute-start.16) | collective-permute-done | bytes 131104 | tf_op jit(solution)/shard_map/ppermute | solution.py:112
  88.3 1.6 %collective-permute-start.18 = (f32[128,256]{1,0:T(8,128)S(1)}, f32[128,256]{1,0:T(8,128)S(1)}, u32[]{:S(2)}, u32[]{:S(2)}) collective-permute-start(f32[128,256]{1,0:T(8,128)S(1)} %fusion.3), channel_id=1, source_target_pairs={{0,16},{16,32},{32,48},{48,0},{1,17},{17,33},{33,49},{49,1},{2,18}... | collective-permute-start | bytes 393224 | tf_op jit(solution)/shard_map/ppermute | solution.py:112
  89.8 2.1 %collective-permute-start.19 = (f32[128,256]{1,0:T(8,128)S(1)}, f32[128,256]{1,0:T(8,128)S(1)}, u32[]{:S(2)}, u32[]{:S(2)}) collective-permute-start(f32[128,256]{1,0:T(8,128)S(1)} %fusion.3), channel_id=1, source_target_pairs={{0,32},{16,48},{32,0},{48,16},{1,33},{17,49},{33,1},{49,17},{2,34}... | collective-permute-start | bytes 393224 | tf_op jit(solution)/shard_map/ppermute | solution.py:112
  92.6 2.5 %collective-permute-start.31 = (f32[64,256]{1,0:T(8,128)S(1)}, f32[64,256]{1,0:T(8,128)S(1)}, u32[]{:S(2)}, u32[]{:S(2)}) collective-permute-start(f32[64,256]{1,0:T(8,128)S(1)} %maximum_select_fusion.1.refs_0_), channel_id=1, source_target_pairs={{0,192},{64,0},{128,64},{192,128},{1,193},{65,1},{129,65},{193,129... | collective-permute-start | bytes 196616 | tf_op jit(solution)/shard_map/ppermute | solution.py:112
  95.1 1.7 %collective-permute-done.30.refs_2_ = f32[64,256]{1,0:T(8,128)S(1)} collective-permute-done((f32[64,256]{1,0:T(8,128)S(1)}, f32[64,256]{1,0:T(8,128)S(1)}, u32[]{:S(2)}, u32[]{:S(2)}) %collective-permute-start.30) | collective-permute-done | bytes 65568 | tf_op jit(solution)/shard_map/ppermute | solution.py:112
  96.8 0.9 collective-permute-done.31.refs_3_
  97.7 8.2 %inverse.3 = f32[256,256]{1,0:T(8,128)S(1)} custom-call(f32[64,256]{1,0:T(8,128)S(1)} %maximum_select_fusion.1.refs_0_, f32[64,256]{1,0:T(8,128)S(1)} %collective-permute-done.29.refs_1_, f32[64,256]{1,0:T(8,128)S(1)} %collective-permute-done.30.refs_2_, f32[64,256]{1,0:T(8,128)S(1)} %collective-permute-done.31.refs_3_, ...), custom_call_target="tpu_custom_call" | custom-call | flops 201326592 | bytes 524288 | tf_op jit(solution)/shard_map/inverse/pallas_call | solution.py:94
  106.3 8.7 %all_to_all.10 = bf16[4,128,256]{2,1,0:T(8,128)(2,1)S(1)} all-to-all(bf16[4,128,256]{2,1,0:T(8,128)(2,1)S(1)} %broadcast_in_dim.4), channel_id=1, replica_groups=mesh['x'=4,'zl'=4,'core'=2,'zh'=2,'y'=4] {'x'}, dimensions={0} | all-to-all | bytes 524288 | tf_op jit(solution)/shard_map/all_to_all | solution.py:107
  115.0 3.6 %collective-permute-start.32 = (bf16[512,256]{1,0:T(8,128)(2,1)S(1)}, bf16[512,256]{1,0:T(8,128)(2,1)S(1)}, u32[]{:S(2)}, u32[]{:S(2)}) collective-permute-start(bf16[512,256]{1,0:T(8,128)(2,1)S(1)} %bitcast.77), channel_id=1, source_target_pairs={{0,8},{8,0},{1,9},{9,1},{2,10},{10,2},{3,11},{11,3},{4,12},{12,4},... | collective-permute-start | bytes 786440 | tf_op jit(solution)/shard_map/ppermute | solution.py:112
  118.6 1.2 collective-permute-done.32
  120.0 5.9 %multiply_reduce_fusion.1 = f32[16,256]{1,0:T(8,128)S(1)} fusion(bf16[16,256,1024]{2,1,0:T(8,128)(2,1)} %param.3, f32[256,256]{1,0:T(8,128)S(1)} %get-tuple-element.7, bf16[1024,256]{1,0:T(8,128)(2,1)S(1)} %maximum_select_fusion), kind=kOutput, calls=%fused_computation.1 | convolution fusion | flops 2149576704 | bytes 9191424 | tf_op jit(solution)/shard_map/ijk,kr->ijr/dot_general | solution.py:220
  126.4 0.8 collective-permute-done.33
  127.6 1.8 %collective-permute-start.35 = (f32[16,256]{1,0:T(8,128)S(1)}, f32[16,256]{1,0:T(8,128)S(1)}, u32[]{:S(2)}, u32[]{:S(2)}) collective-permute-start(f32[16,256]{1,0:T(8,128)S(1)} %add.173), channel_id=1, source_target_pairs={{0,128},{64,192},{128,0},{192,64},{1,129},{65,193},{129,1},{193,65... | collective-permute-start | bytes 49160 | tf_op jit(solution)/shard_map/ppermute | solution.py:112
  129.4 0.7 collective-permute-start.36
  130.0 1.0 collective-permute-done.34
  132.3 17.3 %all_to_all.11 = bf16[32,16,256]{2,1,0:T(8,128)(2,1)S(1)} all-to-all(bf16[32,16,256]{2,1,0:T(8,128)(2,1)S(1)} %broadcast_in_dim.5), channel_id=1, replica_groups=mesh['x'=4,'zl'=4,'core'=2,'zh'=2,'y'=4] {'zl','zh','y'}, dimensions={0} | all-to-all | bytes 524288 | tf_op jit(solution)/shard_map/all_to_all | solution.py:107
  (70 shorter events, 7.1 us)
Async XLA Ops:
  0.6 1.0 copy-start
  2.1 13.6 %collective-permute-start.4 = (f32[64,256]{1,0:T(8,128)S(1)}, f32[64,256]{1,0:T(8,128)S(1)}, u32[]{:S(2)}, u32[]{:S(2)}) collective-permute-start(f32[64,256]{1,0:T(8,128)S(1)} %get-tuple-element.15), channel_id=1, source_target_pairs={{0,1},{1,2},{2,3},{3,0},{4,5},{5,6},{6,7},{7,4},{8,9},{9,10},{10,1... | collective-permute-start | bytes 196616 | tf_op jit(solution)/shard_map/ppermute | solution.py:112
  4.3 13.2 %collective-permute-start.5 = (f32[64,256]{1,0:T(8,128)S(1)}, f32[64,256]{1,0:T(8,128)S(1)}, u32[]{:S(2)}, u32[]{:S(2)}) collective-permute-start(f32[64,256]{1,0:T(8,128)S(1)} %get-tuple-element.17), channel_id=1, source_target_pairs={{0,2},{1,3},{2,0},{3,1},{4,6},{5,7},{6,4},{7,5},{8,10},{9,11},{10,... | collective-permute-start | bytes 196616 | tf_op jit(solution)/shard_map/ppermute | solution.py:112
  6.9 10.5 %collective-permute-start.6 = (f32[64,256]{1,0:T(8,128)S(1)}, f32[64,256]{1,0:T(8,128)S(1)}, u32[]{:S(2)}, u32[]{:S(2)}) collective-permute-start(f32[64,256]{1,0:T(8,128)S(1)} %get-tuple-element.16), channel_id=1, source_target_pairs={{0,3},{1,0},{2,1},{3,2},{4,7},{5,4},{6,5},{7,6},{8,11},{9,8},{10,9... | collective-permute-start | bytes 196616 | tf_op jit(solution)/shard_map/ppermute | solution.py:112
  8.6 22.2 %copy-start.3 = (bf16[16,256]{1,0:T(8,128)(2,1)S(1)}, bf16[16,256]{1,0:T(8,128)(2,1)}, u32[]{:S(2)}) copy-start(bf16[16,256]{1,0:T(8,128)(2,1)} %param.4) | copy-start | bytes 24580
  14.4 10.0 %collective-permute-start = (f32[64,256]{1,0:T(8,128)S(1)}, f32[64,256]{1,0:T(8,128)S(1)}, u32[]{:S(2)}, u32[]{:S(2)}) collective-permute-start(f32[64,256]{1,0:T(8,128)S(1)} %get-tuple-element.12), channel_id=1, source_target_pairs={{0,1},{1,2},{2,3},{3,0},{4,5},{5,6},{6,7},{7,4},{8,9},{9,10},{10,1... | collective-permute-start | bytes 196616 | tf_op jit(solution)/shard_map/ppermute | solution.py:112
  14.9 9.5 %collective-permute-start.1 = (f32[64,256]{1,0:T(8,128)S(1)}, f32[64,256]{1,0:T(8,128)S(1)}, u32[]{:S(2)}, u32[]{:S(2)}) collective-permute-start(f32[64,256]{1,0:T(8,128)S(1)} %get-tuple-element.14), channel_id=1, source_target_pairs={{0,2},{1,3},{2,0},{3,1},{4,6},{5,7},{6,4},{7,5},{8,10},{9,11},{10,... | collective-permute-start | bytes 196616 | tf_op jit(solution)/shard_map/ppermute | solution.py:112
  15.7 8.7 %collective-permute-start.2 = (f32[64,256]{1,0:T(8,128)S(1)}, f32[64,256]{1,0:T(8,128)S(1)}, u32[]{:S(2)}, u32[]{:S(2)}) collective-permute-start(f32[64,256]{1,0:T(8,128)S(1)} %get-tuple-element.13), channel_id=1, source_target_pairs={{0,3},{1,0},{2,1},{3,2},{4,7},{5,4},{6,5},{7,6},{8,11},{9,8},{10,9... | collective-permute-start | bytes 196616 | tf_op jit(solution)/shard_map/ppermute | solution.py:112
  17.4 10.0 %collective-permute-start.7 = (f32[64,256]{1,0:T(8,128)S(1)}, f32[64,256]{1,0:T(8,128)S(1)}, u32[]{:S(2)}, u32[]{:S(2)}) collective-permute-start(f32[64,256]{1,0:T(8,128)S(1)} %fusion.9), channel_id=1, source_target_pairs={{0,4},{4,0},{1,5},{5,1},{2,6},{6,2},{3,7},{7,3},{8,12},{12,8},{9,1... | collective-permute-start | bytes 196616 | tf_op jit(solution)/shard_map/ppermute | solution.py:112
  24.5 18.5 %collective-permute-start.3 = (f32[64,256]{1,0:T(8,128)S(1)}, f32[64,256]{1,0:T(8,128)S(1)}, u32[]{:S(2)}, u32[]{:S(2)}) collective-permute-start(f32[64,256]{1,0:T(8,128)S(1)} %fusion.11), channel_id=1, source_target_pairs={{0,4},{4,0},{1,5},{5,1},{2,6},{6,2},{3,7},{7,3},{8,12},{12,8},{9,1... | collective-permute-start | bytes 196616 | tf_op jit(solution)/shard_map/ppermute | solution.py:112
  27.5 3.6 %collective-permute-start.10 = (f32[64,256]{1,0:T(8,128)S(1)}, f32[64,256]{1,0:T(8,128)S(1)}, u32[]{:S(2)}, u32[]{:S(2)}) collective-permute-start(f32[64,256]{1,0:T(8,128)S(1)} %add.151.refs_0_), channel_id=1, source_target_pairs={{0,3},{1,0},{2,1},{3,2},{4,7},{5,4},{6,5},{7,6},{8,11},{9,8},{10,9... | collective-permute-start | bytes 196616 | tf_op jit(solution)/shard_map/ppermute | solution.py:112
  29.6 5.1 %collective-permute-start.8 = (f32[64,256]{1,0:T(8,128)S(1)}, f32[64,256]{1,0:T(8,128)S(1)}, u32[]{:S(2)}, u32[]{:S(2)}) collective-permute-start(f32[64,256]{1,0:T(8,128)S(1)} %add.151.refs_0_), channel_id=1, source_target_pairs={{0,1},{1,2},{2,3},{3,0},{4,5},{5,6},{6,7},{7,4},{8,9},{9,10},{10,1... | collective-permute-start | bytes 196616 | tf_op jit(solution)/shard_map/ppermute | solution.py:112
  29.6 5.1 %collective-permute-start.9 = (f32[64,256]{1,0:T(8,128)S(1)}, f32[64,256]{1,0:T(8,128)S(1)}, u32[]{:S(2)}, u32[]{:S(2)}) collective-permute-start(f32[64,256]{1,0:T(8,128)S(1)} %add.151.refs_0_), channel_id=1, source_target_pairs={{0,2},{1,3},{2,0},{3,1},{4,6},{5,7},{6,4},{7,5},{8,10},{9,11},{10,... | collective-permute-start | bytes 196616 | tf_op jit(solution)/shard_map/ppermute | solution.py:112
  43.2 4.1 %collective-permute-start.11 = (bf16[64,256]{1,0:T(8,128)(2,1)S(1)}, bf16[64,256]{1,0:T(8,128)(2,1)S(1)}, u32[]{:S(2)}, u32[]{:S(2)}) collective-permute-start(bf16[64,256]{1,0:T(8,128)(2,1)S(1)} %convolution_convert_fusion.1), channel_id=1, source_target_pairs={{0,3},{1,2},{2,1},{3,0},{4,7},{5,6},{6,5},{7,4},{8,11},{9,10},{10,... | collective-permute-start | bytes 98312 | tf_op jit(solution)/shard_map/ppermute | solution.py:135
  45.7 4.3 %collective-permute-start.12 = (bf16[64,256]{1,0:T(8,128)(2,1)S(1)}, bf16[64,256]{1,0:T(8,128)(2,1)S(1)}, u32[]{:S(2)}, u32[]{:S(2)}) collective-permute-start(bf16[64,256]{1,0:T(8,128)(2,1)S(1)} %convolution_convert_fusion.1), channel_id=1, source_target_pairs={{0,2},{1,3},{2,0},{3,1},{4,6},{5,7},{6,4},{7,5},{8,10},{9,11},{10,... | collective-permute-start | bytes 98312 | tf_op jit(solution)/shard_map/ppermute | solution.py:135
  45.7 4.3 %collective-permute-start.13 = (bf16[64,256]{1,0:T(8,128)(2,1)S(1)}, bf16[64,256]{1,0:T(8,128)(2,1)S(1)}, u32[]{:S(2)}, u32[]{:S(2)}) collective-permute-start(bf16[64,256]{1,0:T(8,128)(2,1)S(1)} %convolution_convert_fusion.1), channel_id=1, source_target_pairs={{0,1},{1,0},{2,3},{3,2},{4,5},{5,4},{6,7},{7,6},{8,9},{9,8},{10,11... | collective-permute-start | bytes 98312 | tf_op jit(solution)/shard_map/ppermute | solution.py:135
  50.1 12.3 %copy-start.1 = (bf16[256,256]{1,0:T(8,128)(2,1)}, bf16[256,256]{1,0:T(8,128)(2,1)S(1)}, u32[]{:S(2)}) copy-start(bf16[256,256]{1,0:T(8,128)(2,1)S(1)} %get-tuple-element.8) | copy-start | bytes 393220
  50.3 12.2 %collective-permute-start.21 = (f32[128,256]{1,0:T(8,128)S(1)}, f32[128,256]{1,0:T(8,128)S(1)}, u32[]{:S(2)}, u32[]{:S(2)}) collective-permute-start(f32[128,256]{1,0:T(8,128)S(1)} %slice_select_fusion.1), channel_id=1, source_target_pairs={{0,8},{8,0},{1,9},{9,1},{2,10},{10,2},{3,11},{11,3},{4,12},{12,4},... | collective-permute-start | bytes 393224 | tf_op jit(solution)/shard_map/ppermute | solution.py:112
  62.4 15.6 %collective-permute-start.14 = (f32[512,256]{1,0:T(8,128)S(1)}, f32[512,256]{1,0:T(8,128)S(1)}, u32[]{:S(2)}, u32[]{:S(2)}) collective-permute-start(f32[512,256]{1,0:T(8,128)S(1)} %slice_select_fusion), channel_id=1, source_target_pairs={{0,8},{8,0},{1,9},{9,1},{2,10},{10,2},{3,11},{11,3},{4,12},{12,4},... | collective-permute-start | bytes 1572872 | tf_op jit(solution)/shard_map/ppermute | solution.py:112
  62.6 4.9 %collective-permute-start.22 = (f32[32,256]{1,0:T(8,128)S(1)}, f32[32,256]{1,0:T(8,128)S(1)}, u32[]{:S(2)}, u32[]{:S(2)}) collective-permute-start(f32[32,256]{1,0:T(8,128)S(1)} %get-tuple-element.18), channel_id=1, source_target_pairs={{0,64},{64,128},{128,192},{192,0},{1,65},{65,129},{129,193},{193,1... | collective-permute-start | bytes 98312 | tf_op jit(solution)/shard_map/ppermute | solution.py:112
  63.9 4.3 %collective-permute-start.23 = (f32[32,256]{1,0:T(8,128)S(1)}, f32[32,256]{1,0:T(8,128)S(1)}, u32[]{:S(2)}, u32[]{:S(2)}) collective-permute-start(f32[32,256]{1,0:T(8,128)S(1)} %get-tuple-element.20), channel_id=1, source_target_pairs={{0,128},{64,192},{128,0},{192,64},{1,129},{65,193},{129,1},{193,65... | collective-permute-start | bytes 98312 | tf_op jit(solution)/shard_map/ppermute | solution.py:112
  66.3 3.1 %collective-permute-start.24 = (f32[32,256]{1,0:T(8,128)S(1)}, f32[32,256]{1,0:T(8,128)S(1)}, u32[]{:S(2)}, u32[]{:S(2)}) collective-permute-start(f32[32,256]{1,0:T(8,128)S(1)} %get-tuple-element.19), channel_id=1, source_target_pairs={{0,192},{64,0},{128,64},{192,128},{1,193},{65,1},{129,65},{193,129... | collective-permute-start | bytes 98312 | tf_op jit(solution)/shard_map/ppermute | solution.py:112
  69.4 4.8 %collective-permute-start.25 = (f32[32,256]{1,0:T(8,128)S(1)}, f32[32,256]{1,0:T(8,128)S(1)}, u32[]{:S(2)}, u32[]{:S(2)}) collective-permute-start(f32[32,256]{1,0:T(8,128)S(1)} %fusion.14), channel_id=1, source_target_pairs={{0,16},{16,32},{32,48},{48,0},{1,17},{17,33},{33,49},{49,1},{2,18}... | collective-permute-start | bytes 98312 | tf_op jit(solution)/shard_map/ppermute | solution.py:112
  70.2 4.4 %collective-permute-start.26 = (f32[32,256]{1,0:T(8,128)S(1)}, f32[32,256]{1,0:T(8,128)S(1)}, u32[]{:S(2)}, u32[]{:S(2)}) collective-permute-start(f32[32,256]{1,0:T(8,128)S(1)} %fusion.14), channel_id=1, source_target_pairs={{0,32},{16,48},{32,0},{48,16},{1,33},{17,49},{33,1},{49,17},{2,34}... | collective-permute-start | bytes 98312 | tf_op jit(solution)/shard_map/ppermute | solution.py:112
  71.4 3.2 %collective-permute-start.27 = (f32[32,256]{1,0:T(8,128)S(1)}, f32[32,256]{1,0:T(8,128)S(1)}, u32[]{:S(2)}, u32[]{:S(2)}) collective-permute-start(f32[32,256]{1,0:T(8,128)S(1)} %fusion.14), channel_id=1, source_target_pairs={{0,48},{16,0},{32,16},{48,32},{1,49},{17,1},{33,17},{49,33},{2,50}... | collective-permute-start | bytes 98312 | tf_op jit(solution)/shard_map/ppermute | solution.py:112
  74.6 7.2 %collective-permute-start.28 = (f32[32,256]{1,0:T(8,128)S(1)}, f32[32,256]{1,0:T(8,128)S(1)}, u32[]{:S(2)}, u32[]{:S(2)}) collective-permute-start(f32[32,256]{1,0:T(8,128)S(1)} %add_add_fusion), channel_id=1, source_target_pairs={{0,8},{8,0},{1,9},{9,1},{2,10},{10,2},{3,11},{11,3},{4,12},{12,4},... | collective-permute-start | bytes 98312 | tf_op jit(solution)/shard_map/ppermute | solution.py:112
  78.2 6.3 %collective-permute-start.15 = (f32[128,256]{1,0:T(8,128)S(1)}, f32[128,256]{1,0:T(8,128)S(1)}, u32[]{:S(2)}, u32[]{:S(2)}) collective-permute-start(f32[128,256]{1,0:T(8,128)S(1)} %get-tuple-element.9), channel_id=1, source_target_pairs={{0,64},{64,128},{128,192},{192,0},{1,65},{65,129},{129,193},{193,1... | collective-permute-start | bytes 393224 | tf_op jit(solution)/shard_map/ppermute | solution.py:112
  78.3 10.0 %collective-permute-start.16 = (f32[128,256]{1,0:T(8,128)S(1)}, f32[128,256]{1,0:T(8,128)S(1)}, u32[]{:S(2)}, u32[]{:S(2)}) collective-permute-start(f32[128,256]{1,0:T(8,128)S(1)} %get-tuple-element.11), channel_id=1, source_target_pairs={{0,128},{64,192},{128,0},{192,64},{1,129},{65,193},{129,1},{193,65... | collective-permute-start | bytes 393224 | tf_op jit(solution)/shard_map/ppermute | solution.py:112
  81.8 6.4 %collective-permute-start.17 = (f32[128,256]{1,0:T(8,128)S(1)}, f32[128,256]{1,0:T(8,128)S(1)}, u32[]{:S(2)}, u32[]{:S(2)}) collective-permute-start(f32[128,256]{1,0:T(8,128)S(1)} %get-tuple-element.10), channel_id=1, source_target_pairs={{0,192},{64,0},{128,64},{192,128},{1,193},{65,1},{129,65},{193,129... | collective-permute-start | bytes 393224 | tf_op jit(solution)/shard_map/ppermute | solution.py:112
  81.8 10.8 %collective-permute-start.29 = (f32[64,256]{1,0:T(8,128)S(1)}, f32[64,256]{1,0:T(8,128)S(1)}, u32[]{:S(2)}, u32[]{:S(2)}) collective-permute-start(f32[64,256]{1,0:T(8,128)S(1)} %maximum_select_fusion.1.refs_0_), channel_id=1, source_target_pairs={{0,64},{64,128},{128,192},{192,0},{1,65},{65,129},{129,193},{193,1... | collective-permute-start | bytes 196616 | tf_op jit(solution)/shard_map/ppermute | solution.py:112
  88.3 17.7 %collective-permute-start.18 = (f32[128,256]{1,0:T(8,128)S(1)}, f32[128,256]{1,0:T(8,128)S(1)}, u32[]{:S(2)}, u32[]{:S(2)}) collective-permute-start(f32[128,256]{1,0:T(8,128)S(1)} %fusion.3), channel_id=1, source_target_pairs={{0,16},{16,32},{32,48},{48,0},{1,17},{17,33},{33,49},{49,1},{2,18}... | collective-permute-start | bytes 393224 | tf_op jit(solution)/shard_map/ppermute | solution.py:112
  89.8 16.1 %collective-permute-start.19 = (f32[128,256]{1,0:T(8,128)S(1)}, f32[128,256]{1,0:T(8,128)S(1)}, u32[]{:S(2)}, u32[]{:S(2)}) collective-permute-start(f32[128,256]{1,0:T(8,128)S(1)} %fusion.3), channel_id=1, source_target_pairs={{0,32},{16,48},{32,0},{48,16},{1,33},{17,49},{33,1},{49,17},{2,34}... | collective-permute-start | bytes 393224 | tf_op jit(solution)/shard_map/ppermute | solution.py:112
  91.9 14.0 %collective-permute-start.20 = (f32[128,256]{1,0:T(8,128)S(1)}, f32[128,256]{1,0:T(8,128)S(1)}, u32[]{:S(2)}, u32[]{:S(2)}) collective-permute-start(f32[128,256]{1,0:T(8,128)S(1)} %fusion.3), channel_id=1, source_target_pairs={{0,48},{16,0},{32,16},{48,32},{1,49},{17,1},{33,17},{49,33},{2,50}... | collective-permute-start | bytes 393224 | tf_op jit(solution)/shard_map/ppermute | solution.py:112
  92.0 4.8 %collective-permute-start.30 = (f32[64,256]{1,0:T(8,128)S(1)}, f32[64,256]{1,0:T(8,128)S(1)}, u32[]{:S(2)}, u32[]{:S(2)}) collective-permute-start(f32[64,256]{1,0:T(8,128)S(1)} %maximum_select_fusion.1.refs_0_), channel_id=1, source_target_pairs={{0,128},{64,192},{128,0},{192,64},{1,129},{65,193},{129,1},{193,65... | collective-permute-start | bytes 196616 | tf_op jit(solution)/shard_map/ppermute | solution.py:112
  92.6 5.1 %collective-permute-start.31 = (f32[64,256]{1,0:T(8,128)S(1)}, f32[64,256]{1,0:T(8,128)S(1)}, u32[]{:S(2)}, u32[]{:S(2)}) collective-permute-start(f32[64,256]{1,0:T(8,128)S(1)} %maximum_select_fusion.1.refs_0_), channel_id=1, source_target_pairs={{0,192},{64,0},{128,64},{192,128},{1,193},{65,1},{129,65},{193,129... | collective-permute-start | bytes 196616 | tf_op jit(solution)/shard_map/ppermute | solution.py:112
  115.0 4.8 %collective-permute-start.32 = (bf16[512,256]{1,0:T(8,128)(2,1)S(1)}, bf16[512,256]{1,0:T(8,128)(2,1)S(1)}, u32[]{:S(2)}, u32[]{:S(2)}) collective-permute-start(bf16[512,256]{1,0:T(8,128)(2,1)S(1)} %bitcast.77), channel_id=1, source_target_pairs={{0,8},{8,0},{1,9},{9,1},{2,10},{10,2},{3,11},{11,3},{4,12},{12,4},... | collective-permute-start | bytes 786440 | tf_op jit(solution)/shard_map/ppermute | solution.py:112
  120.0 5.9 %copy-start.2 = (bf16[1024,256]{1,0:T(8,128)(2,1)}, bf16[1024,256]{1,0:T(8,128)(2,1)S(1)}, u32[]{:S(2)}) copy-start(bf16[1024,256]{1,0:T(8,128)(2,1)S(1)} %maximum_select_fusion) | copy-start | bytes 1572868
  126.0 1.3 collective-permute-start.33
  127.3 3.8 %collective-permute-start.34 = (f32[16,256]{1,0:T(8,128)S(1)}, f32[16,256]{1,0:T(8,128)S(1)}, u32[]{:S(2)}, u32[]{:S(2)}) collective-permute-start(f32[16,256]{1,0:T(8,128)S(1)} %add.173), channel_id=1, source_target_pairs={{0,64},{64,128},{128,192},{192,0},{1,65},{65,129},{129,193},{193,1... | collective-permute-start | bytes 49160 | tf_op jit(solution)/shard_map/ppermute | solution.py:112
  127.6 4.1 %collective-permute-start.35 = (f32[16,256]{1,0:T(8,128)S(1)}, f32[16,256]{1,0:T(8,128)S(1)}, u32[]{:S(2)}, u32[]{:S(2)}) collective-permute-start(f32[16,256]{1,0:T(8,128)S(1)} %add.173), channel_id=1, source_target_pairs={{0,128},{64,192},{128,0},{192,64},{1,129},{65,193},{129,1},{193,65... | collective-permute-start | bytes 49160 | tf_op jit(solution)/shard_map/ppermute | solution.py:112
  129.4 2.9 %collective-permute-start.36 = (f32[16,256]{1,0:T(8,128)S(1)}, f32[16,256]{1,0:T(8,128)S(1)}, u32[]{:S(2)}, u32[]{:S(2)}) collective-permute-start(f32[16,256]{1,0:T(8,128)S(1)} %add.173), channel_id=1, source_target_pairs={{0,192},{64,0},{128,64},{192,128},{1,193},{65,1},{129,65},{193,129... | collective-permute-start | bytes 49160 | tf_op jit(solution)/shard_map/ppermute | solution.py:112

commit v11 on v10

--- a/solution.py
+++ b/solution.py
@@ -86,7 +86,13 @@
 
     nothing = jnp.zeros((6 * B, n), jnp.bfloat16)
     lax.fori_loop(0, n // B, step, (m_ref[0:B, :], nothing, nothing))
-    x_ref[...] = cross(m_ref[...], w_ref[...], precision=HIGHEST)
+
+    def finish(h, carry):
+        here = pl.ds(pl.multiple_of(h * 128, 128), 128)
+        x_ref[here, :] = cross(m_ref[:, here], w_ref[...], precision=HIGHEST)
+        return carry
+
+    lax.fori_loop(0, n // 128, finish, 0)
 
 
 def inverse(parts, places, gram_first, total):
@@ -140,6 +146,14 @@
 
 
 def ordered(parts, me):
+    rows = parts[0].shape[0]
+    whole = jnp.zeros((len(parts) * rows, parts[0].shape[1]), parts[0].dtype)
+    for d, part in enumerate(parts):
+        whole = lax.dynamic_update_slice(whole, part, (jnp.bitwise_xor(me, d) * rows, 0))
+    return whole
+
+
+def sorted_rows(parts, me):
     odd = lax.rem(me, 2) == 1
     low = [jnp.where(odd, parts[1], parts[0]), jnp.where(odd, parts[0], parts[1])]
     high = [jnp.where(odd, parts[3], parts[2]), jnp.where(odd, parts[2], parts[3])]
@@ -193,7 +207,7 @@
     row = ring_scatter(partial_second, "y")
     row = ring_sum(row, "zh")
     row = jnp.dot(row, inverse_second, precision=HIGHEST).astype(jnp.bfloat16)
-    second_factor = ordered(quad_gather(row, "y"), lax.axis_index("y"))
+    second_factor = sorted_rows(quad_gather(row, "y"), lax.axis_index("y"))
 
     first_third, tensor = lax.optimization_barrier((first_third, tensor))
     gram_local = jnp.dot(second_factor.T, second_factor, preferred_element_type=jnp.float32)
@@ -212,10 +226,8 @@
     mine = ring_scatter(mine, "x")
     mttkrp_third = ring_sum(mine, "zl")
     third_solution = jnp.dot(mttkrp_third, inverse_third, precision=HIGHEST)
-    block = third_solution.astype(jnp.bfloat16)
-    copies = jnp.broadcast_to(block[None], (lax.axis_size("x"),) + block.shape)
-    mine = exchange(copies, "x").reshape(-1, block.shape[1])
-    third_new = join(mine, shift(mine, "core", 1), core)
+    mine = ordered(quad_gather(third_solution.astype(jnp.bfloat16), "x"), lax.axis_index("x"))
+    third_new = ordered([mine, shift(mine, "core", 1)], core)
 
     back = jnp.einsum("ijk,kr->ijr", tensor, third_new, preferred_element_type=jnp.float32)
     partial_first = jnp.sum(back * second_factor.astype(jnp.float32)[None], axis=1)

time: 153 us -> 152 us (level)
  blocking collectives: 26 us -> 17.1 us
  starting transfers between devices: 62.8 us -> 67 us
  waiting for transfers between devices: 22 us -> 25.9 us
    all_to_all x2 -> x1, blocking collectives: 26 us -> 17.1 us  [exchange(): return lax.all_to_all(x, axes, 0, 0, tiled=True)]
    ppermute x3 -> x6, starting transfers between devices: 3.4 us -> 7.29 us  [pair(): lax.ppermute(x, axis, [(s, s ^ d) for s in range(lax.axis_size(axis))])]
    ppermute x3 -> x6, waiting for transfers between devices: 3.41 us -> 7.2 us  [pair(): lax.ppermute(x, axis, [(s, s ^ d) for s in range(lax.axis_size(axis))])]
  transfers between devices with their start and end apart: 37 -> 40, of which waited for: 16 -> 18; matrix products, arithmetic and copies ran while one was open for 9% -> 9% of each run, Pallas kernels for 11% -> 11%
where the time goes in v11:
time: 152 us; the launch traced here: 150 us
  starting transfers between devices  67 us (44%)
  waiting for transfers between devices  25.9 us (17%)
  matrix products  18.9 us (12%)
  blocking collectives  17.1 us (11%)
  Pallas kernels  16.9 us (11%)
  other arithmetic  1.74 us (1%)
    ppermute x34, starting transfers between devices, shift(): return lax.ppermute(x, axis, [(s, (s + d) % n) for s in range(n)])  59.7 us
    ppermute x34, waiting for transfers between devices, shift(): return lax.ppermute(x, axis, [(s, (s + d) % n) for s in range(n)])  18.7 us
    all_to_all x1, blocking collectives, exchange(): return lax.all_to_all(x, axes, 0, 0, tiled=True)  17.1 us
    pallas_call x2, Pallas kernels, inverse(): pl.pallas_call(functools.partial(inverse_kernel, places, total), out_shap...  16.9 us
    ppermute x6, starting transfers between devices, pair(): lax.ppermute(x, axis, [(s, s ^ d) for s in range(lax.axis_size(axis))])  7.29 us
    ppermute x6, waiting for transfers between devices, pair(): lax.ppermute(x, axis, [(s, s ^ d) for s in range(lax.axis_size(axis))])  7.2 us
    dot_general x1, matrix products, on_device(): jnp.einsum('ijk,kr->ijr', tensor, third_new, preferred_element_type=jnp.f...  5.93 us
    dot_general x1, matrix products, on_device(): jnp.einsum('ijk,jr->ikr', tensor, second_factor, preferred_element_type=j...  5.87 us
  transfers between devices with their start and end apart: 40, of which 18 were waited for; matrix products, arithmetic and copies ran while one was open for 9% of the time, Pallas kernels for 11%

profile of v11, /device:TPU:1, one launch (start us, length us, event | category | flops | bytes accessed | tf_op | source)
XLA Modules:
  0.0 149.8 jit_solution(874220533412945771)
XLA Ops:
  0.7 1.0 copy-done
  2.1 2.2 %collective-permute-start.4 = (f32[64,256]{1,0:T(8,128)S(1)}, f32[64,256]{1,0:T(8,128)S(1)}, u32[]{:S(2)}, u32[]{:S(2)}) collective-permute-start(f32[64,256]{1,0:T(8,128)S(1)} %get-tuple-element.15), channel_id=1, source_target_pairs={{0,1},{1,2},{2,3},{3,0},{4,5},{5,6},{6,7},{7,4},{8,9},{9,10},{10,1... | collective-permute-start | bytes 196616 | tf_op jit(solution)/shard_map/ppermute | solution.py:118
  4.3 2.6 %collective-permute-start.5 = (f32[64,256]{1,0:T(8,128)S(1)}, f32[64,256]{1,0:T(8,128)S(1)}, u32[]{:S(2)}, u32[]{:S(2)}) collective-permute-start(f32[64,256]{1,0:T(8,128)S(1)} %get-tuple-element.17), channel_id=1, source_target_pairs={{0,2},{1,3},{2,0},{3,1},{4,6},{5,7},{6,4},{7,5},{8,10},{9,11},{10,... | collective-permute-start | bytes 196616 | tf_op jit(solution)/shard_map/ppermute | solution.py:118
  6.9 1.1 collective-permute-start.6
  8.7 5.7 %multiply_reduce_fusion.2 = f32[256,256]{1,0:T(8,128)S(1)} fusion(bf16[16,256,1024]{2,1,0:T(8,128)(2,1)} %param.3, f32[16,256]{1,0:T(8,128)S(1)} %convert_multiply_fusion, bf16[1024,256]{1,0:T(8,128)(2,1)S(1)} %copy-done), kind=kOutput, calls=%fused_computation.2 | convolution fusion | flops 2149515264 | bytes 9191424 | tf_op jit(solution)/shard_map/ijk,kr->ijr/dot_general | solution.py:205
  15.7 1.7 %collective-permute-start.2 = (f32[64,256]{1,0:T(8,128)S(1)}, f32[64,256]{1,0:T(8,128)S(1)}, u32[]{:S(2)}, u32[]{:S(2)}) collective-permute-start(f32[64,256]{1,0:T(8,128)S(1)} %get-tuple-element.13), channel_id=1, source_target_pairs={{0,3},{1,0},{2,1},{3,2},{4,7},{5,4},{6,5},{7,6},{8,11},{9,8},{10,9... | collective-permute-start | bytes 196616 | tf_op jit(solution)/shard_map/ppermute | solution.py:118
  17.4 7.0 %collective-permute-start.7 = (f32[64,256]{1,0:T(8,128)S(1)}, f32[64,256]{1,0:T(8,128)S(1)}, u32[]{:S(2)}, u32[]{:S(2)}) collective-permute-start(f32[64,256]{1,0:T(8,128)S(1)} %fusion.9), channel_id=1, source_target_pairs={{0,4},{4,0},{1,5},{5,1},{2,6},{6,2},{3,7},{7,3},{8,12},{12,8},{9,1... | collective-permute-start | bytes 196616 | tf_op jit(solution)/shard_map/ppermute | solution.py:118
  24.5 3.0 %collective-permute-start.3 = (f32[64,256]{1,0:T(8,128)S(1)}, f32[64,256]{1,0:T(8,128)S(1)}, u32[]{:S(2)}, u32[]{:S(2)}) collective-permute-start(f32[64,256]{1,0:T(8,128)S(1)} %fusion.11), channel_id=1, source_target_pairs={{0,4},{4,0},{1,5},{5,1},{2,6},{6,2},{3,7},{7,3},{8,12},{12,8},{9,1... | collective-permute-start | bytes 196616 | tf_op jit(solution)/shard_map/ppermute | solution.py:118
  27.4 2.1 %collective-permute-start.10 = (f32[64,256]{1,0:T(8,128)S(1)}, f32[64,256]{1,0:T(8,128)S(1)}, u32[]{:S(2)}, u32[]{:S(2)}) collective-permute-start(f32[64,256]{1,0:T(8,128)S(1)} %add.169.refs_0_), channel_id=1, source_target_pairs={{0,3},{1,0},{2,1},{3,2},{4,7},{5,4},{6,5},{7,6},{8,11},{9,8},{10,9... | collective-permute-start | bytes 196616 | tf_op jit(solution)/shard_map/ppermute | solution.py:118
  29.6 1.3 collective-permute-start.9
  31.1 3.6 %collective-permute-done.8.refs_1_ = f32[64,256]{1,0:T(8,128)S(1)} collective-permute-done((f32[64,256]{1,0:T(8,128)S(1)}, f32[64,256]{1,0:T(8,128)S(1)}, u32[]{:S(2)}, u32[]{:S(2)}) %collective-permute-start.8) | collective-permute-done | bytes 65568 | tf_op jit(solution)/shard_map/ppermute | solution.py:118
  34.7 8.5 %inverse.2 = f32[256,256]{1,0:T(8,128)S(1)} custom-call(f32[64,256]{1,0:T(8,128)S(1)} %add.169.refs_0_, f32[64,256]{1,0:T(8,128)S(1)} %collective-permute-done.8.refs_1_, f32[64,256]{1,0:T(8,128)S(1)} %collective-permute-done.9.refs_2_, f32[64,256]{1,0:T(8,128)S(1)} %collective-permute-done.10.refs_3_, f32[256,256]{1,0:T(8,128)S(1)} %convolution_multiply_fusion.refs_4_), custom_call_target="tpu_custom_call" | custom-call | flops 201326592 | bytes 524288 | tf_op jit(solution)/shard_map/inverse/pallas_call | solution.py:100
  43.4 2.5 %collective-permute-start.11 = (bf16[64,256]{1,0:T(8,128)(2,1)S(1)}, bf16[64,256]{1,0:T(8,128)(2,1)S(1)}, u32[]{:S(2)}, u32[]{:S(2)}) collective-permute-start(bf16[64,256]{1,0:T(8,128)(2,1)S(1)} %convolution_convert_fusion.1), channel_id=1, source_target_pairs={{0,3},{1,2},{2,1},{3,0},{4,7},{5,6},{6,5},{7,4},{8,11},{9,10},{10,... | collective-permute-start | bytes 98312 | tf_op jit(solution)/shard_map/ppermute | solution.py:141
  46.0 0.8 collective-permute-start.13
  47.5 2.8 %collective-permute-done.12 = bf16[64,256]{1,0:T(8,128)(2,1)S(1)} collective-permute-done((bf16[64,256]{1,0:T(8,128)(2,1)S(1)}, bf16[64,256]{1,0:T(8,128)(2,1)S(1)}, u32[]{:S(2)}, u32[]{:S(2)}) %collective-permute-start.12) | collective-permute-done | bytes 32800 | tf_op jit(solution)/shard_map/ppermute | solution.py:141
  50.6 6.1 %collective-permute-start.21 = (f32[128,256]{1,0:T(8,128)S(1)}, f32[128,256]{1,0:T(8,128)S(1)}, u32[]{:S(2)}, u32[]{:S(2)}) collective-permute-start(f32[128,256]{1,0:T(8,128)S(1)} %slice_select_fusion.1), channel_id=1, source_target_pairs={{0,8},{8,0},{1,9},{9,1},{2,10},{10,2},{3,11},{11,3},{4,12},{12,4},... | collective-permute-start | bytes 393224 | tf_op jit(solution)/shard_map/ppermute | solution.py:118
  56.7 5.9 %multiply_reduce_fusion = f32[1024,256]{1,0:T(8,128)S(1)} fusion(bf16[16,256,1024]{2,1,0:T(8,128)(2,1)} %param.3, f32[16,256]{1,0:T(8,128)S(1)} %convert_multiply_fusion, bf16[256,256]{1,0:T(8,128)(2,1)S(1)} %get-tuple-element.8), kind=kOutput, calls=%fused_computation | convolution fusion | flops 2155610112 | bytes 9584640 | tf_op jit(solution)/shard_map/ijk,jr->ikr/dot_general | solution.py:222
  62.8 1.3 collective-permute-start.22
  64.1 2.5 %collective-permute-start.23 = (f32[32,256]{1,0:T(8,128)S(1)}, f32[32,256]{1,0:T(8,128)S(1)}, u32[]{:S(2)}, u32[]{:S(2)}) collective-permute-start(f32[32,256]{1,0:T(8,128)S(1)} %get-tuple-element.20), channel_id=1, source_target_pairs={{0,128},{64,192},{128,0},{192,64},{1,129},{65,193},{129,1},{193,65... | collective-permute-start | bytes 98312 | tf_op jit(solution)/shard_map/ppermute | solution.py:118
  66.6 1.2 collective-permute-start.24
  68.4 1.2 collective-permute-done.24
  69.6 0.8 collective-permute-start.25
  70.5 1.2 collective-permute-start.26
  71.6 1.6 %collective-permute-start.27 = (f32[32,256]{1,0:T(8,128)S(1)}, f32[32,256]{1,0:T(8,128)S(1)}, u32[]{:S(2)}, u32[]{:S(2)}) collective-permute-start(f32[32,256]{1,0:T(8,128)S(1)} %fusion.14), channel_id=1, source_target_pairs={{0,48},{16,0},{32,16},{48,32},{1,49},{17,1},{33,17},{49,33},{2,50}... | collective-permute-start | bytes 98312 | tf_op jit(solution)/shard_map/ppermute | solution.py:118
  73.3 1.1 collective-permute-done.25
  74.9 3.4 %collective-permute-start.28 = (f32[32,256]{1,0:T(8,128)S(1)}, f32[32,256]{1,0:T(8,128)S(1)}, u32[]{:S(2)}, u32[]{:S(2)}) collective-permute-start(f32[32,256]{1,0:T(8,128)S(1)} %add_add_fusion), channel_id=1, source_target_pairs={{0,8},{8,0},{1,9},{9,1},{2,10},{10,2},{3,11},{11,3},{4,12},{12,4},... | collective-permute-start | bytes 98312 | tf_op jit(solution)/shard_map/ppermute | solution.py:118
  78.5 3.5 %collective-permute-start.16 = (f32[128,256]{1,0:T(8,128)S(1)}, f32[128,256]{1,0:T(8,128)S(1)}, u32[]{:S(2)}, u32[]{:S(2)}) collective-permute-start(f32[128,256]{1,0:T(8,128)S(1)} %get-tuple-element.11), channel_id=1, source_target_pairs={{0,128},{64,192},{128,0},{192,64},{1,129},{65,193},{129,1},{193,65... | collective-permute-start | bytes 393224 | tf_op jit(solution)/shard_map/ppermute | solution.py:118
  82.1 1.5 %collective-permute-start.29 = (f32[64,256]{1,0:T(8,128)S(1)}, f32[64,256]{1,0:T(8,128)S(1)}, u32[]{:S(2)}, u32[]{:S(2)}) collective-permute-start(f32[64,256]{1,0:T(8,128)S(1)} %maximum_select_fusion.refs_0_), channel_id=1, source_target_pairs={{0,64},{64,128},{128,192},{192,0},{1,65},{65,129},{129,193},{193,1... | collective-permute-start | bytes 196616 | tf_op jit(solution)/shard_map/ppermute | solution.py:118
  83.6 1.1 collective-permute-done.15
  84.7 3.7 %collective-permute-done.16 = f32[128,256]{1,0:T(8,128)S(1)} collective-permute-done((f32[128,256]{1,0:T(8,128)S(1)}, f32[128,256]{1,0:T(8,128)S(1)}, u32[]{:S(2)}, u32[]{:S(2)}) %collective-permute-start.16) | collective-permute-done | bytes 131104 | tf_op jit(solution)/shard_map/ppermute | solution.py:118
  88.5 1.8 %collective-permute-start.18 = (f32[128,256]{1,0:T(8,128)S(1)}, f32[128,256]{1,0:T(8,128)S(1)}, u32[]{:S(2)}, u32[]{:S(2)}) collective-permute-start(f32[128,256]{1,0:T(8,128)S(1)} %fusion.3), channel_id=1, source_target_pairs={{0,16},{16,32},{32,48},{48,0},{1,17},{17,33},{33,49},{49,1},{2,18}... | collective-permute-start | bytes 393224 | tf_op jit(solution)/shard_map/ppermute | solution.py:118
  90.3 2.1 %collective-permute-start.19 = (f32[128,256]{1,0:T(8,128)S(1)}, f32[128,256]{1,0:T(8,128)S(1)}, u32[]{:S(2)}, u32[]{:S(2)}) collective-permute-start(f32[128,256]{1,0:T(8,128)S(1)} %fusion.3), channel_id=1, source_target_pairs={{0,32},{16,48},{32,0},{48,16},{1,33},{17,49},{33,1},{49,17},{2,34}... | collective-permute-start | bytes 393224 | tf_op jit(solution)/shard_map/ppermute | solution.py:118
  93.1 2.5 %collective-permute-start.31 = (f32[64,256]{1,0:T(8,128)S(1)}, f32[64,256]{1,0:T(8,128)S(1)}, u32[]{:S(2)}, u32[]{:S(2)}) collective-permute-start(f32[64,256]{1,0:T(8,128)S(1)} %maximum_select_fusion.refs_0_), channel_id=1, source_target_pairs={{0,192},{64,0},{128,64},{192,128},{1,193},{65,1},{129,65},{193,129... | collective-permute-start | bytes 196616 | tf_op jit(solution)/shard_map/ppermute | solution.py:118
  95.5 1.7 %collective-permute-done.30.refs_2_ = f32[64,256]{1,0:T(8,128)S(1)} collective-permute-done((f32[64,256]{1,0:T(8,128)S(1)}, f32[64,256]{1,0:T(8,128)S(1)}, u32[]{:S(2)}, u32[]{:S(2)}) %collective-permute-start.30) | collective-permute-done | bytes 65568 | tf_op jit(solution)/shard_map/ppermute | solution.py:118
  97.2 0.9 collective-permute-done.31.refs_3_
  98.2 8.4 %inverse.3 = f32[256,256]{1,0:T(8,128)S(1)} custom-call(f32[64,256]{1,0:T(8,128)S(1)} %maximum_select_fusion.refs_0_, f32[64,256]{1,0:T(8,128)S(1)} %collective-permute-done.29.refs_1_, f32[64,256]{1,0:T(8,128)S(1)} %collective-permute-done.30.refs_2_, f32[64,256]{1,0:T(8,128)S(1)} %collective-permute-done.31.refs_3_, ...), custom_call_target="tpu_custom_call" | custom-call | flops 201326592 | bytes 524288 | tf_op jit(solution)/shard_map/inverse/pallas_call | solution.py:100
  107.0 0.9 collective-permute-start.32
  107.8 2.5 %collective-permute-start.33 = (bf16[128,256]{1,0:T(8,128)(2,1)S(1)}, bf16[128,256]{1,0:T(8,128)(2,1)S(1)}, u32[]{:S(2)}, u32[]{:S(2)}) collective-permute-start(bf16[128,256]{1,0:T(8,128)(2,1)S(1)} %get-tuple-element.26), channel_id=1, source_target_pairs={{0,128},{64,192},{128,0},{192,64},{1,129},{65,193},{129,1},{193,65... | collective-permute-start | bytes 196616 | tf_op jit(solution)/shard_map/ppermute | solution.py:141
  110.9 1.8 %collective-permute-done.33 = bf16[128,256]{1,0:T(8,128)(2,1)S(1)} collective-permute-done((bf16[128,256]{1,0:T(8,128)(2,1)S(1)}, bf16[128,256]{1,0:T(8,128)(2,1)S(1)}, u32[]{:S(2)}, u32[]{:S(2)}) %collective-permute-start.33) | collective-permute-done | bytes 65568 | tf_op jit(solution)/shard_map/ppermute | solution.py:141
  112.7 2.0 %collective-permute-done.34 = bf16[128,256]{1,0:T(8,128)(2,1)S(1)} collective-permute-done((bf16[128,256]{1,0:T(8,128)(2,1)S(1)}, bf16[128,256]{1,0:T(8,128)(2,1)S(1)}, u32[]{:S(2)}, u32[]{:S(2)}) %collective-permute-start.34) | collective-permute-done | bytes 65568 | tf_op jit(solution)/shard_map/ppermute | solution.py:141
  114.7 4.0 %collective-permute-start.35 = (bf16[512,256]{1,0:T(8,128)(2,1)S(1)}, bf16[512,256]{1,0:T(8,128)(2,1)S(1)}, u32[]{:S(2)}, u32[]{:S(2)}) collective-permute-start(bf16[512,256]{1,0:T(8,128)(2,1)S(1)} %constant_dynamic-update-slice_fusion.2), channel_id=1, source_target_pairs={{0,8},{8,0},{1,9},{9,1},{2,10},{10,2},{3,11},{11,3},{4,12},{12,4},... | collective-permute-start | bytes 786440 | tf_op jit(solution)/shard_map/ppermute | solution.py:118
  118.8 1.1 collective-permute-done.35
  119.9 5.9 %multiply_reduce_fusion.1 = f32[16,256]{1,0:T(8,128)S(1)} fusion(bf16[16,256,1024]{2,1,0:T(8,128)(2,1)} %param.3, f32[256,256]{1,0:T(8,128)S(1)} %get-tuple-element.7, bf16[1024,256]{1,0:T(8,128)(2,1)S(1)} %constant_dynamic-update-slice_fusion), kind=kOutput, calls=%fused_computation.1 | convolution fusion | flops 2149576704 | bytes 9191424 | tf_op jit(solution)/shard_map/ijk,kr->ijr/dot_general | solution.py:232
  126.3 0.8 collective-permute-done.36
  127.1 1.6 %collective-permute-start.38 = (f32[16,256]{1,0:T(8,128)S(1)}, f32[16,256]{1,0:T(8,128)S(1)}, u32[]{:S(2)}, u32[]{:S(2)}) collective-permute-start(f32[16,256]{1,0:T(8,128)S(1)} %add.197), channel_id=1, source_target_pairs={{0,128},{64,192},{128,0},{192,64},{1,129},{65,193},{129,1},{193,65... | collective-permute-start | bytes 49160 | tf_op jit(solution)/shard_map/ppermute | solution.py:118
  128.7 1.1 collective-permute-start.39
  129.8 1.1 collective-permute-done.37
  132.0 17.1 %all_to_all.5 = bf16[32,16,256]{2,1,0:T(8,128)(2,1)S(1)} all-to-all(bf16[32,16,256]{2,1,0:T(8,128)(2,1)S(1)} %broadcast_in_dim.8), channel_id=1, replica_groups=mesh['x'=4,'zl'=4,'core'=2,'zh'=2,'y'=4] {'zl','zh','y'}, dimensions={0} | all-to-all | bytes 524288 | tf_op jit(solution)/shard_map/all_to_all | solution.py:113
  (80 shorter events, 9.4 us)
Async XLA Ops:
  0.6 1.0 copy-start
  2.1 13.6 %collective-permute-start.4 = (f32[64,256]{1,0:T(8,128)S(1)}, f32[64,256]{1,0:T(8,128)S(1)}, u32[]{:S(2)}, u32[]{:S(2)}) collective-permute-start(f32[64,256]{1,0:T(8,128)S(1)} %get-tuple-element.15), channel_id=1, source_target_pairs={{0,1},{1,2},{2,3},{3,0},{4,5},{5,6},{6,7},{7,4},{8,9},{9,10},{10,1... | collective-permute-start | bytes 196616 | tf_op jit(solution)/shard_map/ppermute | solution.py:118
  4.3 13.1 %collective-permute-start.5 = (f32[64,256]{1,0:T(8,128)S(1)}, f32[64,256]{1,0:T(8,128)S(1)}, u32[]{:S(2)}, u32[]{:S(2)}) collective-permute-start(f32[64,256]{1,0:T(8,128)S(1)} %get-tuple-element.17), channel_id=1, source_target_pairs={{0,2},{1,3},{2,0},{3,1},{4,6},{5,7},{6,4},{7,5},{8,10},{9,11},{10,... | collective-permute-start | bytes 196616 | tf_op jit(solution)/shard_map/ppermute | solution.py:118
  6.9 10.5 %collective-permute-start.6 = (f32[64,256]{1,0:T(8,128)S(1)}, f32[64,256]{1,0:T(8,128)S(1)}, u32[]{:S(2)}, u32[]{:S(2)}) collective-permute-start(f32[64,256]{1,0:T(8,128)S(1)} %get-tuple-element.16), channel_id=1, source_target_pairs={{0,3},{1,0},{2,1},{3,2},{4,7},{5,4},{6,5},{7,6},{8,11},{9,8},{10,9... | collective-permute-start | bytes 196616 | tf_op jit(solution)/shard_map/ppermute | solution.py:118
  8.6 22.2 %copy-start.3 = (bf16[16,256]{1,0:T(8,128)(2,1)S(1)}, bf16[16,256]{1,0:T(8,128)(2,1)}, u32[]{:S(2)}) copy-start(bf16[16,256]{1,0:T(8,128)(2,1)} %param.4) | copy-start | bytes 24580
  14.4 10.0 %collective-permute-start = (f32[64,256]{1,0:T(8,128)S(1)}, f32[64,256]{1,0:T(8,128)S(1)}, u32[]{:S(2)}, u32[]{:S(2)}) collective-permute-start(f32[64,256]{1,0:T(8,128)S(1)} %get-tuple-element.12), channel_id=1, source_target_pairs={{0,1},{1,2},{2,3},{3,0},{4,5},{5,6},{6,7},{7,4},{8,9},{9,10},{10,1... | collective-permute-start | bytes 196616 | tf_op jit(solution)/shard_map/ppermute | solution.py:118
  14.9 9.5 %collective-permute-start.1 = (f32[64,256]{1,0:T(8,128)S(1)}, f32[64,256]{1,0:T(8,128)S(1)}, u32[]{:S(2)}, u32[]{:S(2)}) collective-permute-start(f32[64,256]{1,0:T(8,128)S(1)} %get-tuple-element.14), channel_id=1, source_target_pairs={{0,2},{1,3},{2,0},{3,1},{4,6},{5,7},{6,4},{7,5},{8,10},{9,11},{10,... | collective-permute-start | bytes 196616 | tf_op jit(solution)/shard_map/ppermute | solution.py:118
  15.7 8.7 %collective-permute-start.2 = (f32[64,256]{1,0:T(8,128)S(1)}, f32[64,256]{1,0:T(8,128)S(1)}, u32[]{:S(2)}, u32[]{:S(2)}) collective-permute-start(f32[64,256]{1,0:T(8,128)S(1)} %get-tuple-element.13), channel_id=1, source_target_pairs={{0,3},{1,0},{2,1},{3,2},{4,7},{5,4},{6,5},{7,6},{8,11},{9,8},{10,9... | collective-permute-start | bytes 196616 | tf_op jit(solution)/shard_map/ppermute | solution.py:118
  17.4 10.0 %collective-permute-start.7 = (f32[64,256]{1,0:T(8,128)S(1)}, f32[64,256]{1,0:T(8,128)S(1)}, u32[]{:S(2)}, u32[]{:S(2)}) collective-permute-start(f32[64,256]{1,0:T(8,128)S(1)} %fusion.9), channel_id=1, source_target_pairs={{0,4},{4,0},{1,5},{5,1},{2,6},{6,2},{3,7},{7,3},{8,12},{12,8},{9,1... | collective-permute-start | bytes 196616 | tf_op jit(solution)/shard_map/ppermute | solution.py:118
  24.5 18.7 %collective-permute-start.3 = (f32[64,256]{1,0:T(8,128)S(1)}, f32[64,256]{1,0:T(8,128)S(1)}, u32[]{:S(2)}, u32[]{:S(2)}) collective-permute-start(f32[64,256]{1,0:T(8,128)S(1)} %fusion.11), channel_id=1, source_target_pairs={{0,4},{4,0},{1,5},{5,1},{2,6},{6,2},{3,7},{7,3},{8,12},{12,8},{9,1... | collective-permute-start | bytes 196616 | tf_op jit(solution)/shard_map/ppermute | solution.py:118
  27.4 3.6 %collective-permute-start.10 = (f32[64,256]{1,0:T(8,128)S(1)}, f32[64,256]{1,0:T(8,128)S(1)}, u32[]{:S(2)}, u32[]{:S(2)}) collective-permute-start(f32[64,256]{1,0:T(8,128)S(1)} %add.169.refs_0_), channel_id=1, source_target_pairs={{0,3},{1,0},{2,1},{3,2},{4,7},{5,4},{6,5},{7,6},{8,11},{9,8},{10,9... | collective-permute-start | bytes 196616 | tf_op jit(solution)/shard_map/ppermute | solution.py:118
  29.5 5.1 %collective-permute-start.8 = (f32[64,256]{1,0:T(8,128)S(1)}, f32[64,256]{1,0:T(8,128)S(1)}, u32[]{:S(2)}, u32[]{:S(2)}) collective-permute-start(f32[64,256]{1,0:T(8,128)S(1)} %add.169.refs_0_), channel_id=1, source_target_pairs={{0,1},{1,2},{2,3},{3,0},{4,5},{5,6},{6,7},{7,4},{8,9},{9,10},{10,1... | collective-permute-start | bytes 196616 | tf_op jit(solution)/shard_map/ppermute | solution.py:118
  29.6 5.1 %collective-permute-start.9 = (f32[64,256]{1,0:T(8,128)S(1)}, f32[64,256]{1,0:T(8,128)S(1)}, u32[]{:S(2)}, u32[]{:S(2)}) collective-permute-start(f32[64,256]{1,0:T(8,128)S(1)} %add.169.refs_0_), channel_id=1, source_target_pairs={{0,2},{1,3},{2,0},{3,1},{4,6},{5,7},{6,4},{7,5},{8,10},{9,11},{10,... | collective-permute-start | bytes 196616 | tf_op jit(solution)/shard_map/ppermute | solution.py:118
  43.4 4.1 %collective-permute-start.11 = (bf16[64,256]{1,0:T(8,128)(2,1)S(1)}, bf16[64,256]{1,0:T(8,128)(2,1)S(1)}, u32[]{:S(2)}, u32[]{:S(2)}) collective-permute-start(bf16[64,256]{1,0:T(8,128)(2,1)S(1)} %convolution_convert_fusion.1), channel_id=1, source_target_pairs={{0,3},{1,2},{2,1},{3,0},{4,7},{5,6},{6,5},{7,4},{8,11},{9,10},{10,... | collective-permute-start | bytes 98312 | tf_op jit(solution)/shard_map/ppermute | solution.py:141
  46.0 4.3 %collective-permute-start.12 = (bf16[64,256]{1,0:T(8,128)(2,1)S(1)}, bf16[64,256]{1,0:T(8,128)(2,1)S(1)}, u32[]{:S(2)}, u32[]{:S(2)}) collective-permute-start(bf16[64,256]{1,0:T(8,128)(2,1)S(1)} %convolution_convert_fusion.1), channel_id=1, source_target_pairs={{0,2},{1,3},{2,0},{3,1},{4,6},{5,7},{6,4},{7,5},{8,10},{9,11},{10,... | collective-permute-start | bytes 98312 | tf_op jit(solution)/shard_map/ppermute | solution.py:141
  46.0 4.3 %collective-permute-start.13 = (bf16[64,256]{1,0:T(8,128)(2,1)S(1)}, bf16[64,256]{1,0:T(8,128)(2,1)S(1)}, u32[]{:S(2)}, u32[]{:S(2)}) collective-permute-start(bf16[64,256]{1,0:T(8,128)(2,1)S(1)} %convolution_convert_fusion.1), channel_id=1, source_target_pairs={{0,1},{1,0},{2,3},{3,2},{4,5},{5,4},{6,7},{7,6},{8,9},{9,8},{10,11... | collective-permute-start | bytes 98312 | tf_op jit(solution)/shard_map/ppermute | solution.py:141
  50.3 12.3 %copy-start.1 = (bf16[256,256]{1,0:T(8,128)(2,1)}, bf16[256,256]{1,0:T(8,128)(2,1)S(1)}, u32[]{:S(2)}) copy-start(bf16[256,256]{1,0:T(8,128)(2,1)S(1)} %get-tuple-element.8) | copy-start | bytes 393220
  50.6 12.2 %collective-permute-start.21 = (f32[128,256]{1,0:T(8,128)S(1)}, f32[128,256]{1,0:T(8,128)S(1)}, u32[]{:S(2)}, u32[]{:S(2)}) collective-permute-start(f32[128,256]{1,0:T(8,128)S(1)} %slice_select_fusion.1), channel_id=1, source_target_pairs={{0,8},{8,0},{1,9},{9,1},{2,10},{10,2},{3,11},{11,3},{4,12},{12,4},... | collective-permute-start | bytes 393224 | tf_op jit(solution)/shard_map/ppermute | solution.py:118
  62.7 15.6 %collective-permute-start.14 = (f32[512,256]{1,0:T(8,128)S(1)}, f32[512,256]{1,0:T(8,128)S(1)}, u32[]{:S(2)}, u32[]{:S(2)}) collective-permute-start(f32[512,256]{1,0:T(8,128)S(1)} %slice_select_fusion), channel_id=1, source_target_pairs={{0,8},{8,0},{1,9},{9,1},{2,10},{10,2},{3,11},{11,3},{4,12},{12,4},... | collective-permute-start | bytes 1572872 | tf_op jit(solution)/shard_map/ppermute | solution.py:118
  62.8 4.9 %collective-permute-start.22 = (f32[32,256]{1,0:T(8,128)S(1)}, f32[32,256]{1,0:T(8,128)S(1)}, u32[]{:S(2)}, u32[]{:S(2)}) collective-permute-start(f32[32,256]{1,0:T(8,128)S(1)} %get-tuple-element.18), channel_id=1, source_target_pairs={{0,64},{64,128},{128,192},{192,0},{1,65},{65,129},{129,193},{193,1... | collective-permute-start | bytes 98312 | tf_op jit(solution)/shard_map/ppermute | solution.py:118
  64.1 4.3 %collective-permute-start.23 = (f32[32,256]{1,0:T(8,128)S(1)}, f32[32,256]{1,0:T(8,128)S(1)}, u32[]{:S(2)}, u32[]{:S(2)}) collective-permute-start(f32[32,256]{1,0:T(8,128)S(1)} %get-tuple-element.20), channel_id=1, source_target_pairs={{0,128},{64,192},{128,0},{192,64},{1,129},{65,193},{129,1},{193,65... | collective-permute-start | bytes 98312 | tf_op jit(solution)/shard_map/ppermute | solution.py:118
  66.6 3.1 %collective-permute-start.24 = (f32[32,256]{1,0:T(8,128)S(1)}, f32[32,256]{1,0:T(8,128)S(1)}, u32[]{:S(2)}, u32[]{:S(2)}) collective-permute-start(f32[32,256]{1,0:T(8,128)S(1)} %get-tuple-element.19), channel_id=1, source_target_pairs={{0,192},{64,0},{128,64},{192,128},{1,193},{65,1},{129,65},{193,129... | collective-permute-start | bytes 98312 | tf_op jit(solution)/shard_map/ppermute | solution.py:118
  69.6 4.8 %collective-permute-start.25 = (f32[32,256]{1,0:T(8,128)S(1)}, f32[32,256]{1,0:T(8,128)S(1)}, u32[]{:S(2)}, u32[]{:S(2)}) collective-permute-start(f32[32,256]{1,0:T(8,128)S(1)} %fusion.14), channel_id=1, source_target_pairs={{0,16},{16,32},{32,48},{48,0},{1,17},{17,33},{33,49},{49,1},{2,18}... | collective-permute-start | bytes 98312 | tf_op jit(solution)/shard_map/ppermute | solution.py:118
  70.5 4.4 %collective-permute-start.26 = (f32[32,256]{1,0:T(8,128)S(1)}, f32[32,256]{1,0:T(8,128)S(1)}, u32[]{:S(2)}, u32[]{:S(2)}) collective-permute-start(f32[32,256]{1,0:T(8,128)S(1)} %fusion.14), channel_id=1, source_target_pairs={{0,32},{16,48},{32,0},{48,16},{1,33},{17,49},{33,1},{49,17},{2,34}... | collective-permute-start | bytes 98312 | tf_op jit(solution)/shard_map/ppermute | solution.py:118
  71.6 3.2 %collective-permute-start.27 = (f32[32,256]{1,0:T(8,128)S(1)}, f32[32,256]{1,0:T(8,128)S(1)}, u32[]{:S(2)}, u32[]{:S(2)}) collective-permute-start(f32[32,256]{1,0:T(8,128)S(1)} %fusion.14), channel_id=1, source_target_pairs={{0,48},{16,0},{32,16},{48,32},{1,49},{17,1},{33,17},{49,33},{2,50}... | collective-permute-start | bytes 98312 | tf_op jit(solution)/shard_map/ppermute | solution.py:118
  74.9 7.2 %collective-permute-start.28 = (f32[32,256]{1,0:T(8,128)S(1)}, f32[32,256]{1,0:T(8,128)S(1)}, u32[]{:S(2)}, u32[]{:S(2)}) collective-permute-start(f32[32,256]{1,0:T(8,128)S(1)} %add_add_fusion), channel_id=1, source_target_pairs={{0,8},{8,0},{1,9},{9,1},{2,10},{10,2},{3,11},{11,3},{4,12},{12,4},... | collective-permute-start | bytes 98312 | tf_op jit(solution)/shard_map/ppermute | solution.py:118
  78.4 6.3 %collective-permute-start.15 = (f32[128,256]{1,0:T(8,128)S(1)}, f32[128,256]{1,0:T(8,128)S(1)}, u32[]{:S(2)}, u32[]{:S(2)}) collective-permute-start(f32[128,256]{1,0:T(8,128)S(1)} %get-tuple-element.9), channel_id=1, source_target_pairs={{0,64},{64,128},{128,192},{192,0},{1,65},{65,129},{129,193},{193,1... | collective-permute-start | bytes 393224 | tf_op jit(solution)/shard_map/ppermute | solution.py:118
  78.5 10.0 %collective-permute-start.16 = (f32[128,256]{1,0:T(8,128)S(1)}, f32[128,256]{1,0:T(8,128)S(1)}, u32[]{:S(2)}, u32[]{:S(2)}) collective-permute-start(f32[128,256]{1,0:T(8,128)S(1)} %get-tuple-element.11), channel_id=1, source_target_pairs={{0,128},{64,192},{128,0},{192,64},{1,129},{65,193},{129,1},{193,65... | collective-permute-start | bytes 393224 | tf_op jit(solution)/shard_map/ppermute | solution.py:118
  82.0 6.4 %collective-permute-start.17 = (f32[128,256]{1,0:T(8,128)S(1)}, f32[128,256]{1,0:T(8,128)S(1)}, u32[]{:S(2)}, u32[]{:S(2)}) collective-permute-start(f32[128,256]{1,0:T(8,128)S(1)} %get-tuple-element.10), channel_id=1, source_target_pairs={{0,192},{64,0},{128,64},{192,128},{1,193},{65,1},{129,65},{193,129... | collective-permute-start | bytes 393224 | tf_op jit(solution)/shard_map/ppermute | solution.py:118
  82.1 11.0 %collective-permute-start.29 = (f32[64,256]{1,0:T(8,128)S(1)}, f32[64,256]{1,0:T(8,128)S(1)}, u32[]{:S(2)}, u32[]{:S(2)}) collective-permute-start(f32[64,256]{1,0:T(8,128)S(1)} %maximum_select_fusion.refs_0_), channel_id=1, source_target_pairs={{0,64},{64,128},{128,192},{192,0},{1,65},{65,129},{129,193},{193,1... | collective-permute-start | bytes 196616 | tf_op jit(solution)/shard_map/ppermute | solution.py:118
  88.5 18.1 %collective-permute-start.18 = (f32[128,256]{1,0:T(8,128)S(1)}, f32[128,256]{1,0:T(8,128)S(1)}, u32[]{:S(2)}, u32[]{:S(2)}) collective-permute-start(f32[128,256]{1,0:T(8,128)S(1)} %fusion.3), channel_id=1, source_target_pairs={{0,16},{16,32},{32,48},{48,0},{1,17},{17,33},{33,49},{49,1},{2,18}... | collective-permute-start | bytes 393224 | tf_op jit(solution)/shard_map/ppermute | solution.py:118
  90.3 16.3 %collective-permute-start.19 = (f32[128,256]{1,0:T(8,128)S(1)}, f32[128,256]{1,0:T(8,128)S(1)}, u32[]{:S(2)}, u32[]{:S(2)}) collective-permute-start(f32[128,256]{1,0:T(8,128)S(1)} %fusion.3), channel_id=1, source_target_pairs={{0,32},{16,48},{32,0},{48,16},{1,33},{17,49},{33,1},{49,17},{2,34}... | collective-permute-start | bytes 393224 | tf_op jit(solution)/shard_map/ppermute | solution.py:118
  92.4 14.3 %collective-permute-start.20 = (f32[128,256]{1,0:T(8,128)S(1)}, f32[128,256]{1,0:T(8,128)S(1)}, u32[]{:S(2)}, u32[]{:S(2)}) collective-permute-start(f32[128,256]{1,0:T(8,128)S(1)} %fusion.3), channel_id=1, source_target_pairs={{0,48},{16,0},{32,16},{48,32},{1,49},{17,1},{33,17},{49,33},{2,50}... | collective-permute-start | bytes 393224 | tf_op jit(solution)/shard_map/ppermute | solution.py:118
  92.5 4.8 %collective-permute-start.30 = (f32[64,256]{1,0:T(8,128)S(1)}, f32[64,256]{1,0:T(8,128)S(1)}, u32[]{:S(2)}, u32[]{:S(2)}) collective-permute-start(f32[64,256]{1,0:T(8,128)S(1)} %maximum_select_fusion.refs_0_), channel_id=1, source_target_pairs={{0,128},{64,192},{128,0},{192,64},{1,129},{65,193},{129,1},{193,65... | collective-permute-start | bytes 196616 | tf_op jit(solution)/shard_map/ppermute | solution.py:118
  93.1 5.1 %collective-permute-start.31 = (f32[64,256]{1,0:T(8,128)S(1)}, f32[64,256]{1,0:T(8,128)S(1)}, u32[]{:S(2)}, u32[]{:S(2)}) collective-permute-start(f32[64,256]{1,0:T(8,128)S(1)} %maximum_select_fusion.refs_0_), channel_id=1, source_target_pairs={{0,192},{64,0},{128,64},{192,128},{1,193},{65,1},{129,65},{193,129... | collective-permute-start | bytes 196616 | tf_op jit(solution)/shard_map/ppermute | solution.py:118
  107.0 3.9 %collective-permute-start.32 = (bf16[128,256]{1,0:T(8,128)(2,1)S(1)}, bf16[128,256]{1,0:T(8,128)(2,1)S(1)}, u32[]{:S(2)}, u32[]{:S(2)}) collective-permute-start(bf16[128,256]{1,0:T(8,128)(2,1)S(1)} %get-tuple-element.26), channel_id=1, source_target_pairs={{0,64},{64,0},{128,192},{192,128},{1,65},{65,1},{129,193},{193,129... | collective-permute-start | bytes 196616 | tf_op jit(solution)/shard_map/ppermute | solution.py:141
  107.8 4.9 %collective-permute-start.33 = (bf16[128,256]{1,0:T(8,128)(2,1)S(1)}, bf16[128,256]{1,0:T(8,128)(2,1)S(1)}, u32[]{:S(2)}, u32[]{:S(2)}) collective-permute-start(bf16[128,256]{1,0:T(8,128)(2,1)S(1)} %get-tuple-element.26), channel_id=1, source_target_pairs={{0,128},{64,192},{128,0},{192,64},{1,129},{65,193},{129,1},{193,65... | collective-permute-start | bytes 196616 | tf_op jit(solution)/shard_map/ppermute | solution.py:141
  110.3 4.3 %collective-permute-start.34 = (bf16[128,256]{1,0:T(8,128)(2,1)S(1)}, bf16[128,256]{1,0:T(8,128)(2,1)S(1)}, u32[]{:S(2)}, u32[]{:S(2)}) collective-permute-start(bf16[128,256]{1,0:T(8,128)(2,1)S(1)} %get-tuple-element.26), channel_id=1, source_target_pairs={{0,192},{64,128},{128,64},{192,0},{1,193},{65,129},{129,65},{193,1... | collective-permute-start | bytes 196616 | tf_op jit(solution)/shard_map/ppermute | solution.py:141
  114.7 5.2 %collective-permute-start.35 = (bf16[512,256]{1,0:T(8,128)(2,1)S(1)}, bf16[512,256]{1,0:T(8,128)(2,1)S(1)}, u32[]{:S(2)}, u32[]{:S(2)}) collective-permute-start(bf16[512,256]{1,0:T(8,128)(2,1)S(1)} %constant_dynamic-update-slice_fusion.2), channel_id=1, source_target_pairs={{0,8},{8,0},{1,9},{9,1},{2,10},{10,2},{3,11},{11,3},{4,12},{12,4},... | collective-permute-start | bytes 786440 | tf_op jit(solution)/shard_map/ppermute | solution.py:118
  119.9 5.9 %copy-start.2 = (bf16[1024,256]{1,0:T(8,128)(2,1)}, bf16[1024,256]{1,0:T(8,128)(2,1)S(1)}, u32[]{:S(2)}) copy-start(bf16[1024,256]{1,0:T(8,128)(2,1)S(1)} %constant_dynamic-update-slice_fusion) | copy-start | bytes 1572868
  125.8 1.3 collective-permute-start.36
  127.1 3.8 %collective-permute-start.37 = (f32[16,256]{1,0:T(8,128)S(1)}, f32[16,256]{1,0:T(8,128)S(1)}, u32[]{:S(2)}, u32[]{:S(2)}) collective-permute-start(f32[16,256]{1,0:T(8,128)S(1)} %add.197), channel_id=1, source_target_pairs={{0,64},{64,128},{128,192},{192,0},{1,65},{65,129},{129,193},{193,1... | collective-permute-start | bytes 49160 | tf_op jit(solution)/shard_map/ppermute | solution.py:118
  127.1 4.2 %collective-permute-start.38 = (f32[16,256]{1,0:T(8,128)S(1)}, f32[16,256]{1,0:T(8,128)S(1)}, u32[]{:S(2)}, u32[]{:S(2)}) collective-permute-start(f32[16,256]{1,0:T(8,128)S(1)} %add.197), channel_id=1, source_target_pairs={{0,128},{64,192},{128,0},{192,64},{1,129},{65,193},{129,1},{193,65... | collective-permute-start | bytes 49160 | tf_op jit(solution)/shard_map/ppermute | solution.py:118
  128.7 3.3 %collective-permute-start.39 = (f32[16,256]{1,0:T(8,128)S(1)}, f32[16,256]{1,0:T(8,128)S(1)}, u32[]{:S(2)}, u32[]{:S(2)}) collective-permute-start(f32[16,256]{1,0:T(8,128)S(1)} %add.197), channel_id=1, source_target_pairs={{0,192},{64,0},{128,64},{192,128},{1,193},{65,1},{129,65},{193,129... | collective-permute-start | bytes 49160 | tf_op jit(solution)/shard_map/ppermute | solution.py:118
